TPU v7x, 32 devices: a whole 2x2x4 slice. The times are simulated.
32 devices in a mesh: dp: 16 (over z, x, core), tensor: 2 (over y).
Axes of the slice: x: 2, y: 2, z: 4, core: 2. Of those that a mesh axis runs over, the one named last changes fastest.
Arguments:
- tokens: bfloat16 [16, 1024, 768], P('dp'), may hold values from -6 to 6
- lengths: int32 [16], P('dp'), may hold values from 256 to 1024, as said below
- entity_flags: int32 [16, 1024], P('dp'), may hold values 0 or 1
- query_weight: bfloat16 [4, 768, 768], P(None, None, 'tensor'), may hold values from -0.21875 to 0.21875
- query_bias: float32 [4, 768], P(None, 'tensor'), may hold values from -3 to 3
- key_weight: bfloat16 [768, 768], P(None, 'tensor'), may hold values from -0.21875 to 0.21875
- key_bias: float32 [768], P('tensor'), may hold values from -3 to 3
- value_weight: bfloat16 [768, 768], P(None, 'tensor'), may hold values from -0.21875 to 0.21875
- value_bias: float32 [768], P('tensor'), may hold values from -3 to 3
- output_weight: bfloat16 [768, 768], P('tensor'), may hold values from -1.75 to 1.75
- output_bias: float32 [768], replicated, may hold values from -3 to 3
- attn_gain: float32 [768], replicated, may hold values from 0.1 to 1.9
- attn_shift: float32 [768], replicated, may hold values from -3 to 3
- inner_weight: bfloat16 [768, 3072], P(None, 'tensor'), may hold values from -0.21875 to 0.21875
- inner_bias: float32 [3072], P('tensor'), may hold values from -3 to 3
- outer_weight: bfloat16 [3072, 768], P('tensor'), may hold values from -0.109375 to 0.109375
- outer_bias: float32 [768], replicated, may hold values from -3 to 3
- final_gain: float32 [768], replicated, may hold values from 0.1 to 1.9
- final_shift: float32 [768], replicated, may hold values from -3 to 3
- cotangent: bfloat16 [16, 1024, 768], P('dp'), may hold values from -6 to 6
Outputs:
- layer_out: bfloat16 [16, 1024, 768], P('dp')
- input_grad: bfloat16 [16, 1024, 768], P('dp')
- grad_query_weight: float32 [4, 768, 768], P(None, 'dp', 'tensor')
- grad_query_bias: float32 [4, 768], P(None, ('tensor', 'dp'))
- grad_key_weight: float32 [768, 768], P('dp', 'tensor')
- grad_key_bias: float32 [768], P(('tensor', 'dp'))
- grad_value_weight: float32 [768, 768], P('dp', 'tensor')
- grad_value_bias: float32 [768], P(('tensor', 'dp'))
- grad_output_weight: float32 [768, 768], P('tensor', 'dp')
- grad_output_bias: float32 [768], P('dp')
- grad_attn_gain: float32 [768], P('dp')
- grad_attn_shift: float32 [768], P('dp')
- grad_inner_weight: float32 [768, 3072], P('dp', 'tensor')
- grad_inner_bias: float32 [3072], P(('tensor', 'dp'))
- grad_outer_weight: float32 [3072, 768], P('tensor', 'dp')
- grad_outer_bias: float32 [768], P('dp')
- grad_final_gain: float32 [768], P('dp')
- grad_final_shift: float32 [768], P('dp')
Inputs may be any that keep to these rules, and one draw needn't show every extreme that they name: `lengths`: each sequence's number of valid leading slots; some sequence has all 1024.
All inputs are finite; a program needn't handle non-finite values. No bound on the sum of `entity_flags` on one device may be relied on, other than what follows from the above.
Results may differ from a plain program's by a relative error of at most 0.019.
Values sent between devices are 32-bit elements; how exact they have to be, the bound alone decides.
No kernel may reach another device: no remote copies, remote signals or barrier semaphores. Data moves between devices by JAX's collectives and lax.ppermute only.
A program may use at most 192 MiB of HBM per device.

v0:
```python
import math

import jax
import jax.numpy as jnp
from jax import lax
from jax.sharding import PartitionSpec as P

HD = 64


norm_eps = 1e-05


def norm_forward(values, scaling, offset):
    centre = values - jnp.mean(values, axis=-1, keepdims=True)
    spread = jnp.mean(centre * centre, axis=-1, keepdims=True)
    inverse = lax.rsqrt(spread + norm_eps)
    normal = centre * inverse
    return (normal * scaling + offset, normal, inverse)


def norm_backward(upstream, normal, inverse, scaling):
    grad_scaling = jnp.sum(upstream * normal, axis=0)
    grad_offset = jnp.sum(upstream, axis=0)
    scaled = upstream * scaling
    inner_mean = jnp.mean(scaled, axis=-1, keepdims=True)
    cross_mean = jnp.mean(scaled * normal, axis=-1, keepdims=True)
    return (inverse * (scaled - inner_mean - normal * cross_mean), grad_scaling, grad_offset)


def gelu_pair(values):
    cumulative = 0.5 * (1.0 + jax.scipy.special.erf(values * (1.0 / math.sqrt(2.0))))
    density = jnp.exp(-0.5 * values * values) * (1.0 / math.sqrt(2.0 * math.pi))
    return (values * cumulative, cumulative + values * density)


def per_device(
    tokens,
    lengths,
    entity_flags,
    query_weight,
    query_bias,
    key_weight,
    key_bias,
    value_weight,
    value_bias,
    output_weight,
    output_bias,
    attn_gain,
    attn_shift,
    inner_weight,
    inner_bias,
    outer_weight,
    outer_bias,
    final_gain,
    final_shift,
    cotangent,
):
    seq_len = tokens.shape[1]
    local_width = key_weight.shape[1]
    local_heads = local_width // HD
    block_rows = min(512, seq_len)
    blocks = seq_len // block_rows
    score_scale = 1.0 / math.sqrt(HD)
    inputs = tokens[0]
    positions = lax.broadcasted_iota(jnp.int32, (seq_len,), 0)
    live_slot = positions < lengths[0]
    entity_key = entity_flags[0] == 1
    entity_row = entity_key[:, None]
    queries = (
        jnp.einsum("ld,cde->cle", inputs, query_weight, preferred_element_type=jnp.float32)
        + query_bias[:, None, :]
    ).astype(jnp.bfloat16)
    key_rows = (jnp.dot(inputs, key_weight, preferred_element_type=jnp.float32) + key_bias).astype(
        jnp.bfloat16
    )
    value_rows = (
        jnp.dot(inputs, value_weight, preferred_element_type=jnp.float32) + value_bias
    ).astype(jnp.bfloat16)
    to_word = jnp.where(entity_row, queries[2], queries[0])
    to_entity = jnp.where(entity_row, queries[3], queries[1])
    keys_heads = key_rows.reshape(seq_len, local_heads, HD)
    values_heads = value_rows.reshape(seq_len, local_heads, HD)
    word_blocks = to_word.reshape(blocks, block_rows, local_heads, HD)
    entity_blocks = to_entity.reshape(blocks, block_rows, local_heads, HD)

    def block_scores(word_block, entity_block):
        word_scores = jnp.einsum(
            "qhe,khe->hqk", word_block, keys_heads, preferred_element_type=jnp.float32
        )
        entity_scores = jnp.einsum(
            "qhe,khe->hqk", entity_block, keys_heads, preferred_element_type=jnp.float32
        )
        selected = jnp.where(entity_key[None, None, :], entity_scores, word_scores) * score_scale
        return jnp.where(live_slot[None, None, :], selected, -jnp.inf)

    def forward_block(operands):
        word_block, entity_block = operands
        masked = block_scores(word_block, entity_block)
        row_max = jnp.max(masked, axis=-1, keepdims=True)
        weights = jnp.exp(masked - row_max)
        row_total = jnp.sum(weights, axis=-1, keepdims=True)
        attn_probs = (weights / row_total).astype(jnp.bfloat16)
        context_block = jnp.einsum(
            "hqk,khe->qhe", attn_probs, values_heads, preferred_element_type=jnp.float32
        )
        return (context_block.astype(jnp.bfloat16), row_max + jnp.log(row_total))

    context_blocks, log_totals = lax.map(forward_block, (word_blocks, entity_blocks))
    context = context_blocks.reshape(seq_len, local_width)
    attn_part = jnp.dot(context, output_weight, preferred_element_type=jnp.float32)
    attn_out = lax.psum(attn_part, "tensor")
    first_sum = attn_out + output_bias + inputs.astype(jnp.float32)
    normed, first_normal, first_inverse = norm_forward(first_sum, attn_gain, attn_shift)
    normed_low = normed.astype(jnp.bfloat16)
    inner_pre = jnp.dot(normed_low, inner_weight, preferred_element_type=jnp.float32) + inner_bias
    activated, gelu_slope = gelu_pair(inner_pre)
    hidden = activated.astype(jnp.bfloat16)
    ffn_part = jnp.dot(hidden, outer_weight, preferred_element_type=jnp.float32)
    ffn_out = lax.psum(ffn_part, "tensor")
    second_sum = ffn_out + outer_bias + normed
    result, second_normal, second_inverse = norm_forward(second_sum, final_gain, final_shift)
    layer_out = jnp.where(live_slot[:, None], result, 0.0).astype(jnp.bfloat16)
    upstream = jnp.where(live_slot[:, None], cotangent[0].astype(jnp.float32), 0.0)
    grad_second, grad_final_gain, grad_final_shift = norm_backward(
        upstream, second_normal, second_inverse, final_gain
    )
    grad_outer_bias = jnp.sum(grad_second, axis=0)
    grad_ffn = grad_second.astype(jnp.bfloat16)
    grad_outer_weight = jnp.einsum(
        "lf,ld->fd", hidden, grad_ffn, preferred_element_type=jnp.float32
    )
    grad_hidden = jnp.einsum(
        "ld,fd->lf", grad_ffn, outer_weight, preferred_element_type=jnp.float32
    )
    grad_inner = (grad_hidden * gelu_slope).astype(jnp.bfloat16)
    grad_inner_bias = jnp.sum(grad_inner.astype(jnp.float32), axis=0)
    grad_inner_weight = jnp.einsum(
        "ld,lf->df", normed_low, grad_inner, preferred_element_type=jnp.float32
    )
    normed_part = jnp.einsum(
        "lf,df->ld", grad_inner, inner_weight, preferred_element_type=jnp.float32
    )
    grad_normed = lax.psum(normed_part, "tensor") + grad_second
    grad_first, grad_attn_gain, grad_attn_shift = norm_backward(
        grad_normed, first_normal, first_inverse, attn_gain
    )
    grad_output_bias = jnp.sum(grad_first, axis=0)
    grad_attn = grad_first.astype(jnp.bfloat16)
    grad_output_weight = jnp.einsum(
        "lh,ld->hd", context, grad_attn, preferred_element_type=jnp.float32
    )
    grad_context = jnp.einsum(
        "ld,hd->lh", grad_attn, output_weight, preferred_element_type=jnp.float32
    ).astype(jnp.bfloat16)
    context_grad_blocks = grad_context.reshape(blocks, block_rows, local_heads, HD)

    def backward_block(running, pieces):
        key_sum, value_sum = running
        word_block, entity_block, grad_block, log_total = pieces
        masked = block_scores(word_block, entity_block)
        attn_probs = jnp.exp(masked - log_total)
        grad_probs = jnp.einsum(
            "qhe,khe->hqk", grad_block, values_heads, preferred_element_type=jnp.float32
        )
        inner_sum = jnp.sum(attn_probs * grad_probs, axis=-1, keepdims=True)
        grad_scores = (attn_probs * (grad_probs - inner_sum) * score_scale).astype(jnp.bfloat16)
        zero_scores = jnp.zeros_like(grad_scores)
        grad_entity = jnp.where(entity_key[None, None, :], grad_scores, zero_scores)
        grad_word = jnp.where(entity_key[None, None, :], zero_scores, grad_scores)
        value_sum = value_sum + jnp.einsum(
            "hqk,qhe->khe",
            attn_probs.astype(jnp.bfloat16),
            grad_block,
            preferred_element_type=jnp.float32,
        )
        key_sum = (
            key_sum
            + jnp.einsum("hqk,qhe->khe", grad_word, word_block, preferred_element_type=jnp.float32)
            + jnp.einsum(
                "hqk,qhe->khe", grad_entity, entity_block, preferred_element_type=jnp.float32
            )
        )
        word_query = jnp.einsum(
            "hqk,khe->qhe", grad_word, keys_heads, preferred_element_type=jnp.float32
        )
        entity_query = jnp.einsum(
            "hqk,khe->qhe", grad_entity, keys_heads, preferred_element_type=jnp.float32
        )
        return (
            (key_sum, value_sum),
            (word_query.astype(jnp.bfloat16), entity_query.astype(jnp.bfloat16)),
        )

    zero_state = jnp.zeros((seq_len, local_heads, HD), jnp.float32)
    (key_sums, value_sums), (word_grads, entity_grads) = lax.scan(
        backward_block,
        (zero_state, zero_state),
        (word_blocks, entity_blocks, context_grad_blocks, log_totals),
    )
    grad_keys = key_sums.reshape(seq_len, local_width).astype(jnp.bfloat16)
    grad_values = value_sums.reshape(seq_len, local_width).astype(jnp.bfloat16)
    grad_to_word = word_grads.reshape(seq_len, local_width)
    grad_to_entity = entity_grads.reshape(seq_len, local_width)
    zero_rows = jnp.zeros_like(grad_to_word)
    grad_queries = jnp.stack(
        [
            jnp.where(entity_row, zero_rows, grad_to_word),
            jnp.where(entity_row, zero_rows, grad_to_entity),
            jnp.where(entity_row, grad_to_word, zero_rows),
            jnp.where(entity_row, grad_to_entity, zero_rows),
        ]
    )
    grad_query_weight = jnp.einsum(
        "ld,cle->cde", inputs, grad_queries, preferred_element_type=jnp.float32
    )
    grad_query_bias = jnp.sum(grad_queries.astype(jnp.float32), axis=1)
    grad_key_weight = jnp.einsum("ld,le->de", inputs, grad_keys, preferred_element_type=jnp.float32)
    grad_key_bias = jnp.sum(grad_keys.astype(jnp.float32), axis=0)
    grad_value_weight = jnp.einsum(
        "ld,le->de", inputs, grad_values, preferred_element_type=jnp.float32
    )
    grad_value_bias = jnp.sum(grad_values.astype(jnp.float32), axis=0)
    input_part = (
        jnp.einsum("cle,cde->ld", grad_queries, query_weight, preferred_element_type=jnp.float32)
        + jnp.einsum("le,de->ld", grad_keys, key_weight, preferred_element_type=jnp.float32)
        + jnp.einsum("le,de->ld", grad_values, value_weight, preferred_element_type=jnp.float32)
    )
    input_grad = (lax.psum(input_part, "tensor") + grad_first).astype(jnp.bfloat16)
    shards = tuple(
        (
            lax.psum_scatter(grad_query_weight, "dp", scatter_dimension=1, tiled=True),
            lax.psum_scatter(grad_query_bias, "dp", scatter_dimension=1, tiled=True),
            lax.psum_scatter(grad_key_weight, "dp", scatter_dimension=0, tiled=True),
            lax.psum_scatter(grad_key_bias, "dp", scatter_dimension=0, tiled=True),
            lax.psum_scatter(grad_value_weight, "dp", scatter_dimension=0, tiled=True),
            lax.psum_scatter(grad_value_bias, "dp", scatter_dimension=0, tiled=True),
            lax.psum_scatter(grad_output_weight, "dp", scatter_dimension=1, tiled=True),
            lax.psum_scatter(grad_output_bias, "dp", scatter_dimension=0, tiled=True),
            lax.psum_scatter(grad_attn_gain, "dp", scatter_dimension=0, tiled=True),
            lax.psum_scatter(grad_attn_shift, "dp", scatter_dimension=0, tiled=True),
            lax.psum_scatter(grad_inner_weight, "dp", scatter_dimension=0, tiled=True),
            lax.psum_scatter(grad_inner_bias, "dp", scatter_dimension=0, tiled=True),
            lax.psum_scatter(grad_outer_weight, "dp", scatter_dimension=1, tiled=True),
            lax.psum_scatter(grad_outer_bias, "dp", scatter_dimension=0, tiled=True),
            lax.psum_scatter(grad_final_gain, "dp", scatter_dimension=0, tiled=True),
            lax.psum_scatter(grad_final_shift, "dp", scatter_dimension=0, tiled=True),
        )
    )
    return (
        layer_out[None],
        input_grad[None],
        shards[0],
        shards[1],
        shards[2],
        shards[3],
        shards[4],
        shards[5],
        shards[6],
        shards[7],
        shards[8],
        shards[9],
        shards[10],
        shards[11],
        shards[12],
        shards[13],
        shards[14],
        shards[15],
    )


def solution(mesh):
    return jax.shard_map(
        per_device,
        mesh=mesh,
        in_specs=(
            P("dp", None, None),
            P("dp"),
            P("dp", None),
            P(None, None, "tensor"),
            P(None, "tensor"),
            P(None, "tensor"),
            P("tensor"),
            P(None, "tensor"),
            P("tensor"),
            P("tensor", None),
            P(),
            P(),
            P(),
            P(None, "tensor"),
            P("tensor"),
            P("tensor", None),
            P(),
            P(),
            P(),
            P("dp", None, None),
        ),
        out_specs=(
            P("dp", None, None),
            P("dp", None, None),
            P(None, "dp", "tensor"),
            P(None, ("tensor", "dp")),
            P("dp", "tensor"),
            P(("tensor", "dp")),
            P("dp", "tensor"),
            P(("tensor", "dp")),
            P("tensor", "dp"),
            P("dp"),
            P("dp"),
            P("dp"),
            P("dp", "tensor"),
            P(("tensor", "dp")),
            P("tensor", "dp"),
            P("dp"),
            P("dp"),
            P("dp"),
        ),
        check_vma=False,
    )
```

profile of v0, /device:TPU:0, one launch (start us, length us, event | category | flops | bytes accessed | tf_op | source)
XLA Modules:
  0.0 1180.1 jit_solution(7626846847422397774)
XLA Ops:
  33.1 41.7 %while.30 = (s32[]{:T(128)}, bf16[2,512,6,64]{1,3,2,0:T(8,128)(2,1)}, f32[2,6,512,1]{2,1,3,0:T(8,128)S(1)}, pred[1024]{0:T(1024)(128)(4,1)S(1)}, bf16[2,512,6,64...) while((s32[]{:T(128)}, ...), condition=%wide.region_3.4_spmd.clone, body=%wide.region_0.3_spmd.clone.sunk | while | flops 1236465664 | bytes 79158520 | solution.py:109
  80.6 88.6 %all-reduce.18.cloned.1.call-done = f32[1024,768]{1,0:T(8,128)} async-done(((f32[1024,768]{1,0:T(8,128)}), f32[1024,768]{1,0:T(8,128)}) %all-reduce.18.cloned.1.call-update) | async-done | bytes 3145744 | tf_op jit(solution)/shard_map/psum | solution.py:112
  184.7 85.2 %all-reduce.20.cloned.1.call-done = f32[1024,768]{1,0:T(8,128)} async-done(((f32[1024,768]{1,0:T(8,128)}), f32[1024,768]{1,0:T(8,128)}) %all-reduce.20.cloned.1.call-update) | async-done | bytes 3145744 | tf_op jit(solution)/shard_map/psum | solution.py:120
  292.7 85.9 %all-reduce.22.cloned.1.call-done = f32[1024,768]{1,0:T(8,128)} async-done(((f32[1024,768]{1,0:T(8,128)}), f32[1024,768]{1,0:T(8,128)}) %all-reduce.22.cloned.1.call-update) | async-done | bytes 3145744 | tf_op jit(solution)/shard_map/psum | solution.py:144
  398.9 199.5 %while.31 = (s32[]{:T(128)}, f32[1024,6,64]{0,2,1:T(8,128)}, f32[1024,6,64]{0,2,1:T(8,128)S(1)}, bf16[2,512,6,64]{1,3,2,0:T(8,128)(2,1)}, bf16[2,512,6,64]{1,3,2...) while((s32[]{:T(128)}, f32[1024,6,64]{0,2,1:T(8,128)}, ...), condition=%wide.region_17.18_spmd.clone, body=%wide.region_15.17_spmd.clone.sunk | while | flops 3314828288 | bytes 283950304 | solution.py:196
  399.7 7.6 fusion.247
  415.4 19.3 %fusion.250 = bf16[2,512,6,64]{1,3,2,0:T(8,128)(2,1)} fusion(bf16[2,512,6,64]{1,3,2,0:T(8,128)(2,1)} %get-tuple-element.584, s32[]{:T(128)S(6)} %copy.121, bf16[1024,6,64]{0,2,1:T(8,128)(2,1)S(1)} %get-tuple-element.603, pred[1024]{0:T(1024)(128)(4,1)S(1)} %get-tuple-element.601, f32[6,512,1024]{2,1,0:T(8,128)} %subtract_exponential_fusion.3, ...), kind=kOutput, calls=%fused_computation.44.clone.1 | convolution fusion | flops 421728256 | bytes 51512324 | tf_op jit(solution)/shard_map/while/body/eval_jaxpr/hqk,khe->qhe/dot_general | solution.py:187
  434.7 19.3 %fusion.249 = bf16[2,512,6,64]{1,3,2,0:T(8,128)(2,1)} fusion(bf16[2,512,6,64]{1,3,2,0:T(8,128)(2,1)} %get-tuple-element.583, s32[]{:T(128)S(6)} %copy.121, bf16[1024,6,64]{0,2,1:T(8,128)(2,1)S(1)} %get-tuple-element.603, pred[1024]{0:T(1024)(128)(4,1)S(1)} %get-tuple-element.601, f32[6,512,1024]{2,1,0:T(8,128)} %subtract_exponential_fusion.3, ...), kind=kOutput, calls=%fused_computation.42.clone.1 | convolution fusion | flops 421728256 | bytes 51512324 | tf_op jit(solution)/shard_map/while/body/eval_jaxpr/hqk,khe->qhe/dot_general | solution.py:184
  460.1 19.5 %fusion.248 = f32[6,64,1024]{2,1,0:T(8,128)} fusion(pred[1024]{0:T(1024)(128)(4,1)S(1)} %get-tuple-element.601, f32[6,512,1024]{2,1,0:T(8,128)} %subtract_exponential_fusion.3, f32[6,512,1024]{2,1,0:T(8,128)} %fusion.247, bf16[2,512,6,64]{1,3,2,0:T(8,128)(2,1)} %get-tuple-element.600, s32[]{:T(128)S(6)} %copy.121), kind=kOutput, calls=%fused_computation.29.clone.1 | convolution fusion | flops 421531648 | bytes 52298756 | tf_op jit(solution)/shard_map/while/body/eval_jaxpr/hqk,qhe->khe/dot_general | solution.py:179
  479.6 18.8 %bitcast_add_fusion.6 = f32[1024,6,64]{0,2,1:T(8,128)} fusion(f32[6,64,1024]{2,1,0:T(8,128)} %fusion.248, f32[1024,6,64]{0,2,1:T(8,128)} %get-tuple-element.581, pred[1024]{0:T(1024)(128)(4,1)S(1)} %get-tuple-element.601, f32[6,512,1024]{2,1,0:T(8,128)} %subtract_exponential_fusion.3, f32[6,512,1024]{2,1,0:T(8,128)} %fusion.247, pred[]{:T(512)S(6)} %compare.3, ...), kind=kOutput, calls=%fused_computation.37.clone.1 | convolution fusion | flops 422711296 | bytes 55444484 | tf_op jit(solution)/shard_map/while/body/eval_jaxpr/hqk,qhe->khe/dot_general | solution.py:180
  499.1 7.6 fusion.247
  514.8 19.3 %fusion.250 = bf16[2,512,6,64]{1,3,2,0:T(8,128)(2,1)} fusion(bf16[2,512,6,64]{1,3,2,0:T(8,128)(2,1)} %get-tuple-element.584, s32[]{:T(128)S(6)} %copy.121, bf16[1024,6,64]{0,2,1:T(8,128)(2,1)S(1)} %get-tuple-element.603, pred[1024]{0:T(1024)(128)(4,1)S(1)} %get-tuple-element.601, f32[6,512,1024]{2,1,0:T(8,128)} %subtract_exponential_fusion.3, ...), kind=kOutput, calls=%fused_computation.44.clone.1 | convolution fusion | flops 421728256 | bytes 51512324 | tf_op jit(solution)/shard_map/while/body/eval_jaxpr/hqk,khe->qhe/dot_general | solution.py:187
  534.0 19.3 %fusion.249 = bf16[2,512,6,64]{1,3,2,0:T(8,128)(2,1)} fusion(bf16[2,512,6,64]{1,3,2,0:T(8,128)(2,1)} %get-tuple-element.583, s32[]{:T(128)S(6)} %copy.121, bf16[1024,6,64]{0,2,1:T(8,128)(2,1)S(1)} %get-tuple-element.603, pred[1024]{0:T(1024)(128)(4,1)S(1)} %get-tuple-element.601, f32[6,512,1024]{2,1,0:T(8,128)} %subtract_exponential_fusion.3, ...), kind=kOutput, calls=%fused_computation.42.clone.1 | convolution fusion | flops 421728256 | bytes 51512324 | tf_op jit(solution)/shard_map/while/body/eval_jaxpr/hqk,khe->qhe/dot_general | solution.py:184
  559.4 19.5 %fusion.248 = f32[6,64,1024]{2,1,0:T(8,128)} fusion(pred[1024]{0:T(1024)(128)(4,1)S(1)} %get-tuple-element.601, f32[6,512,1024]{2,1,0:T(8,128)} %subtract_exponential_fusion.3, f32[6,512,1024]{2,1,0:T(8,128)} %fusion.247, bf16[2,512,6,64]{1,3,2,0:T(8,128)(2,1)} %get-tuple-element.600, s32[]{:T(128)S(6)} %copy.121), kind=kOutput, calls=%fused_computation.29.clone.1 | convolution fusion | flops 421531648 | bytes 52298756 | tf_op jit(solution)/shard_map/while/body/eval_jaxpr/hqk,qhe->khe/dot_general | solution.py:179
  578.9 19.3 %bitcast_add_fusion.6 = f32[1024,6,64]{0,2,1:T(8,128)} fusion(f32[6,64,1024]{2,1,0:T(8,128)} %fusion.248, f32[1024,6,64]{0,2,1:T(8,128)} %get-tuple-element.581, pred[1024]{0:T(1024)(128)(4,1)S(1)} %get-tuple-element.601, f32[6,512,1024]{2,1,0:T(8,128)} %subtract_exponential_fusion.3, f32[6,512,1024]{2,1,0:T(8,128)} %fusion.247, pred[]{:T(512)S(6)} %compare.3, ...), kind=kOutput, calls=%fused_computation.37.clone.1 | convolution fusion | flops 422711296 | bytes 55444484 | tf_op jit(solution)/shard_map/while/body/eval_jaxpr/hqk,qhe->khe/dot_general | solution.py:180
  652.0 7.8 fusion.144
  660.5 8.0 fusion.147
  672.4 62.3 %all-reduce.11 = (f32[4,384]{1,0:T(4,128)S(1)}, f32[384]{0:T(512)S(1)}, f32[384]{0:T(512)S(1)}, f32[768]{0:T(1024)S(1)}, f32[768]{0:T(1024)S(1)}, /*index=5*/f32...) all-reduce(f32[4,384]{1,0:T(4,128)S(1)} %convert_reduce_fusion.1, ...), channel_id=3, replica_groups=mesh['dp'=16,'tensor'=2] {'dp'}, use_global_device_ids=true, to_apply=%region_21.22.clone | all-reduce | flops 8448 | bytes 67584
  743.7 85.9 %all-reduce.24.cloned.1.call-done = f32[1024,768]{1,0:T(8,128)} async-done(((f32[1024,768]{1,0:T(8,128)}), f32[1024,768]{1,0:T(8,128)}) %all-reduce.24.cloned.1.call-update) | async-done | bytes 3145744 | tf_op jit(solution)/shard_map/psum | solution.py:229
  833.9 57.9 %reduce-scatter.11.cloned.1.call-done = f32[384,48]{0,1:T(8,128)} async-done(((f32[384,768]{0,1:T(8,128)}), f32[384,48]{0,1:T(8,128)}) %reduce-scatter.11.cloned.1.call-update) | async-done | bytes 73744 | tf_op jit(solution)/shard_map/reduce_scatter | solution.py:238
  891.8 61.3 %reduce-scatter.19.cloned.1.call-done = f32[48,384]{1,0:T(8,128)} async-done(((f32[768,384]{1,0:T(8,128)}), f32[48,384]{1,0:T(8,128)}) %reduce-scatter.19.cloned.1.call-update) | async-done | bytes 73744
  953.1 61.3 %reduce-scatter.17.cloned.1.call-done = f32[48,384]{1,0:T(8,128)} async-done(((f32[768,384]{1,0:T(8,128)}), f32[48,384]{1,0:T(8,128)}) %reduce-scatter.17.cloned.1.call-update) | async-done | bytes 73744
  1014.4 79.0 %reduce-scatter.15.cloned.1.call-done = f32[1536,48]{0,1:T(8,128)} async-done(((f32[1536,768]{0,1:T(8,128)}), f32[1536,48]{0,1:T(8,128)}) %reduce-scatter.15.cloned.1.call-update) | async-done | bytes 294928 | tf_op jit(solution)/shard_map/reduce_scatter | solution.py:244
  1093.4 79.4 %reduce-scatter.13.cloned.1.call-done = f32[48,1536]{1,0:T(8,128)} async-done(((f32[768,1536]{1,0:T(8,128)}), f32[48,1536]{1,0:T(8,128)}) %reduce-scatter.13.cloned.1.call-update) | async-done | bytes 294928 | tf_op jit(solution)/shard_map/reduce_scatter | solution.py:242
  (276 shorter events, 229.2 us)
Async XLA Ops:
  7.2 165.4 %copy-start = (bf16[768,1536]{1,0:T(8,128)(2,1)S(1)}, bf16[768,1536]{1,0:T(8,128)(2,1)}, u32[]{:S(2)}) copy-start(bf16[768,1536]{1,0:T(8,128)(2,1)} %param.37) | copy-start | bytes 7077892
  7.2 162.0 %all-reduce.18.cloned.1.call-start = ((), (), s32[]{:S(2)}) async-start(), calls=%async_computation.5 | async-start | bytes 6291456 | tf_op jit(solution)/shard_map/psum | solution.py:112
  14.7 11.4 copy-start.64
  33.8 7.4 copy-start.6
  54.4 7.4 copy-start.6
  77.9 91.3 %copy-start.55 = (f32[768]{0:T(1024)S(1)}, f32[768]{0:T(1024)}, u32[]{:S(2)}) copy-start(f32[768]{0:T(1024)} %param.34) | copy-start | bytes 9220
  80.6 189.4 %all-reduce.20.cloned.1.call-start = ((), (), s32[]{:S(2)}) async-start(), calls=%async_computation.6 | async-start | bytes 6291456 | tf_op jit(solution)/shard_map/psum | solution.py:120
  172.1 6.0 copy-start.2
  172.1 211.8 %copy-start.41 = (f32[1024]{0:T(1024)}, f32[1024]{0:T(1024)S(1)}, u32[]{:S(2)}) copy-start(f32[1024]{0:T(1024)S(1)} %broadcast_multiply_fusion.5) | copy-start | bytes 12292
  172.9 211.1 %copy-start.43 = (f32[1024]{0:T(1024)}, f32[1024]{0:T(1024)S(1)}, u32[]{:S(2)}) copy-start(f32[1024]{0:T(1024)S(1)} %add_rsqrt_fusion.1) | copy-start | bytes 12292
  172.9 6.8 copy-start.60
  184.0 86.0 %copy-start.56 = (f32[768]{0:T(1024)S(1)}, f32[768]{0:T(1024)}, u32[]{:S(2)}) copy-start(f32[768]{0:T(1024)} %param.40) | copy-start | bytes 9220
  184.0 194.5 %all-reduce.22.cloned.1.call-start = ((), (), s32[]{:S(2)}) async-start(), calls=%async_computation.7 | async-start | bytes 6291456 | tf_op jit(solution)/shard_map/psum | solution.py:144
  269.9 11.2 slice-start
  292.6 449.4 %all-reduce.26.cloned.1.call-start = ((), (), s32[]{:S(2)}) async-start(), calls=%async_computation.14 | async-start | bytes 9437184
  389.2 9.7 copy-start.5
  624.5 205.2 %all-reduce.24.cloned.1.call-start = ((), (), s32[]{:S(2)}) async-start(), calls=%async_computation.8 | async-start | bytes 6291456 | tf_op jit(solution)/shard_map/psum | solution.py:229
  634.7 257.1 %reduce-scatter.11.cloned.1.call-start = ((), (), s32[]{:S(2)}) async-start(), calls=%async_computation.9 | async-start | bytes 1253376 | tf_op jit(solution)/shard_map/reduce_scatter | solution.py:238
  639.9 6.2 copy-start.31
  639.9 313.3 %reduce-scatter.19.cloned.1.call-start = ((), (), s32[]{:S(2)}) async-start(), calls=%async_computation.13 | async-start | bytes 1253376
  646.0 368.5 %reduce-scatter.17.cloned.1.call-start = ((), (), s32[]{:S(2)}) async-start(), calls=%async_computation.12 | async-start | bytes 1253376
  652.0 441.5 %reduce-scatter.15.cloned.1.call-start = ((), (), s32[]{:S(2)}) async-start(), calls=%async_computation.11 | async-start | bytes 5013504 | tf_op jit(solution)/shard_map/reduce_scatter | solution.py:244
  659.9 513.0 %reduce-scatter.13.cloned.1.call-start = ((), (), s32[]{:S(2)}) async-start(), calls=%async_computation.10 | async-start | bytes 5013504 | tf_op jit(solution)/shard_map/reduce_scatter | solution.py:242
  743.0 429.9 %copy-start.1 = (bf16[768,1536]{1,0:T(8,128)(2,1)S(1)}, bf16[768,1536]{1,0:T(8,128)(2,1)}, u32[]{:S(2)}) copy-start(bf16[768,1536]{1,0:T(8,128)(2,1)} %param.37) | copy-start | bytes 7077892
  (62 other events, 151.6 us)
Sparse Core Ops, SparseCore 0:
  80.7 88.4 all-reduce.17
  184.1 85.7 all-reduce.19
  292.7 85.7 all-reduce.21
  624.6 117.3 all-reduce.25
  744.2 85.3 all-reduce.23
  833.7 58.0 reduce-scatter.10
  896.0 57.0 reduce-scatter.18
  957.3 57.0 reduce-scatter.16
  1018.9 74.5 reduce-scatter.14
  1098.2 74.5 reduce-scatter.12
where the time goes:
time: 1180 us
  waiting for transfers between devices  686 us (58%)
  matrix products  302 us (26%)
  local copies, waits for them, and re-layouts  72.1 us (6%)
  blocking collectives  62.3 us (5%)
  other arithmetic  38 us (3%)
  between operations  17.9 us (2%)
    unnamed x13, waiting for transfers between devices  124 us
    psum x1, waiting for transfers between devices, per_device(): attn_out = lax.psum(attn_part, 'tensor')  88.6 us
    psum x1, waiting for transfers between devices, per_device(): lax.psum(input_part, 'tensor') + grad_first  85.9 us
    psum x1, waiting for transfers between devices, per_device(): grad_normed = lax.psum(normed_part, 'tensor') + grad_second  85.9 us
    psum x1, waiting for transfers between devices, per_device(): ffn_out = lax.psum(ffn_part, 'tensor')  85.2 us
    reduce_scatter x1, waiting for transfers between devices, per_device(): lax.psum_scatter(grad_inner_weight, 'dp', scatter_dimension=0, tiled=True)  79.4 us
    reduce_scatter x1, waiting for transfers between devices, per_device(): lax.psum_scatter(grad_outer_weight, 'dp', scatter_dimension=1, tiled=True)  79 us
    unnamed x1, blocking collectives  62.3 us
  transfers between devices with their start and end apart: 10, of which 10 were waited for; matrix products, arithmetic and copies ran while one was open for 4% of the time, Pallas kernels for 0%

commit v1 on v0

v1 whole, which is shorter than its diff:
```python
import functools
import math

import jax
import jax.numpy as jnp
from jax import lax
from jax.experimental import pallas as pl
from jax.experimental.pallas import tpu as pltpu
from jax.sharding import PartitionSpec as P

HD = 64
SLICES = 8
MASKED = -1e30
NORM_EPS = 1e-05

F32 = jnp.float32
BF16 = jnp.bfloat16
NN = (((1,), (0,)), ((), ()))
NT = (((1,), (1,)), ((), ()))
TN = (((0,), (0,)), ((), ()))


def mm(left, right, dims):
    return lax.dot_general(left, right, dims, preferred_element_type=F32)


def struct(shape, kind):
    return jax.ShapeDtypeStruct(shape, kind)


def params(mib):
    return pltpu.CompilerParams(vmem_limit_bytes=mib << 20)


def cost(flops, moved, special=0):
    return pl.CostEstimate(flops=int(flops), bytes_accessed=int(moved), transcendentals=int(special))


def whole_block(shape):
    return pl.BlockSpec(shape, lambda *_: (0,) * len(shape), pipeline_mode=pl.Buffered(1))


def three_pieces(value):
    high = value.astype(BF16).astype(F32)
    rest = value - high
    middle = rest.astype(BF16).astype(F32)
    return high, middle, rest - middle


def project_kernel(x_ref, kind_ref, wq_ref, bq_ref, wk_ref, bk_ref, wv_ref, bv_ref, q2_ref, k2_ref, v_ref):
    x = x_ref[...]
    entity = kind_ref[...] > 0.5
    rows = x.shape[0]
    width = wk_ref.shape[1]

    def query(c):
        return mm(x, wq_ref[c], NN) + bq_ref[c : c + 1, :]

    scale = 1.0 / math.sqrt(HD)
    to_word = jnp.where(entity, query(2), query(0)).astype(BF16).astype(F32) * scale
    to_entity = jnp.where(entity, query(3), query(1)).astype(BF16).astype(F32) * scale
    keys = (mm(x, wk_ref[...], NN) + bk_ref[...]).astype(BF16).astype(F32)
    v_ref[...] = (mm(x, wv_ref[...], NN) + bv_ref[...]).astype(BF16)
    left = lax.broadcasted_iota(jnp.int32, (rows, 2 * HD), 1) < HD
    held = left != entity
    for p in range(width // (2 * HD)):
        cols = slice(2 * HD * p, 2 * HD * (p + 1))
        w, e, k = to_word[:, cols], to_entity[:, cols], keys[:, cols]
        w_roll, e_roll, k_roll = (pltpu.roll(t, HD, 1) for t in (w, e, k))
        even = slice(4 * HD * p, 4 * HD * p + 2 * HD)
        odd = slice(4 * HD * p + 2 * HD, 4 * HD * (p + 1))
        q2_ref[:, even] = jnp.where(left, w, e_roll).astype(BF16)
        q2_ref[:, odd] = jnp.where(left, w_roll, e).astype(BF16)
        k2_ref[:, even] = jnp.where(held, jnp.where(left, k, k_roll), 0.0).astype(BF16)
        k2_ref[:, odd] = jnp.where(held, jnp.where(left, k_roll, k), 0.0).astype(BF16)


def project(x, kind, wq, bq, wk, bk, wv, bv, rows=256):
    length, model = x.shape
    width = wk.shape[1]
    rows = min(rows, length)
    tile = lambda w: pl.BlockSpec((rows, w), lambda i: (i, 0))
    return pl.pallas_call(
        project_kernel,
        grid=(length // rows,),
        in_specs=[
            tile(model),
            tile(1),
            whole_block(wq.shape),
            whole_block(bq.shape),
            whole_block(wk.shape),
            whole_block((1, width)),
            whole_block(wv.shape),
            whole_block((1, width)),
        ],
        out_specs=[tile(2 * width), tile(2 * width), tile(width)],
        out_shape=[
            struct((length, 2 * width), BF16),
            struct((length, 2 * width), BF16),
            struct((length, width), BF16),
        ],
        compiler_params=params(48),
        cost_estimate=cost(12 * length * model * width, 16 * model * width + 12 * length * width),
        name="project",
    )(x, kind, wq, bq, wk, bk.reshape(1, width), wv, bv.reshape(1, width))


def key_extra(live, rows):
    lane = lax.broadcasted_iota(jnp.int32, (rows, 2 * HD), 1)
    return jnp.where(
        lane == 0, jnp.where(live, 0.0, MASKED), jnp.where(lane < 4, 1.0, 0.0)
    ).astype(BF16)


def attend_kernel(block, q2_ref, k2_ref, v_ref, live_ref, out_ref, extra_ref):
    length = k2_ref.shape[0]
    total = q2_ref.shape[0]
    extra = key_extra(live_ref[...] > 0.5, length)
    turned = v_ref[...].astype(F32).T.astype(BF16)
    lane = lax.broadcasted_iota(jnp.int32, (block, 2 * HD), 1)
    one = jnp.where(lane == 0, 1.0, 0.0).astype(BF16)
    keys = [
        jnp.concatenate([k2_ref[:, 2 * HD * h : 2 * HD * (h + 1)], extra], axis=1) for h in range(2)
    ]
    for i in range(total // block):
        rows = slice(i * block, (i + 1) * block)
        outs = []
        for h in range(2):
            cols = slice(2 * HD * h, 2 * HD * (h + 1))
            query = jnp.concatenate([q2_ref[rows, cols], one], axis=1)
            scores = mm(keys[h], query, NT)
            top = jnp.max(scores, axis=0, keepdims=True)
            weights = jnp.exp(scores - top)
            norm = jnp.sum(weights, axis=0, keepdims=True)
            summed = mm(turned[HD * h : HD * (h + 1)], weights.astype(BF16), NN)
            outs.append(summed * (1.0 / norm))
            pieces = three_pieces(-(top + jnp.log(norm)))
            filled = jnp.concatenate(
                [jnp.ones((1, block), F32), *pieces, jnp.zeros((2 * HD - 4, block), F32)], axis=0
            )
            extra_ref[rows, cols] = filled.T.astype(BF16)
        out_ref[rows, :] = jnp.concatenate(outs, axis=0).T.astype(BF16)


def attend(q2, k2, v, live, block=1024):
    length, width = v.shape
    block = min(block, length)
    pair = lambda w: pl.BlockSpec((length, w), lambda p: (0, p))
    return pl.pallas_call(
        functools.partial(attend_kernel, block),
        grid=(width // (2 * HD),),
        in_specs=[pair(4 * HD), pair(4 * HD), pair(2 * HD), whole_block((length, 1))],
        out_specs=[pair(2 * HD), pair(4 * HD)],
        out_shape=[struct((length, width), BF16), struct((length, 2 * width), BF16)],
        compiler_params=params(56),
        cost_estimate=cost(10 * length * length * width, 20 * length * width, length * length * width // HD),
        name="attend",
    )(q2, k2, v, live)


def attend_back_kernel(
    block, y_ref, q2_ref, extra_ref, k2_ref, v_ref, o_ref, own_ref, got_ref, live_ref, kind_ref,
    grad_ref, sums_ref, dk_ref, dv_ref, dq_ref,
):
    length = k2_ref.shape[0]
    half = own_ref.shape[0]
    first = y_ref[0] == 0
    own, got = own_ref[...], got_ref[...]
    d_context = jnp.concatenate([jnp.where(first, own, got), jnp.where(first, got, own)], axis=0)
    product = d_context * o_ref[...].astype(F32)
    d_context = d_context.astype(BF16)
    lane = lax.broadcasted_iota(jnp.int32, (length, 2 * HD), 1)
    left = lane < HD
    lane_keys = lax.broadcasted_iota(jnp.int32, (block, 2 * HD), 1)
    for h in range(2):
        mine = left if h == 0 else jnp.logical_not(left)
        delta = jnp.sum(jnp.where(mine, product, 0.0), axis=1, keepdims=True)
        high, middle, low = three_pieces(-delta)
        base = HD * (1 - h)
        pieces = jnp.where(
            lane == base, high, jnp.where(lane == base + 1, middle, jnp.where(lane == base + 2, low, 0.0))
        ).astype(BF16)
        d_wide = jnp.where(mine, d_context, pieces)
        cols = slice(2 * HD * h, 2 * HD * (h + 1))
        q2 = q2_ref[:, cols]
        query = jnp.concatenate([q2, extra_ref[:, cols]], axis=1)
        dq = None
        for j in range(length // block):
            rows = slice(j * block, (j + 1) * block)
            k2 = k2_ref[rows, cols]
            keys = jnp.concatenate([k2, key_extra(live_ref[rows, :] > 0.5, block)], axis=1)
            probs = jnp.exp(mm(keys, query, NT))
            own_keys = (lane_keys < HD) if h == 0 else (lane_keys >= HD)
            ones = jnp.where((lane_keys >= base) & (lane_keys < base + 3), 1.0, 0.0).astype(BF16)
            d_probs = mm(jnp.where(own_keys, v_ref[rows, :], ones), d_wide, NT)
            d_scores = (probs * d_probs).astype(BF16)
            dv_ref[h, rows, :] = mm(probs.astype(BF16), d_context, NN)
            dk_ref[h, rows, :] = mm(d_scores, q2, NN)
            part = mm(k2, d_scores, TN)
            dq = part if dq is None else dq + part
        dq_ref[h] = dq.T * (1.0 / math.sqrt(HD))
    entity = kind_ref[...] > 0.5
    even, odd = dq_ref[0], dq_ref[1]
    to_word = jnp.where(left, even, pltpu.roll(odd, HD, 1)).astype(BF16).astype(F32)
    to_entity = jnp.where(left, pltpu.roll(even, HD, 1), odd).astype(BF16).astype(F32)
    even, odd = dk_ref[0], dk_ref[1]
    even = jnp.where(entity, pltpu.roll(even, HD, 1), even)
    odd = jnp.where(entity, odd, pltpu.roll(odd, HD, 1))
    grads = [
        jnp.where(entity, 0.0, to_word),
        jnp.where(entity, 0.0, to_entity),
        jnp.where(entity, to_word, 0.0),
        jnp.where(entity, to_entity, 0.0),
        jnp.where(left, even, odd).astype(BF16).astype(F32),
        jnp.where(left, dv_ref[0], dv_ref[1]).astype(BF16).astype(F32),
    ]
    for c, grad in enumerate(grads):
        grad_ref[c] = grad.astype(BF16)
    sums = [jnp.sum(grad, axis=0, keepdims=True) for grad in grads]
    sums_ref[...] = jnp.concatenate([*sums, jnp.zeros((2, 2 * HD), F32)], axis=0)


def attend_back(y, q2, extra, k2, v, o, own, got, live, kind, block=1024):
    length, width = v.shape
    half = own.shape[0]
    block = min(block, length)
    pair = lambda w: pl.BlockSpec((length, w), lambda p, *_: (0, p))
    part = pl.BlockSpec((half, 2 * HD), lambda p, *_: (0, p))
    return pl.pallas_call(
        functools.partial(attend_back_kernel, block),
        grid_spec=pltpu.PrefetchScalarGridSpec(
            num_scalar_prefetch=1,
            grid=(width // (2 * HD),),
            in_specs=[
                pair(4 * HD), pair(4 * HD), pair(4 * HD), pair(2 * HD), pair(2 * HD),
                part, part, whole_block((length, 1)), whole_block((length, 1)),
            ],
            out_specs=[
                pl.BlockSpec((6, length, 2 * HD), lambda p, *_: (0, 0, p)),
                pl.BlockSpec((8, 2 * HD), lambda p, *_: (0, p)),
            ],
            scratch_shapes=[pltpu.VMEM((2, length, 2 * HD), F32)] * 3,
        ),
        out_shape=[struct((6, length, width), BF16), struct((8, width), F32)],
        compiler_params=params(60),
        cost_estimate=cost(20 * length * length * width, 40 * length * width, length * length * width // HD),
        name="attend_back",
    )(y, q2, extra, k2, v, o, own, got, live, kind)


def normalise(value):
    centre = value - jnp.mean(value, axis=-1, keepdims=True)
    inverse = lax.rsqrt(jnp.mean(centre * centre, axis=-1, keepdims=True) + NORM_EPS)
    return centre * inverse, inverse


def normalise_back(scaled, normal, inverse):
    return inverse * (
        scaled
        - jnp.mean(scaled, axis=-1, keepdims=True)
        - normal * jnp.mean(scaled * normal, axis=-1, keepdims=True)
    )


def gelu_pair(values):
    cumulative = 0.5 * (1.0 + lax.erf(values * (1.0 / math.sqrt(2.0))))
    density = jnp.exp(-0.5 * values * values) * (1.0 / math.sqrt(2.0 * math.pi))
    return values * cumulative, cumulative + values * density


def column_sum(value):
    return jnp.sum(value, axis=0, keepdims=True)


def middle_kernel(at_ref, x_ref, cot_ref, live_ref, own_ref, got_ref, wo_ref, wi_ref, wu_ref, *rest):
    arrived = rest[:SLICES]
    (
        vec_ref, bias_ref, out_ref, first_ref, dco_ref, dcf_ref, left_ref, right_ref, sums_ref,
        inner_sums_ref, slope_ref, buf_ref,
    ) = rest[SLICES:]
    step = pl.program_id(0)
    me = at_ref[1]
    hidden, model, width = wi_ref.shape[1], x_ref.shape[1], wo_ref.shape[0]
    half = hidden // 2
    ends = [width // SLICES, (width + hidden) // SLICES, (width + hidden + model) // SLICES]
    ends.append(ends[-1] + model // SLICES)

    @pl.when(step == 0)
    def _():
        for k in range(SLICES):
            buf_ref[me ^ k] = arrived[k][...].astype(BF16)

    def foreign(a, b):
        block = buf_ref[:, a:b, :]
        return block.reshape(SLICES * (b - a), model)

    vec = [vec_ref[k : k + 1, :] for k in range(6)]
    got = got_ref[...].astype(BF16)
    own = own_ref[...]
    wo_far = foreign(0, ends[0])
    first = mm(own, wo_ref[...], NN) + mm(got, wo_far, NN) + vec[0] + x_ref[...].astype(F32)
    n1, inv1 = normalise(first)
    normed = n1 * vec[1] + vec[2]
    low = normed.astype(BF16)
    left_ref[0] = low

    def inner(part):
        if part < 2:
            return wi_ref[:, half * part : half * (part + 1)]
        return foreign(ends[part - 1], ends[part])

    def outer(part):
        if part < 2:
            return wu_ref[half * part : half * (part + 1), :]
        per = (ends[1] - ends[0]) // 2
        whole = foreign(ends[0], ends[1])
        return whole[half * (part - 2) : half * (part - 1), :]

    second = vec[3] + normed
    for part in range(4):
        pre = mm(low, inner(part), NN) + bias_ref[part : part + 1, :]
        active, slope = gelu_pair(pre)
        active = active.astype(BF16)
        slope_ref[:, half * part : half * (part + 1)] = slope
        at = hidden + half * (part % 2)
        right_ref[part // 2, :, at : at + half] = active
        second = second + mm(active, outer(part), NN)
    n2, inv2 = normalise(second)
    live = live_ref[...] > 0.5
    out_ref[...] = jnp.where(live, n2 * vec[4] + vec[5], 0.0).astype(BF16).astype(F32)
    dz = jnp.where(live, cot_ref[...].astype(F32), 0.0)
    d_second = normalise_back(dz * vec[4], n2, inv2)
    d_low = d_second.astype(BF16)
    left_ref[1] = d_low
    d_normed = d_second
    inner_sums = []
    for part in range(4):
        d_hidden = mm(d_low, outer(part), NT)
        d_inner = (d_hidden * slope_ref[:, half * part : half * (part + 1)]).astype(BF16)
        at = half * (part % 2)
        right_ref[part // 2, :, at : at + half] = d_inner
        inner_sums.append(column_sum(d_inner.astype(F32)))
        d_normed = d_normed + mm(d_inner, inner(part), NT)
    d_first = normalise_back(d_normed * vec[1], n1, inv1)
    first_ref[...] = d_first
    d_attn = d_first.astype(BF16)
    left_ref[2] = d_attn
    dco_ref[...] = mm(d_attn, wo_ref[...], NT).astype(BF16).astype(F32)
    dcf_ref[...] = mm(d_attn, wo_far, NT).astype(BF16).astype(F32)
    right_ref[0, :, 2 * hidden :] = own
    right_ref[1, :, 2 * hidden :] = got
    sums = jnp.concatenate(
        [
            column_sum(d_first),
            column_sum(d_normed * n1),
            column_sum(d_normed),
            column_sum(d_second),
            column_sum(dz * n2),
            column_sum(dz),
            jnp.zeros((2, model), F32),
        ],
        axis=0,
    )
    inner_sums = jnp.concatenate([*inner_sums, jnp.zeros((4, half), F32)], axis=0)

    @pl.when(step == 0)
    def _():
        sums_ref[...] = sums
        inner_sums_ref[...] = inner_sums

    @pl.when(step != 0)
    def _():
        sums_ref[...] += sums
        inner_sums_ref[...] += inner_sums


def middle(at, x, cot, live, context, got, wo, wi, wu, arrived, vec, bias, rows=256):
    half, width = got.shape
    model, hidden = wi.shape
    rows = min(rows, half)
    steps = half // rows
    mine = lambda w: pl.BlockSpec((rows, w), lambda i, s: (i + s[0] * steps, 0))
    tile = lambda w: pl.BlockSpec((rows, w), lambda i, s: (i, 0))
    packed = 2 * hidden + width
    return pl.pallas_call(
        middle_kernel,
        grid_spec=pltpu.PrefetchScalarGridSpec(
            num_scalar_prefetch=1,
            grid=(steps,),
            in_specs=[
                mine(model), mine(model), mine(1), mine(width), tile(width),
                whole_block(wo.shape), whole_block(wi.shape), whole_block(wu.shape),
                *(whole_block(a.shape) for a in arrived),
                whole_block(vec.shape), whole_block(bias.shape),
            ],
            out_specs=[
                tile(model), tile(model), tile(width), tile(width),
                pl.BlockSpec((3, rows, model), lambda i, s: (0, i, 0)),
                pl.BlockSpec((2, rows, packed), lambda i, s: (0, i, 0)),
                pl.BlockSpec((8, model), lambda i, s: (0, 0)),
                pl.BlockSpec((8, hidden // 2), lambda i, s: (0, 0)),
            ],
            scratch_shapes=[
                pltpu.VMEM((rows, 2 * hidden), F32),
                pltpu.VMEM((SLICES, *arrived[0].shape), BF16),
            ],
        ),
        out_shape=[
            struct((half, model), F32), struct((half, model), F32),
            struct((half, width), F32), struct((half, width), F32),
            struct((3, half, model), BF16), struct((2, half, packed), BF16),
            struct((8, model), F32), struct((8, hidden // 2), F32),
        ],
        compiler_params=params(62),
        cost_estimate=cost(
            16 * half * model * (hidden + width // 2), 12 * model * packed + 40 * half * model, 6 * half * hidden
        ),
        name="middle",
    )(at, x, cot, live, context, got, wo, wi, wu, *arrived, vec, bias)


def weight_kernel(tiles, left_ref, right_ref, *rest):
    out_ref = rest[-1]
    end = 0
    for index, source, target, size in tiles:
        out_ref[0, :, target : target + size] = mm(left_ref[index], right_ref[0, :, source : source + size], TN)
        end = max(end, target + size)
    if len(rest) == 2:
        out_ref[0, :, end:] = rest[0][0]


def weight_grads(left, right, extra, tiles, rows=256):
    kinds, depth, model = left.shape
    pieces, _, packed = right.shape
    columns = sum(tile[3] for tile in tiles) + (extra.shape[-1] if extra is not None else 0)
    args, specs = [left, right], [
        pl.BlockSpec((kinds, depth, rows), lambda k, i: (0, 0, i)),
        pl.BlockSpec((1, depth, packed), lambda k, i: (k, 0, 0)),
    ]
    if extra is not None:
        args.append(extra)
        specs.append(pl.BlockSpec((1, rows, extra.shape[-1]), lambda k, i: (k, i, 0)))
    return pl.pallas_call(
        functools.partial(weight_kernel, tiles),
        grid=(pieces, model // rows),
        in_specs=specs,
        out_specs=pl.BlockSpec((1, rows, columns), lambda k, i: (k, i, 0)),
        out_shape=struct((pieces, model, columns), F32),
        compiler_params=params(56),
        cost_estimate=cost(2 * pieces * depth * model * columns, 4 * pieces * model * columns),
        name="weight_grads",
    )(*args)


def project_weight_kernel(chosen, x_ref, grad_ref, *rest):
    out_ref = rest[-1]
    width = grad_ref.shape[2]
    for k, c in enumerate(chosen):
        out_ref[:, width * k : width * (k + 1)] = mm(x_ref[...], grad_ref[c], TN)
    if len(rest) == 2:
        out_ref[:, width * len(chosen) :] = rest[0][...]


def project_weight_grads(x, grads, chosen, extra, rows=256):
    length, model = x.shape
    width = grads.shape[2]
    columns = width * len(chosen) + (extra.shape[-1] if extra is not None else 0)
    args = [x, grads]
    specs = [pl.BlockSpec((length, rows), lambda i: (0, i)), whole_block(grads.shape)]
    if extra is not None:
        args.append(extra)
        specs.append(pl.BlockSpec((rows, extra.shape[-1]), lambda i: (i, 0)))
    return pl.pallas_call(
        functools.partial(project_weight_kernel, chosen),
        grid=(model // rows,),
        in_specs=specs,
        out_specs=pl.BlockSpec((rows, columns), lambda i: (i, 0)),
        out_shape=struct((model, columns), F32),
        compiler_params=params(48),
        cost_estimate=cost(2 * length * model * columns, 4 * model * columns + 12 * length * width),
        name="project_weight_grads",
    )(*args)


def input_kernel(steps, y_ref, grad_ref, wq_ref, wk_ref, wv_ref, first_ref, out_ref):
    total = mm(grad_ref[4], wk_ref[...], NT) + mm(grad_ref[5], wv_ref[...], NT)
    for c in range(4):
        total = total + mm(grad_ref[c], wq_ref[c], NT)
    mine = pl.program_id(0) // steps == y_ref[0]
    out_ref[...] = total + jnp.where(mine, first_ref[...], 0.0)


def input_part(y, grads, wq, wk, wv, first, rows=256):
    _, length, width = grads.shape
    half, model = first.shape
    rows = min(rows, half)
    steps = half // rows
    return pl.pallas_call(
        functools.partial(input_kernel, steps),
        grid_spec=pltpu.PrefetchScalarGridSpec(
            num_scalar_prefetch=1,
            grid=(length // rows,),
            in_specs=[
                pl.BlockSpec((6, rows, width), lambda i, s: (0, i, 0)),
                whole_block(wq.shape), whole_block(wk.shape), whole_block(wv.shape),
                pl.BlockSpec((rows, model), lambda i, s: (jnp.clip(i - s[0] * steps, 0, steps - 1), 0)),
            ],
            out_specs=pl.BlockSpec((rows, model), lambda i, s: (i, 0)),
        ),
        out_shape=struct((length, model), F32),
        compiler_params=params(48),
        cost_estimate=cost(12 * length * model * width, 16 * model * width + 8 * length * model),
        name="input_part",
    )(y, grads, wq, wk, wv, first)


def place_kernel(y_ref, own_ref, got_ref, out_ref):
    mine = pl.program_id(0) == y_ref[0]
    out_ref[...] = jnp.where(mine, own_ref[...], got_ref[...]).astype(BF16)


def place_rows(y, own, got):
    half, model = own.shape
    return pl.pallas_call(
        place_kernel,
        grid_spec=pltpu.PrefetchScalarGridSpec(
            num_scalar_prefetch=1,
            grid=(2,),
            in_specs=[whole_block(own.shape), whole_block(got.shape)],
            out_specs=pl.BlockSpec((half, model), lambda i, s: (i, 0)),
        ),
        out_shape=struct((2 * half, model), BF16),
        compiler_params=params(32),
        cost_estimate=cost(half * model, 12 * half * model),
        name="place_rows",
    )(y, own, got)


def per_device(
    devices,
    tokens,
    lengths,
    entity_flags,
    query_weight,
    query_bias,
    key_weight,
    key_bias,
    value_weight,
    value_bias,
    output_weight,
    output_bias,
    attn_gain,
    attn_shift,
    inner_weight,
    inner_bias,
    outer_weight,
    outer_bias,
    final_gain,
    final_shift,
    cotangent,
):
    x = tokens[0]
    length, model = x.shape
    width = key_weight.shape[1]
    hidden = inner_weight.shape[1]
    half = length // 2
    bits = devices.bit_length() - 1
    y = lax.axis_index("tensor")
    d = lax.axis_index("dp")

    def swap(value, mask):
        return lax.ppermute(value, "dp", [(i, i ^ mask) for i in range(devices)])

    def cross(value):
        return lax.ppermute(value, "tensor", [(0, 1), (1, 0)])

    me = d % SLICES
    at = jnp.stack([y, me]).astype(jnp.int32)

    def pack(index):
        cut = lambda a: lax.dynamic_slice_in_dim(
            a, index * (a.shape[0] // SLICES), a.shape[0] // SLICES, 0
        )
        wide = cut(inner_weight)
        return jnp.concatenate(
            [cut(output_weight), cut(outer_weight), wide[:, :model], wide[:, model:]], axis=0
        ).astype(F32)

    near = cross(pack(me))
    last = cross(pack(me ^ 6))
    by_two = swap(near, 2)
    by_four = swap(near, 4)
    arrived = []
    for piece in (near, by_two, by_four, last):
        arrived += [piece, swap(piece, 1)]
    arrived = tuple(arrived)
    far_bias = cross(inner_bias)

    live = (lax.broadcasted_iota(jnp.int32, (length, 1), 0) < lengths[0]).astype(F32)
    kind = (entity_flags[0] == 1).astype(F32).reshape(length, 1)

    q2, k2, v = project(
        x, kind, query_weight, query_bias, key_weight, key_bias, value_weight, value_bias
    )
    context, extra = attend(q2, k2, v, live)
    got = cross(lax.dynamic_slice_in_dim(context, half * (1 - y), half, 0).astype(F32))

    vec = jnp.stack(
        [output_bias, attn_gain, attn_shift, outer_bias, final_gain, final_shift, outer_bias, outer_bias]
    )
    bias = jnp.concatenate([inner_bias, far_bias, inner_bias, far_bias]).reshape(8, hidden // 2)
    out_rows, d_first, dco, dcf, left, right, sums, inner_sums = middle(
        at, x, cotangent[0], live, context, got, output_weight, inner_weight, outer_weight,
        arrived, vec, bias,
    )
    d_got = cross(dcf)

    inner_columns = inner_sums[:4].reshape(2, model, 2)
    shared = jnp.broadcast_to(sums[:6].T[None], (2, model, 6))
    columns = jnp.pad(jnp.concatenate([shared, inner_columns], axis=2), ((0, 0), (0, 0), (0, 120)))
    grads_a = weight_grads(left, right, None, ((0, 0, 0, hidden), (2, 2 * hidden, hidden, width)))
    grads_b = weight_grads(left, right, columns, ((1, hidden, 0, hidden),))

    def spread(array):
        return array.reshape(array.shape[0], *([2] * bits), model // devices, array.shape[-1])

    def halve(array, mask):
        axis = 1 + bits - mask.bit_length()
        bit = (d // mask) % 2
        send = lax.dynamic_slice_in_dim(array, 1 - bit, 1, axis)
        keep = lax.dynamic_slice_in_dim(array, bit, 1, axis)
        return keep + swap(send, mask)

    def across(array):
        return array[:1] + cross(array[1:])

    def finish(array, done):
        for k in range(bits):
            if (1 << k) not in done:
                array = halve(array, 1 << k)
        return array.reshape(model // devices, array.shape[-1])

    d_all, bias_sums = attend_back(at, q2, extra, k2, v, context, dco, d_got, live, kind)
    got_out = cross(out_rows)

    a = halve(halve(spread(grads_a), 1), 2)
    b = halve(halve(spread(grads_b), 1), 4)
    a = halve(across(a), 4)
    b = across(halve(b, 2))
    a = finish(a, (1, 2, 4))
    b = finish(b, (1, 2, 4))
    layer_out = place_rows(at, out_rows, got_out)

    part = input_part(at, d_all, query_weight, key_weight, value_weight, d_first)
    input_grad = (part + cross(part)).astype(BF16)

    per = width // devices
    rows = model // devices
    bias_columns = jnp.pad(
        bias_sums[:6].reshape(6, devices, per), ((0, 0), (0, 0), (0, rows - per))
    ).reshape(6, model)
    bias_columns = jnp.pad(bias_columns.T, ((0, 0), (0, 122)))
    grads_c = project_weight_grads(x, d_all, (0, 1, 2), None)[None]
    grads_d = project_weight_grads(x, d_all, (3, 4, 5), bias_columns)[None]
    c = halve(halve(halve(spread(grads_c), 1), 2), 4)
    e = halve(halve(halve(spread(grads_d), 1), 4), 2)
    c = finish(c, (1, 2, 4))
    e = finish(e, (1, 2, 4))

    shared = b[:, hidden:]
    cut = lambda k: c[:, width * k : width * (k + 1)]
    grad_query_weight = jnp.stack([cut(0), cut(1), cut(2), e[:, :width]])
    biases = e[:per, 3 * width : 3 * width + 6].T
    return (
        layer_out[None],
        input_grad[None],
        grad_query_weight,
        biases[:4],
        e[:, width : 2 * width],
        biases[4],
        e[:, 2 * width : 3 * width],
        biases[5],
        a[:, hidden:].T,
        shared[:, 0],
        shared[:, 1],
        shared[:, 2],
        a[:, :hidden],
        shared[:, 6:8].reshape(2 * rows),
        b[:, :hidden].T,
        shared[:, 3],
        shared[:, 4],
        shared[:, 5],
    )


def solution(mesh):
    return jax.shard_map(
        functools.partial(per_device, mesh.shape["dp"]),
        mesh=mesh,
        in_specs=(
            P("dp", None, None),
            P("dp"),
            P("dp", None),
            P(None, None, "tensor"),
            P(None, "tensor"),
            P(None, "tensor"),
            P("tensor"),
            P(None, "tensor"),
            P("tensor"),
            P("tensor", None),
            P(),
            P(),
            P(),
            P(None, "tensor"),
            P("tensor"),
            P("tensor", None),
            P(),
            P(),
            P(),
            P("dp", None, None),
        ),
        out_specs=(
            P("dp", None, None),
            P("dp", None, None),
            P(None, "dp", "tensor"),
            P(None, ("tensor", "dp")),
            P("dp", "tensor"),
            P(("tensor", "dp")),
            P("dp", "tensor"),
            P(("tensor", "dp")),
            P("tensor", "dp"),
            P("dp"),
            P("dp"),
            P("dp"),
            P("dp", "tensor"),
            P(("tensor", "dp")),
            P("tensor", "dp"),
            P("dp"),
            P("dp"),
            P("dp"),
        ),
        check_vma=False,
    )
```

time: 1180 us -> 421 us (0.36)
  waiting for transfers between devices: 686 us -> 201 us
  matrix products: 302 us -> 0 us
  Pallas kernels: 0 us -> 115 us
  blocking collectives: 62.3 us -> 0 us
  starting transfers between devices: 0.67 us -> 33.8 us
  local copies, waits for them, and re-layouts: 72.1 us -> 42.9 us
  between operations: 17.9 us -> 2.12 us
  other arithmetic: 38 us -> 25.2 us
    psum x4 -> x0, waiting for transfers between devices: 346 us -> none  [the longest x1 88.6 us: per_device(): attn_out = lax.psum(attn_part, 'tensor')]
    dot_general x40 -> x0, matrix products: 302 us -> none  [the longest x2 39 us: backward_block(): jnp.einsum('hqk,qhe->khe', grad_word, word_block, preferred_element_type=...]
    reduce_scatter x3 -> x0, waiting for transfers between devices: 216 us -> none  [the longest x1 79.4 us: per_device(): lax.psum_scatter(grad_inner_weight, 'dp', scatter_dimension=0, tiled=True)]
    ppermute x0 -> x31, waiting for transfers between devices: none -> 201 us  [the longest x9 141 us: cross(): return lax.ppermute(value, 'tensor', [(0, 1), (1, 0)])]
    unnamed x13 -> x0, waiting for transfers between devices: 124 us -> none
    pallas_call x0 -> x10, Pallas kernels: none -> 115 us  [the longest x1 26.5 us: middle(): pl.pallas_call(middle_kernel, grid_spec=pltpu.PrefetchScalarGridSpec(num_...]
    unnamed x1 -> x0, blocking collectives: 62.3 us -> none
    ppermute x0 -> x31, starting transfers between devices: none -> 33.8 us  [the longest x22 21.8 us: swap(): return lax.ppermute(value, 'dp', [(i, i ^ mask) for i in range(devices)])]
  transfers between devices with their start and end apart: 10 -> 31, of which waited for: 10 -> 13; matrix products, arithmetic and copies ran while one was open for 4% -> 12% of each run, Pallas kernels for 0% -> 21%
where the time goes in v1:
time: 421 us; the launch traced here: 420 us
  waiting for transfers between devices  201 us (48%)
  Pallas kernels  115 us (27%)
  local copies, waits for them, and re-layouts  42.9 us (10%)
  starting transfers between devices  33.8 us (8%)
  other arithmetic  25.2 us (6%)
    ppermute x9, waiting for transfers between devices, cross(): return lax.ppermute(value, 'tensor', [(0, 1), (1, 0)])  141 us
    ppermute x22, waiting for transfers between devices, swap(): return lax.ppermute(value, 'dp', [(i, i ^ mask) for i in range(devices)])  60.2 us
    pallas_call x1, Pallas kernels, middle(): pl.pallas_call(middle_kernel, grid_spec=pltpu.PrefetchScalarGridSpec(num_...  26.5 us
    pallas_call x2, Pallas kernels, weight_grads(): pl.pallas_call(functools.partial(weight_kernel, tiles), grid=(pieces, mod...  23.7 us
    pallas_call x1, Pallas kernels, attend_back(): pl.pallas_call(functools.partial(attend_back_kernel, block), grid_spec=pl...  22.4 us
    ppermute x22, starting transfers between devices, swap(): return lax.ppermute(value, 'dp', [(i, i ^ mask) for i in range(devices)])  21.8 us
    dynamic_slice x16, local copies, waits for them, and re-layouts, halve(): send = lax.dynamic_slice_in_dim(array, 1 - bit, 1, axis)  17.1 us
    add x12, other arithmetic, halve(): return keep + swap(send, mask)  15.3 us
  transfers between devices with their start and end apart: 31, of which 13 were waited for; matrix products, arithmetic and copies ran while one was open for 12% of the time, Pallas kernels for 21%

profile of v1, /device:TPU:0, one launch (start us, length us, event | category | flops | bytes accessed | tf_op | source)
XLA Modules:
  0.0 420.3 jit_solution(9298049852332606234)
XLA Ops:
  7.3 29.9 %collective-permute-done.1.rest_0_ = f32[432,768]{1,0:T(8,128)} collective-permute-done((f32[432,768]{1,0:T(8,128)S(1)}, f32[432,768]{1,0:T(8,128)}, u32[]{:S(2)}, u32[]{:S(2)}) %collective-permute-start.1) | collective-permute-done | bytes 1327136 | tf_op jit(solution)/shard_map/ppermute | solution.py:575
  43.3 7.7 %project.1 = (bf16[1024,768]{1,0:T(8,128)(2,1)S(1)}, bf16[1024,768]{1,0:T(8,128)(2,1)S(1)}, bf16[1024,384]{1,0:T(8,128)(2,1)S(1)}) custom-call(bf16[1024,768]{1,0:T(8,128)(2,1)} %bitcast.49, f32[1024,1]{1,0:T(8,128)S(1)} %copy.52.kind_ref, bf16[4,768,384]{2,1,0:T(8,128)(2,1)} %wq_ref.3, f32[4,384]{1,0:T(4,128)S(1)} %copy-done.12, ...), custom_call_target="tpu_custom_call" | custom-call | flops 3623878656 | bytes 9437184 | tf_op jit(solution)/shard_map/project/pallas_call | solution.py:83
  54.2 10.6 %collective-permute-done.7.rest_6_ = f32[432,768]{1,0:T(8,128)} collective-permute-done((f32[432,768]{1,0:T(8,128)S(1)}, f32[432,768]{1,0:T(8,128)}, u32[]{:S(2)}, u32[]{:S(2)}) %collective-permute-start.7) | collective-permute-done | bytes 1327136 | tf_op jit(solution)/shard_map/ppermute | solution.py:575
  69.1 13.5 %attend.1 = (bf16[1024,384]{1,0:T(8,128)(2,1)}, bf16[1024,768]{1,0:T(8,128)(2,1)}) custom-call(bf16[1024,768]{1,0:T(8,128)(2,1)} %copy-done.14, bf16[1024,768]{1,0:T(8,128)(2,1)} %copy-done.15, bf16[1024,384]{1,0:T(8,128)(2,1)} %copy-done.16, f32[1024,1]{1,0:T(8,128)} %fusion.1.live_ref), custom_call_target="tpu_custom_call" | custom-call | flops 4026531840 | bytes 7864320 | tf_op jit(solution)/shard_map/attend/pallas_call | solution.py:149
  87.3 16.5 %collective-permute-done.got_ref = f32[512,384]{1,0:T(8,128)} collective-permute-done((f32[512,384]{1,0:T(8,128)S(1)}, f32[512,384]{1,0:T(8,128)}, u32[]{:S(2)}, u32[]{:S(2)}) %collective-permute-start) | collective-permute-done | bytes 786464 | tf_op jit(solution)/shard_map/ppermute | solution.py:575
  104.9 26.5 %middle.1 = (f32[512,768]{1,0:T(8,128)}, f32[512,768]{1,0:T(8,128)}, f32[512,384]{1,0:T(8,128)}, f32[512,384]{1,0:T(8,128)}, bf16[3,512,768]{2,1,0:T(8,128)(2,1)...) custom-call(s32[2]{0:T(128)} %pad_add_fusion.at_ref.y_ref, bf16[1024,768]{1,0:T(8,128)(2,1)} %bitcast.50, ...), custom_call_target="tpu_custom_call" | custom-call | flops 10871635968 | bytes 47579136 | tf_op jit(solution)/shard_map/middle/pallas_call | solution.py:385
  136.6 11.5 %weight_grads.3 = f32[2,768,1664]{2,1,0:T(8,128)} custom-call(bf16[3,512,768]{2,1,0:T(8,128)(2,1)} %get-tuple-element.44.left_ref, bf16[2,512,3456]{2,1,0:T(8,128)(2,1)} %get-tuple-element.45.right_ref, f32[2,768,128]{2,1,0:T(8,128)} %select_maximum_fusion.rest_0_), custom_call_target="tpu_custom_call" | custom-call | flops 2617245696 | bytes 10223616 | tf_op jit(solution)/shard_map/weight_grads/pallas_call | solution.py:443
  148.2 5.1 %constant_dynamic-slice_fusion.4 = f32[2,2,2,2,1,48,1664]{6,5,4,3,2,1,0:T(8,128)} fusion(f32[2,2,2,2,2,48,1664]{6,5,4,3,2,1,0:T(8,128)} %bitcast.57, s32[]{:T(128)S(6)} %select_n.149), kind=kLoop, calls=%fused_computation.50 | loop fusion | bytes 10223620 | tf_op jit(solution)/shard_map/dynamic_slice | solution.py:630
  154.2 22.4 %attend_back.1 = (bf16[6,1024,384]{2,1,0:T(8,128)(2,1)}, f32[8,384]{1,0:T(8,128)}) custom-call(s32[2]{0:T(128)} %pad_add_fusion.at_ref.y_ref, bf16[1024,768]{1,0:T(8,128)(2,1)} %copy-done.14, bf16[1024,768]{1,0:T(8,128)(2,1)} %get-tuple-element.38.extra_ref, bf16[1024,768]{1,0:T(8,128)(2,1)} %copy-done.15, bf16[1024,384]{1,0:T(8,128)(2,1)} %copy-done.16, ...), custom_call_target="tpu_custom_call" | custom-call | flops 8053063680 | bytes 15728640 | tf_op jit(solution)/shard_map/attend_back/pallas_call | solution.py:229
  178.0 5.5 %project_weight_grads.2 = f32[768,1152]{1,0:T(8,128)S(1)} custom-call(bf16[1024,768]{1,0:T(8,128)(2,1)S(1)} %bitcast.51, bf16[6,1024,384]{2,1,0:T(8,128)(2,1)} %get-tuple-element.41.grad_ref), custom_call_target="tpu_custom_call" | custom-call | flops 1811939328 | bytes 8257536 | tf_op jit(solution)/shard_map/project_weight_grads/pallas_call | solution.py:473
  185.5 12.2 %weight_grads.2 = f32[2,768,1920]{2,1,0:T(8,128)} custom-call(bf16[3,512,768]{2,1,0:T(8,128)(2,1)} %get-tuple-element.44.left_ref, bf16[2,512,3456]{2,1,0:T(8,128)(2,1)} %get-tuple-element.45.right_ref), custom_call_target="tpu_custom_call" | custom-call | flops 3019898880 | bytes 11796480 | tf_op jit(solution)/shard_map/weight_grads/pallas_call | solution.py:443
  200.9 5.5 %project_weight_grads.3 = f32[768,1280]{1,0:T(8,128)S(1)} custom-call(bf16[1024,768]{1,0:T(8,128)(2,1)S(1)} %bitcast.52, bf16[6,1024,384]{2,1,0:T(8,128)(2,1)} %get-tuple-element.41.grad_ref, f32[768,128]{1,0:T(8,128)S(1)} %pad.13.rest_0_), custom_call_target="tpu_custom_call" | custom-call | flops 2013265920 | bytes 8650752 | tf_op jit(solution)/shard_map/project_weight_grads/pallas_call | solution.py:473
  208.9 5.6 %constant_dynamic-slice_fusion.8 = f32[2,2,2,2,1,48,1920]{6,5,4,3,2,1,0:T(8,128)} fusion(f32[2,2,2,2,2,48,1920]{6,5,4,3,2,1,0:T(8,128)} %bitcast.53, s32[]{:T(128)S(6)} %select_n.149), kind=kLoop, calls=%fused_computation.54 | loop fusion | bytes 11796484 | tf_op jit(solution)/shard_map/dynamic_slice | solution.py:630
  222.4 8.5 %input_part.1 = f32[1024,768]{1,0:T(8,128)} custom-call(s32[2]{0:T(128)S(1)} %copy-done.6, bf16[6,1024,384]{2,1,0:T(8,128)(2,1)} %get-tuple-element.41.grad_ref, bf16[4,768,384]{2,1,0:T(8,128)(2,1)S(1)} %copy-done.7, bf16[768,384]{1,0:T(8,128)(2,1)S(1)} %copy-done.9, bf16[768,384]{1,0:T(8,128)(2,1)S(1)} %copy-done.11, f32[512,768]{1,0:T(8,128)S(1)} %copy-done.13), custom_call_target="tpu_custom_call" | custom-call | flops 3623878656 | bytes 11010048 | tf_op jit(solution)/shard_map/input_part/pallas_call | solution.py:498
  230.9 20.6 %collective-permute-done.10.got_ref = f32[512,768]{1,0:T(8,128)S(1)} collective-permute-done((f32[512,768]{1,0:T(8,128)}, f32[512,768]{1,0:T(8,128)S(1)}, u32[]{:S(2)}, u32[]{:S(2)}) %collective-permute-start.10) | collective-permute-done | bytes 1572896 | tf_op jit(solution)/shard_map/ppermute | solution.py:575
  256.3 5.2 %dynamic-slice_add_fusion.1 = f32[2,2,2,2,1,48,1664]{6,5,4,3,2,1,0:T(8,128)S(1)} fusion(f32[2,2,2,2,1,48,1664]{6,5,4,3,2,1,0:T(8,128)} %collective-permute-done.26, f32[2,2,2,2,2,48,1664]{6,5,4,3,2,1,0:T(8,128)} %bitcast.58, s32[]{:T(128)S(6)} %select_n.148), kind=kLoop, calls=%fused_computation.1 | loop fusion | flops 1277952 | bytes 15335428 | tf_op jit(solution)/shard_map/add | solution.py:632
  266.2 3.5 dynamic-slice_add_fusion
  273.4 47.7 %collective-permute-done.12 = f32[1024,768]{1,0:T(8,128)} collective-permute-done((f32[1024,768]{1,0:T(8,128)}, f32[1024,768]{1,0:T(8,128)}, u32[]{:S(2)}, u32[]{:S(2)}) %collective-permute-start.12) | collective-permute-done | bytes 3145760 | tf_op jit(solution)/shard_map/ppermute | solution.py:575
  331.6 5.2 %collective-permute-done.22 = f32[2,2,2,1,1,48,1920]{6,5,4,3,2,1,0:T(8,128)S(1)} collective-permute-done((f32[2,2,2,1,1,48,1920]{6,5,4,3,2,1,0:T(8,128)S(1)}, f32[2,2,2,1,1,48,1920]{6,5,4,3,2,1,0:T(8,128)S(1)}, u32[]{:S(2)}, u32[]{:S(2)}) %collective-permute-start.22) | collective-permute-done | bytes 2949152 | tf_op jit(solution)/shard_map/ppermute | solution.py:572
  338.9 22.0 %collective-permute-done.28 = f32[2,2,1,1,1,48,1664]{6,5,4,3,2,1,0:T(8,128)S(1)} collective-permute-done((f32[2,2,1,1,1,48,1664]{6,5,4,3,2,1,0:T(8,128)S(1)}, f32[2,2,1,1,1,48,1664]{6,5,4,3,2,1,0:T(8,128)S(1)}, u32[]{:S(2)}, u32[]{:S(2)}) %collective-permute-start.28) | collective-permute-done | bytes 1277984 | tf_op jit(solution)/shard_map/ppermute | solution.py:572
  363.4 15.4 %collective-permute-done.29 = f32[1,2,1,1,1,48,1664]{6,5,4,3,2,1,0:T(8,128)S(1)} collective-permute-done((f32[1,2,1,1,1,48,1664]{6,5,4,3,2,1,0:T(8,128)S(1)}, f32[1,2,1,1,1,48,1664]{6,5,4,3,2,1,0:T(8,128)S(1)}, u32[]{:S(2)}, u32[]{:S(2)}) %collective-permute-start.29) | collective-permute-done | bytes 639008 | tf_op jit(solution)/shard_map/ppermute | solution.py:575
  386.8 5.1 %collective-permute-done.30 = f32[1,1,1,1,1,48,1664]{6,5,4,3,2,1,0:T(8,128)S(1)} collective-permute-done((f32[1,1,1,1,1,48,1664]{6,5,4,3,2,1,0:T(8,128)S(1)}, f32[1,1,1,1,1,48,1664]{6,5,4,3,2,1,0:T(8,128)S(1)}, u32[]{:S(2)}, u32[]{:S(2)}) %collective-permute-start.30) | collective-permute-done | bytes 319520 | tf_op jit(solution)/shard_map/ppermute | solution.py:572
  393.4 9.4 %collective-permute-done.24 = f32[1,2,1,1,1,48,1920]{6,5,4,3,2,1,0:T(8,128)S(1)} collective-permute-done((f32[1,2,1,1,1,48,1920]{6,5,4,3,2,1,0:T(8,128)}, f32[1,2,1,1,1,48,1920]{6,5,4,3,2,1,0:T(8,128)S(1)}, u32[]{:S(2)}, u32[]{:S(2)}) %collective-permute-start.24) | collective-permute-done | bytes 737312 | tf_op jit(solution)/shard_map/ppermute | solution.py:572
  403.8 15.1 %collective-permute-done.25 = f32[1,1,1,1,1,48,1920]{6,5,4,3,2,1,0:T(8,128)S(1)} collective-permute-done((f32[1,1,1,1,1,48,1920]{6,5,4,3,2,1,0:T(8,128)S(1)}, f32[1,1,1,1,1,48,1920]{6,5,4,3,2,1,0:T(8,128)S(1)}, u32[]{:S(2)}, u32[]{:S(2)}) %collective-permute-start.25) | collective-permute-done | bytes 368672 | tf_op jit(solution)/shard_map/ppermute | solution.py:572
  (208 shorter events, 87.8 us)
Async XLA Ops:
  4.1 33.1 %collective-permute-start.1 = (f32[432,768]{1,0:T(8,128)S(1)}, f32[432,768]{1,0:T(8,128)}, u32[]{:S(2)}, u32[]{:S(2)}) collective-permute-start(f32[432,768]{1,0:T(8,128)S(1)} %maximum_convert_fusion), channel_id=1, source_target_pairs={{0,1},{1,0},{2,3},{3,2},{4,5},{5,4},{6,7},{7,6},{8,9},{9,8},{10,11... | collective-permute-start | bytes 3981320 | tf_op jit(solution)/shard_map/ppermute | solution.py:575
  7.2 57.7 %collective-permute-start.7 = (f32[432,768]{1,0:T(8,128)S(1)}, f32[432,768]{1,0:T(8,128)}, u32[]{:S(2)}, u32[]{:S(2)}) collective-permute-start(f32[432,768]{1,0:T(8,128)S(1)} %maximum_convert_fusion.1), channel_id=1, source_target_pairs={{0,1},{1,0},{2,3},{3,2},{4,5},{5,4},{6,7},{7,6},{8,9},{9,8},{10,11... | collective-permute-start | bytes 3981320 | tf_op jit(solution)/shard_map/ppermute | solution.py:575
  37.2 29.8 %collective-permute-start.5 = (f32[432,768]{1,0:T(8,128)}, f32[432,768]{1,0:T(8,128)}, u32[]{:S(2)}, u32[]{:S(2)}) collective-permute-start(f32[432,768]{1,0:T(8,128)} %collective-permute-done.1.rest_0_), channel_id=1, source_target_pairs={{0,8},{2,10},{4,12},{6,14},{8,0},{10,2},{12,4},{14,6},{16,24},{18,... | collective-permute-start | bytes 3981320 | tf_op jit(solution)/shard_map/ppermute | solution.py:572
  39.3 28.9 %collective-permute-start.3 = (f32[432,768]{1,0:T(8,128)}, f32[432,768]{1,0:T(8,128)}, u32[]{:S(2)}, u32[]{:S(2)}) collective-permute-start(f32[432,768]{1,0:T(8,128)} %collective-permute-done.1.rest_0_), channel_id=1, source_target_pairs={{0,4},{2,6},{4,0},{6,2},{8,12},{10,14},{12,8},{14,10},{16,20},{18,... | collective-permute-start | bytes 3981320 | tf_op jit(solution)/shard_map/ppermute | solution.py:572
  40.8 42.9 %collective-permute-start.9 = (f32[1536]{0:T(1024)S(1)}, f32[1536]{0:T(1024)S(1)}, u32[]{:S(2)}, u32[]{:S(2)}) collective-permute-start(f32[1536]{0:T(1024)S(1)} %copy-done.22), channel_id=1, source_target_pairs={{0,1},{1,0},{2,3},{3,2},{4,5},{5,4},{6,7},{7,6},{8,9},{9,8},{10,11... | collective-permute-start | bytes 18440 | tf_op jit(solution)/shard_map/ppermute | solution.py:575
  54.2 49.6 %collective-permute-start.2 = (f32[432,768]{1,0:T(8,128)}, f32[432,768]{1,0:T(8,128)}, u32[]{:S(2)}, u32[]{:S(2)}) collective-permute-start(f32[432,768]{1,0:T(8,128)} %collective-permute-done.1.rest_0_), channel_id=1, source_target_pairs={{0,2},{2,0},{4,6},{6,4},{8,10},{10,8},{12,14},{14,12},{16,18},{18,... | collective-permute-start | bytes 3981320 | tf_op jit(solution)/shard_map/ppermute | solution.py:572
  64.9 39.0 %collective-permute-start.8 = (f32[432,768]{1,0:T(8,128)}, f32[432,768]{1,0:T(8,128)S(1)}, u32[]{:S(2)}, u32[]{:S(2)}) collective-permute-start(f32[432,768]{1,0:T(8,128)} %collective-permute-done.7.rest_6_), channel_id=1, source_target_pairs={{0,2},{2,0},{4,6},{6,4},{8,10},{10,8},{12,14},{14,12},{16,18},{18,... | collective-permute-start | bytes 3981320 | tf_op jit(solution)/shard_map/ppermute | solution.py:572
  67.0 36.9 %collective-permute-start.6 = (f32[432,768]{1,0:T(8,128)}, f32[432,768]{1,0:T(8,128)}, u32[]{:S(2)}, u32[]{:S(2)}) collective-permute-start(f32[432,768]{1,0:T(8,128)} %collective-permute-done.5.rest_4_), channel_id=1, source_target_pairs={{0,2},{2,0},{4,6},{6,4},{8,10},{10,8},{12,14},{14,12},{16,18},{18,... | collective-permute-start | bytes 3981320 | tf_op jit(solution)/shard_map/ppermute | solution.py:572
  68.2 35.7 %collective-permute-start.4 = (f32[432,768]{1,0:T(8,128)}, f32[432,768]{1,0:T(8,128)}, u32[]{:S(2)}, u32[]{:S(2)}) collective-permute-start(f32[432,768]{1,0:T(8,128)} %collective-permute-done.3.rest_2_), channel_id=1, source_target_pairs={{0,2},{2,0},{4,6},{6,4},{8,10},{10,8},{12,14},{14,12},{16,18},{18,... | collective-permute-start | bytes 3981320 | tf_op jit(solution)/shard_map/ppermute | solution.py:572
  131.4 21.9 %collective-permute-start.11 = (f32[512,384]{1,0:T(8,128)}, f32[512,384]{1,0:T(8,128)S(1)}, u32[]{:S(2)}, u32[]{:S(2)}) collective-permute-start(f32[512,384]{1,0:T(8,128)} %get-tuple-element.40), channel_id=1, source_target_pairs={{0,1},{1,0},{2,3},{3,2},{4,5},{5,4},{6,7},{7,6},{8,9},{9,8},{10,11... | collective-permute-start | bytes 2359304 | tf_op jit(solution)/shard_map/ppermute | solution.py:575
  153.3 103.0 %collective-permute-start.26 = (f32[2,2,2,2,1,48,1664]{6,5,4,3,2,1,0:T(8,128)}, f32[2,2,2,2,1,48,1664]{6,5,4,3,2,1,0:T(8,128)}, u32[]{:S(2)}, u32[]{:S(2)}) collective-permute-start(f32[2,2,2,2,1,48,1664]{6,5,4,3,2,1,0:T(8,128)} %constant_dynamic-slice_fusion.4), channel_id=1, source_target_pairs={{0,2},{2,0},{4,6},{6,4},{8,10},{10,8},{12,14},{14,12},{16,18},{18,... | collective-permute-start | bytes 15335432 | tf_op jit(solution)/shard_map/ppermute | solution.py:572
  185.0 30.5 %collective-permute-start.13 = (f32[1,2,2,2,1,48,1152]{6,5,4,3,2,1,0:T(8,128)}, f32[1,2,2,2,1,48,1152]{6,5,4,3,2,1,0:T(8,128)}, u32[]{:S(2)}, u32[]{:S(2)}) collective-permute-start(f32[1,2,2,2,1,48,1152]{6,5,4,3,2,1,0:T(8,128)} %constant_dynamic-slice_fusion.16), channel_id=1, source_target_pairs={{0,2},{2,0},{4,6},{6,4},{8,10},{10,8},{12,14},{14,12},{16,18},{18,... | collective-permute-start | bytes 5308424 | tf_op jit(solution)/shard_map/ppermute | solution.py:572
  214.5 51.6 %collective-permute-start.21 = (f32[2,2,2,2,1,48,1920]{6,5,4,3,2,1,0:T(8,128)}, f32[2,2,2,2,1,48,1920]{6,5,4,3,2,1,0:T(8,128)}, u32[]{:S(2)}, u32[]{:S(2)}) collective-permute-start(f32[2,2,2,2,1,48,1920]{6,5,4,3,2,1,0:T(8,128)} %constant_dynamic-slice_fusion.8), channel_id=1, source_target_pairs={{0,2},{2,0},{4,6},{6,4},{8,10},{10,8},{12,14},{14,12},{16,18},{18,... | collective-permute-start | bytes 17694728 | tf_op jit(solution)/shard_map/ppermute | solution.py:572
  215.0 36.5 %collective-permute-start.10 = (f32[512,768]{1,0:T(8,128)}, f32[512,768]{1,0:T(8,128)S(1)}, u32[]{:S(2)}, u32[]{:S(2)}) collective-permute-start(f32[512,768]{1,0:T(8,128)} %get-tuple-element.37.own_ref), channel_id=1, source_target_pairs={{0,1},{1,0},{2,3},{3,2},{4,5},{5,4},{6,7},{7,6},{8,9},{9,8},{10,11... | collective-permute-start | bytes 4718600 | tf_op jit(solution)/shard_map/ppermute | solution.py:575
  217.4 36.5 %collective-permute-start.14 = (f32[1,2,2,1,1,48,1152]{6,5,4,3,2,1,0:T(8,128)S(1)}, f32[1,2,2,1,1,48,1152]{6,5,4,3,2,1,0:T(8,128)S(1)}, u32[]{:S(2)}, u32[]{:S(2)}) collective-permute-start(f32[1,2,2,1,1,48,1152]{6,5,4,3,2,1,0:T(8,128)S(1)} %constant_dynamic-slice_fusion.15), channel_id=1, source_target_pairs={{0,4},{2,6},{4,0},{6,2},{8,12},{10,14},{12,8},{14,10},{16,20},{18,... | collective-permute-start | bytes 2654216 | tf_op jit(solution)/shard_map/ppermute | solution.py:572
  221.1 33.6 %collective-permute-start.18 = (f32[1,2,1,2,1,48,1280]{6,5,4,3,2,1,0:T(8,128)S(1)}, f32[1,2,1,2,1,48,1280]{6,5,4,3,2,1,0:T(8,128)S(1)}, u32[]{:S(2)}, u32[]{:S(2)}) collective-permute-start(f32[1,2,1,2,1,48,1280]{6,5,4,3,2,1,0:T(8,128)S(1)} %constant_dynamic-slice_fusion.11), channel_id=1, source_target_pairs={{0,8},{2,10},{4,12},{6,14},{8,0},{10,2},{12,4},{14,6},{16,24},{18,... | collective-permute-start | bytes 2949128 | tf_op jit(solution)/shard_map/ppermute | solution.py:572
  251.5 69.5 %collective-permute-start.12 = (f32[1024,768]{1,0:T(8,128)}, f32[1024,768]{1,0:T(8,128)}, u32[]{:S(2)}, u32[]{:S(2)}) collective-permute-start(f32[1024,768]{1,0:T(8,128)} %input_part.1), channel_id=1, source_target_pairs={{0,1},{1,0},{2,3},{3,2},{4,5},{5,4},{6,7},{7,6},{8,9},{9,8},{10,11... | collective-permute-start | bytes 9437192 | tf_op jit(solution)/shard_map/ppermute | solution.py:575
  254.9 73.9 %collective-permute-start.19 = (f32[1,2,1,1,1,48,1280]{6,5,4,3,2,1,0:T(8,128)S(1)}, f32[1,2,1,1,1,48,1280]{6,5,4,3,2,1,0:T(8,128)S(1)}, u32[]{:S(2)}, u32[]{:S(2)}) collective-permute-start(f32[1,2,1,1,1,48,1280]{6,5,4,3,2,1,0:T(8,128)S(1)} %constant_dynamic-slice_fusion.10), channel_id=1, source_target_pairs={{0,4},{2,6},{4,0},{6,2},{8,12},{10,14},{12,8},{14,10},{16,20},{18,... | collective-permute-start | bytes 1474568 | tf_op jit(solution)/shard_map/ppermute | solution.py:572
  264.5 60.6 %collective-permute-start.27 = (f32[2,2,1,2,1,48,1664]{6,5,4,3,2,1,0:T(8,128)}, f32[2,2,1,2,1,48,1664]{6,5,4,3,2,1,0:T(8,128)}, u32[]{:S(2)}, u32[]{:S(2)}) collective-permute-start(f32[2,2,1,2,1,48,1664]{6,5,4,3,2,1,0:T(8,128)} %constant_dynamic-slice_fusion.3), channel_id=1, source_target_pairs={{0,8},{2,10},{4,12},{6,14},{8,0},{10,2},{12,4},{14,6},{16,24},{18,... | collective-permute-start | bytes 7667720 | tf_op jit(solution)/shard_map/ppermute | solution.py:572
  269.9 66.9 %collective-permute-start.22 = (f32[2,2,2,1,1,48,1920]{6,5,4,3,2,1,0:T(8,128)S(1)}, f32[2,2,2,1,1,48,1920]{6,5,4,3,2,1,0:T(8,128)S(1)}, u32[]{:S(2)}, u32[]{:S(2)}) collective-permute-start(f32[2,2,2,1,1,48,1920]{6,5,4,3,2,1,0:T(8,128)S(1)} %constant_dynamic-slice_fusion.7), channel_id=1, source_target_pairs={{0,4},{2,6},{4,0},{6,2},{8,12},{10,14},{12,8},{14,10},{16,20},{18,... | collective-permute-start | bytes 8847368 | tf_op jit(solution)/shard_map/ppermute | solution.py:572
  270.7 53.7 %collective-permute-start.16 = (f32[1,1,1,1,1,48,1152]{6,5,4,3,2,1,0:T(8,128)S(1)}, f32[1,1,1,1,1,48,1152]{6,5,4,3,2,1,0:T(8,128)S(1)}, u32[]{:S(2)}, u32[]{:S(2)}) collective-permute-start(f32[1,1,1,1,1,48,1152]{6,5,4,3,2,1,0:T(8,128)S(1)} %constant_dynamic-slice_fusion.13), channel_id=1, source_target_pairs={{0,16},{2,18},{4,20},{6,22},{8,24},{10,26},{12,28},{14,30},{16,0},... | collective-permute-start | bytes 663560 | tf_op jit(solution)/shard_map/ppermute | solution.py:572
  327.2 33.7 %collective-permute-start.28 = (f32[2,2,1,1,1,48,1664]{6,5,4,3,2,1,0:T(8,128)S(1)}, f32[2,2,1,1,1,48,1664]{6,5,4,3,2,1,0:T(8,128)S(1)}, u32[]{:S(2)}, u32[]{:S(2)}) collective-permute-start(f32[2,2,1,1,1,48,1664]{6,5,4,3,2,1,0:T(8,128)S(1)} %constant_dynamic-slice_fusion.2), channel_id=1, source_target_pairs={{0,4},{2,6},{4,0},{6,2},{8,12},{10,14},{12,8},{14,10},{16,20},{18,... | collective-permute-start | bytes 3833864 | tf_op jit(solution)/shard_map/ppermute | solution.py:572
  328.8 33.8 %collective-permute-start.20 = (f32[1,1,1,1,1,48,1280]{6,5,4,3,2,1,0:T(8,128)S(1)}, f32[1,1,1,1,1,48,1280]{6,5,4,3,2,1,0:T(8,128)S(1)}, u32[]{:S(2)}, u32[]{:S(2)}) collective-permute-start(f32[1,1,1,1,1,48,1280]{6,5,4,3,2,1,0:T(8,128)S(1)} %constant_dynamic-slice_fusion.9), channel_id=1, source_target_pairs={{0,16},{2,18},{4,20},{6,22},{8,24},{10,26},{12,28},{14,30},{16,0},... | collective-permute-start | bytes 737288 | tf_op jit(solution)/shard_map/ppermute | solution.py:572
  337.3 44.2 %collective-permute-start.23 = (f32[1,2,2,1,1,48,1920]{6,5,4,3,2,1,0:T(8,128)S(1)}, f32[1,2,2,1,1,48,1920]{6,5,4,3,2,1,0:T(8,128)S(1)}, u32[]{:S(2)}, u32[]{:S(2)}) collective-permute-start(f32[1,2,2,1,1,48,1920]{6,5,4,3,2,1,0:T(8,128)S(1)} %slice.143), channel_id=1, source_target_pairs={{0,1},{1,0},{2,3},{3,2},{4,5},{5,4},{6,7},{7,6},{8,9},{9,8},{10,11... | collective-permute-start | bytes 4423688 | tf_op jit(solution)/shard_map/ppermute | solution.py:575
  (46 other events, 773.3 us)

commit v2 on v1

v2 whole, which is shorter than its diff:
```python
import functools
import math

import jax
import jax.numpy as jnp
from jax import lax
from jax.experimental import pallas as pl
from jax.experimental.pallas import tpu as pltpu
from jax.sharding import PartitionSpec as P

HD = 64
SLICES = 8
MASKED = -1e30
NORM_EPS = 1e-05

F32 = jnp.float32
BF16 = jnp.bfloat16
NN = (((1,), (0,)), ((), ()))
NT = (((1,), (1,)), ((), ()))
TN = (((0,), (0,)), ((), ()))


def mm(left, right, dims):
    return lax.dot_general(left, right, dims, preferred_element_type=F32)


def struct(shape, kind):
    return jax.ShapeDtypeStruct(shape, kind)


def params(mib):
    return pltpu.CompilerParams(vmem_limit_bytes=mib << 20)


def cost(flops, moved, special=0):
    return pl.CostEstimate(flops=int(flops), bytes_accessed=int(moved), transcendentals=int(special))


def whole_block(shape):
    return pl.BlockSpec(shape, lambda *_: (0,) * len(shape), pipeline_mode=pl.Buffered(1))


def three_pieces(value):
    high = value.astype(BF16).astype(F32)
    rest = value - high
    middle = rest.astype(BF16).astype(F32)
    return high, middle, rest - middle


def project_kernel(x_ref, kind_ref, wq_ref, bq_ref, wk_ref, bk_ref, wv_ref, bv_ref, q2_ref, k2_ref, v_ref):
    x = x_ref[...]
    entity = kind_ref[...] > 0.5
    rows = x.shape[0]
    width = wk_ref.shape[1]

    weights = jnp.concatenate([*(wq_ref[c] for c in range(4)), wk_ref[...], wv_ref[...]], axis=1)
    biases = jnp.concatenate([*(bq_ref[c : c + 1, :] for c in range(4)), bk_ref[...], bv_ref[...]], axis=1)
    products = mm(x, weights, NN) + biases

    def query(c):
        return products[:, width * c : width * (c + 1)]

    scale = 1.0 / math.sqrt(HD)
    to_word = jnp.where(entity, query(2), query(0)).astype(BF16).astype(F32) * scale
    to_entity = jnp.where(entity, query(3), query(1)).astype(BF16).astype(F32) * scale
    keys = query(4).astype(BF16).astype(F32)
    v_ref[...] = query(5).astype(BF16)
    left = lax.broadcasted_iota(jnp.int32, (rows, 2 * HD), 1) < HD
    held = left != entity
    for p in range(width // (2 * HD)):
        cols = slice(2 * HD * p, 2 * HD * (p + 1))
        w, e, k = to_word[:, cols], to_entity[:, cols], keys[:, cols]
        w_roll, e_roll, k_roll = (pltpu.roll(t, HD, 1) for t in (w, e, k))
        even = slice(4 * HD * p, 4 * HD * p + 2 * HD)
        odd = slice(4 * HD * p + 2 * HD, 4 * HD * (p + 1))
        q2_ref[:, even] = jnp.where(left, w, e_roll).astype(BF16)
        q2_ref[:, odd] = jnp.where(left, w_roll, e).astype(BF16)
        k2_ref[:, even] = jnp.where(held, jnp.where(left, k, k_roll), 0.0).astype(BF16)
        k2_ref[:, odd] = jnp.where(held, jnp.where(left, k_roll, k), 0.0).astype(BF16)


def project(x, kind, wq, bq, wk, bk, wv, bv, rows=256):
    length, model = x.shape
    width = wk.shape[1]
    rows = min(rows, length)
    tile = lambda w: pl.BlockSpec((rows, w), lambda i: (i, 0))
    return pl.pallas_call(
        project_kernel,
        grid=(length // rows,),
        in_specs=[
            tile(model),
            tile(1),
            whole_block(wq.shape),
            whole_block(bq.shape),
            whole_block(wk.shape),
            whole_block((1, width)),
            whole_block(wv.shape),
            whole_block((1, width)),
        ],
        out_specs=[tile(2 * width), tile(2 * width), tile(width)],
        out_shape=[
            struct((length, 2 * width), BF16),
            struct((length, 2 * width), BF16),
            struct((length, width), BF16),
        ],
        compiler_params=params(48),
        cost_estimate=cost(12 * length * model * width, 16 * model * width + 12 * length * width),
        name="project",
    )(x, kind, wq, bq, wk, bk.reshape(1, width), wv, bv.reshape(1, width))


def key_extra(live, rows):
    lane = lax.broadcasted_iota(jnp.int32, (rows, 2 * HD), 1)
    return jnp.where(
        lane == 0, jnp.where(live, 0.0, MASKED), jnp.where(lane < 4, 1.0, 0.0)
    ).astype(BF16)


def attend_kernel(q2_ref, k2_ref, v_ref, live_ref, out_ref, extra_ref, turned_ref, both_ref):
    length = k2_ref.shape[0]
    h = pl.program_id(1)

    @pl.when(h == 0)
    def _():
        turned = v_ref[...].astype(F32).T.astype(BF16)
        turned_ref[0] = turned[:HD]
        turned_ref[1] = turned[HD:]

    lane = lax.broadcasted_iota(jnp.int32, (length, 2 * HD), 1)
    one = jnp.where(lane == 0, 1.0, 0.0).astype(BF16)
    keys = jnp.concatenate([k2_ref[...], key_extra(live_ref[...] > 0.5, length)], axis=1)
    query = jnp.concatenate([q2_ref[...], one], axis=1)
    scores = mm(keys, query, NT)
    top = jnp.max(scores, axis=0, keepdims=True)
    weights = jnp.exp(scores - top)
    norm = jnp.sum(weights, axis=0, keepdims=True)
    summed = mm(turned_ref[h], weights.astype(BF16), NN)
    both_ref[h] = summed * (1.0 / norm)
    pieces = three_pieces(-(top + jnp.log(norm)))
    filled = jnp.concatenate(
        [jnp.ones((1, length), F32), *pieces, jnp.zeros((2 * HD - 4, length), F32)], axis=0
    )
    extra_ref[...] = filled.T.astype(BF16)

    @pl.when(h == 1)
    def _():
        out_ref[...] = jnp.concatenate([both_ref[0], both_ref[1]], axis=0).T.astype(BF16)


def attend(q2, k2, v, live):
    length, width = v.shape
    head = pl.BlockSpec((length, 2 * HD), lambda p, h: (0, 2 * p + h))
    pair = pl.BlockSpec((length, 2 * HD), lambda p, h: (0, p))
    return pl.pallas_call(
        attend_kernel,
        grid=(width // (2 * HD), 2),
        in_specs=[head, head, pair, whole_block((length, 1))],
        out_specs=[pair, head],
        out_shape=[struct((length, width), BF16), struct((length, 2 * width), BF16)],
        scratch_shapes=[pltpu.VMEM((2, HD, length), BF16), pltpu.VMEM((2, HD, length), F32)],
        compiler_params=params(56),
        cost_estimate=cost(10 * length * length * width, 20 * length * width, length * length * width // HD),
        name="attend",
    )(q2, k2, v, live)


def attend_back_kernel(
    y_ref, q2_ref, extra_ref, k2_ref, v_ref, o_ref, own_ref, got_ref, live_ref, kind_ref,
    grad_ref, sums_ref, dk_ref, dv_ref, dq_ref, product_ref, d_ref,
):
    length = k2_ref.shape[0]
    h = pl.program_id(1)
    lane = lax.broadcasted_iota(jnp.int32, (length, 2 * HD), 1)
    left = lane < HD

    @pl.when(h == 0)
    def _():
        first = y_ref[0] == 0
        own, got = own_ref[...], got_ref[...]
        joined = jnp.concatenate([jnp.where(first, own, got), jnp.where(first, got, own)], axis=0)
        product_ref[...] = joined * o_ref[...].astype(F32)
        d_ref[...] = joined.astype(BF16)

    d_context = d_ref[...]
    base = HD * (1 - h)
    mine = jnp.logical_and(lane >= HD - base, lane < 2 * HD - base)
    delta = jnp.sum(jnp.where(mine, product_ref[...], 0.0), axis=1, keepdims=True)
    high, middle, low = three_pieces(-delta)
    pieces = jnp.where(
        lane == base, high, jnp.where(lane == base + 1, middle, jnp.where(lane == base + 2, low, 0.0))
    ).astype(BF16)
    d_wide = jnp.where(mine, d_context, pieces)
    q2, k2 = q2_ref[...], k2_ref[...]
    query = jnp.concatenate([q2, extra_ref[...]], axis=1)
    keys = jnp.concatenate([k2, key_extra(live_ref[...] > 0.5, length)], axis=1)
    probs = jnp.exp(mm(keys, query, NT))
    ones = jnp.where((lane >= base) & (lane < base + 3), 1.0, 0.0).astype(BF16)
    d_probs = mm(jnp.where(mine, v_ref[...], ones), d_wide, NT)
    d_scores = (probs * d_probs).astype(BF16)
    dv_ref[h] = mm(probs.astype(BF16), d_context, NN)
    dk_ref[h] = mm(d_scores, q2, NN)
    dq_ref[h] = mm(k2, d_scores, TN).T * (1.0 / math.sqrt(HD))

    @pl.when(h == 1)
    def _():
        entity = kind_ref[...] > 0.5
        even, odd = dq_ref[0], dq_ref[1]
        to_word = jnp.where(left, even, pltpu.roll(odd, HD, 1)).astype(BF16).astype(F32)
        to_entity = jnp.where(left, pltpu.roll(even, HD, 1), odd).astype(BF16).astype(F32)
        even, odd = dk_ref[0], dk_ref[1]
        even = jnp.where(entity, pltpu.roll(even, HD, 1), even)
        odd = jnp.where(entity, odd, pltpu.roll(odd, HD, 1))
        grads = [
            jnp.where(entity, 0.0, to_word),
            jnp.where(entity, 0.0, to_entity),
            jnp.where(entity, to_word, 0.0),
            jnp.where(entity, to_entity, 0.0),
            jnp.where(left, even, odd).astype(BF16).astype(F32),
            jnp.where(left, dv_ref[0], dv_ref[1]).astype(BF16).astype(F32),
        ]
        for c, grad in enumerate(grads):
            grad_ref[c] = grad.astype(BF16)
        sums = [jnp.sum(grad, axis=0, keepdims=True) for grad in grads]
        sums_ref[...] = jnp.concatenate([*sums, jnp.zeros((2, 2 * HD), F32)], axis=0)


def attend_back(y, q2, extra, k2, v, o, own, got, live, kind):
    length, width = v.shape
    half = own.shape[0]
    head = pl.BlockSpec((length, 2 * HD), lambda p, h, *_: (0, 2 * p + h))
    pair = pl.BlockSpec((length, 2 * HD), lambda p, h, *_: (0, p))
    part = pl.BlockSpec((half, 2 * HD), lambda p, h, *_: (0, p))
    return pl.pallas_call(
        attend_back_kernel,
        grid_spec=pltpu.PrefetchScalarGridSpec(
            num_scalar_prefetch=1,
            grid=(width // (2 * HD), 2),
            in_specs=[
                head, head, head, pair, pair, part, part, whole_block((length, 1)), whole_block((length, 1)),
            ],
            out_specs=[
                pl.BlockSpec((6, length, 2 * HD), lambda p, h, *_: (0, 0, p)),
                pl.BlockSpec((8, 2 * HD), lambda p, h, *_: (0, p)),
            ],
            scratch_shapes=[
                *[pltpu.VMEM((2, length, 2 * HD), F32)] * 3,
                pltpu.VMEM((length, 2 * HD), F32),
                pltpu.VMEM((length, 2 * HD), BF16),
            ],
        ),
        out_shape=[struct((6, length, width), BF16), struct((8, width), F32)],
        compiler_params=params(60),
        cost_estimate=cost(20 * length * length * width, 40 * length * width, length * length * width // HD),
        name="attend_back",
    )(y, q2, extra, k2, v, o, own, got, live, kind)


def normalise(value):
    centre = value - jnp.mean(value, axis=-1, keepdims=True)
    inverse = lax.rsqrt(jnp.mean(centre * centre, axis=-1, keepdims=True) + NORM_EPS)
    return centre * inverse, inverse


def normalise_back(scaled, normal, inverse):
    return inverse * (
        scaled
        - jnp.mean(scaled, axis=-1, keepdims=True)
        - normal * jnp.mean(scaled * normal, axis=-1, keepdims=True)
    )


def gelu_pair(values):
    cumulative = 0.5 * (1.0 + lax.erf(values * (1.0 / math.sqrt(2.0))))
    density = jnp.exp(-0.5 * values * values) * (1.0 / math.sqrt(2.0 * math.pi))
    return values * cumulative, cumulative + values * density


def column_sum(value):
    return jnp.sum(value, axis=0, keepdims=True)


def group_cuts(half):
    return half // 2, half // 128 * 5 // 6 * 128


def middle_kernel(at_ref, x_ref, cot_ref, live_ref, own_ref, got_ref, wo_ref, wi_ref, wu_ref, *rest):
    arrived = rest[:SLICES]
    arrived_late = rest[SLICES : 2 * SLICES]
    (
        vec_ref, bias_ref, out_ref, first_ref, dco_ref, cross_ref, late_out_ref, left_ref,
        keep0_ref, keep1_ref, keep2_ref, left_send_ref, send0_ref, send1_ref, send2_ref,
        sums_ref, inner_sums_ref, slope_ref, early_ref, late_ref,
    ) = rest[2 * SLICES :]
    step = pl.program_id(0)
    me = at_ref[1]
    lower = me % 2 == 0
    hidden, model, width = wi_ref.shape[1], x_ref.shape[1], wo_ref.shape[0]
    half = hidden // 2
    ca, cb = group_cuts(half)

    @pl.when(step == 0)
    def _():
        for k in range(SLICES):
            early_ref[me ^ k] = arrived[k][...].astype(BF16)
            late_ref[me ^ k] = arrived_late[k][...].astype(BF16)

    def foreign(ref, a, b):
        return ref[:, a:b, :].reshape(SLICES * (b - a), model)

    vec = [vec_ref[k : k + 1, :] for k in range(6)]
    got = got_ref[...].astype(BF16)
    own = own_ref[...]
    cut = [width // SLICES, (width + model) // SLICES, (width + 2 * model) // SLICES]
    wo_far = foreign(early_ref, 0, cut[0])
    first = mm(own, wo_ref[...], NN) + mm(got, wo_far, NN) + vec[0] + x_ref[...].astype(F32)
    n1, inv1 = normalise(first)
    normed = n1 * vec[1] + vec[2]
    low = normed.astype(BF16)

    def inner(part):
        if part < 2:
            return wi_ref[:, half * part : half * (part + 1)]
        return foreign(early_ref, cut[part - 2], cut[part - 1])

    def outer(part):
        if part < 2:
            return wu_ref[half * part : half * (part + 1), :]
        per = SLICES // 2
        block = late_ref[per * (part - 2) : per * (part - 1), :, :]
        return block.reshape(half, model)

    def both(index, value):
        turned = value.astype(F32).T
        left_ref[index] = turned.astype(BF16)
        left_send_ref[model * index : model * (index + 1), :] = turned

    def split(values):
        first, second = (value.astype(F32) for value in values)
        keep = jnp.where(lower, first, second).astype(BF16)
        return keep, jnp.where(lower, second, first)

    both(0, low)
    second = vec[3] + normed
    for far in range(2):
        pair = []
        for part in (2 * far, 2 * far + 1):
            pre = mm(low, inner(part), NN) + bias_ref[part : part + 1, :]
            active, slope = gelu_pair(pre)
            active = active.astype(BF16)
            slope_ref[:, half * part : half * (part + 1)] = slope
            pair.append(active)
            second = second + mm(active, outer(part), NN)
        keep, send = split(pair)
        at1 = (half - ca + half - cb) * far + half - ca
        for value, ref1, ref2 in ((keep, keep1_ref, keep2_ref), (send, send1_ref, send2_ref)):
            ref2[:, cb * far : cb * (far + 1)] = value[:, :cb]
            ref1[:, at1 : at1 + half - cb] = value[:, cb:]
    n2, inv2 = normalise(second)
    live = live_ref[...] > 0.5
    result = jnp.where(live, n2 * vec[4] + vec[5], 0.0).astype(BF16)
    out_ref[...] = result
    cross_ref[:, width:] = result[:, : model // 2].astype(F32)
    late_out_ref[...] = result[:, model // 2 :].astype(F32)
    dz = jnp.where(live, cot_ref[...].astype(F32), 0.0)
    d_second = normalise_back(dz * vec[4], n2, inv2)
    d_low = d_second.astype(BF16)
    both(1, d_low)
    d_normed = d_second
    inner_sums = []
    for far in range(2):
        pair = []
        for part in (2 * far, 2 * far + 1):
            d_hidden = mm(d_low, outer(part), NT)
            d_inner = (d_hidden * slope_ref[:, half * part : half * (part + 1)]).astype(BF16)
            pair.append(d_inner)
            inner_sums.append(column_sum(d_inner.astype(F32)))
            d_normed = d_normed + mm(d_inner, inner(part), NT)
        keep, send = split(pair)
        at1 = (half - ca + half - cb) * far
        for value, ref0, ref1 in ((keep, keep0_ref, keep1_ref), (send, send0_ref, send1_ref)):
            ref0[:, ca * far : ca * (far + 1)] = value[:, :ca]
            ref1[:, at1 : at1 + half - ca] = value[:, ca:]
    d_first = normalise_back(d_normed * vec[1], n1, inv1)
    first_ref[...] = d_first
    d_attn = d_first.astype(BF16)
    both(2, d_attn)
    dco_ref[...] = mm(d_attn, wo_ref[...], NT).astype(BF16).astype(F32)
    cross_ref[:, :width] = mm(d_attn, wo_far, NT).astype(BF16).astype(F32)
    keep, send = split((own, got))
    keep0_ref[:, 2 * ca :] = keep
    send0_ref[:, 2 * ca :] = send
    sums = jnp.concatenate(
        [
            column_sum(d_first),
            column_sum(d_normed * n1),
            column_sum(d_normed),
            column_sum(d_second),
            column_sum(dz * n2),
            column_sum(dz),
            jnp.zeros((2, model), F32),
        ],
        axis=0,
    )
    inner_sums = jnp.concatenate([*inner_sums, jnp.zeros((4, half), F32)], axis=0)

    @pl.when(step == 0)
    def _():
        sums_ref[...] = sums
        inner_sums_ref[...] = inner_sums

    @pl.when(step != 0)
    def _():
        sums_ref[...] += sums
        inner_sums_ref[...] += inner_sums


def middle(at, x, cot, live, context, got, wo, wi, wu, early, late, vec, bias, rows=256):
    half, width = got.shape
    model, hidden = wi.shape
    rows = min(rows, half)
    steps = half // rows
    mine = lambda w: pl.BlockSpec((rows, w), lambda i, s: (i + s[0] * steps, 0))
    tile = lambda w: pl.BlockSpec((rows, w), lambda i, s: (i, 0))
    ca, cb = group_cuts(hidden // 2)
    widths = (2 * ca + width, 2 * (hidden - ca - cb), 2 * cb)
    return pl.pallas_call(
        middle_kernel,
        grid_spec=pltpu.PrefetchScalarGridSpec(
            num_scalar_prefetch=1,
            grid=(steps,),
            in_specs=[
                mine(model), mine(model), mine(1), mine(width), tile(width),
                whole_block(wo.shape), whole_block(wi.shape), whole_block(wu.shape),
                *(whole_block(a.shape) for a in (*early, *late)),
                whole_block(vec.shape), whole_block(bias.shape),
            ],
            out_specs=[
                tile(model), tile(model), tile(width), tile(width + model // 2), tile(model // 2),
                pl.BlockSpec((3, model, rows), lambda i, s: (0, 0, i)),
                *(tile(w) for w in widths),
                pl.BlockSpec((3 * model, rows), lambda i, s: (0, i)),
                *(tile(w) for w in widths),
                pl.BlockSpec((8, model), lambda i, s: (0, 0)),
                pl.BlockSpec((8, hidden // 2), lambda i, s: (0, 0)),
            ],
            scratch_shapes=[
                pltpu.VMEM((rows, 2 * hidden), F32),
                pltpu.VMEM((SLICES, *early[0].shape), BF16),
                pltpu.VMEM((SLICES, *late[0].shape), BF16),
            ],
        ),
        out_shape=[
            struct((half, model), BF16), struct((half, model), F32),
            struct((half, width), F32), struct((half, width + model // 2), F32),
            struct((half, model // 2), F32),
            struct((3, model, half), BF16),
            *(struct((half, w), BF16) for w in widths),
            struct((3 * model, half), F32),
            *(struct((half, w), F32) for w in widths),
            struct((8, model), F32), struct((8, hidden // 2), F32),
        ],
        compiler_params=params(63),
        cost_estimate=cost(
            16 * half * model * (hidden + width // 2), 24 * model * hidden + 80 * half * model, 6 * half * hidden
        ),
        name="middle",
    )(at, x, cot, live, context, got, wo, wi, wu, *early, *late, vec, bias)


def weight_kernel(slot, group, tiles, bit_ref, right_ref, right_got_ref, *rest):
    keep_ref, send_ref = rest[-2:]
    lefts = [rest[2 * k][0] for k in range(len(rest) // 2 - 1)]
    lefts_got = [rest[2 * k + 1][...].astype(BF16) for k in range(len(rest) // 2 - 1)]

    def product(index, a, b):
        value = mm(lefts[index], right_ref[:, a:b], NN)
        return value + mm(lefts_got[index], right_got_ref[:, a:b].astype(BF16), NN)

    if slot is None:
        middle_column = right_ref.shape[1] // 2
        for index, a, b in tiles:
            ref, base = (keep_ref, 0) if b <= middle_column else (send_ref, middle_column)
            ref[:, a - base : b - base] = product(index, a, b)
        return
    kept = bit_ref[slot] == 0
    for index, a, b in tiles:
        value = product(index, a, b)
        pairs = value.reshape(value.shape[0] // (2 * group), 2, group, b - a)
        first, second = pairs[:, 0], pairs[:, 1]
        keep_ref[:, :, a:b] = jnp.where(kept, first, second)
        send_ref[:, :, a:b] = jnp.where(kept, second, first)


def weight_grads(at, slot, left, left_got, right, right_got, indices, tiles, group):
    _, model, depth = left.shape
    rows = model // 2
    columns = right.shape[1]
    args = [right, right_got]
    specs = [whole_block(right.shape), whole_block(right_got.shape)]
    for index in indices:
        args += [left, left_got]
        specs += [
            pl.BlockSpec((1, rows, depth), lambda i, s, index=index: (index, i, 0)),
            pl.BlockSpec((rows, depth), lambda i, s, index=index: (2 * index + i, 0)),
        ]
    if slot is None:
        shape = (model, columns // 2)
        out = pl.BlockSpec((rows, columns // 2), lambda i, s: (i, 0))
    else:
        blocks = rows // (2 * group)
        shape = (2 * blocks, group, columns)
        out = pl.BlockSpec((blocks, group, columns), lambda i, s: (i, 0, 0))
    return pl.pallas_call(
        functools.partial(weight_kernel, slot, group, tiles),
        grid_spec=pltpu.PrefetchScalarGridSpec(
            num_scalar_prefetch=1, grid=(2,), in_specs=specs, out_specs=[out, out]
        ),
        out_shape=[struct(shape, F32)] * 2,
        compiler_params=params(56),
        cost_estimate=cost(4 * depth * model * columns, 4 * model * columns + 8 * depth * columns),
        name="weight_grads",
    )(at, *args)


def project_weight_kernel(turned_ref, grad_ref, extra_ref, out_ref):
    width = grad_ref.shape[2]
    grads = jnp.concatenate([grad_ref[c] for c in range(6)], axis=1)
    out_ref[:, : 6 * width] = mm(turned_ref[...], grads, NN)
    out_ref[:, 6 * width :] = extra_ref[...]


def project_weight_grads(turned, grads, extra, rows=256):
    model, length = turned.shape
    width = grads.shape[2]
    columns = 6 * width + extra.shape[1]
    return pl.pallas_call(
        project_weight_kernel,
        grid=(model // rows,),
        in_specs=[
            pl.BlockSpec((rows, length), lambda i: (i, 0)),
            whole_block(grads.shape),
            pl.BlockSpec((rows, extra.shape[1]), lambda i: (i, 0)),
        ],
        out_specs=pl.BlockSpec((rows, columns), lambda i: (i, 0)),
        out_shape=struct((model, columns), F32),
        compiler_params=params(48),
        cost_estimate=cost(2 * length * model * columns, 4 * model * columns + 12 * length * width),
        name="project_weight_grads",
    )(turned, grads, extra)


def turn_kernel(value_ref, out_ref):
    out_ref[...] = value_ref[...].astype(F32).T.astype(BF16)


def turn(value, columns=256):
    length, model = value.shape
    return pl.pallas_call(
        turn_kernel,
        grid=(model // columns,),
        in_specs=[pl.BlockSpec((length, columns), lambda i: (0, i))],
        out_specs=pl.BlockSpec((columns, length), lambda i: (i, 0)),
        out_shape=struct((model, length), BF16),
        compiler_params=params(32),
        cost_estimate=cost(length * model, 4 * length * model),
        name="turn",
    )(value)


def input_kernel(steps, y_ref, grad_ref, wq_ref, wk_ref, wv_ref, first_ref, out_ref):
    grads = jnp.concatenate([grad_ref[c] for c in range(6)], axis=1)
    weights = jnp.concatenate([*(wq_ref[c] for c in range(4)), wk_ref[...], wv_ref[...]], axis=1)
    total = mm(grads, weights, NT)
    mine = pl.program_id(0) // steps == y_ref[0]
    out_ref[...] = total + jnp.where(mine, first_ref[...], 0.0)


def input_part(y, grads, wq, wk, wv, first, rows=256):
    _, length, width = grads.shape
    half, model = first.shape
    rows = min(rows, half)
    steps = half // rows
    return pl.pallas_call(
        functools.partial(input_kernel, steps),
        grid_spec=pltpu.PrefetchScalarGridSpec(
            num_scalar_prefetch=1,
            grid=(length // rows,),
            in_specs=[
                pl.BlockSpec((6, rows, width), lambda i, s: (0, i, 0)),
                whole_block(wq.shape), whole_block(wk.shape), whole_block(wv.shape),
                pl.BlockSpec((rows, model), lambda i, s: (jnp.clip(i - s[0] * steps, 0, steps - 1), 0)),
            ],
            out_specs=pl.BlockSpec((rows, model), lambda i, s: (i, 0)),
        ),
        out_shape=struct((length, model), F32),
        compiler_params=params(48),
        cost_estimate=cost(12 * length * model * width, 16 * model * width + 8 * length * model),
        name="input_part",
    )(y, grads, wq, wk, wv, first)


def place_kernel(y_ref, own_ref, first_ref, second_ref, out_ref):
    mine = pl.program_id(0) == y_ref[0]
    got = jnp.concatenate([first_ref[...], second_ref[...]], axis=1)
    out_ref[...] = jnp.where(mine, own_ref[...].astype(F32), got).astype(BF16)


def place_rows(y, own, first, second):
    half, model = own.shape
    return pl.pallas_call(
        place_kernel,
        grid_spec=pltpu.PrefetchScalarGridSpec(
            num_scalar_prefetch=1,
            grid=(2,),
            in_specs=[
                whole_block(own.shape),
                pl.BlockSpec((half, model // 2), lambda i, s: (0, 1)),
                whole_block(second.shape),
            ],
            out_specs=pl.BlockSpec((half, model), lambda i, s: (i, 0)),
        ),
        out_shape=struct((2 * half, model), BF16),
        compiler_params=params(32),
        cost_estimate=cost(half * model, 12 * half * model),
        name="place_rows",
    )(y, own, first, second)


def round_kernel(value_ref, out_ref):
    out_ref[...] = value_ref[...].astype(BF16)


def round_rows(value):
    length, model = value.shape
    rows = min(512, length)
    tile = pl.BlockSpec((rows, model), lambda i: (i, 0))
    return pl.pallas_call(
        round_kernel,
        grid=(length // rows,),
        in_specs=[tile],
        out_specs=tile,
        out_shape=struct((length, model), BF16),
        cost_estimate=cost(length * model, 6 * length * model),
        name="round_rows",
    )(value)


def per_device(
    devices,
    tokens,
    lengths,
    entity_flags,
    query_weight,
    query_bias,
    key_weight,
    key_bias,
    value_weight,
    value_bias,
    output_weight,
    output_bias,
    attn_gain,
    attn_shift,
    inner_weight,
    inner_bias,
    outer_weight,
    outer_bias,
    final_gain,
    final_shift,
    cotangent,
):
    x = tokens[0]
    length, model = x.shape
    width = key_weight.shape[1]
    hidden = inner_weight.shape[1]
    half = length // 2
    bits = devices.bit_length() - 1
    y = lax.axis_index("tensor")
    d = lax.axis_index("dp")

    def swap(value, mask):
        return lax.ppermute(value, "dp", [(i, i ^ mask) for i in range(devices)])

    def cross(value):
        return lax.ppermute(value, "tensor", [(0, 1), (1, 0)])

    me = d % SLICES
    core = d % 2
    rows = model // devices
    near_mask, far_mask = 96 // rows, 192 // rows
    at = jnp.stack([y, me, (d // near_mask) % 2, (d // far_mask) % 2]).astype(jnp.int32)
    tie = lax.optimization_barrier

    def cut(array, index):
        size = array.shape[0] // SLICES
        return lax.dynamic_slice_in_dim(array, index * size, size, 0)

    def pack(index):
        wide = cut(inner_weight, index)
        early = jnp.concatenate([cut(output_weight, index), wide[:, :model], wide[:, model:]], axis=0)
        return early.astype(F32)

    def pack_late(index):
        return cut(outer_weight, index).astype(F32)

    live = (lax.broadcasted_iota(jnp.int32, (length, 1), 0) < lengths[0]).astype(F32)
    kind = (entity_flags[0] == 1).astype(F32).reshape(length, 1)

    e0 = cross(pack(me))
    far_bias = cross(inner_bias)
    q2, k2, v = project(
        x, kind, query_weight, query_bias, key_weight, key_bias, value_weight, value_bias
    )
    e0, l0, q2 = tie((e0, pack_late(me), q2))
    e2 = swap(e0, 2)
    e4 = swap(e0, 4)
    e1 = swap(e0, 1)
    l0 = cross(l0)
    context, extra = attend(q2, k2, v, live)
    sent = lax.dynamic_slice_in_dim(context, half * (1 - y), half, 0).astype(F32)
    e1, e2, e4, l0, sent, l6 = tie((e1, e2, e4, l0, sent, pack_late(me ^ 6)))
    got = cross(sent)
    l2 = swap(l0, 2)
    l4 = swap(l0, 4)
    e6 = swap(e4, 2)
    l6 = cross(l6)
    l1 = swap(l0, 1)
    e3 = swap(e2, 1)
    e5 = swap(e4, 1)
    x_turned = turn(x)
    got, l2, l4, e6, l6, l1, e3, e5, x_turned = tie((got, l2, l4, e6, l6, l1, e3, e5, x_turned))
    e7 = swap(e6, 1)
    l3 = swap(l2, 1)
    l5 = swap(l4, 1)
    l7 = swap(l6, 1)
    early = (e0, e1, e2, e3, e4, e5, e6, e7)
    late = (l0, l1, l2, l3, l4, l5, l6, l7)

    vec = jnp.stack(
        [output_bias, attn_gain, attn_shift, outer_bias, final_gain, final_shift, outer_bias, outer_bias]
    )
    bias = jnp.concatenate([inner_bias, far_bias, inner_bias, far_bias]).reshape(8, hidden // 2)
    (
        out_rows, d_first, dco, first_cross, out_late, left, keep0, keep1, keep2, left_send, send0, send1, send2,
        sums, inner_sums,
    ) = middle(
        at, x, cotangent[0], live, context, got, output_weight, inner_weight, outer_weight,
        early, late, vec, bias,
    )
    d_got = cross(first_cross)
    left_got = swap(left_send, 1)
    got0 = swap(send0, 1)
    got1 = swap(send1, 1)
    got2 = swap(send2, 1)

    ca, cb = group_cuts(hidden // 2)
    da, db = hidden // 2 - ca, hidden // 2 - cb
    g0_keep, g0_send = weight_grads(
        at, 2, left, left_got, keep0, got0, (0, 2),
        ((0, 0, ca), (0, ca, 2 * ca), (1, 2 * ca, 2 * ca + width)), near_mask * rows,
    )
    g2_keep, g2_send = weight_grads(
        at, 3, left, left_got, keep2, got2, (1,), ((0, 0, cb), (0, cb, 2 * cb)), far_mask * rows
    )
    g1_keep, g1_send = weight_grads(
        at, None, left, left_got, keep1, got1, (0, 1),
        (
            (0, 0, da), (1, da, da + db),
            (0, da + db, 2 * da + db), (1, 2 * da + db, 2 * (da + db)),
        ),
        None,
    )
    g0_got = swap(g0_send, near_mask)
    g2_got = swap(g2_send, far_mask)
    g1_got = cross(g1_send)

    inner_columns = inner_sums[:4].reshape(2, model, 2)
    shared = jnp.broadcast_to(sums[:6].T[None], (2, model, 6))
    columns = jnp.concatenate([shared, inner_columns], axis=2)
    columns = columns[0] + cross(columns[1])

    g0_send, g1_send, g2_send, dco, d_got = tie((g0_send, g1_send, g2_send, dco, d_got))
    d_all, bias_sums = attend_back(at, q2, extra, k2, v, context, dco, d_got, live, kind)
    part = input_part(at, d_all, query_weight, key_weight, value_weight, d_first)
    per = width // devices
    bias_columns = jnp.pad(
        bias_sums[:6].reshape(6, devices, per), ((0, 0), (0, 0), (0, rows - per))
    ).reshape(6, model)
    extra_columns = jnp.pad(jnp.concatenate([bias_columns.T, columns], axis=1), ((0, 0), (0, 114)))
    projections = project_weight_grads(x_turned, d_all, extra_columns)
    got_late = cross(out_late)
    input_sum = lax.psum(part, "tensor")
    summed = lax.psum_scatter(projections, "dp", scatter_dimension=0, tiled=True)

    def spread(array, done):
        dims = [1 if (1 << (bits - 1 - k)) in done else 2 for k in range(bits)]
        return array.reshape(*dims, rows, array.shape[-1])

    def halves(array, mask):
        axis = bits - mask.bit_length()
        bit = (d // mask) % 2
        send = lax.dynamic_slice_in_dim(array, 1 - bit, 1, axis)
        return lax.dynamic_slice_in_dim(array, bit, 1, axis), send

    g0_got, g1_got, g2_got, got_late, part, projections = tie(
        (g0_got, g1_got, g2_got, got_late, part, projections)
    )
    g0 = spread(g0_keep + g0_got, (near_mask,))
    g1 = spread(g1_keep + g1_got, ())
    g2 = spread(g2_keep + g2_got, (far_mask,))
    g0_keep, g0_send = g0[..., :ca], g0[..., ca : 2 * ca]
    t_keep, t_send = halves(g0[..., 2 * ca :], far_mask)
    g1_keep, g1_send = halves(g1, far_mask)
    g2_keep, g2_send = halves(g2, near_mask)
    g0_got = cross(g0_send)
    t_got = swap(t_send, far_mask)
    g1_got = swap(g1_send, far_mask)
    g2_got = swap(g2_send, near_mask)
    g0_got, g1_got, g2_got, t_got = tie((g0_got, g1_got, g2_got, t_got))
    t_send = t_keep + t_got
    g0_keep, g0_send = halves(g0_keep + g0_got, far_mask)
    g1_keep, g1_send = halves(g1_keep + g1_got, near_mask)
    g2 = g2_keep + g2_got
    g2_keep, g2_send = g2[..., :cb], g2[..., cb:]
    g0_got = swap(g0_send, far_mask)
    t_got = cross(t_send)
    g1_got = swap(g1_send, near_mask)
    g2_got = cross(g2_send)
    g0_got, g1_got, g2_got, t_got = tie((g0_got, g1_got, g2_got, t_got))
    t_sum = jnp.where(core == 0, t_send, t_got)
    whole = jnp.concatenate([g0_keep + g0_got, t_sum, g1_keep + g1_got, g2_keep + g2_got], axis=-1)
    for k in range(1, bits):
        if (1 << k) not in (near_mask, far_mask):
            keep, send = halves(whole, 1 << k)
            whole = keep + swap(send, 1 << k)
    keep, send = halves(whole, 1)
    got_last = swap(send, 1).reshape(rows, -1)
    keep = keep.reshape(rows, -1)
    low_half = jnp.where(core == 0, keep, got_last)
    high_half = jnp.where(core == 0, got_last, keep)
    at1 = ca + width
    at2 = at1 + da + db

    def inner_half(array):
        return [array[:, :ca], array[:, at1 : at1 + da]]

    def outer_half(array):
        return [array[:, at2:], array[:, at1 + da : at2]]

    grad_inner = jnp.concatenate(inner_half(low_half) + inner_half(high_half), axis=1)
    grad_outer = jnp.concatenate(outer_half(low_half) + outer_half(high_half), axis=1).T
    grad_output = (keep[:, ca:at1] + got_last[:, ca:at1]).T
    layer_out = place_rows(at, out_rows, d_got, got_late)
    input_grad = round_rows(input_sum)

    small = summed[:, 6 * width + 6 :]
    piece = lambda k: summed[:, width * k : width * (k + 1)]
    grad_query_weight = jnp.stack([piece(0), piece(1), piece(2), piece(3)])
    biases = summed[:per, 6 * width : 6 * width + 6].T
    return (
        layer_out[None],
        input_grad[None],
        grad_query_weight,
        biases[:4],
        piece(4),
        biases[4],
        piece(5),
        biases[5],
        grad_output,
        small[:, 0],
        small[:, 1],
        small[:, 2],
        grad_inner,
        small[:, 6:8].reshape(2 * rows),
        grad_outer,
        small[:, 3],
        small[:, 4],
        small[:, 5],
    )


def solution(mesh):
    return jax.shard_map(
        functools.partial(per_device, mesh.shape["dp"]),
        mesh=mesh,
        in_specs=(
            P("dp", None, None),
            P("dp"),
            P("dp", None),
            P(None, None, "tensor"),
            P(None, "tensor"),
            P(None, "tensor"),
            P("tensor"),
            P(None, "tensor"),
            P("tensor"),
            P("tensor", None),
            P(),
            P(),
            P(),
            P(None, "tensor"),
            P("tensor"),
            P("tensor", None),
            P(),
            P(),
            P(),
            P("dp", None, None),
        ),
        out_specs=(
            P("dp", None, None),
            P("dp", None, None),
            P(None, "dp", "tensor"),
            P(None, ("tensor", "dp")),
            P("dp", "tensor"),
            P(("tensor", "dp")),
            P("dp", "tensor"),
            P(("tensor", "dp")),
            P("tensor", "dp"),
            P("dp"),
            P("dp"),
            P("dp"),
            P("dp", "tensor"),
            P(("tensor", "dp")),
            P("tensor", "dp"),
            P("dp"),
            P("dp"),
            P("dp"),
        ),
        check_vma=False,
    )
```

time: 421 us -> 361 us (0.86)
  waiting for transfers between devices: 201 us -> 134 us
  between operations: 2.12 us -> 17 us
  local copies, waits for them, and re-layouts: 42.9 us -> 35.8 us
    ppermute x9 -> x12, waiting for transfers between devices: 141 us -> 41.1 us  [cross(): return lax.ppermute(value, 'tensor', [(0, 1), (1, 0)])]
    ppermute x22 -> x26, waiting for transfers between devices: 60.2 us -> 92.4 us  [swap(): return lax.ppermute(value, 'dp', [(i, i ^ mask) for i in range(devices)])]
    dynamic_slice x18 -> x8, local copies, waits for them, and re-layouts: 19.1 us -> 6.93 us  [the longest x7 6.03 us: halves(): send = lax.dynamic_slice_in_dim(array, 1 - bit, 1, axis)]
    ppermute x22 -> x26, starting transfers between devices: 21.8 us -> 16.7 us  [swap(): return lax.ppermute(value, 'dp', [(i, i ^ mask) for i in range(devices)])]
    unnamed x79 -> x93, local copies, waits for them, and re-layouts: 11.6 us -> 15 us
    pallas_call x6 -> x8, Pallas kernels: 70.7 us -> 72.5 us  [the longest x1 24 us: attend_back(): pl.pallas_call(attend_back_kernel, grid_spec=pltpu.PrefetchScalarGridSpec...]
    ppermute x9 -> x12, starting transfers between devices: 12 us -> 13.3 us  [cross(): return lax.ppermute(value, 'tensor', [(0, 1), (1, 0)])]
    add x14 -> x12, other arithmetic: 15.5 us -> 15.9 us  [the longest x1 2.37 us: per_device(): g2 = spread(g2_keep + g2_got, (far_mask,))]
  transfers between devices with their start and end apart: 31 -> 40, of which waited for: 13 -> 15; matrix products, arithmetic and copies ran while one was open for 12% -> 10% of each run, Pallas kernels for 21% -> 25%
where the time goes in v2:
time: 361 us; the launch traced here: 358 us
  waiting for transfers between devices  134 us (37%)
  Pallas kernels  117 us (32%)
  local copies, waits for them, and re-layouts  35.8 us (10%)
  starting transfers between devices  30.1 us (8%)
  other arithmetic  24.3 us (7%)
  between operations  17 us (5%)
    ppermute x26, waiting for transfers between devices, swap(): return lax.ppermute(value, 'dp', [(i, i ^ mask) for i in range(devices)])  92.4 us
    ppermute x12, waiting for transfers between devices, cross(): return lax.ppermute(value, 'tensor', [(0, 1), (1, 0)])  41.1 us
    pallas_call x1, Pallas kernels, middle(): pl.pallas_call(middle_kernel, grid_spec=pltpu.PrefetchScalarGridSpec(num_...  28.5 us
    pallas_call x1, Pallas kernels, attend_back(): pl.pallas_call(attend_back_kernel, grid_spec=pltpu.PrefetchScalarGridSpec...  24 us
    pallas_call x3, Pallas kernels, weight_grads(): pl.pallas_call(functools.partial(weight_kernel, slot, group, tiles), grid...  22.6 us
    ppermute x26, starting transfers between devices, swap(): return lax.ppermute(value, 'dp', [(i, i ^ mask) for i in range(devices)])  16.7 us
    unnamed x93, local copies, waits for them, and re-layouts  15 us
    pallas_call x1, Pallas kernels, attend(): pl.pallas_call(attend_kernel, grid=(width // (2 * HD), 2), in_specs=[head...  14.1 us
  transfers between devices with their start and end apart: 40, of which 15 were waited for; matrix products, arithmetic and copies ran while one was open for 10% of the time, Pallas kernels for 25%

profile of v2, /device:TPU:0, one launch (start us, length us, event | category | flops | bytes accessed | tf_op | source)
XLA Modules:
  0.0 358.5 jit_solution(15025326643044053587)
XLA Ops:
  10.1 3.0 collective-permute-start
  15.6 6.7 %project.1 = (bf16[1024,768]{1,0:T(8,128)(2,1)S(1)}, bf16[1024,768]{1,0:T(8,128)(2,1)S(1)}, bf16[1024,384]{1,0:T(8,128)(2,1)S(1)}) custom-call(bf16[1024,768]{1,0:T(8,128)(2,1)} %bitcast.50, f32[1024,1]{1,0:T(8,128)S(1)} %copy.56.kind_ref, bf16[4,768,384]{2,1,0:T(8,128)(2,1)} %wq_ref.3, f32[4,384]{1,0:T(4,128)S(1)} %copy-done.13, ...), custom_call_target="tpu_custom_call" | custom-call | flops 3623878656 | bytes 9437184 | tf_op jit(solution)/shard_map/project/pallas_call | solution.py:87
  25.4 4.3 %collective-permute-done.rest_0_ = f32[240,768]{1,0:T(8,128)} collective-permute-done((f32[240,768]{1,0:T(8,128)S(1)}, f32[240,768]{1,0:T(8,128)}, u32[]{:S(2)}, u32[]{:S(2)}) %collective-permute-start) | collective-permute-done | bytes 737312 | tf_op jit(solution)/shard_map/ppermute | solution.py:684
  36.1 14.1 %attend.1 = (bf16[1024,384]{1,0:T(8,128)(2,1)}, bf16[1024,768]{1,0:T(8,128)(2,1)}) custom-call(bf16[1024,768]{1,0:T(8,128)(2,1)} %copy-done.15, bf16[1024,768]{1,0:T(8,128)(2,1)} %copy-done.16, bf16[1024,384]{1,0:T(8,128)(2,1)} %copy-done.17, f32[1024,1]{1,0:T(8,128)} %fusion.live_ref), custom_call_target="tpu_custom_call" | custom-call | flops 4026531840 | bytes 7864320 | tf_op jit(solution)/shard_map/attend/pallas_call | solution.py:154
  54.8 12.6 %collective-permute-done.6.rest_10_ = f32[192,768]{1,0:T(8,128)} collective-permute-done((f32[192,768]{1,0:T(8,128)S(1)}, f32[192,768]{1,0:T(8,128)}, u32[]{:S(2)}, u32[]{:S(2)}) %collective-permute-start.6) | collective-permute-done | bytes 589856 | tf_op jit(solution)/shard_map/ppermute | solution.py:681
  70.4 14.3 %collective-permute-done.9.rest_14_ = f32[192,768]{1,0:T(8,128)} collective-permute-done((f32[192,768]{1,0:T(8,128)S(1)}, f32[192,768]{1,0:T(8,128)}, u32[]{:S(2)}, u32[]{:S(2)}) %collective-permute-start.9) | collective-permute-done | bytes 589856 | tf_op jit(solution)/shard_map/ppermute | solution.py:684
  91.2 28.5 %middle.1 = (bf16[512,768]{1,0:T(8,128)(2,1)}, f32[512,768]{1,0:T(8,128)}, f32[512,384]{1,0:T(8,128)}, f32[512,768]{1,0:T(8,128)}, f32[512,384]{1,0:T(8,128)}, /...) custom-call(s32[4]{0:T(128)} %pad_add_fusion.at_ref.bit_ref.y_ref, ...), custom_call_target="tpu_custom_call" | custom-call | flops 10871635968 | bytes 59768832 | tf_op jit(solution)/shard_map/middle/pallas_call | solution.py:426
  123.9 7.9 %collective-permute-done.21.right_got_ref = f32[512,1280]{1,0:T(8,128)} collective-permute-done((f32[512,1280]{1,0:T(8,128)}, f32[512,1280]{1,0:T(8,128)}, u32[]{:S(2)}, u32[]{:S(2)}) %collective-permute-start.21) | collective-permute-done | bytes 2621472 | tf_op jit(solution)/shard_map/ppermute | solution.py:681
  133.8 7.3 %weight_grads.5 = (f32[2,192,1280]{2,1,0:T(8,128)}, f32[2,192,1280]{2,1,0:T(8,128)}) custom-call(s32[4]{0:T(128)} %pad_add_fusion.at_ref.bit_ref.y_ref, bf16[512,1280]{1,0:T(8,128)(2,1)} %get-tuple-element.108.right_ref, f32[512,1280]{1,0:T(8,128)} %collective-permute-done.21.right_got_ref, bf16[3,768,512]{2,1,0:T(8,128)(2,1)} %get-tuple-element.102.rest_0_.rest_2_, ...), custom_call_target="tpu_custom_call" | custom-call | flops 2013265920 | bytes 9175040 | tf_op jit(solution)/shard_map/weight_grads/pallas_call | solution.py:513
  141.8 7.3 %weight_grads.4 = (f32[768,512]{1,0:T(8,128)}, f32[768,512]{1,0:T(8,128)}) custom-call(s32[4]{0:T(128)} %pad_add_fusion.at_ref.bit_ref.y_ref, bf16[512,1024]{1,0:T(8,128)(2,1)} %get-tuple-element.105.right_ref, f32[512,1024]{1,0:T(8,128)} %collective-permute-done.20.right_got_ref, bf16[3,768,512]{2,1,0:T(8,128)(2,1)} %get-tuple-element.102.rest_0_.rest_2_, ...), custom_call_target="tpu_custom_call" | custom-call | flops 1610612736 | bytes 7340032 | tf_op jit(solution)/shard_map/weight_grads/pallas_call | solution.py:513
  150.6 8.0 %weight_grads.3 = (f32[4,96,1152]{2,1,0:T(8,128)}, f32[4,96,1152]{2,1,0:T(8,128)}) custom-call(s32[4]{0:T(128)} %pad_add_fusion.at_ref.bit_ref.y_ref, bf16[512,1152]{1,0:T(8,128)(2,1)} %get-tuple-element.100.right_ref, f32[512,1152]{1,0:T(8,128)} %collective-permute-done.18.right_got_ref, bf16[3,768,512]{2,1,0:T(8,128)(2,1)} %get-tuple-element.102.rest_0_.rest_2_, ...), custom_call_target="tpu_custom_call" | custom-call | flops 1811939328 | bytes 8257536 | tf_op jit(solution)/shard_map/weight_grads/pallas_call | solution.py:513
  160.5 24.0 %attend_back.1 = (bf16[6,1024,384]{2,1,0:T(8,128)(2,1)}, f32[8,384]{1,0:T(8,128)}) custom-call(s32[4]{0:T(128)} %pad_add_fusion.at_ref.bit_ref.y_ref, bf16[1024,768]{1,0:T(8,128)(2,1)} %copy-done.15, bf16[1024,768]{1,0:T(8,128)(2,1)} %get-tuple-element.115.extra_ref, bf16[1024,768]{1,0:T(8,128)(2,1)} %copy-done.16, bf16[1024,384]{1,0:T(8,128)(2,1)} %copy-done.17, ...), custom_call_target="tpu_custom_call" | custom-call | flops 8053063680 | bytes 15728640 | tf_op jit(solution)/shard_map/attend_back/pallas_call | solution.py:233
  190.9 7.7 %input_part.1 = f32[1024,768]{1,0:T(8,128)} custom-call(s32[4]{0:T(128)S(1)} %copy-done.7, bf16[6,1024,384]{2,1,0:T(8,128)(2,1)} %get-tuple-element.117.grad_ref, bf16[4,768,384]{2,1,0:T(8,128)(2,1)S(1)} %copy-done.8, bf16[768,384]{1,0:T(8,128)(2,1)S(1)} %copy-done.10, bf16[768,384]{1,0:T(8,128)(2,1)S(1)} %copy-done.12, f32[512,768]{1,0:T(8,128)S(1)} %copy-done.14), custom_call_target="tpu_custom_call" | custom-call | flops 3623878656 | bytes 11010048 | tf_op jit(solution)/shard_map/input_part/pallas_call | solution.py:583
  198.6 8.1 %project_weight_grads.1 = f32[768,2432]{1,0:T(8,128)} custom-call(bf16[768,1024]{1,0:T(8,128)(2,1)S(1)} %copy-done.4, bf16[6,1024,384]{2,1,0:T(8,128)(2,1)} %get-tuple-element.117.grad_ref, f32[768,128]{1,0:T(8,128)S(1)} %pad.9.extra_ref), custom_call_target="tpu_custom_call" | custom-call | flops 3825205248 | bytes 12189696 | tf_op jit(solution)/shard_map/project_weight_grads/pallas_call | solution.py:536
  209.2 2.4 add.134
  224.5 17.5 %collective-permute-done.31 = f32[2,1,1,2,48,384]{5,4,3,2,1,0:T(8,128)} collective-permute-done((f32[2,1,1,2,48,384]{5,4,3,2,1,0:T(8,128)}, f32[2,1,1,2,48,384]{5,4,3,2,1,0:T(8,128)}, u32[]{:S(2)}, u32[]{:S(2)}) %collective-permute-start.31) | collective-permute-done | bytes 294944 | tf_op jit(solution)/shard_map/ppermute | solution.py:681
  242.1 8.2 %collective-permute-done.28 = f32[2,2,1,2,48,384]{5,4,3,2,1,0:T(8,128)} collective-permute-done((f32[2,2,1,2,48,384]{5,4,3,2,1,0:T(8,128)}, f32[2,2,1,2,48,384]{5,4,3,2,1,0:T(8,128)}, u32[]{:S(2)}, u32[]{:S(2)}) %collective-permute-start.28) | collective-permute-done | bytes 589856 | tf_op jit(solution)/shard_map/ppermute | solution.py:684
  262.4 6.0 %collective-permute-done.35 = f32[2,1,1,2,48,384]{5,4,3,2,1,0:T(8,128)} collective-permute-done((f32[2,1,1,2,48,384]{5,4,3,2,1,0:T(8,128)}, f32[2,1,1,2,48,384]{5,4,3,2,1,0:T(8,128)}, u32[]{:S(2)}, u32[]{:S(2)}) %collective-permute-start.35) | collective-permute-done | bytes 294944 | tf_op jit(solution)/shard_map/ppermute | solution.py:684
  268.4 2.3 collective-permute-done.32
  270.7 3.7 %collective-permute-done.33 = f32[2,1,1,2,48,512]{5,4,3,2,1,0:T(8,128)S(1)} collective-permute-done((f32[2,1,1,2,48,512]{5,4,3,2,1,0:T(8,128)}, f32[2,1,1,2,48,512]{5,4,3,2,1,0:T(8,128)S(1)}, u32[]{:S(2)}, u32[]{:S(2)}) %collective-permute-start.33) | collective-permute-done | bytes 393248 | tf_op jit(solution)/shard_map/ppermute | solution.py:681
  274.4 4.3 %collective-permute-done.34 = f32[2,1,1,2,48,640]{5,4,3,2,1,0:T(8,128)} collective-permute-done((f32[2,1,1,2,48,640]{5,4,3,2,1,0:T(8,128)}, f32[2,1,1,2,48,640]{5,4,3,2,1,0:T(8,128)}, u32[]{:S(2)}, u32[]{:S(2)}) %collective-permute-start.34) | collective-permute-done | bytes 491552 | tf_op jit(solution)/shard_map/ppermute | solution.py:684
  283.3 2.5 collective-permute-start.36
  285.8 47.2 %collective-permute-done.36 = f32[1,1,1,2,48,1920]{5,4,3,2,1,0:T(8,128)} collective-permute-done((f32[1,1,1,2,48,1920]{5,4,3,2,1,0:T(8,128)}, f32[1,1,1,2,48,1920]{5,4,3,2,1,0:T(8,128)}, u32[]{:S(2)}, u32[]{:S(2)}) %collective-permute-start.36) | collective-permute-done | bytes 737312 | tf_op jit(solution)/shard_map/ppermute | solution.py:681
  340.3 2.8 round_rows.1
  (236 shorter events, 90.6 us)
Async XLA Ops:
  8.1 332.3 %all-reduce.4.cloned.1.call-start = ((), (), s32[]{:S(2)}) async-start(), calls=%async_computation.1 | async-start | bytes 6291456 | tf_op jit(solution)/shard_map/psum | solution.py:791
  10.1 19.6 %collective-permute-start = (f32[240,768]{1,0:T(8,128)S(1)}, f32[240,768]{1,0:T(8,128)}, u32[]{:S(2)}, u32[]{:S(2)}) collective-permute-start(f32[240,768]{1,0:T(8,128)S(1)} %maximum_convert_fusion), channel_id=1, source_target_pairs={{0,1},{1,0},{2,3},{3,2},{4,5},{5,4},{6,7},{7,6},{8,9},{9,8},{10,11... | collective-permute-start | bytes 2211848 | tf_op jit(solution)/shard_map/ppermute | solution.py:684
  29.7 21.7 %collective-permute-start.1 = (f32[240,768]{1,0:T(8,128)}, f32[240,768]{1,0:T(8,128)S(1)}, u32[]{:S(2)}, u32[]{:S(2)}) collective-permute-start(f32[240,768]{1,0:T(8,128)} %collective-permute-done.rest_0_), channel_id=1, source_target_pairs={{0,2},{2,0},{4,6},{6,4},{8,10},{10,8},{12,14},{14,12},{16,18},{18,... | collective-permute-start | bytes 2211848 | tf_op jit(solution)/shard_map/ppermute | solution.py:681
  29.7 21.7 %collective-permute-start.2 = (f32[240,768]{1,0:T(8,128)}, f32[240,768]{1,0:T(8,128)S(1)}, u32[]{:S(2)}, u32[]{:S(2)}) collective-permute-start(f32[240,768]{1,0:T(8,128)} %collective-permute-done.rest_0_), channel_id=1, source_target_pairs={{0,4},{2,6},{4,0},{6,2},{8,12},{10,14},{12,8},{14,10},{16,20},{18,... | collective-permute-start | bytes 2211848 | tf_op jit(solution)/shard_map/ppermute | solution.py:681
  31.5 20.0 %collective-permute-start.3 = (f32[240,768]{1,0:T(8,128)}, f32[240,768]{1,0:T(8,128)S(1)}, u32[]{:S(2)}, u32[]{:S(2)}) collective-permute-start(f32[240,768]{1,0:T(8,128)} %collective-permute-done.rest_0_), channel_id=1, source_target_pairs={{0,8},{2,10},{4,12},{6,14},{8,0},{10,2},{12,4},{14,6},{16,24},{18,... | collective-permute-start | bytes 2211848 | tf_op jit(solution)/shard_map/ppermute | solution.py:681
  52.8 33.0 %collective-permute-start.5 = (f32[512,384]{1,0:T(8,128)S(1)}, f32[512,384]{1,0:T(8,128)S(1)}, u32[]{:S(2)}, u32[]{:S(2)}) collective-permute-start(f32[512,384]{1,0:T(8,128)S(1)} %dynamic-slice_convert_fusion), channel_id=1, source_target_pairs={{0,1},{1,0},{2,3},{3,2},{4,5},{5,4},{6,7},{7,6},{8,9},{9,8},{10,11... | collective-permute-start | bytes 2359304 | tf_op jit(solution)/shard_map/ppermute | solution.py:684
  54.3 30.4 %collective-permute-start.11 = (f32[240,768]{1,0:T(8,128)S(1)}, f32[240,768]{1,0:T(8,128)S(1)}, u32[]{:S(2)}, u32[]{:S(2)}) collective-permute-start(f32[240,768]{1,0:T(8,128)S(1)} %collective-permute-done.2.rest_2_), channel_id=1, source_target_pairs={{0,2},{2,0},{4,6},{6,4},{8,10},{10,8},{12,14},{14,12},{16,18},{18,... | collective-permute-start | bytes 2211848 | tf_op jit(solution)/shard_map/ppermute | solution.py:681
  54.3 30.4 %collective-permute-start.12 = (f32[240,768]{1,0:T(8,128)}, f32[240,768]{1,0:T(8,128)S(1)}, u32[]{:S(2)}, u32[]{:S(2)}) collective-permute-start(f32[240,768]{1,0:T(8,128)} %copy-done.42), channel_id=1, source_target_pairs={{0,2},{2,0},{4,6},{6,4},{8,10},{10,8},{12,14},{14,12},{16,18},{18,... | collective-permute-start | bytes 2211848 | tf_op jit(solution)/shard_map/ppermute | solution.py:681
  67.4 18.4 %collective-permute-start.8 = (f32[240,768]{1,0:T(8,128)}, f32[240,768]{1,0:T(8,128)}, u32[]{:S(2)}, u32[]{:S(2)}) collective-permute-start(f32[240,768]{1,0:T(8,128)} %copy-done.42), channel_id=1, source_target_pairs={{0,4},{2,6},{4,0},{6,2},{8,12},{10,14},{12,8},{14,10},{16,20},{18,... | collective-permute-start | bytes 2211848 | tf_op jit(solution)/shard_map/ppermute | solution.py:681
  120.3 28.8 %collective-permute-start.18 = (f32[512,1152]{1,0:T(8,128)}, f32[512,1152]{1,0:T(8,128)}, u32[]{:S(2)}, u32[]{:S(2)}) collective-permute-start(f32[512,1152]{1,0:T(8,128)} %get-tuple-element.101), channel_id=1, source_target_pairs={{0,2},{2,0},{4,6},{6,4},{8,10},{10,8},{12,14},{14,12},{16,18},{18,... | collective-permute-start | bytes 7077896 | tf_op jit(solution)/shard_map/ppermute | solution.py:681
  120.4 20.8 %collective-permute-start.20 = (f32[512,1024]{1,0:T(8,128)}, f32[512,1024]{1,0:T(8,128)}, u32[]{:S(2)}, u32[]{:S(2)}) collective-permute-start(f32[512,1024]{1,0:T(8,128)} %get-tuple-element.106), channel_id=1, source_target_pairs={{0,2},{2,0},{4,6},{6,4},{8,10},{10,8},{12,14},{14,12},{16,18},{18,... | collective-permute-start | bytes 6291464 | tf_op jit(solution)/shard_map/ppermute | solution.py:681
  120.8 38.5 %collective-permute-start.22 = (f32[512,768]{1,0:T(8,128)}, f32[512,768]{1,0:T(8,128)S(1)}, u32[]{:S(2)}, u32[]{:S(2)}) collective-permute-start(f32[512,768]{1,0:T(8,128)} %get-tuple-element.112), channel_id=1, source_target_pairs={{0,1},{1,0},{2,3},{3,2},{4,5},{5,4},{6,7},{7,6},{8,9},{9,8},{10,11... | collective-permute-start | bytes 4718600 | tf_op jit(solution)/shard_map/ppermute | solution.py:684
  131.8 27.0 %collective-permute-start.27 = (f32[768,8]{0,1:T(8,128)S(1)}, f32[768,8]{0,1:T(8,128)S(1)}, u32[]{:S(2)}, u32[]{:S(2)}) collective-permute-start(f32[768,8]{0,1:T(8,128)S(1)} %fusion.5), channel_id=1, source_target_pairs={{0,1},{1,0},{2,3},{3,2},{4,5},{5,4},{6,7},{7,6},{8,9},{9,8},{10,11... | collective-permute-start | bytes 73736 | tf_op jit(solution)/shard_map/ppermute | solution.py:684
  132.3 74.4 %collective-permute-start.26 = (f32[512,384]{1,0:T(8,128)S(1)}, f32[512,384]{1,0:T(8,128)S(1)}, u32[]{:S(2)}, u32[]{:S(2)}) collective-permute-start(f32[512,384]{1,0:T(8,128)S(1)} %copy-done.39), channel_id=1, source_target_pairs={{0,1},{1,0},{2,3},{3,2},{4,5},{5,4},{6,7},{7,6},{8,9},{9,8},{10,11... | collective-permute-start | bytes 2359304 | tf_op jit(solution)/shard_map/ppermute | solution.py:684
  141.2 67.4 %collective-permute-start.25 = (f32[2,192,1280]{2,1,0:T(8,128)}, f32[2,192,1280]{2,1,0:T(8,128)}, u32[]{:S(2)}, u32[]{:S(2)}) collective-permute-start(f32[2,192,1280]{2,1,0:T(8,128)} %get-tuple-element.110), channel_id=1, source_target_pairs={{0,8},{2,10},{4,12},{6,14},{8,0},{10,2},{12,4},{14,6},{16,24},{18,... | collective-permute-start | bytes 5898248 | tf_op jit(solution)/shard_map/ppermute | solution.py:681
  149.1 59.4 %collective-permute-start.24 = (f32[768,512]{1,0:T(8,128)}, f32[768,512]{1,0:T(8,128)}, u32[]{:S(2)}, u32[]{:S(2)}) collective-permute-start(f32[768,512]{1,0:T(8,128)} %get-tuple-element.107), channel_id=1, source_target_pairs={{0,1},{1,0},{2,3},{3,2},{4,5},{5,4},{6,7},{7,6},{8,9},{9,8},{10,11... | collective-permute-start | bytes 4718600 | tf_op jit(solution)/shard_map/ppermute | solution.py:684
  158.8 49.8 %collective-permute-start.23 = (f32[4,96,1152]{2,1,0:T(8,128)}, f32[4,96,1152]{2,1,0:T(8,128)}, u32[]{:S(2)}, u32[]{:S(2)}) collective-permute-start(f32[4,96,1152]{2,1,0:T(8,128)} %get-tuple-element.104), channel_id=1, source_target_pairs={{0,4},{2,6},{4,0},{6,2},{8,12},{10,14},{12,8},{14,10},{16,20},{18,... | collective-permute-start | bytes 5308424 | tf_op jit(solution)/shard_map/ppermute | solution.py:681
  208.6 134.5 %reduce-scatter.2.cloned.1.call-start = ((), (), s32[]{:S(2)}) async-start(), calls=%async_computation.2 | async-start | bytes 7938048 | tf_op jit(solution)/shard_map/reduce_scatter | solution.py:792
  212.6 37.6 %collective-permute-start.30 = (f32[2,1,1,2,48,1280]{5,4,3,2,1,0:T(8,128)}, f32[2,1,1,2,48,1280]{5,4,3,2,1,0:T(8,128)}, u32[]{:S(2)}, u32[]{:S(2)}) collective-permute-start(f32[2,1,1,2,48,1280]{5,4,3,2,1,0:T(8,128)} %constant_dynamic-slice_fusion.6), channel_id=1, source_target_pairs={{0,4},{2,6},{4,0},{6,2},{8,12},{10,14},{12,8},{14,10},{16,20},{18,... | collective-permute-start | bytes 2949128 | tf_op jit(solution)/shard_map/ppermute | solution.py:681
  216.7 33.5 %collective-permute-start.29 = (f32[2,1,2,2,48,512]{5,4,3,2,1,0:T(8,128)}, f32[2,1,2,2,48,512]{5,4,3,2,1,0:T(8,128)}, u32[]{:S(2)}, u32[]{:S(2)}) collective-permute-start(f32[2,1,2,2,48,512]{5,4,3,2,1,0:T(8,128)} %constant_dynamic-slice_fusion.7), channel_id=1, source_target_pairs={{0,8},{2,10},{4,12},{6,14},{8,0},{10,2},{12,4},{14,6},{16,24},{18,... | collective-permute-start | bytes 2359304 | tf_op jit(solution)/shard_map/ppermute | solution.py:681
  222.0 28.2 %collective-permute-start.28 = (f32[2,2,1,2,48,384]{5,4,3,2,1,0:T(8,128)}, f32[2,2,1,2,48,384]{5,4,3,2,1,0:T(8,128)}, u32[]{:S(2)}, u32[]{:S(2)}) collective-permute-start(f32[2,2,1,2,48,384]{5,4,3,2,1,0:T(8,128)} %get-tuple-element.207), channel_id=1, source_target_pairs={{0,1},{1,0},{2,3},{3,2},{4,5},{5,4},{6,7},{7,6},{8,9},{9,8},{10,11... | collective-permute-start | bytes 1769480 | tf_op jit(solution)/shard_map/ppermute | solution.py:684
  223.0 19.0 %collective-permute-start.31 = (f32[2,1,1,2,48,384]{5,4,3,2,1,0:T(8,128)}, f32[2,1,1,2,48,384]{5,4,3,2,1,0:T(8,128)}, u32[]{:S(2)}, u32[]{:S(2)}) collective-permute-start(f32[2,1,1,2,48,384]{5,4,3,2,1,0:T(8,128)} %constant_dynamic-slice_fusion.5), channel_id=1, source_target_pairs={{0,8},{2,10},{4,12},{6,14},{8,0},{10,2},{12,4},{14,6},{16,24},{18,... | collective-permute-start | bytes 884744 | tf_op jit(solution)/shard_map/ppermute | solution.py:681
  254.7 24.1 %collective-permute-start.34 = (f32[2,1,1,2,48,640]{5,4,3,2,1,0:T(8,128)}, f32[2,1,1,2,48,640]{5,4,3,2,1,0:T(8,128)}, u32[]{:S(2)}, u32[]{:S(2)}) collective-permute-start(f32[2,1,1,2,48,640]{5,4,3,2,1,0:T(8,128)} %slice.179), channel_id=1, source_target_pairs={{0,1},{1,0},{2,3},{3,2},{4,5},{5,4},{6,7},{7,6},{8,9},{9,8},{10,11... | collective-permute-start | bytes 1474568 | tf_op jit(solution)/shard_map/ppermute | solution.py:684
  283.3 49.7 %collective-permute-start.36 = (f32[1,1,1,2,48,1920]{5,4,3,2,1,0:T(8,128)}, f32[1,1,1,2,48,1920]{5,4,3,2,1,0:T(8,128)}, u32[]{:S(2)}, u32[]{:S(2)}) collective-permute-start(f32[1,1,1,2,48,1920]{5,4,3,2,1,0:T(8,128)} %constant_dynamic-slice_fusion.2), channel_id=1, source_target_pairs={{0,16},{2,18},{4,20},{6,22},{8,24},{10,26},{12,28},{14,30},{16,0},... | collective-permute-start | bytes 2211848 | tf_op jit(solution)/shard_map/ppermute | solution.py:681
  (62 other events, 800.4 us)
Sparse Core Ops, SparseCore 0:
  208.7 107.2 all-reduce.3
Sparse Core Ops, SparseCore 1:
  213.6 122.6 reduce-scatter.1

commit v3 on v2

v3 whole, which is shorter than its diff:
```python
import functools
import math

import jax
import jax.numpy as jnp
from jax import lax
from jax.experimental import pallas as pl
from jax.experimental.pallas import tpu as pltpu
from jax.sharding import PartitionSpec as P

HD = 64
SLICES = 8
MASKED = -1e30
NORM_EPS = 1e-05

F32 = jnp.float32
BF16 = jnp.bfloat16
NN = (((1,), (0,)), ((), ()))
NT = (((1,), (1,)), ((), ()))
TN = (((0,), (0,)), ((), ()))


def mm(left, right, dims):
    return lax.dot_general(left, right, dims, preferred_element_type=F32)


def struct(shape, kind):
    return jax.ShapeDtypeStruct(shape, kind)


def params(mib):
    return pltpu.CompilerParams(vmem_limit_bytes=mib << 20)


def cost(flops, moved, special=0):
    return pl.CostEstimate(flops=int(flops), bytes_accessed=int(moved), transcendentals=int(special))


def whole_block(shape):
    return pl.BlockSpec(shape, lambda *_: (0,) * len(shape), pipeline_mode=pl.Buffered(1))


def three_pieces(value):
    high = value.astype(BF16).astype(F32)
    rest = value - high
    middle = rest.astype(BF16).astype(F32)
    return high, middle, rest - middle


def project_kernel(x_ref, kind_ref, wq_ref, bq_ref, wk_ref, bk_ref, wv_ref, bv_ref, q2_ref, k2_ref, v_ref):
    x = x_ref[...]
    entity = kind_ref[...] > 0.5
    rows = x.shape[0]
    width = wk_ref.shape[1]

    weights = jnp.concatenate([*(wq_ref[c] for c in range(4)), wk_ref[...], wv_ref[...]], axis=1)
    biases = jnp.concatenate([*(bq_ref[c : c + 1, :] for c in range(4)), bk_ref[...], bv_ref[...]], axis=1)
    products = mm(x, weights, NN) + biases

    def query(c):
        return products[:, width * c : width * (c + 1)]

    scale = 1.0 / math.sqrt(HD)
    to_word = jnp.where(entity, query(2), query(0)).astype(BF16).astype(F32) * scale
    to_entity = jnp.where(entity, query(3), query(1)).astype(BF16).astype(F32) * scale
    keys = query(4).astype(BF16).astype(F32)
    v_ref[...] = query(5).astype(BF16)
    left = lax.broadcasted_iota(jnp.int32, (rows, 2 * HD), 1) < HD
    held = left != entity
    for p in range(width // (2 * HD)):
        cols = slice(2 * HD * p, 2 * HD * (p + 1))
        w, e, k = to_word[:, cols], to_entity[:, cols], keys[:, cols]
        w_roll, e_roll, k_roll = (pltpu.roll(t, HD, 1) for t in (w, e, k))
        even = slice(4 * HD * p, 4 * HD * p + 2 * HD)
        odd = slice(4 * HD * p + 2 * HD, 4 * HD * (p + 1))
        q2_ref[:, even] = jnp.where(left, w, e_roll).astype(BF16)
        q2_ref[:, odd] = jnp.where(left, w_roll, e).astype(BF16)
        k2_ref[:, even] = jnp.where(held, jnp.where(left, k, k_roll), 0.0).astype(BF16)
        k2_ref[:, odd] = jnp.where(held, jnp.where(left, k_roll, k), 0.0).astype(BF16)


def project(x, kind, wq, bq, wk, bk, wv, bv, rows=512):
    length, model = x.shape
    width = wk.shape[1]
    rows = min(rows, length)
    tile = lambda w: pl.BlockSpec((rows, w), lambda i: (i, 0))
    return pl.pallas_call(
        project_kernel,
        grid=(length // rows,),
        in_specs=[
            tile(model),
            tile(1),
            whole_block(wq.shape),
            whole_block(bq.shape),
            whole_block(wk.shape),
            whole_block((1, width)),
            whole_block(wv.shape),
            whole_block((1, width)),
        ],
        out_specs=[tile(2 * width), tile(2 * width), tile(width)],
        out_shape=[
            struct((length, 2 * width), BF16),
            struct((length, 2 * width), BF16),
            struct((length, width), BF16),
        ],
        compiler_params=params(63),
        cost_estimate=cost(12 * length * model * width, 16 * model * width + 12 * length * width),
        name="project",
    )(x, kind, wq, bq, wk, bk.reshape(1, width), wv, bv.reshape(1, width))


def key_extra(live, rows):
    lane = lax.broadcasted_iota(jnp.int32, (rows, 2 * HD), 1)
    return jnp.where(
        lane == 0, jnp.where(live, 0.0, MASKED), jnp.where(lane < 4, 1.0, 0.0)
    ).astype(BF16)


def attend_kernel(q2_ref, k2_ref, v_ref, live_ref, out_ref, extra_ref, turned_ref, both_ref):
    length = k2_ref.shape[0]
    h = pl.program_id(1)

    @pl.when(h == 0)
    def _():
        turned = v_ref[...].astype(F32).T.astype(BF16)
        turned_ref[0] = turned[:HD]
        turned_ref[1] = turned[HD:]

    lane = lax.broadcasted_iota(jnp.int32, (length, 2 * HD), 1)
    one = jnp.where(lane == 0, 1.0, 0.0).astype(BF16)
    keys = jnp.concatenate([k2_ref[...], key_extra(live_ref[...] > 0.5, length)], axis=1)
    query = jnp.concatenate([q2_ref[...], one], axis=1)
    scores = mm(keys, query, NT)
    top = jnp.max(scores, axis=0, keepdims=True)
    weights = jnp.exp(scores - top)
    norm = jnp.sum(weights, axis=0, keepdims=True)
    summed = mm(turned_ref[h], weights.astype(BF16), NN)
    both_ref[h] = summed * (1.0 / norm)
    pieces = three_pieces(-(top + jnp.log(norm)))
    filled = jnp.concatenate(
        [jnp.ones((1, length), F32), *pieces, jnp.zeros((2 * HD - 4, length), F32)], axis=0
    )
    extra_ref[...] = filled.T.astype(BF16)

    @pl.when(h == 1)
    def _():
        out_ref[...] = jnp.concatenate([both_ref[0], both_ref[1]], axis=0).T.astype(BF16)


def attend(q2, k2, v, live):
    length, width = v.shape
    head = pl.BlockSpec((length, 2 * HD), lambda p, h: (0, 2 * p + h))
    pair = pl.BlockSpec((length, 2 * HD), lambda p, h: (0, p))
    return pl.pallas_call(
        attend_kernel,
        grid=(width // (2 * HD), 2),
        in_specs=[head, head, pair, whole_block((length, 1))],
        out_specs=[pair, head],
        out_shape=[struct((length, width), BF16), struct((length, 2 * width), BF16)],
        scratch_shapes=[pltpu.VMEM((2, HD, length), BF16), pltpu.VMEM((2, HD, length), F32)],
        compiler_params=params(63),
        cost_estimate=cost(10 * length * length * width, 20 * length * width, length * length * width // HD),
        name="attend",
    )(q2, k2, v, live)


def attend_back_kernel(
    count, group, y_ref, q2_ref, extra_ref, k2_ref, v_ref, o_ref, own_ref, got_ref, live_ref, kind_ref, columns_ref, pick_ref,
    wq_hbm, wk_hbm, wv_hbm, turned_hbm, first_hbm, *rest,
):
    outs = count + (2 if group is None else 4)
    part_hbm, grads_hbm = rest[:count], rest[count:outs]
    (
        dk_ref, dv_ref, dq_ref, product_ref, d_ref, all_ref, sums_ref, weights_ref, turned_ref, first_ref,
        part_ref, grads_ref, in_sem, out_sem,
    ) = rest[outs:]
    length = k2_ref.shape[0]
    width = wk_hbm.shape[1]
    p, h = pl.program_id(0), pl.program_id(1)
    pairs = width // (2 * HD)
    lane = lax.broadcasted_iota(jnp.int32, (length, 2 * HD), 1)
    left = lane < HD

    def arriving():
        copies = [
            pltpu.make_async_copy(wq_hbm.at[c], weights_ref.at[:, width * c : width * (c + 1)], in_sem.at[c])
            for c in range(4)
        ]
        copies.append(pltpu.make_async_copy(wk_hbm, weights_ref.at[:, 4 * width : 5 * width], in_sem.at[4]))
        copies.append(pltpu.make_async_copy(wv_hbm, weights_ref.at[:, 5 * width : 6 * width], in_sem.at[5]))
        copies.append(pltpu.make_async_copy(turned_hbm, turned_ref, in_sem.at[6]))
        copies.append(pltpu.make_async_copy(first_hbm, first_ref, in_sem.at[7]))
        return copies

    @pl.when(jnp.logical_and(p == 0, h == 0))
    def _():
        for copy in arriving():
            copy.start()

    @pl.when(h == 0)
    def _():
        first = y_ref[0] == 0
        own, got = own_ref[...], got_ref[...]
        joined = jnp.concatenate([jnp.where(first, own, got), jnp.where(first, got, own)], axis=0)
        product_ref[...] = joined * o_ref[...].astype(F32)
        d_ref[...] = joined.astype(BF16)

    d_context = d_ref[...]
    base = HD * (1 - h)
    mine = jnp.logical_and(lane >= HD - base, lane < 2 * HD - base)
    delta = jnp.sum(jnp.where(mine, product_ref[...], 0.0), axis=1, keepdims=True)
    high, middle, low = three_pieces(-delta)
    pieces = jnp.where(
        lane == base, high, jnp.where(lane == base + 1, middle, jnp.where(lane == base + 2, low, 0.0))
    ).astype(BF16)
    d_wide = jnp.where(mine, d_context, pieces)
    q2, k2 = q2_ref[...], k2_ref[...]
    query = jnp.concatenate([q2, extra_ref[...]], axis=1)
    keys = jnp.concatenate([k2, key_extra(live_ref[...] > 0.5, length)], axis=1)
    probs = jnp.exp(mm(keys, query, NT))
    ones = jnp.where((lane >= base) & (lane < base + 3), 1.0, 0.0).astype(BF16)
    d_probs = mm(jnp.where(mine, v_ref[...], ones), d_wide, NT)
    d_scores = (probs * d_probs).astype(BF16)
    dv_ref[h] = mm(probs.astype(BF16), d_context, NN)
    dk_ref[h] = mm(d_scores, q2, NN)
    dq_ref[h] = mm(k2, d_scores, TN).T * (1.0 / math.sqrt(HD))

    @pl.when(h == 1)
    def _():
        entity = kind_ref[...] > 0.5
        even, odd = dq_ref[0], dq_ref[1]
        to_word = jnp.where(left, even, pltpu.roll(odd, HD, 1)).astype(BF16).astype(F32)
        to_entity = jnp.where(left, pltpu.roll(even, HD, 1), odd).astype(BF16).astype(F32)
        even, odd = dk_ref[0], dk_ref[1]
        even = jnp.where(entity, pltpu.roll(even, HD, 1), even)
        odd = jnp.where(entity, odd, pltpu.roll(odd, HD, 1))
        grads = [
            jnp.where(entity, 0.0, to_word),
            jnp.where(entity, 0.0, to_entity),
            jnp.where(entity, to_word, 0.0),
            jnp.where(entity, to_entity, 0.0),
            jnp.where(left, even, odd).astype(BF16).astype(F32),
            jnp.where(left, dv_ref[0], dv_ref[1]).astype(BF16).astype(F32),
        ]
        for c, grad in enumerate(grads):
            all_ref[p, c] = grad.astype(BF16)
        sums = [jnp.sum(grad, axis=0, keepdims=True) for grad in grads]
        sums_ref[p] = jnp.concatenate([*sums, jnp.zeros((2, 2 * HD), F32)], axis=0)

    @pl.when(jnp.logical_and(p == pairs - 1, h == 1))
    def _():
        for copy in arriving():
            copy.wait()
        grads = jnp.concatenate([all_ref[k, c] for c in range(6) for k in range(pairs)], axis=1)
        half = first_ref.shape[0]
        leaving = []

        def leave(source, target):
            copy = pltpu.make_async_copy(source, target, out_sem.at[len(leaving)])
            copy.start()
            leaving.append(copy)

        for i in range(2):
            rows = slice(i * half, (i + 1) * half)
            total = mm(grads[rows], weights_ref[...], NT)
            part_ref[rows, :] = total + jnp.where(y_ref[0] == i, first_ref[...], 0.0)
        begin = 0
        for target in part_hbm:
            leave(part_ref.at[begin : begin + target.shape[0], :], target)
            begin += target.shape[0]
        model = turned_ref.shape[0]
        sums = jnp.concatenate([sums_ref[k] for k in range(pairs)], axis=1)
        pieces = jnp.concatenate([piece.astype(BF16) for piece in three_pieces(sums)], axis=0)
        picked = mm(pick_ref[...], pieces, NT)
        biases = picked[:, :6] + picked[:, 8:14] + picked[:, 16:22]
        extra = jnp.concatenate(
            [biases, columns_ref[...], jnp.zeros((model, 128 - 6 - columns_ref.shape[1]), F32)], axis=1
        )
        lower = y_ref[1] % 2 == 0

        def place(array, a, b, value):
            if group is None:
                grads_ref[array, :, a:b] = value
                return
            blocks = value.reshape(model // (2 * group), 2, group, b - a)
            first, second = blocks[:, 0], blocks[:, 1]
            for k, (one, other) in enumerate(((first, second), (second, first))):
                picked_rows = jnp.where(lower, one, other).reshape(model // 2, b - a)
                grads_ref[array, k * (model // 2) : (k + 1) * (model // 2), a:b] = picked_rows

        for array in range(2):
            for i in range(3):
                cols = slice(width * (3 * array + i), width * (3 * array + i + 1))
                place(array, width * i, width * (i + 1), mm(turned_ref[...], grads[:, cols], NN))
            wide = 3 * width
            if array:
                place(array, wide, wide + 128, extra)
                wide += 128
            if group is None:
                leave(grads_ref.at[array, :, :wide], grads_hbm[array])
            else:
                for k in (1, 0):
                    rows = slice(k * (model // 2), (k + 1) * (model // 2))
                    leave(grads_ref.at[array, rows, :wide], grads_hbm[2 * array + k])
        for copy in leaving:
            copy.wait()


def attend_back(
    y, q2, extra, k2, v, o, own, got, live, kind, columns, pick, wq, wk, wv, turned, first, chunks, group
):
    length, width = v.shape
    half, model = first.shape
    pairs = width // (2 * HD)
    head = pl.BlockSpec((length, 2 * HD), lambda p, h, *_: (0, 2 * p + h))
    pair = pl.BlockSpec((length, 2 * HD), lambda p, h, *_: (0, p))
    part = pl.BlockSpec((half, 2 * HD), lambda p, h, *_: (0, p))
    anywhere = pl.BlockSpec(memory_space=pl.ANY)
    shapes = [struct((rows, model), F32) for rows in chunks]
    for wide in (3 * width, 3 * width + 128):
        shapes += [struct((model, wide), F32)] if group is None else [struct((model // 2, wide), F32)] * 2
    return pl.pallas_call(
        functools.partial(attend_back_kernel, len(chunks), group),
        grid_spec=pltpu.PrefetchScalarGridSpec(
            num_scalar_prefetch=1,
            grid=(pairs, 2),
            in_specs=[
                head, head, head, pair, pair, part, part, whole_block((length, 1)), whole_block((length, 1)),
                whole_block(columns.shape), whole_block(pick.shape),
                *[anywhere] * 5,
            ],
            out_specs=[anywhere] * len(shapes),
            scratch_shapes=[
                *[pltpu.VMEM((2, length, 2 * HD), F32)] * 3,
                pltpu.VMEM((length, 2 * HD), F32),
                pltpu.VMEM((length, 2 * HD), BF16),
                pltpu.VMEM((pairs, 6, length, 2 * HD), BF16),
                pltpu.VMEM((pairs, 8, 2 * HD), F32),
                pltpu.VMEM((model, 6 * width), BF16),
                pltpu.VMEM((model, length), BF16),
                pltpu.VMEM((half, model), F32),
                pltpu.VMEM((length, model), F32),
                pltpu.VMEM((2, model, 3 * width + 128), F32),
                pltpu.SemaphoreType.DMA((8,)),
                pltpu.SemaphoreType.DMA((len(shapes),)),
            ],
        ),
        out_shape=shapes,
        compiler_params=params(63),
        cost_estimate=cost(20 * length * length * width, 40 * length * width, length * length * width // HD),
        name="attend_back",
    )(y, q2, extra, k2, v, o, own, got, live, kind, columns, pick, wq, wk, wv, turned, first)


def normalise(value):
    centre = value - jnp.mean(value, axis=-1, keepdims=True)
    inverse = lax.rsqrt(jnp.mean(centre * centre, axis=-1, keepdims=True) + NORM_EPS)
    return centre * inverse, inverse


def normalise_back(scaled, normal, inverse):
    return inverse * (
        scaled
        - jnp.mean(scaled, axis=-1, keepdims=True)
        - normal * jnp.mean(scaled * normal, axis=-1, keepdims=True)
    )


def gelu_pair(values):
    cumulative = 0.5 * (1.0 + lax.erf(values * (1.0 / math.sqrt(2.0))))
    density = jnp.exp(-0.5 * values * values) * (1.0 / math.sqrt(2.0 * math.pi))
    return values * cumulative, cumulative + values * density


def column_sum(value):
    return jnp.sum(value, axis=0, keepdims=True)


def group_cuts(half):
    return half // 384 * 256, half // 128 * 5 // 6 * 128


def middle_kernel(at_ref, x_ref, cot_ref, live_ref, own_ref, got_ref, wo_ref, wi_hbm, wu_hbm, *rest):
    arrived = rest[:SLICES]
    arrived_late = rest[SLICES : 2 * SLICES]
    (
        vec_ref, bias_ref, out_ref, out_late_ref, first_ref, dco_ref, cross_ref, left_ref,
        keep0_ref, keep1_ref, keep2_ref, early_send_ref, late_send_ref,
        sums_ref, inner_sums_ref, slope_ref, early_ref, late_ref, wi_ref, wu_ref, raw_ref, raw_late_ref, in_sem,
    ) = rest[2 * SLICES :]
    step = pl.program_id(0)
    me = at_ref[1]
    lower = me % 2 == 0
    hidden, model, width = wi_hbm.shape[1], x_ref.shape[1], wo_ref.shape[0]
    half = hidden // 2
    cut = [width // SLICES, (width + model) // SLICES, (width + 2 * model) // SLICES]
    ca, cb = group_cuts(half)
    left_sends = ((late_send_ref, 0), (early_send_ref, 0), (late_send_ref, model))
    start0, start1 = 2 * model, 2 * model + 2 * ca + width

    def weight_copies():
        stages = [[], [], [], [], []]
        for k in range(SLICES):
            for stage, source, target in (
                (0, arrived[k].at[: cut[0], :], raw_ref.at[k, : cut[0], :]),
                (2, arrived[k].at[cut[0] :, :], raw_ref.at[k, cut[0] :, :]),
                (4, arrived_late[k], raw_late_ref.at[k]),
            ):
                stages[stage].append(pltpu.make_async_copy(source, target, in_sem.at[stage * SLICES + k]))
        stages[1].append(pltpu.make_async_copy(wi_hbm, wi_ref, in_sem.at[SLICES]))
        stages[3].append(pltpu.make_async_copy(wu_hbm, wu_ref, in_sem.at[3 * SLICES]))
        return stages

    def arrive(*wanted):
        @pl.when(step == 0)
        def _():
            stages = weight_copies()
            for stage in wanted:
                for copy in stages[stage]:
                    copy.wait()
            for k in range(SLICES):
                if 0 in wanted:
                    early_ref[me ^ k, : cut[0], :] = raw_ref[k, : cut[0], :].astype(BF16)
                if 2 in wanted:
                    early_ref[me ^ k, cut[0] :, :] = raw_ref[k, cut[0] :, :].astype(BF16)
                if 4 in wanted:
                    late_ref[me ^ k] = raw_late_ref[k].astype(BF16)

    @pl.when(step == 0)
    def _():
        for stage in weight_copies():
            for copy in stage:
                copy.start()

    arrive(0)

    def foreign(ref, a, b):
        return ref[:, a:b, :].reshape(SLICES * (b - a), model)

    vec = [vec_ref[k : k + 1, :] for k in range(6)]
    got = got_ref[...].astype(BF16)
    own = own_ref[...]
    wo_far = foreign(early_ref, 0, cut[0])
    first = mm(own, wo_ref[...], NN) + mm(got, wo_far, NN) + vec[0] + x_ref[...].astype(F32)
    n1, inv1 = normalise(first)
    normed = n1 * vec[1] + vec[2]
    low = normed.astype(BF16)

    def inner(part):
        if part < 2:
            return wi_ref[:, half * part : half * (part + 1)]
        return foreign(early_ref, cut[part - 2], cut[part - 1])

    def outer(part):
        if part < 2:
            return wu_ref[half * part : half * (part + 1), :]
        per = SLICES // 2
        block = late_ref[per * (part - 2) : per * (part - 1), :, :]
        return block.reshape(half, model)

    def both(index, value):
        left_ref[index] = value
        ref, at = left_sends[index]
        ref[:, at : at + model] = value.astype(F32)

    def split(values):
        first, second = (value.astype(F32) for value in values)
        keep = jnp.where(lower, first, second).astype(BF16)
        return keep, jnp.where(lower, second, first)

    both(0, low)
    second = vec[3] + normed
    arrive(1, 3)
    for far in range(2):
        if far:
            arrive(2, 4)
        pair = []
        for part in (2 * far, 2 * far + 1):
            pre = mm(low, inner(part), NN) + bias_ref[part : part + 1, :]
            active, slope = gelu_pair(pre)
            active = active.astype(BF16)
            slope_ref[:, half * part : half * (part + 1)] = slope
            pair.append(active)
            second = second + mm(active, outer(part), NN)
        keep, send = split(pair)
        at1 = (half - ca + half - cb) * far + half - ca
        keep2_ref[:, cb * far : cb * (far + 1)] = keep[:, :cb]
        keep1_ref[:, at1 : at1 + half - cb] = keep[:, cb:]
        early_send_ref[:, model + cb * far : model + cb * (far + 1)] = send[:, :cb]
        late_send_ref[:, start1 + at1 : start1 + at1 + half - cb] = send[:, cb:]
    n2, inv2 = normalise(second)
    live = live_ref[...] > 0.5
    result = jnp.where(live, n2 * vec[4] + vec[5], 0.0).astype(BF16)
    out_ref[...] = result
    cross_ref[:, width:] = result[:, : model // 2].astype(F32)
    out_late_ref[...] = result[:, model // 2 :].astype(F32)
    dz = jnp.where(live, cot_ref[...].astype(F32), 0.0)
    d_second = normalise_back(dz * vec[4], n2, inv2)
    d_low = d_second.astype(BF16)
    both(1, d_low)
    d_normed = d_second
    inner_sums = []
    for far in range(2):
        pair = []
        for part in (2 * far, 2 * far + 1):
            d_hidden = mm(d_low, outer(part), NT)
            d_inner = (d_hidden * slope_ref[:, half * part : half * (part + 1)]).astype(BF16)
            pair.append(d_inner)
            inner_sums.append(column_sum(d_inner.astype(F32)))
            d_normed = d_normed + mm(d_inner, inner(part), NT)
        keep, send = split(pair)
        at1 = (half - ca + half - cb) * far
        keep0_ref[:, ca * far : ca * (far + 1)] = keep[:, :ca]
        keep1_ref[:, at1 : at1 + half - ca] = keep[:, ca:]
        late_send_ref[:, start0 + ca * far : start0 + ca * (far + 1)] = send[:, :ca]
        late_send_ref[:, start1 + at1 : start1 + at1 + half - ca] = send[:, ca:]
    d_first = normalise_back(d_normed * vec[1], n1, inv1)
    first_ref[...] = d_first
    d_attn = d_first.astype(BF16)
    both(2, d_attn)
    dco_ref[...] = mm(d_attn, wo_ref[...], NT).astype(BF16).astype(F32)
    cross_ref[:, :width] = mm(d_attn, wo_far, NT).astype(BF16).astype(F32)
    keep, send = split((own, got))
    keep0_ref[:, 2 * ca :] = keep
    late_send_ref[:, start0 + 2 * ca : start1] = send
    sums = jnp.concatenate(
        [
            column_sum(d_first),
            column_sum(d_normed * n1),
            column_sum(d_normed),
            column_sum(d_second),
            column_sum(dz * n2),
            column_sum(dz),
            jnp.zeros((2, model), F32),
        ],
        axis=0,
    )
    inner_sums = jnp.concatenate([*inner_sums, jnp.zeros((4, half), F32)], axis=0)

    @pl.when(step == 0)
    def _():
        sums_ref[...] = sums
        inner_sums_ref[...] = inner_sums

    @pl.when(step != 0)
    def _():
        sums_ref[...] += sums
        inner_sums_ref[...] += inner_sums


def middle(at, x, cot, live, context, got, wo, wi, wu, early, late, vec, bias, rows=256):
    half, width = got.shape
    model, hidden = wi.shape
    rows = min(rows, half)
    steps = half // rows
    mine = lambda w: pl.BlockSpec((rows, w), lambda i, s: (i + s[0] * steps, 0))
    tile = lambda w: pl.BlockSpec((rows, w), lambda i, s: (i, 0))
    ca, cb = group_cuts(hidden // 2)
    widths = (2 * ca + width, 2 * (hidden - ca - cb), 2 * cb)
    return pl.pallas_call(
        middle_kernel,
        grid_spec=pltpu.PrefetchScalarGridSpec(
            num_scalar_prefetch=1,
            grid=(steps,),
            in_specs=[
                mine(model), mine(model), mine(1), mine(width), tile(width),
                whole_block(wo.shape), *[pl.BlockSpec(memory_space=pl.ANY)] * (2 + 2 * SLICES),
                whole_block(vec.shape), whole_block(bias.shape),
            ],
            out_specs=[
                tile(model), tile(model // 2), tile(model), tile(width), tile(width + model // 2),
                pl.BlockSpec((3, rows, model), lambda i, s: (0, i, 0)),
                *(tile(w) for w in widths),
                tile(model + widths[2]), tile(2 * model + widths[0] + widths[1]),
                pl.BlockSpec((8, model), lambda i, s: (0, 0)),
                pl.BlockSpec((8, hidden // 2), lambda i, s: (0, 0)),
            ],
            scratch_shapes=[
                pltpu.VMEM((rows, 2 * hidden), F32),
                pltpu.VMEM((SLICES, *early[0].shape), BF16),
                pltpu.VMEM((SLICES, *late[0].shape), BF16),
                pltpu.VMEM(wi.shape, BF16),
                pltpu.VMEM(wu.shape, BF16),
                pltpu.VMEM((SLICES, *early[0].shape), F32),
                pltpu.VMEM((SLICES, *late[0].shape), F32),
                pltpu.SemaphoreType.DMA((5 * SLICES,)),
            ],
        ),
        out_shape=[
            struct((half, model), BF16), struct((half, model // 2), F32), struct((half, model), F32),
            struct((half, width), F32), struct((half, width + model // 2), F32),
            struct((3, half, model), BF16),
            *(struct((half, w), BF16) for w in widths),
            struct((half, model + widths[2]), F32),
            struct((half, 2 * model + widths[0] + widths[1]), F32),
            struct((8, model), F32), struct((8, hidden // 2), F32),
        ],
        compiler_params=params(63),
        cost_estimate=cost(
            16 * half * model * (hidden + width // 2), 24 * model * hidden + 80 * half * model, 6 * half * hidden
        ),
        name="middle",
    )(at, x, cot, live, context, got, wo, wi, wu, *early, *late, vec, bias)


def weight_kernel(plan, count, bit_ref, left_hbm, *rest):
    groups = len(plan)
    keep_hbm, rest = rest[:groups], rest[groups:]
    got_hbm, rest = rest[:count], rest[count:]
    outs, rest = rest[: 2 * groups], rest[2 * groups :]
    left_ref, left_got_ref, rest = rest[0], rest[1], rest[2:]
    keep_refs, rest = rest[:groups], rest[groups:]
    got_refs, rest = rest[:groups], rest[groups:]
    stage_refs, (in_sem, out_sem) = rest[:groups], rest[groups:]
    model = left_ref.shape[2]

    arriving, ready = [], {}

    def bring(key, source, target):
        if key not in ready:
            ready[key] = pltpu.make_async_copy(source, target, in_sem.at[len(arriving)])
            arriving.append(ready[key])

    for g, (_, _, tiles, (right_array, right_at)) in enumerate(plan):
        for index, (left_array, left_at), a, b in tiles:
            bring(("left", index), left_hbm.at[index], left_ref.at[index])
            bring(
                ("left got", index), got_hbm[left_array].at[:, left_at : left_at + model], left_got_ref.at[index]
            )
            bring(("keep", g, a), keep_hbm[g].at[:, a:b], keep_refs[g].at[:, a:b])
            bring(
                ("got", g, a), got_hbm[right_array].at[:, right_at + a : right_at + b], got_refs[g].at[:, a:b]
            )
    for copy in arriving:
        copy.start()
    waited = set()

    def need(*keys):
        for key in keys:
            if key not in waited:
                waited.add(key)
                ready[key].wait()

    leaving = []
    for g, (slot, group, tiles, _) in enumerate(plan):
        width = keep_refs[g].shape[1]
        for index, _, a, b in tiles:
            need(("left", index), ("left got", index), ("keep", g, a), ("got", g, a))
            left = jnp.concatenate([left_ref[index], left_got_ref[index].astype(BF16)], axis=0)
            right = jnp.concatenate([keep_refs[g][:, a:b], got_refs[g][:, a:b].astype(BF16)], axis=0)
            value = mm(left, right, TN)
            if slot is None:
                part, base = (0, 0) if 2 * b <= width else (1, width // 2)
                stage_refs[g][part, :, a - base : b - base] = value
                parts = ((part, a - base, b - base),)
            else:
                pairs = value.reshape(model // (2 * group), 2, group, b - a)
                kept = bit_ref[slot] == 0
                first, second = pairs[:, 0], pairs[:, 1]
                for part, (one, other) in enumerate(((first, second), (second, first))):
                    picked = jnp.where(kept, one, other)
                    stage_refs[g][part, :, a:b] = picked.reshape(model // 2, b - a)
                parts = ((1, a, b), (0, a, b))
            for part, a, b in parts:
                copy = pltpu.make_async_copy(
                    stage_refs[g].at[part, :, a:b], outs[2 * g + part].at[:, a:b], out_sem.at[len(leaving)]
                )
                copy.start()
                leaving.append(copy)
    for copy in leaving:
        copy.wait()


def weight_grads(at, left, keeps, received, plan):
    _, depth, model = left.shape
    stages, shapes, steps = [], [], 0
    for (slot, _, tiles, _), keep in zip(plan, keeps):
        width = keep.shape[1]
        shape = (model, width // 2) if slot is None else (model // 2, width)
        stages.append(pltpu.VMEM((2, *shape), F32))
        shapes += [struct(shape, F32)] * 2
        steps += len(tiles)
    columns = sum(keep.shape[1] for keep in keeps)
    anywhere = pl.BlockSpec(memory_space=pl.ANY)
    return pl.pallas_call(
        functools.partial(weight_kernel, plan, len(received)),
        grid_spec=pltpu.PrefetchScalarGridSpec(
            num_scalar_prefetch=1,
            grid=(1,),
            in_specs=[anywhere] * (1 + len(keeps) + len(received)),
            out_specs=[anywhere] * len(shapes),
            scratch_shapes=[
                pltpu.VMEM(left.shape, BF16),
                pltpu.VMEM(left.shape, F32),
                *(pltpu.VMEM(keep.shape, BF16) for keep in keeps),
                *(pltpu.VMEM(keep.shape, F32) for keep in keeps),
                *stages,
                pltpu.SemaphoreType.DMA((6 + 2 * steps,)),
                pltpu.SemaphoreType.DMA((2 * steps,)),
            ],
        ),
        out_shape=shapes,
        compiler_params=params(63),
        cost_estimate=cost(4 * depth * model * columns, 4 * model * columns + 8 * depth * columns),
        name="weight_grads",
    )(at, left, *keeps, *received)


def combine_kernel(plan, count, bits_ref, *rest):
    outs = len(plan)
    arrays, targets = rest[:count], rest[count : count + outs]
    buffers, (in_sem, out_sem) = rest[count + outs : -2], rest[-2:]
    copies = []
    for pieces in plan:
        for _, terms in pieces:
            for array, chosen, a, b, _ in terms:
                index = [slice(None)] * len(arrays[array].shape)
                for axis, (bit, mine) in chosen:
                    index[axis] = pl.ds(bits_ref[bit] if mine else 1 - bits_ref[bit], 1)
                index[-1] = slice(a, b)
                k = len(copies)
                copies.append(pltpu.make_async_copy(arrays[array].at[tuple(index)], buffers[k], in_sem.at[k]))
    for copy in copies:
        copy.start()
    k = 0
    leaving = []
    for target, pieces in zip(targets, plan):
        for at, terms in pieces:
            first = k
            total = None
            for *_, gate in terms:
                copies[k].wait()
                value = buffers[k][...]
                if gate is not None:
                    value = jnp.where(bits_ref[0] == gate, value, 0.0)
                total = value if total is None else total + value
                k += 1
            if len(terms) > 1:
                buffers[first][...] = total
            width = buffers[first].shape[-1]
            index = (*[slice(None)] * (len(target.shape) - 1), slice(at, at + width))
            copy = pltpu.make_async_copy(buffers[first], target.at[index], out_sem.at[len(leaving)])
            copy.start()
            leaving.append(copy)
    for copy in leaving:
        copy.wait()


def combine(bit_values, outputs):
    arrays, plan, shapes, buffers, moved = [], [], [], [], 0
    for pieces in outputs:
        at, planned = 0, []
        for terms in pieces:
            named = []
            for array, chosen, a, b, gate in terms:
                place = [k for k, other in enumerate(arrays) if other is array]
                if not place:
                    place = [len(arrays)]
                    arrays.append(array)
                named.append((place[0], tuple(sorted(chosen.items())), a, b, gate))
                block = tuple(1 if k in chosen else size for k, size in enumerate(array.shape[:-1]))
                buffers.append(pltpu.VMEM((*block, b - a), F32))
                moved += 4 * math.prod(block) * (b - a)
            planned.append((at, named))
            at += b - a
        plan.append(planned)
        shapes.append(struct((*block, at), F32))
    anywhere = pl.BlockSpec(memory_space=pl.ANY)
    pieces = sum(len(planned) for planned in plan)
    return pl.pallas_call(
        functools.partial(combine_kernel, plan, len(arrays)),
        grid_spec=pltpu.PrefetchScalarGridSpec(
            num_scalar_prefetch=1,
            grid=(1,),
            in_specs=[anywhere] * len(arrays),
            out_specs=[anywhere] * len(shapes),
            scratch_shapes=[
                *buffers,
                pltpu.SemaphoreType.DMA((len(buffers),)),
                pltpu.SemaphoreType.DMA((pieces,)),
            ],
        ),
        out_shape=shapes,
        compiler_params=params(63),
        cost_estimate=cost(moved, 2 * moved),
        name="combine",
    )(bit_values, *arrays)


def turn_kernel(value_ref, out_ref):
    out_ref[...] = value_ref[...].astype(F32).T.astype(BF16)


def turn(value, columns=256):
    length, model = value.shape
    return pl.pallas_call(
        turn_kernel,
        grid=(model // columns,),
        in_specs=[pl.BlockSpec((length, columns), lambda i: (0, i))],
        out_specs=pl.BlockSpec((columns, length), lambda i: (i, 0)),
        out_shape=struct((model, length), BF16),
        compiler_params=params(63),
        cost_estimate=cost(length * model, 4 * length * model),
        name="turn",
    )(value)


def place_kernel(y_ref, own_ref, first_ref, second_ref, out_ref):
    mine = pl.program_id(0) == y_ref[0]
    got = jnp.concatenate([first_ref[...], second_ref[...]], axis=1)
    out_ref[...] = jnp.where(mine, own_ref[...].astype(F32), got).astype(BF16)


def place_rows(y, own, first, second):
    half, model = own.shape
    return pl.pallas_call(
        place_kernel,
        grid_spec=pltpu.PrefetchScalarGridSpec(
            num_scalar_prefetch=1,
            grid=(2,),
            in_specs=[
                whole_block(own.shape),
                pl.BlockSpec((half, model // 2), lambda i, s: (0, 1)),
                whole_block(second.shape),
            ],
            out_specs=pl.BlockSpec((half, model), lambda i, s: (i, 0)),
        ),
        out_shape=struct((2 * half, model), BF16),
        compiler_params=params(63),
        cost_estimate=cost(half * model, 12 * half * model),
        name="place_rows",
    )(y, own, first, second)


def per_device(
    devices,
    tokens,
    lengths,
    entity_flags,
    query_weight,
    query_bias,
    key_weight,
    key_bias,
    value_weight,
    value_bias,
    output_weight,
    output_bias,
    attn_gain,
    attn_shift,
    inner_weight,
    inner_bias,
    outer_weight,
    outer_bias,
    final_gain,
    final_shift,
    cotangent,
):
    x = tokens[0]
    length, model = x.shape
    width = key_weight.shape[1]
    hidden = inner_weight.shape[1]
    half = length // 2
    bits = devices.bit_length() - 1
    y = lax.axis_index("tensor")
    d = lax.axis_index("dp")

    def swap(value, mask):
        return lax.ppermute(value, "dp", [(i, i ^ mask) for i in range(devices)])

    def cross(value):
        return lax.ppermute(value, "tensor", [(0, 1), (1, 0)])

    me = d % SLICES
    core = d % 2
    rows = model // devices
    near_mask, far_mask = 96 // rows, 192 // rows
    at = jnp.stack([y, me, (d // near_mask) % 2, (d // far_mask) % 2]).astype(jnp.int32)
    tie = lax.optimization_barrier

    def cut(array, index):
        size = array.shape[0] // SLICES
        return lax.dynamic_slice_in_dim(array, index * size, size, 0)

    def pack(index):
        wide = cut(inner_weight, index)
        early = jnp.concatenate([cut(output_weight, index), wide[:, :model], wide[:, model:]], axis=0)
        return early.astype(F32)

    def pack_late(index):
        return cut(outer_weight, index).astype(F32)

    live = (lax.broadcasted_iota(jnp.int32, (length, 1), 0) < lengths[0]).astype(F32)
    kind = (entity_flags[0] == 1).astype(F32).reshape(length, 1)

    e0 = cross(pack(me))
    far_bias = cross(inner_bias)
    q2, k2, v = project(
        x, kind, query_weight, query_bias, key_weight, key_bias, value_weight, value_bias
    )
    e0, far_bias, l0, l6, q2 = tie((e0, far_bias, pack_late(me), pack_late(me ^ 6), q2))
    e2 = swap(e0, 2)
    e4 = swap(e0, 4)
    l0 = cross(l0)
    e1 = swap(e0, 1)
    context, extra = attend(q2, k2, v, live)
    sent = lax.dynamic_slice_in_dim(context, half * (1 - y), half, 0).astype(F32)
    e1, e2, e4, l0, l6, sent = tie((e1, e2, e4, l0, l6, sent))
    l2 = swap(l0, 2)
    l4 = swap(l0, 4)
    got = cross(sent)
    e6 = swap(e4, 2)
    l6 = cross(l6)
    per = width // devices
    where_row = lax.broadcasted_iota(jnp.int32, (model, width), 0)
    where_bias = lax.broadcasted_iota(jnp.int32, (model, width), 1)
    pick = (where_row == (where_bias // per) * rows + where_bias % per).astype(BF16)
    x_turned = turn(x)
    l2, l4, e2, e4, pick, x_turned = tie((l2, l4, e2, e4, pick, x_turned))
    e3 = swap(e2, 1)
    e5 = swap(e4, 1)
    got, e6, l6, e3, e5, l0, l2, l4 = tie((got, e6, l6, e3, e5, l0, l2, l4))
    l1 = swap(l0, 1)
    l3 = swap(l2, 1)
    l5 = swap(l4, 1)
    l7 = swap(l6, 1)
    e7 = swap(e6, 1)
    early = (e0, e1, e2, e3, e4, e5, e6, e7)
    late = (l0, l1, l2, l3, l4, l5, l6, l7)

    vec = jnp.stack(
        [output_bias, attn_gain, attn_shift, outer_bias, final_gain, final_shift, outer_bias, outer_bias]
    )
    bias = jnp.concatenate([inner_bias, far_bias, inner_bias, far_bias]).reshape(8, hidden // 2)
    (
        out_rows, out_late, d_first, dco, first_cross, left, keep0, keep1, keep2, early_send, late_send,
        sums, inner_sums,
    ) = middle(
        at, x, cotangent[0], live, context, got, output_weight, inner_weight, outer_weight,
        early, late, vec, bias,
    )
    inner_columns = inner_sums[:4].reshape(2, model, 2)
    columns = jnp.concatenate([sums[:6].T, inner_columns[0], inner_columns[1]], axis=1)
    d_got = cross(first_cross)
    early_got = swap(early_send, 1)
    late_got = swap(late_send, 1)
    early_got, columns = tie((early_got, columns))

    ca, cb = group_cuts(hidden // 2)
    da, db = hidden // 2 - ca, hidden // 2 - cb
    normed_at, d_second_at, d_attn_at = (1, 0), (0, 0), (1, model)
    g0_keep, g0_send, g1_keep, g1_send = weight_grads(
        at, left, (keep0, keep1), (early_got, late_got),
        (
            (
                2, near_mask * rows,
                (
                    (0, normed_at, 0, ca), (0, normed_at, ca, 2 * ca),
                    (2, d_attn_at, 2 * ca, 2 * ca + width),
                ),
                (1, 2 * model),
            ),
            (
                None, None,
                (
                    (0, normed_at, 0, da), (1, d_second_at, da, da + db),
                    (0, normed_at, da + db, 2 * da + db), (1, d_second_at, 2 * da + db, 2 * (da + db)),
                ),
                (1, 2 * model + 2 * ca + width),
            ),
        ),
    )
    early_got, g0_send = tie((early_got, g0_send))
    g2_keep, g2_send = weight_grads(
        at, left, (keep2,), (early_got,),
        ((3, far_mask * rows, ((1, (0, 0), 0, cb), (1, (0, 0), cb, 2 * cb)), (0, model)),),
    )
    g0_got = swap(g0_send, near_mask)
    g2_got = swap(g2_send, far_mask)
    g1_got = cross(g1_send)

    g0_send, g1_send, g2_send, dco, d_got = tie((g0_send, g1_send, g2_send, dco, d_got))
    chunks = tuple(length * k // 32 for k in (2, 4, 14, 12))
    group = rows if rows % 8 == 0 else None
    results = attend_back(
        at, q2, extra, k2, v, context, dco, d_got, live, kind, columns, pick,
        query_weight, key_weight, value_weight, x_turned, d_first, chunks, group,
    )
    parts, products = results[: len(chunks)], results[len(chunks) :]
    got_out = cross(out_late)

    def spread(array, done):
        dims = [1 if (1 << (bits - 1 - k)) in done else 2 for k in range(bits)]
        return array.reshape(*dims, rows, array.shape[-1])

    bit_values = jnp.stack([(d >> k) % 2 for k in range(bits)]).astype(jnp.int32)
    rest_masks = [1 << k for k in range(1, bits) if (1 << k) not in (near_mask, far_mask)]

    def term(array, *done):
        array = spread(array, done)
        return (array, {}, 0, array.shape[-1], None)

    def half_of(terms, mask, mine):
        k = mask.bit_length() - 1
        return [(array, {**chosen, bits - 1 - k: (k, mine)}, a, b, gate) for array, chosen, a, b, gate in terms]

    def kept(terms, mask):
        return half_of(terms, mask, True)

    def other(terms, mask):
        return half_of(terms, mask, False)

    def columns_of(terms, first, last):
        return [(array, chosen, a + first, a + last, gate) for array, chosen, a, _, gate in terms]

    def on_core(terms, core_index):
        return [(array, chosen, a, b, core_index) for array, chosen, a, b, _ in terms]

    def whole_of(array):
        return (array, {}, 0, array.shape[-1], None)

    def part_of(array, a, b):
        return (array, {}, a, b, None)

    g0_got, g1_got, g2_got, got_out, parts, products = tie((g0_got, g1_got, g2_got, got_out, parts, products))
    if group is None:
        c = [term(products[0])]
        e = [term(products[1])]
        c_send, e_send = combine(bit_values, [[other(c, 1)], [other(e, 1)]])
        c, e = kept(c, 1), kept(e, 1)
    else:
        c, e = [term(products[0], 1)], [term(products[2], 1)]
        c_send, e_send = spread(products[1], (1,)), spread(products[3], (1,))
    e_got = swap(e_send, 1)
    c_got = swap(c_send, 1)
    g0 = [term(g0_keep, near_mask), term(g0_got, near_mask)]
    g1 = [term(g1_keep), term(g1_got)]
    g2 = [term(g2_keep, far_mask), term(g2_got, far_mask)]
    sends = combine(
        bit_values, [[columns_of(g0, ca, 2 * ca + width)], [other(g1, near_mask)], [other(g2, near_mask)]]
    )
    e_got, c_got, sends, parts = tie((e_got, c_got, sends, parts))
    e.append(whole_of(e_got))
    c.append(whole_of(c_got))
    g0_got = cross(sends[0])
    g2_got = swap(sends[2], near_mask)
    g1_got = swap(sends[1], near_mask)
    (e_send,) = combine(bit_values, [[other(e, far_mask)]])
    e_got = swap(e_send, far_mask)
    part0 = cross(parts[0])
    g0_got, g1_got, g2_got, e_got, part0, parts = tie((g0_got, g1_got, g2_got, e_got, part0, parts))
    t = [
        *on_core(columns_of(g0, 2 * ca, 2 * ca + width), 0),
        *on_core([part_of(g0_got, ca, ca + width)], 1),
    ]
    g0 = [*columns_of(g0, 0, ca), part_of(g0_got, 0, ca)]
    g1 = [*kept(g1, near_mask), whole_of(g1_got)]
    g2 = [*kept(g2, near_mask), whole_of(g2_got)]
    e = [*kept(e, far_mask), whole_of(e_got)]

    sends = combine(
        bit_values,
        [
            [other(terms, far_mask) for terms in (g0, t, g1)],
            [columns_of(g2, cb, 2 * cb)],
            [other(c, near_mask)],
        ],
    )
    sends, parts = tie((sends, parts))
    g2_got = cross(sends[1])
    three_got = swap(sends[0], far_mask)
    c_got = swap(sends[2], near_mask)
    part1 = cross(parts[1])
    three_got, g2_got, c_got, part1, parts = tie((three_got, g2_got, c_got, part1, parts))
    g0 = [*kept(g0, far_mask), part_of(three_got, 0, ca)]
    t = [*kept(t, far_mask), part_of(three_got, ca, ca + width)]
    g1 = [*kept(g1, far_mask), part_of(three_got, ca + width, three_got.shape[-1])]
    g2 = [*columns_of(g2, 0, cb), whole_of(g2_got)]
    c = [*kept(c, near_mask), whole_of(c_got)]

    main = (g0, g1, g2, t)
    sizes = (ca, da + db, cb, width)
    ends = [sum(sizes[:k]) for k in range(len(sizes) + 1)]
    mask = rest_masks[0]
    sends = combine(
        bit_values,
        [[other(terms, mask) for terms in main], [other(e, near_mask)], [other(c, far_mask)]],
    )
    sends, parts = tie((sends, parts))
    got_z = swap(sends[0], mask)
    part2 = cross(parts[2])
    c_got = swap(sends[2], far_mask)
    e_got = swap(sends[1], near_mask)
    layer_out = place_rows(at, out_rows, d_got, got_out)
    got_z, e_got, c_got, part2, parts, layer_out = tie((got_z, e_got, c_got, part2, parts, layer_out))
    main = [[*kept(terms, mask), part_of(got_z, ends[n], ends[n + 1])] for n, terms in enumerate(main)]
    e = [*kept(e, near_mask), whole_of(e_got)]
    c = [*kept(c, far_mask), whole_of(c_got)]
    for mask in rest_masks[1:]:
        (send,) = combine(bit_values, [[other(terms, mask) for terms in main]])
        got_z = swap(send, mask)
        main = [[*kept(terms, mask), part_of(got_z, ends[n], ends[n + 1])] for n, terms in enumerate(main)]

    for k, mask in enumerate(rest_masks):
        outputs = [[other(c, mask), other(e, mask)], [kept(c, mask), kept(e, mask)]]
        if k == 0:
            outputs += [[other(terms, 1) for terms in main], [kept(terms, 1) for terms in main]]
        sends = combine(bit_values, outputs)
        if k == 0:
            sends, parts = tie((sends, parts))
        pair_got = swap(sends[0], mask)
        if k == 0:
            part3 = cross(parts[3])
            got_last = swap(sends[2], 1)
            keep = sends[3]
            pair_got, got_last, part3 = tie((pair_got, got_last, part3))
        c = [part_of(sends[1], 0, 3 * width), part_of(pair_got, 0, 3 * width)]
        e = [part_of(sends[1], 3 * width, sends[1].shape[-1]), part_of(pair_got, 3 * width, sends[1].shape[-1])]
    pair = (sends[1] + pair_got).reshape(rows, -1)
    c, e = pair[:, : 3 * width], pair[:, 3 * width :]
    last = e[:, 3 * width + 6 : 3 * width + 16]
    last_got = cross(last)
    small = last[:, :6] + last_got[:, :6]
    inner_two = last[:, 6:8] + last_got[:, 8:]

    got_last = got_last.reshape(rows, -1)
    keep = keep.reshape(rows, -1)
    low_half = jnp.where(core == 0, keep, got_last)
    high_half = jnp.where(core == 0, got_last, keep)
    at2 = ca + da + db
    inner_half = lambda array: [array[:, : ca + da]]
    at3 = at2 + cb
    outer_half = lambda array: [array[:, at2:at3], array[:, ca + da : at2]]
    t = keep[:, at3:] + got_last[:, at3:]
    grad_inner = jnp.concatenate(inner_half(low_half) + inner_half(high_half), axis=1)
    grad_outer = jnp.concatenate(outer_half(low_half) + outer_half(high_half), axis=1).T
    sent_parts = (part0, part1, part2, part3)
    input_grad = jnp.concatenate([(a + b).astype(BF16) for a, b in zip(parts, sent_parts)], axis=0)

    piece = lambda array, k: array[:, width * k : width * (k + 1)]
    grad_query_weight = jnp.stack([piece(c, 0), piece(c, 1), piece(c, 2), piece(e, 0)])
    biases = e[:per, 3 * width : 3 * width + 6].T
    return (
        layer_out[None],
        input_grad[None],
        grad_query_weight,
        biases[:4],
        piece(e, 1),
        biases[4],
        piece(e, 2),
        biases[5],
        t.T,
        small[:, 0],
        small[:, 1],
        small[:, 2],
        grad_inner,
        inner_two.reshape(2 * rows),
        grad_outer,
        small[:, 3],
        small[:, 4],
        small[:, 5],
    )


def solution(mesh):
    return jax.shard_map(
        functools.partial(per_device, mesh.shape["dp"]),
        mesh=mesh,
        in_specs=(
            P("dp", None, None),
            P("dp"),
            P("dp", None),
            P(None, None, "tensor"),
            P(None, "tensor"),
            P(None, "tensor"),
            P("tensor"),
            P(None, "tensor"),
            P("tensor"),
            P("tensor", None),
            P(),
            P(),
            P(),
            P(None, "tensor"),
            P("tensor"),
            P("tensor", None),
            P(),
            P(),
            P(),
            P("dp", None, None),
        ),
        out_specs=(
            P("dp", None, None),
            P("dp", None, None),
            P(None, "dp", "tensor"),
            P(None, ("tensor", "dp")),
            P("dp", "tensor"),
            P(("tensor", "dp")),
            P("dp", "tensor"),
            P(("tensor", "dp")),
            P("tensor", "dp"),
            P("dp"),
            P("dp"),
            P("dp"),
            P("dp", "tensor"),
            P(("tensor", "dp")),
            P("tensor", "dp"),
            P("dp"),
            P("dp"),
            P("dp"),
        ),
        check_vma=False,
    )
```

time: 361 us -> 364 us (level)
  waiting for transfers between devices: 134 us -> 153 us
  local copies, waits for them, and re-layouts: 35.8 us -> 17.1 us
  Pallas kernels: 117 us -> 135 us
  between operations: 17 us -> 2.18 us
  other arithmetic: 24.3 us -> 15.1 us
  starting transfers between devices: 30.1 us -> 36.2 us
    ppermute x12 -> x15, waiting for transfers between devices: 41.1 us -> 75.5 us  [cross(): return lax.ppermute(value, 'tensor', [(0, 1), (1, 0)])]
    add x12 -> x3, other arithmetic: 15.9 us -> 0.15 us  [the longest x1 0.07 us: per_device(): inner_two = last[:, 6:8] + last_got[:, 8:]]
    ppermute x26 -> x29, waiting for transfers between devices: 92.4 us -> 77.3 us  [swap(): return lax.ppermute(value, 'dp', [(i, i ^ mask) for i in range(devices)])]
    pallas_call x7 -> x8, Pallas kernels: 65.3 us -> 76.1 us  [the longest x1 34.4 us: attend_back(): pl.pallas_call(functools.partial(attend_back_kernel, len(chunks), group),...]
    unnamed x93 -> x59, local copies, waits for them, and re-layouts: 15 us -> 6.62 us
    dynamic_slice x7 -> x0, local copies, waits for them, and re-layouts: 6.03 us -> none  [halves(): send = lax.dynamic_slice_in_dim(array, 1 - bit, 1, axis)]
    convert_element_type x0 -> x5, other arithmetic: none -> 4.8 us  [the longest x4 3.84 us: per_device(): (a + b).astype(BF16)]
    ppermute x26 -> x29, starting transfers between devices: 16.7 us -> 21.2 us  [swap(): return lax.ppermute(value, 'dp', [(i, i ^ mask) for i in range(devices)])]
  transfers between devices with their start and end apart: 40 -> 44, of which waited for: 15 -> 18; matrix products, arithmetic and copies ran while one was open for 10% -> 6% of each run, Pallas kernels for 25% -> 25%
where the time goes in v3:
time: 364 us; the launch traced here: 358 us
  waiting for transfers between devices  153 us (42%)
  Pallas kernels  135 us (37%)
  starting transfers between devices  36.2 us (10%)
  local copies, waits for them, and re-layouts  17.1 us (5%)
  other arithmetic  15.1 us (4%)
    ppermute x29, waiting for transfers between devices, swap(): return lax.ppermute(value, 'dp', [(i, i ^ mask) for i in range(devices)])  77.3 us
    ppermute x15, waiting for transfers between devices, cross(): return lax.ppermute(value, 'tensor', [(0, 1), (1, 0)])  75.5 us
    pallas_call x1, Pallas kernels, attend_back(): pl.pallas_call(functools.partial(attend_back_kernel, len(chunks), group),...  34.4 us
    pallas_call x1, Pallas kernels, middle(): pl.pallas_call(middle_kernel, grid_spec=pltpu.PrefetchScalarGridSpec(num_...  29.3 us
    pallas_call x5, Pallas kernels, combine(): pl.pallas_call(functools.partial(combine_kernel, plan, len(arrays)), grid...  22.9 us
    ppermute x29, starting transfers between devices, swap(): return lax.ppermute(value, 'dp', [(i, i ^ mask) for i in range(devices)])  21.2 us
    pallas_call x2, Pallas kernels, weight_grads(): pl.pallas_call(functools.partial(weight_kernel, plan, len(received)), gri...  18.8 us
    ppermute x15, starting transfers between devices, cross(): return lax.ppermute(value, 'tensor', [(0, 1), (1, 0)])  14.9 us
  transfers between devices with their start and end apart: 44, of which 18 were waited for; matrix products, arithmetic and copies ran while one was open for 6% of the time, Pallas kernels for 25%

profile of v3, /device:TPU:0, one launch (start us, length us, event | category | flops | bytes accessed | tf_op | source)
XLA Modules:
  0.0 358.0 jit_solution(9502602544853858056)
XLA Ops:
  8.0 7.9 %project.1 = (bf16[1024,768]{1,0:T(8,128)(2,1)}, bf16[1024,768]{1,0:T(8,128)(2,1)}, bf16[1024,384]{1,0:T(8,128)(2,1)}) custom-call(bf16[1024,768]{1,0:T(8,128)(2,1)} %bitcast.71, f32[1024,1]{1,0:T(8,128)} %copy.44.kind_ref, bf16[4,768,384]{2,1,0:T(8,128)(2,1)} %wq_hbm.1, f32[4,384]{1,0:T(4,128)} %bq_ref.1, bf16[768,384]{1,0:T(8,128)(2,1)} %wk_hbm.1, ...), custom_call_target="tpu_custom_call" | custom-call | flops 3623878656 | bytes 9437184 | tf_op jit(solution)/shard_map/project/pallas_call | solution.py:87
  18.0 4.4 %collective-permute-done.1 = f32[1536]{0:T(1024)S(1)} collective-permute-done((f32[1536]{0:T(1024)S(1)}, f32[1536]{0:T(1024)S(1)}, u32[]{:S(2)}, u32[]{:S(2)}) %collective-permute-start.1) | collective-permute-done | bytes 6176 | tf_op jit(solution)/shard_map/ppermute | solution.py:871
  28.8 14.0 %attend.1 = (bf16[1024,384]{1,0:T(8,128)(2,1)}, bf16[1024,768]{1,0:T(8,128)(2,1)}) custom-call(bf16[1024,768]{1,0:T(8,128)(2,1)} %get-tuple-element.167.q2_ref, bf16[1024,768]{1,0:T(8,128)(2,1)} %get-tuple-element.168.k2_ref, bf16[1024,384]{1,0:T(8,128)(2,1)} %get-tuple-element.169.v_ref, f32[1024,1]{1,0:T(8,128)} %fusion.1.live_ref), custom_call_target="tpu_custom_call" | custom-call | flops 4026531840 | bytes 7864320 | tf_op jit(solution)/shard_map/attend/pallas_call | solution.py:154
  46.3 3.8 %turn.1.turned_hbm = bf16[768,1024]{1,0:T(8,128)(2,1)} custom-call(bf16[1024,768]{1,0:T(8,128)(2,1)} %bitcast.72), custom_call_target="tpu_custom_call" | custom-call | flops 786432 | bytes 3145728 | tf_op jit(solution)/shard_map/turn/pallas_call | solution.py:796
  51.8 7.9 %collective-permute-done.10.rest_12_ = f32[192,768]{1,0:T(8,128)} collective-permute-done((f32[192,768]{1,0:T(8,128)}, f32[192,768]{1,0:T(8,128)}, u32[]{:S(2)}, u32[]{:S(2)}) %collective-permute-start.10) | collective-permute-done | bytes 589856 | tf_op jit(solution)/shard_map/ppermute | solution.py:868
  61.9 15.0 %collective-permute-done.8.rest_14_ = f32[192,768]{1,0:T(8,128)} collective-permute-done((f32[192,768]{1,0:T(8,128)}, f32[192,768]{1,0:T(8,128)}, u32[]{:S(2)}, u32[]{:S(2)}) %collective-permute-start.8) | collective-permute-done | bytes 589856 | tf_op jit(solution)/shard_map/ppermute | solution.py:871
  83.9 29.3 %middle.1 = (bf16[512,768]{1,0:T(8,128)(2,1)}, f32[512,384]{1,0:T(8,128)}, f32[512,768]{1,0:T(8,128)}, f32[512,384]{1,0:T(8,128)}, f32[512,768]{1,0:T(8,128)}, /...) custom-call(s32[4]{0:T(128)} %pad_add_fusion.1.at_ref.bit_ref.y_ref,, ...), custom_call_target="tpu_custom_call" | custom-call | flops 10871635968 | bytes 59768832 | tf_op jit(solution)/shard_map/middle/pallas_call | solution.py:560
  116.2 15.5 %collective-permute-done.18.rest_2_.rest_1_ = f32[512,2048]{1,0:T(8,128)} collective-permute-done((f32[512,2048]{1,0:T(8,128)}, f32[512,2048]{1,0:T(8,128)}, u32[]{:S(2)}, u32[]{:S(2)}) %collective-permute-start.18) | collective-permute-done | bytes 4194336 | tf_op jit(solution)/shard_map/ppermute | solution.py:868
  131.7 10.8 %weight_grads.2 = (f32[384,1408]{1,0:T(8,128)}, f32[384,1408]{1,0:T(8,128)}, f32[768,384]{1,0:T(8,128)}, f32[768,384]{1,0:T(8,128)}) custom-call(s32[4]{0:T(128)} %pad_add_fusion.1.at_ref.bit_ref.y_ref, bf16[3,512,768]{2,1,0:T(8,128)(2,1)} %get-tuple-element.193.left_hbm, bf16[512,1408]{1,0:T(8,128)(2,1)} %get-tuple-element.194.rest_0_, ...), custom_call_target="tpu_custom_call" | custom-call | flops 3422552064 | bytes 15597568 | tf_op jit(solution)/shard_map/weight_grads/pallas_call | solution.py:685
  144.0 8.0 %weight_grads.3 = (f32[384,1280]{1,0:T(8,128)}, f32[384,1280]{1,0:T(8,128)}) custom-call(s32[4]{0:T(128)} %pad_add_fusion.1.at_ref.bit_ref.y_ref, bf16[3,512,768]{2,1,0:T(8,128)(2,1)} %get-tuple-element.193.left_hbm, bf16[512,1280]{1,0:T(8,128)(2,1)} %get-tuple-element.205.rest_0_, f32[512,2048]{1,0:T(8,128)} %collective-permute-done.18.rest_2_.rest_1_), custom_call_target="tpu_custom_call" | custom-call | flops 2013265920 | bytes 9175040 | tf_op jit(solution)/shard_map/weight_grads/pallas_call | solution.py:685
  156.5 34.4 %attend_back.1 = (f32[64,768]{1,0:T(8,128)}, f32[128,768]{1,0:T(8,128)}, f32[448,768]{1,0:T(8,128)}, f32[384,768]{1,0:T(8,128)}, f32[384,1152]{1,0:T(8,128)}, /*...) custom-call(s32[4]{0:T(128)} %pad_add_fusion.1.at_ref.bit_ref.y_ref, ...), custom_call_target="tpu_custom_call" | custom-call | flops 8053063680 | bytes 15728640 | tf_op jit(solution)/shard_map/attend_back/pallas_call | solution.py:322
  191.0 7.1 %collective-permute-done.23.second_ref = f32[512,384]{1,0:T(8,128)S(1)} collective-permute-done((f32[512,384]{1,0:T(8,128)}, f32[512,384]{1,0:T(8,128)S(1)}, u32[]{:S(2)}, u32[]{:S(2)}) %collective-permute-start.23) | collective-permute-done | bytes 786464 | tf_op jit(solution)/shard_map/ppermute | solution.py:871
  199.3 4.5 %combine.5 = (f32[2,2,1,2,48,896]{5,4,3,2,1,0:T(8,128)}, f32[2,2,1,2,48,384]{5,4,3,2,1,0:T(8,128)}, f32[2,1,1,2,48,1280]{5,4,3,2,1,0:T(8,128)}) custom-call(s32[4]{0:T(128)} %pad_add_fusion.bits_ref, f32[2,2,1,2,48,1408]{5,4,3,2,1,0:T(8,128)} %bitcast.52, f32[2,2,1,2,48,1408]{5,4,3,2,1,0:T(8,128)} %bitcast.14.rest_1_.rest_9_, ...), custom_call_target="tpu_custom_call" | custom-call | flops 5898240 | bytes 11796480 | tf_op jit(solution)/shard_map/combine/pallas_call | solution.py:770
  205.5 3.2 combine.6
  212.8 28.8 %collective-permute-done.31 = f32[64,768]{1,0:T(8,128)S(1)} collective-permute-done((f32[64,768]{1,0:T(8,128)}, f32[64,768]{1,0:T(8,128)S(1)}, u32[]{:S(2)}, u32[]{:S(2)}) %collective-permute-start.31) | collective-permute-done | bytes 196640 | tf_op jit(solution)/shard_map/ppermute | solution.py:871
  241.7 3.7 %collective-permute-done.28.rest_5_.rest_6_.rest_15_ = f32[2,2,1,2,48,384]{5,4,3,2,1,0:T(8,128)S(1)} collective-permute-done((f32[2,2,1,2,48,384]{5,4,3,2,1,0:T(8,128)}, f32[2,2,1,2,48,384]{5,4,3,2,1,0:T(8,128)S(1)}, u32[]{:S(2)}, u32[]{:S(2)}) %collective-permute-start.28) | collective-permute-done | bytes 589856 | tf_op jit(solution)/shard_map/ppermute | solution.py:868
  247.2 5.0 %combine.7 = (f32[2,1,1,2,48,1280]{5,4,3,2,1,0:T(8,128)}, f32[2,1,1,2,48,640]{5,4,3,2,1,0:T(8,128)}, f32[2,2,1,1,48,1152]{5,4,3,2,1,0:T(8,128)}) custom-call(s32[4]{0:T(128)} %pad_add_fusion.bits_ref, f32[2,2,1,2,48,1408]{5,4,3,2,1,0:T(8,128)} %bitcast.53, f32[2,2,1,2,48,1408]{5,4,3,2,1,0:T(8,128)} %bitcast.14.rest_1_.rest_9_, ...), custom_call_target="tpu_custom_call" | custom-call | flops 6193152 | bytes 12386304 | tf_op jit(solution)/shard_map/combine/pallas_call | solution.py:770
  256.5 17.8 %collective-permute-done.35 = f32[128,768]{1,0:T(8,128)S(1)} collective-permute-done((f32[128,768]{1,0:T(8,128)}, f32[128,768]{1,0:T(8,128)S(1)}, u32[]{:S(2)}, u32[]{:S(2)}) %collective-permute-start.35) | collective-permute-done | bytes 393248 | tf_op jit(solution)/shard_map/ppermute | solution.py:871
  276.2 4.7 %combine.8 = (f32[1,1,1,2,48,1920]{5,4,3,2,1,0:T(8,128)}, f32[2,1,1,1,48,1280]{5,4,3,2,1,0:T(8,128)}, f32[2,1,1,1,48,1152]{5,4,3,2,1,0:T(8,128)}) custom-call(s32[4]{0:T(128)} %pad_add_fusion.bits_ref, f32[2,2,1,2,48,1408]{5,4,3,2,1,0:T(8,128)} %bitcast.54, f32[2,2,1,2,48,1408]{5,4,3,2,1,0:T(8,128)} %bitcast.14.rest_1_.rest_9_, ...), custom_call_target="tpu_custom_call" | custom-call | flops 5750784 | bytes 11501568 | tf_op jit(solution)/shard_map/combine/pallas_call | solution.py:770
  286.9 3.6 place_rows.1
  290.5 17.4 %collective-permute-done.38.rest_3_ = f32[2,1,1,1,48,1152]{5,4,3,2,1,0:T(8,128)} collective-permute-done((f32[2,1,1,1,48,1152]{5,4,3,2,1,0:T(8,128)}, f32[2,1,1,1,48,1152]{5,4,3,2,1,0:T(8,128)}, u32[]{:S(2)}, u32[]{:S(2)}) %collective-permute-start.38) | collective-permute-done | bytes 442400 | tf_op jit(solution)/shard_map/ppermute | solution.py:868
  307.9 7.0 %collective-permute-done.36.rest_12_ = f32[1,1,1,2,48,1920]{5,4,3,2,1,0:T(8,128)S(1)} collective-permute-done((f32[1,1,1,2,48,1920]{5,4,3,2,1,0:T(8,128)}, f32[1,1,1,2,48,1920]{5,4,3,2,1,0:T(8,128)S(1)}, u32[]{:S(2)}, u32[]{:S(2)}) %collective-permute-start.36) | collective-permute-done | bytes 737312 | tf_op jit(solution)/shard_map/ppermute | solution.py:868
  315.8 5.5 %combine.9 = (f32[1,1,1,1,48,2432]{5,4,3,2,1,0:T(8,128)}, f32[1,1,1,1,48,2432]{5,4,3,2,1,0:T(8,128)}, f32[1,1,1,1,48,1920]{5,4,3,2,1,0:T(8,128)}, f32[1,1,1,1,48,1920]{5,4,3,2,1,0:T(8,128)}) custom-call(s32[4]{0:T(128)} %pad_add_fusion.bits_ref, f32[2,2,2,1,48,1152]{5,4,3,2,1,0:T(8,128)} %bitcast.69, ...), custom_call_target="tpu_custom_call" | custom-call | flops 7421952 | bytes 14843904 | tf_op jit(solution)/shard_map/combine/pallas_call | solution.py:770
  325.7 20.5 %collective-permute-done.40 = f32[1,1,1,1,48,2432]{5,4,3,2,1,0:T(8,128)S(1)} collective-permute-done((f32[1,1,1,1,48,2432]{5,4,3,2,1,0:T(8,128)}, f32[1,1,1,1,48,2432]{5,4,3,2,1,0:T(8,128)S(1)}, u32[]{:S(2)}, u32[]{:S(2)}) %collective-permute-start.40) | collective-permute-done | bytes 466976 | tf_op jit(solution)/shard_map/ppermute | solution.py:868
  (195 shorter events, 75.9 us)
Async XLA Ops:
  2.7 19.7 %collective-permute-start = (f32[240,768]{1,0:T(8,128)S(1)}, f32[240,768]{1,0:T(8,128)}, u32[]{:S(2)}, u32[]{:S(2)}) collective-permute-start(f32[240,768]{1,0:T(8,128)S(1)} %maximum_convert_fusion), channel_id=1, source_target_pairs={{0,1},{1,0},{2,3},{3,2},{4,5},{5,4},{6,7},{7,6},{8,9},{9,8},{10,11... | collective-permute-start | bytes 2211848 | tf_op jit(solution)/shard_map/ppermute | solution.py:871
  22.4 21.4 %collective-permute-start.4 = (f32[240,768]{1,0:T(8,128)}, f32[240,768]{1,0:T(8,128)}, u32[]{:S(2)}, u32[]{:S(2)}) collective-permute-start(f32[240,768]{1,0:T(8,128)} %collective-permute-done.rest_0_), channel_id=1, source_target_pairs={{0,8},{2,10},{4,12},{6,14},{8,0},{10,2},{12,4},{14,6},{16,24},{18,... | collective-permute-start | bytes 2211848 | tf_op jit(solution)/shard_map/ppermute | solution.py:868
  24.2 19.6 %collective-permute-start.3 = (f32[240,768]{1,0:T(8,128)}, f32[240,768]{1,0:T(8,128)}, u32[]{:S(2)}, u32[]{:S(2)}) collective-permute-start(f32[240,768]{1,0:T(8,128)} %collective-permute-done.rest_0_), channel_id=1, source_target_pairs={{0,4},{2,6},{4,0},{6,2},{8,12},{10,14},{12,8},{14,10},{16,20},{18,... | collective-permute-start | bytes 2211848 | tf_op jit(solution)/shard_map/ppermute | solution.py:868
  44.9 32.0 %collective-permute-start.6 = (f32[512,384]{1,0:T(8,128)S(1)}, f32[512,384]{1,0:T(8,128)}, u32[]{:S(2)}, u32[]{:S(2)}) collective-permute-start(f32[512,384]{1,0:T(8,128)S(1)} %dynamic-slice_convert_fusion), channel_id=1, source_target_pairs={{0,1},{1,0},{2,3},{3,2},{4,5},{5,4},{6,7},{7,6},{8,9},{9,8},{10,11... | collective-permute-start | bytes 2359304 | tf_op jit(solution)/shard_map/ppermute | solution.py:871
  50.1 26.9 %collective-permute-start.7 = (f32[240,768]{1,0:T(8,128)}, f32[240,768]{1,0:T(8,128)S(1)}, u32[]{:S(2)}, u32[]{:S(2)}) collective-permute-start(f32[240,768]{1,0:T(8,128)} %collective-permute-done.4.rest_4_), channel_id=1, source_target_pairs={{0,4},{2,6},{4,0},{6,2},{8,12},{10,14},{12,8},{14,10},{16,20},{18,... | collective-permute-start | bytes 2211848 | tf_op jit(solution)/shard_map/ppermute | solution.py:868
  115.6 40.9 %collective-permute-start.24 = (f32[512,768]{1,0:T(8,128)}, f32[512,768]{1,0:T(8,128)}, u32[]{:S(2)}, u32[]{:S(2)}) collective-permute-start(f32[512,768]{1,0:T(8,128)} %get-tuple-element.211), channel_id=1, source_target_pairs={{0,1},{1,0},{2,3},{3,2},{4,5},{5,4},{6,7},{7,6},{8,9},{9,8},{10,11... | collective-permute-start | bytes 4718600 | tf_op jit(solution)/shard_map/ppermute | solution.py:871
  142.5 55.6 %collective-permute-start.20 = (f32[384,1408]{1,0:T(8,128)}, f32[384,1408]{1,0:T(8,128)}, u32[]{:S(2)}, u32[]{:S(2)}) collective-permute-start(f32[384,1408]{1,0:T(8,128)} %get-tuple-element.203), channel_id=1, source_target_pairs={{0,4},{2,6},{4,0},{6,2},{8,12},{10,14},{12,8},{14,10},{16,20},{18,... | collective-permute-start | bytes 6488072 | tf_op jit(solution)/shard_map/ppermute | solution.py:868
  151.9 46.2 %collective-permute-start.22 = (f32[384,1280]{1,0:T(8,128)}, f32[384,1280]{1,0:T(8,128)}, u32[]{:S(2)}, u32[]{:S(2)}) collective-permute-start(f32[384,1280]{1,0:T(8,128)} %get-tuple-element.207), channel_id=1, source_target_pairs={{0,8},{2,10},{4,12},{6,14},{8,0},{10,2},{12,4},{14,6},{16,24},{18,... | collective-permute-start | bytes 5898248 | tf_op jit(solution)/shard_map/ppermute | solution.py:868
  153.6 44.5 %collective-permute-start.21 = (f32[768,384]{1,0:T(8,128)}, f32[768,384]{1,0:T(8,128)}, u32[]{:S(2)}, u32[]{:S(2)}) collective-permute-start(f32[768,384]{1,0:T(8,128)} %get-tuple-element.204), channel_id=1, source_target_pairs={{0,1},{1,0},{2,3},{3,2},{4,5},{5,4},{6,7},{7,6},{8,9},{9,8},{10,11... | collective-permute-start | bytes 3538952 | tf_op jit(solution)/shard_map/ppermute | solution.py:871
  154.1 44.0 %collective-permute-start.23 = (f32[512,384]{1,0:T(8,128)}, f32[512,384]{1,0:T(8,128)S(1)}, u32[]{:S(2)}, u32[]{:S(2)}) collective-permute-start(f32[512,384]{1,0:T(8,128)} %get-tuple-element.208), channel_id=1, source_target_pairs={{0,1},{1,0},{2,3},{3,2},{4,5},{5,4},{6,7},{7,6},{8,9},{9,8},{10,11... | collective-permute-start | bytes 2359304 | tf_op jit(solution)/shard_map/ppermute | solution.py:871
  205.0 41.2 %collective-permute-start.27 = (f32[2,2,1,2,48,896]{5,4,3,2,1,0:T(8,128)}, f32[2,2,1,2,48,896]{5,4,3,2,1,0:T(8,128)}, u32[]{:S(2)}, u32[]{:S(2)}) collective-permute-start(f32[2,2,1,2,48,896]{5,4,3,2,1,0:T(8,128)} %get-tuple-element.240), channel_id=1, source_target_pairs={{0,1},{1,0},{2,3},{3,2},{4,5},{5,4},{6,7},{7,6},{8,9},{9,8},{10,11... | collective-permute-start | bytes 4128776 | tf_op jit(solution)/shard_map/ppermute | solution.py:871
  208.8 36.6 %collective-permute-start.30 = (f32[2,1,2,1,48,1280]{5,4,3,2,1,0:T(8,128)}, f32[2,1,2,1,48,1280]{5,4,3,2,1,0:T(8,128)S(1)}, u32[]{:S(2)}, u32[]{:S(2)}) collective-permute-start(f32[2,1,2,1,48,1280]{5,4,3,2,1,0:T(8,128)} %combine.6), channel_id=1, source_target_pairs={{0,8},{2,10},{4,12},{6,14},{8,0},{10,2},{12,4},{14,6},{16,24},{18,... | collective-permute-start | bytes 2949128 | tf_op jit(solution)/shard_map/ppermute | solution.py:868
  209.3 36.1 %collective-permute-start.29 = (f32[2,1,1,2,48,1280]{5,4,3,2,1,0:T(8,128)}, f32[2,1,1,2,48,1280]{5,4,3,2,1,0:T(8,128)S(1)}, u32[]{:S(2)}, u32[]{:S(2)}) collective-permute-start(f32[2,1,1,2,48,1280]{5,4,3,2,1,0:T(8,128)} %get-tuple-element.242), channel_id=1, source_target_pairs={{0,4},{2,6},{4,0},{6,2},{8,12},{10,14},{12,8},{14,10},{16,20},{18,... | collective-permute-start | bytes 2949128 | tf_op jit(solution)/shard_map/ppermute | solution.py:868
  209.9 35.5 %collective-permute-start.28 = (f32[2,2,1,2,48,384]{5,4,3,2,1,0:T(8,128)}, f32[2,2,1,2,48,384]{5,4,3,2,1,0:T(8,128)S(1)}, u32[]{:S(2)}, u32[]{:S(2)}) collective-permute-start(f32[2,2,1,2,48,384]{5,4,3,2,1,0:T(8,128)} %get-tuple-element.241), channel_id=1, source_target_pairs={{0,4},{2,6},{4,0},{6,2},{8,12},{10,14},{12,8},{14,10},{16,20},{18,... | collective-permute-start | bytes 1769480 | tf_op jit(solution)/shard_map/ppermute | solution.py:868
  211.3 30.4 %collective-permute-start.31 = (f32[64,768]{1,0:T(8,128)}, f32[64,768]{1,0:T(8,128)S(1)}, u32[]{:S(2)}, u32[]{:S(2)}) collective-permute-start(f32[64,768]{1,0:T(8,128)} %get-tuple-element.300), channel_id=1, source_target_pairs={{0,1},{1,0},{2,3},{3,2},{4,5},{5,4},{6,7},{7,6},{8,9},{9,8},{10,11... | collective-permute-start | bytes 589832 | tf_op jit(solution)/shard_map/ppermute | solution.py:871
  252.2 23.1 %collective-permute-start.32 = (f32[2,1,1,2,48,1280]{5,4,3,2,1,0:T(8,128)}, f32[2,1,1,2,48,1280]{5,4,3,2,1,0:T(8,128)S(1)}, u32[]{:S(2)}, u32[]{:S(2)}) collective-permute-start(f32[2,1,1,2,48,1280]{5,4,3,2,1,0:T(8,128)} %get-tuple-element.261), channel_id=1, source_target_pairs={{0,8},{2,10},{4,12},{6,14},{8,0},{10,2},{12,4},{14,6},{16,24},{18,... | collective-permute-start | bytes 2949128 | tf_op jit(solution)/shard_map/ppermute | solution.py:868
  253.8 21.3 %collective-permute-start.34 = (f32[2,2,1,1,48,1152]{5,4,3,2,1,0:T(8,128)}, f32[2,2,1,1,48,1152]{5,4,3,2,1,0:T(8,128)}, u32[]{:S(2)}, u32[]{:S(2)}) collective-permute-start(f32[2,2,1,1,48,1152]{5,4,3,2,1,0:T(8,128)} %get-tuple-element.263), channel_id=1, source_target_pairs={{0,4},{2,6},{4,0},{6,2},{8,12},{10,14},{12,8},{14,10},{16,20},{18,... | collective-permute-start | bytes 2654216 | tf_op jit(solution)/shard_map/ppermute | solution.py:868
  254.4 19.9 %collective-permute-start.33 = (f32[2,1,1,2,48,640]{5,4,3,2,1,0:T(8,128)}, f32[2,1,1,2,48,640]{5,4,3,2,1,0:T(8,128)S(1)}, u32[]{:S(2)}, u32[]{:S(2)}) collective-permute-start(f32[2,1,1,2,48,640]{5,4,3,2,1,0:T(8,128)} %get-tuple-element.262), channel_id=1, source_target_pairs={{0,1},{1,0},{2,3},{3,2},{4,5},{5,4},{6,7},{7,6},{8,9},{9,8},{10,11... | collective-permute-start | bytes 1474568 | tf_op jit(solution)/shard_map/ppermute | solution.py:871
  280.9 34.0 %collective-permute-start.39 = (f32[448,768]{1,0:T(8,128)}, f32[448,768]{1,0:T(8,128)}, u32[]{:S(2)}, u32[]{:S(2)}) collective-permute-start(f32[448,768]{1,0:T(8,128)} %get-tuple-element.304), channel_id=1, source_target_pairs={{0,1},{1,0},{2,3},{3,2},{4,5},{5,4},{6,7},{7,6},{8,9},{9,8},{10,11... | collective-permute-start | bytes 4128776 | tf_op jit(solution)/shard_map/ppermute | solution.py:871
  282.5 32.4 %collective-permute-start.36 = (f32[1,1,1,2,48,1920]{5,4,3,2,1,0:T(8,128)}, f32[1,1,1,2,48,1920]{5,4,3,2,1,0:T(8,128)S(1)}, u32[]{:S(2)}, u32[]{:S(2)}) collective-permute-start(f32[1,1,1,2,48,1920]{5,4,3,2,1,0:T(8,128)} %get-tuple-element.279), channel_id=1, source_target_pairs={{0,16},{2,18},{4,20},{6,22},{8,24},{10,26},{12,28},{14,30},{16,0},... | collective-permute-start | bytes 2211848 | tf_op jit(solution)/shard_map/ppermute | solution.py:868
  285.1 22.8 %collective-permute-start.37 = (f32[2,1,1,1,48,1280]{5,4,3,2,1,0:T(8,128)}, f32[2,1,1,1,48,1280]{5,4,3,2,1,0:T(8,128)}, u32[]{:S(2)}, u32[]{:S(2)}) collective-permute-start(f32[2,1,1,1,48,1280]{5,4,3,2,1,0:T(8,128)} %get-tuple-element.280), channel_id=1, source_target_pairs={{0,4},{2,6},{4,0},{6,2},{8,12},{10,14},{12,8},{14,10},{16,20},{18,... | collective-permute-start | bytes 1474568 | tf_op jit(solution)/shard_map/ppermute | solution.py:868
  286.5 21.5 %collective-permute-start.38 = (f32[2,1,1,1,48,1152]{5,4,3,2,1,0:T(8,128)}, f32[2,1,1,1,48,1152]{5,4,3,2,1,0:T(8,128)}, u32[]{:S(2)}, u32[]{:S(2)}) collective-permute-start(f32[2,1,1,1,48,1152]{5,4,3,2,1,0:T(8,128)} %get-tuple-element.281), channel_id=1, source_target_pairs={{0,8},{2,10},{4,12},{6,14},{8,0},{10,2},{12,4},{14,6},{16,24},{18,... | collective-permute-start | bytes 1327112 | tf_op jit(solution)/shard_map/ppermute | solution.py:868
  321.4 27.1 %collective-permute-start.42 = (f32[384,768]{1,0:T(8,128)}, f32[384,768]{1,0:T(8,128)S(1)}, u32[]{:S(2)}, u32[]{:S(2)}) collective-permute-start(f32[384,768]{1,0:T(8,128)} %get-tuple-element.306), channel_id=1, source_target_pairs={{0,1},{1,0},{2,3},{3,2},{4,5},{5,4},{6,7},{7,6},{8,9},{9,8},{10,11... | collective-permute-start | bytes 3538952 | tf_op jit(solution)/shard_map/ppermute | solution.py:871
  321.9 24.2 %collective-permute-start.40 = (f32[1,1,1,1,48,2432]{5,4,3,2,1,0:T(8,128)}, f32[1,1,1,1,48,2432]{5,4,3,2,1,0:T(8,128)S(1)}, u32[]{:S(2)}, u32[]{:S(2)}) collective-permute-start(f32[1,1,1,1,48,2432]{5,4,3,2,1,0:T(8,128)} %get-tuple-element.307), channel_id=1, source_target_pairs={{0,16},{2,18},{4,20},{6,22},{8,24},{10,26},{12,28},{14,30},{16,0},... | collective-permute-start | bytes 1400840 | tf_op jit(solution)/shard_map/ppermute | solution.py:868
  (49 other events, 567.9 us)

commit v4 on v3

--- a/solution.py
+++ b/solution.py
@@ -79,7 +79,7 @@
         k2_ref[:, odd] = jnp.where(held, jnp.where(left, k_roll, k), 0.0).astype(BF16)
 
 
-def project(x, kind, wq, bq, wk, bk, wv, bv, rows=512):
+def project(x, kind, wq, bq, wk, bk, wv, bv, rows=256):
     length, model = x.shape
     width = wk.shape[1]
     rows = min(rows, length)
@@ -278,23 +278,28 @@
         )
         lower = y_ref[1] % 2 == 0
 
-        def place(array, a, b, value):
+        def place(array, cols, value):
             if group is None:
-                grads_ref[array, :, a:b] = value
+                grads_ref[array, :, cols] = value
                 return
-            blocks = value.reshape(model // (2 * group), 2, group, b - a)
+            blocks = value.reshape(model // (2 * group), 2, group, value.shape[1])
             first, second = blocks[:, 0], blocks[:, 1]
             for k, (one, other) in enumerate(((first, second), (second, first))):
-                picked_rows = jnp.where(lower, one, other).reshape(model // 2, b - a)
-                grads_ref[array, k * (model // 2) : (k + 1) * (model // 2), a:b] = picked_rows
+                picked_rows = jnp.where(lower, one, other).reshape(model // 2, value.shape[1])
+                grads_ref[array, k * (model // 2) : (k + 1) * (model // 2), cols] = picked_rows
 
         for array in range(2):
-            for i in range(3):
-                cols = slice(width * (3 * array + i), width * (3 * array + i + 1))
-                place(array, width * i, width * (i + 1), mm(turned_ref[...], grads[:, cols], NN))
+
+            def one(i, carry, array=array):
+                grad = jnp.concatenate([all_ref[k, 3 * array + i] for k in range(pairs)], axis=1)
+                at = pl.multiple_of(width * i, 128)
+                place(array, pl.ds(at, width), mm(turned_ref[...], grad, NN))
+                return carry
+
+            lax.fori_loop(0, 3, one, 0)
             wide = 3 * width
             if array:
-                place(array, wide, wide + 128, extra)
+                place(array, slice(wide, wide + 128), extra)
                 wide += 128
             if group is None:
                 leave(grads_ref.at[array, :, :wide], grads_hbm[array])
@@ -376,27 +381,43 @@
     return jnp.sum(value, axis=0, keepdims=True)
 
 
-def group_cuts(half):
-    return half // 384 * 256, half // 128 * 5 // 6 * 128
-
-
-def middle_kernel(at_ref, x_ref, cot_ref, live_ref, own_ref, got_ref, wo_ref, wi_hbm, wu_hbm, *rest):
+def first_cut(half):
+    return half // 2
+
+
+def middle_sizes(wi, wo, early):
+    hidden, model, width = wi.shape[1], wo.shape[1], wo.shape[0]
+    cut = [width // SLICES, (width + model) // SLICES, (width + 2 * model) // SLICES]
+    return hidden, hidden // 2, model, width, cut
+
+
+def far_block(ref, a, b):
+    return ref[:, a:b, :].reshape(SLICES * (b - a), ref.shape[2])
+
+
+def far_outer(ref, part, half):
+    per = SLICES // 2
+    return ref[per * (part - 2) : per * (part - 1), :, :].reshape(half, ref.shape[2])
+
+
+def by_core(lower, values):
+    first, second = (value.astype(F32) for value in values)
+    keep = jnp.where(lower, first, second).astype(BF16)
+    return keep, jnp.where(lower, second, first)
+
+
+def forward_kernel(at_ref, x_ref, cot_ref, live_ref, own_ref, got_ref, wo_ref, wi_hbm, wu_hbm, *rest):
     arrived = rest[:SLICES]
     arrived_late = rest[SLICES : 2 * SLICES]
     (
-        vec_ref, bias_ref, out_ref, out_late_ref, first_ref, dco_ref, cross_ref, left_ref,
-        keep0_ref, keep1_ref, keep2_ref, early_send_ref, late_send_ref,
-        sums_ref, inner_sums_ref, slope_ref, early_ref, late_ref, wi_ref, wu_ref, raw_ref, raw_late_ref, in_sem,
+        vec_ref, bias_ref, out_ref, out_first_ref, out_late_ref, low_ref, d_low_ref, keep_ref, send_ref,
+        slope_ref, n1_ref, inv1_ref, d_second_ref, sums_ref, early_hbm, late_hbm,
+        early_ref, late_ref, wi_ref, wu_ref, raw_ref, raw_late_ref, in_sem, out_sem,
     ) = rest[2 * SLICES :]
     step = pl.program_id(0)
     me = at_ref[1]
     lower = me % 2 == 0
-    hidden, model, width = wi_hbm.shape[1], x_ref.shape[1], wo_ref.shape[0]
-    half = hidden // 2
-    cut = [width // SLICES, (width + model) // SLICES, (width + 2 * model) // SLICES]
-    ca, cb = group_cuts(half)
-    left_sends = ((late_send_ref, 0), (early_send_ref, 0), (late_send_ref, model))
-    start0, start1 = 2 * model, 2 * model + 2 * ca + width
+    hidden, half, model, width, cut = middle_sizes(wi_hbm, wo_ref, early_ref)
 
     def weight_copies():
         stages = [[], [], [], [], []]
@@ -410,6 +431,12 @@
         stages[1].append(pltpu.make_async_copy(wi_hbm, wi_ref, in_sem.at[SLICES]))
         stages[3].append(pltpu.make_async_copy(wu_hbm, wu_ref, in_sem.at[3 * SLICES]))
         return stages
+
+    def leaving():
+        return [
+            pltpu.make_async_copy(early_ref, early_hbm, out_sem.at[0]),
+            pltpu.make_async_copy(late_ref, late_hbm, out_sem.at[1]),
+        ]
 
     def arrive(*wanted):
         @pl.when(step == 0)
@@ -425,6 +452,9 @@
                     early_ref[me ^ k, cut[0] :, :] = raw_ref[k, cut[0] :, :].astype(BF16)
                 if 4 in wanted:
                     late_ref[me ^ k] = raw_late_ref[k].astype(BF16)
+            if 4 in wanted:
+                for copy in leaving():
+                    copy.start()
 
     @pl.when(step == 0)
     def _():
@@ -433,42 +463,20 @@
                 copy.start()
 
     arrive(0)
-
-    def foreign(ref, a, b):
-        return ref[:, a:b, :].reshape(SLICES * (b - a), model)
-
     vec = [vec_ref[k : k + 1, :] for k in range(6)]
     got = got_ref[...].astype(BF16)
     own = own_ref[...]
-    wo_far = foreign(early_ref, 0, cut[0])
-    first = mm(own, wo_ref[...], NN) + mm(got, wo_far, NN) + vec[0] + x_ref[...].astype(F32)
+    first = mm(own, wo_ref[...], NN) + mm(got, far_block(early_ref, 0, cut[0]), NN) + vec[0] + x_ref[...].astype(F32)
     n1, inv1 = normalise(first)
+    n1_ref[...] = n1
+    inv1_ref[...] = inv1
     normed = n1 * vec[1] + vec[2]
     low = normed.astype(BF16)
-
-    def inner(part):
-        if part < 2:
-            return wi_ref[:, half * part : half * (part + 1)]
-        return foreign(early_ref, cut[part - 2], cut[part - 1])
-
-    def outer(part):
-        if part < 2:
-            return wu_ref[half * part : half * (part + 1), :]
-        per = SLICES // 2
-        block = late_ref[per * (part - 2) : per * (part - 1), :, :]
-        return block.reshape(half, model)
-
-    def both(index, value):
-        left_ref[index] = value
-        ref, at = left_sends[index]
-        ref[:, at : at + model] = value.astype(F32)
-
-    def split(values):
-        first, second = (value.astype(F32) for value in values)
-        keep = jnp.where(lower, first, second).astype(BF16)
-        return keep, jnp.where(lower, second, first)
-
-    both(0, low)
+    low_ref[...] = low
+    at_low = model + hidden
+    send_ref[:, at_low : at_low + model] = low.astype(F32)
+    _, send = by_core(lower, (own, got))
+    send_ref[:, at_low + model :] = send
     second = vec[3] + normed
     arrive(1, 3)
     for far in range(2):
@@ -476,135 +484,207 @@
             arrive(2, 4)
         pair = []
         for part in (2 * far, 2 * far + 1):
-            pre = mm(low, inner(part), NN) + bias_ref[part : part + 1, :]
+            inner = wi_ref[:, half * part : half * (part + 1)] if part < 2 else far_block(early_ref, cut[part - 2], cut[part - 1])
+            pre = mm(low, inner, NN) + bias_ref[part : part + 1, :]
             active, slope = gelu_pair(pre)
             active = active.astype(BF16)
-            slope_ref[:, half * part : half * (part + 1)] = slope
+            slope_ref[:, half * part : half * (part + 1)] = slope.astype(BF16)
             pair.append(active)
-            second = second + mm(active, outer(part), NN)
-        keep, send = split(pair)
-        at1 = (half - ca + half - cb) * far + half - ca
-        keep2_ref[:, cb * far : cb * (far + 1)] = keep[:, :cb]
-        keep1_ref[:, at1 : at1 + half - cb] = keep[:, cb:]
-        early_send_ref[:, model + cb * far : model + cb * (far + 1)] = send[:, :cb]
-        late_send_ref[:, start1 + at1 : start1 + at1 + half - cb] = send[:, cb:]
+            outer = wu_ref[half * part : half * (part + 1), :] if part < 2 else far_outer(late_ref, part, half)
+            second = second + mm(active, outer, NN)
+        keep, send = by_core(lower, pair)
+        keep_ref[:, half * far : half * (far + 1)] = keep
+        send_ref[:, model + half * far : model + half * (far + 1)] = send
     n2, inv2 = normalise(second)
     live = live_ref[...] > 0.5
     result = jnp.where(live, n2 * vec[4] + vec[5], 0.0).astype(BF16)
     out_ref[...] = result
-    cross_ref[:, width:] = result[:, : model // 2].astype(F32)
+    out_first_ref[...] = result[:, : model // 2].astype(F32)
     out_late_ref[...] = result[:, model // 2 :].astype(F32)
     dz = jnp.where(live, cot_ref[...].astype(F32), 0.0)
     d_second = normalise_back(dz * vec[4], n2, inv2)
+    d_second_ref[...] = d_second
     d_low = d_second.astype(BF16)
-    both(1, d_low)
-    d_normed = d_second
-    inner_sums = []
-    for far in range(2):
-        pair = []
-        for part in (2 * far, 2 * far + 1):
-            d_hidden = mm(d_low, outer(part), NT)
-            d_inner = (d_hidden * slope_ref[:, half * part : half * (part + 1)]).astype(BF16)
-            pair.append(d_inner)
-            inner_sums.append(column_sum(d_inner.astype(F32)))
-            d_normed = d_normed + mm(d_inner, inner(part), NT)
-        keep, send = split(pair)
-        at1 = (half - ca + half - cb) * far
-        keep0_ref[:, ca * far : ca * (far + 1)] = keep[:, :ca]
-        keep1_ref[:, at1 : at1 + half - ca] = keep[:, ca:]
-        late_send_ref[:, start0 + ca * far : start0 + ca * (far + 1)] = send[:, :ca]
-        late_send_ref[:, start1 + at1 : start1 + at1 + half - ca] = send[:, ca:]
-    d_first = normalise_back(d_normed * vec[1], n1, inv1)
-    first_ref[...] = d_first
-    d_attn = d_first.astype(BF16)
-    both(2, d_attn)
-    dco_ref[...] = mm(d_attn, wo_ref[...], NT).astype(BF16).astype(F32)
-    cross_ref[:, :width] = mm(d_attn, wo_far, NT).astype(BF16).astype(F32)
-    keep, send = split((own, got))
-    keep0_ref[:, 2 * ca :] = keep
-    late_send_ref[:, start0 + 2 * ca : start1] = send
+    d_low_ref[...] = d_low
+    send_ref[:, :model] = d_low.astype(F32)
     sums = jnp.concatenate(
-        [
-            column_sum(d_first),
-            column_sum(d_normed * n1),
-            column_sum(d_normed),
-            column_sum(d_second),
-            column_sum(dz * n2),
-            column_sum(dz),
-            jnp.zeros((2, model), F32),
-        ],
-        axis=0,
-    )
-    inner_sums = jnp.concatenate([*inner_sums, jnp.zeros((4, half), F32)], axis=0)
+        [column_sum(d_second), column_sum(dz * n2), column_sum(dz), jnp.zeros((5, model), F32)], axis=0
+    )
 
     @pl.when(step == 0)
     def _():
         sums_ref[...] = sums
-        inner_sums_ref[...] = inner_sums
 
     @pl.when(step != 0)
     def _():
         sums_ref[...] += sums
-        inner_sums_ref[...] += inner_sums
-
-
-def middle(at, x, cot, live, context, got, wo, wi, wu, early, late, vec, bias, rows=256):
+
+    @pl.when(step == pl.num_programs(0) - 1)
+    def _():
+        for copy in leaving():
+            copy.wait()
+
+
+def forward(at, x, cot, live, context, got, wo, wi, wu, early, late, vec, bias, rows=256):
     half, width = got.shape
     model, hidden = wi.shape
     rows = min(rows, half)
     steps = half // rows
     mine = lambda w: pl.BlockSpec((rows, w), lambda i, s: (i + s[0] * steps, 0))
     tile = lambda w: pl.BlockSpec((rows, w), lambda i, s: (i, 0))
-    ca, cb = group_cuts(hidden // 2)
-    widths = (2 * ca + width, 2 * (hidden - ca - cb), 2 * cb)
+    anywhere = pl.BlockSpec(memory_space=pl.ANY)
+    widths = (
+        (model, BF16), (model // 2, F32), (model // 2, F32), (model, BF16), (model, BF16), (hidden, BF16),
+        (2 * model + hidden + width, F32), (2 * hidden, BF16), (model, F32), (1, F32), (model, F32),
+    )
+    far_shapes = [(SLICES, *early[0].shape), (SLICES, *late[0].shape)]
     return pl.pallas_call(
-        middle_kernel,
+        forward_kernel,
         grid_spec=pltpu.PrefetchScalarGridSpec(
             num_scalar_prefetch=1,
             grid=(steps,),
             in_specs=[
                 mine(model), mine(model), mine(1), mine(width), tile(width),
-                whole_block(wo.shape), *[pl.BlockSpec(memory_space=pl.ANY)] * (2 + 2 * SLICES),
+                whole_block(wo.shape), *[anywhere] * (2 + 2 * SLICES),
                 whole_block(vec.shape), whole_block(bias.shape),
             ],
             out_specs=[
-                tile(model), tile(model // 2), tile(model), tile(width), tile(width + model // 2),
-                pl.BlockSpec((3, rows, model), lambda i, s: (0, i, 0)),
-                *(tile(w) for w in widths),
-                tile(model + widths[2]), tile(2 * model + widths[0] + widths[1]),
+                *(tile(w) for w, _ in widths), pl.BlockSpec((8, model), lambda i, s: (0, 0)), anywhere, anywhere,
+            ],
+            scratch_shapes=[
+                *(pltpu.VMEM(shape, BF16) for shape in far_shapes),
+                pltpu.VMEM(wi.shape, BF16),
+                pltpu.VMEM(wu.shape, BF16),
+                *(pltpu.VMEM(shape, F32) for shape in far_shapes),
+                pltpu.SemaphoreType.DMA((5 * SLICES,)),
+                pltpu.SemaphoreType.DMA((2,)),
+            ],
+        ),
+        out_shape=[
+            *(struct((half, w), kind) for w, kind in widths), struct((8, model), F32),
+            *(struct(shape, BF16) for shape in far_shapes),
+        ],
+        compiler_params=params(63),
+        cost_estimate=cost(8 * half * model * hidden, 24 * model * hidden, 4 * half * hidden),
+        name="forward",
+    )(at, x, cot, live, context, got, wo, wi, wu, *early, *late, vec, bias)
+
+
+def backward_kernel(
+    at_ref, slope_ref, n1_ref, inv1_ref, d_second_ref, d_low_ref, own_ref, got_ref, wo_ref, vec_ref,
+    wi_hbm, wu_hbm, early_hbm, late_hbm,
+    first_ref, dco_ref, dcf_ref, d_attn_ref, keep0_ref, keep1_ref, send_ref, sums_ref, inner_sums_ref,
+    wi_ref, wu_ref, early_ref, late_ref, in_sem,
+):
+    step = pl.program_id(0)
+    lower = at_ref[1] % 2 == 0
+    hidden, half, model, width, cut = middle_sizes(wi_hbm, wo_ref, early_ref)
+    ca = first_cut(half)
+
+    def copies():
+        pairs = ((wu_hbm, wu_ref), (wi_hbm, wi_ref), (late_hbm, late_ref), (early_hbm, early_ref))
+        return [pltpu.make_async_copy(*pair, in_sem.at[k]) for k, pair in enumerate(pairs)]
+
+    @pl.when(step == 0)
+    def _():
+        for copy in copies():
+            copy.start()
+
+    d_low = d_low_ref[...]
+    n1 = n1_ref[...]
+    d_normed = d_second_ref[...]
+    inner_sums = []
+    for far in range(2):
+
+        @pl.when(step == 0)
+        def _():
+            for copy in copies()[2 * far : 2 * far + 2]:
+                copy.wait()
+
+        pair = []
+        for part in (2 * far, 2 * far + 1):
+            outer = wu_ref[half * part : half * (part + 1), :] if part < 2 else far_outer(late_ref, part, half)
+            inner = wi_ref[:, half * part : half * (part + 1)] if part < 2 else far_block(early_ref, cut[part - 2], cut[part - 1])
+            d_hidden = mm(d_low, outer, NT)
+            d_inner = (d_hidden * slope_ref[:, half * part : half * (part + 1)].astype(F32)).astype(BF16)
+            pair.append(d_inner)
+            inner_sums.append(column_sum(d_inner.astype(F32)))
+            d_normed = d_normed + mm(d_inner, inner, NT)
+        keep, send = by_core(lower, pair)
+        da = half - ca
+        keep0_ref[:, ca * far : ca * (far + 1)] = keep[:, :ca]
+        keep1_ref[:, da * far : da * (far + 1)] = keep[:, ca:]
+        send_ref[:, ca * far : ca * (far + 1)] = send[:, :ca]
+        send_ref[:, 2 * ca + da * far : 2 * ca + da * (far + 1)] = send[:, ca:]
+    d_first = normalise_back(d_normed * vec_ref[1:2, :], n1, inv1_ref[...])
+    first_ref[...] = d_first
+    d_attn = d_first.astype(BF16)
+    d_attn_ref[...] = d_attn
+    send_ref[:, hidden:] = d_attn.astype(F32)
+    dco_ref[...] = mm(d_attn, wo_ref[...], NT).astype(BF16).astype(F32)
+    dcf_ref[...] = mm(d_attn, far_block(early_ref, 0, cut[0]), NT).astype(BF16).astype(F32)
+    keep, _ = by_core(lower, (own_ref[...], got_ref[...]))
+    keep0_ref[:, 2 * ca :] = keep
+    sums = jnp.concatenate(
+        [column_sum(d_first), column_sum(d_normed * n1), column_sum(d_normed), jnp.zeros((5, model), F32)], axis=0
+    )
+    inner_sums = jnp.concatenate([*inner_sums, jnp.zeros((4, half), F32)], axis=0)
+
+    @pl.when(step == 0)
+    def _():
+        sums_ref[...] = sums
+        inner_sums_ref[...] = inner_sums
+
+    @pl.when(step != 0)
+    def _():
+        sums_ref[...] += sums
+        inner_sums_ref[...] += inner_sums
+
+
+def backward(at, slope, n1, inv1, d_second, d_low, context, got, wo, vec, wi, wu, early, late, rows=256):
+    half, width = got.shape
+    model, hidden = wi.shape
+    rows = min(rows, half)
+    steps = half // rows
+    ca = first_cut(hidden // 2)
+    mine = lambda w: pl.BlockSpec((rows, w), lambda i, s: (i + s[0] * steps, 0))
+    tile = lambda w: pl.BlockSpec((rows, w), lambda i, s: (i, 0))
+    anywhere = pl.BlockSpec(memory_space=pl.ANY)
+    widths = (
+        (model, F32), (width, F32), (width, F32), (model, BF16), (2 * ca + width, BF16), (hidden - 2 * ca, BF16),
+        (hidden + model, F32),
+    )
+    return pl.pallas_call(
+        backward_kernel,
+        grid_spec=pltpu.PrefetchScalarGridSpec(
+            num_scalar_prefetch=1,
+            grid=(steps,),
+            in_specs=[
+                tile(2 * hidden), tile(model), tile(1), tile(model), tile(model), mine(width), tile(width),
+                whole_block(wo.shape), whole_block(vec.shape), *[anywhere] * 4,
+            ],
+            out_specs=[
+                *(tile(w) for w, _ in widths),
                 pl.BlockSpec((8, model), lambda i, s: (0, 0)),
                 pl.BlockSpec((8, hidden // 2), lambda i, s: (0, 0)),
             ],
             scratch_shapes=[
-                pltpu.VMEM((rows, 2 * hidden), F32),
-                pltpu.VMEM((SLICES, *early[0].shape), BF16),
-                pltpu.VMEM((SLICES, *late[0].shape), BF16),
-                pltpu.VMEM(wi.shape, BF16),
-                pltpu.VMEM(wu.shape, BF16),
-                pltpu.VMEM((SLICES, *early[0].shape), F32),
-                pltpu.VMEM((SLICES, *late[0].shape), F32),
-                pltpu.SemaphoreType.DMA((5 * SLICES,)),
+                *(pltpu.VMEM(a.shape, BF16) for a in (wi, wu, early, late)),
+                pltpu.SemaphoreType.DMA((4,)),
             ],
         ),
         out_shape=[
-            struct((half, model), BF16), struct((half, model // 2), F32), struct((half, model), F32),
-            struct((half, width), F32), struct((half, width + model // 2), F32),
-            struct((3, half, model), BF16),
-            *(struct((half, w), BF16) for w in widths),
-            struct((half, model + widths[2]), F32),
-            struct((half, 2 * model + widths[0] + widths[1]), F32),
-            struct((8, model), F32), struct((8, hidden // 2), F32),
+            *(struct((half, w), kind) for w, kind in widths), struct((8, model), F32), struct((8, hidden // 2), F32),
         ],
         compiler_params=params(63),
-        cost_estimate=cost(
-            16 * half * model * (hidden + width // 2), 24 * model * hidden + 80 * half * model, 6 * half * hidden
-        ),
-        name="middle",
-    )(at, x, cot, live, context, got, wo, wi, wu, *early, *late, vec, bias)
-
-
-def weight_kernel(plan, count, bit_ref, left_hbm, *rest):
+        cost_estimate=cost(8 * half * model * hidden, 24 * model * hidden),
+        name="backward",
+    )(at, slope, n1, inv1, d_second, d_low, context, got, wo, vec, wi, wu, early, late)
+
+
+def weight_kernel(plan, count, kinds, bit_ref, *rest):
     groups = len(plan)
+    left_hbm, rest = rest[:kinds], rest[kinds:]
     keep_hbm, rest = rest[:groups], rest[groups:]
     got_hbm, rest = rest[:count], rest[count:]
     outs, rest = rest[: 2 * groups], rest[2 * groups :]
@@ -619,20 +699,18 @@
     def bring(key, source, target):
         if key not in ready:
             ready[key] = pltpu.make_async_copy(source, target, in_sem.at[len(arriving)])
-            arriving.append(ready[key])
-
-    for g, (_, _, tiles, (right_array, right_at)) in enumerate(plan):
-        for index, (left_array, left_at), a, b in tiles:
-            bring(("left", index), left_hbm.at[index], left_ref.at[index])
-            bring(
-                ("left got", index), got_hbm[left_array].at[:, left_at : left_at + model], left_got_ref.at[index]
-            )
+            ready[key].start()
+            arriving.append(key)
+
+    for g, (_, _, tiles) in enumerate(plan):
+        for index, (left_array, left_at), (right_array, right_at), a, b in tiles:
+            bring(("left", index), left_hbm[index], left_ref.at[index])
+            if ("left got", index) not in ready:
+                columns = slice(left_at, left_at + model)
+                bring(("left got", index), got_hbm[left_array].at[:, columns], left_got_ref.at[index])
             bring(("keep", g, a), keep_hbm[g].at[:, a:b], keep_refs[g].at[:, a:b])
-            bring(
-                ("got", g, a), got_hbm[right_array].at[:, right_at + a : right_at + b], got_refs[g].at[:, a:b]
-            )
-    for copy in arriving:
-        copy.start()
+            columns = slice(right_at, right_at + b - a)
+            bring(("got", g, a), got_hbm[right_array].at[:, columns], got_refs[g].at[:, a:b])
     waited = set()
 
     def need(*keys):
@@ -642,9 +720,9 @@
                 ready[key].wait()
 
     leaving = []
-    for g, (slot, group, tiles, _) in enumerate(plan):
+    for g, (slot, group, tiles) in enumerate(plan):
         width = keep_refs[g].shape[1]
-        for index, _, a, b in tiles:
+        for index, _, _, a, b in tiles:
             need(("left", index), ("left got", index), ("keep", g, a), ("got", g, a))
             left = jnp.concatenate([left_ref[index], left_got_ref[index].astype(BF16)], axis=0)
             right = jnp.concatenate([keep_refs[g][:, a:b], got_refs[g][:, a:b].astype(BF16)], axis=0)
@@ -671,10 +749,10 @@
         copy.wait()
 
 
-def weight_grads(at, left, keeps, received, plan):
-    _, depth, model = left.shape
+def weight_grads(at, lefts, keeps, received, plan):
+    depth, model = lefts[0].shape
     stages, shapes, steps = [], [], 0
-    for (slot, _, tiles, _), keep in zip(plan, keeps):
+    for (slot, _, tiles), keep in zip(plan, keeps):
         width = keep.shape[1]
         shape = (model, width // 2) if slot is None else (model // 2, width)
         stages.append(pltpu.VMEM((2, *shape), F32))
@@ -683,19 +761,19 @@
     columns = sum(keep.shape[1] for keep in keeps)
     anywhere = pl.BlockSpec(memory_space=pl.ANY)
     return pl.pallas_call(
-        functools.partial(weight_kernel, plan, len(received)),
+        functools.partial(weight_kernel, plan, len(received), len(lefts)),
         grid_spec=pltpu.PrefetchScalarGridSpec(
             num_scalar_prefetch=1,
             grid=(1,),
-            in_specs=[anywhere] * (1 + len(keeps) + len(received)),
+            in_specs=[anywhere] * (len(lefts) + len(keeps) + len(received)),
             out_specs=[anywhere] * len(shapes),
             scratch_shapes=[
-                pltpu.VMEM(left.shape, BF16),
-                pltpu.VMEM(left.shape, F32),
+                pltpu.VMEM((len(lefts), depth, model), BF16),
+                pltpu.VMEM((len(lefts), depth, model), F32),
                 *(pltpu.VMEM(keep.shape, BF16) for keep in keeps),
                 *(pltpu.VMEM(keep.shape, F32) for keep in keeps),
                 *stages,
-                pltpu.SemaphoreType.DMA((6 + 2 * steps,)),
+                pltpu.SemaphoreType.DMA((2 * len(lefts) + 2 * steps,)),
                 pltpu.SemaphoreType.DMA((2 * steps,)),
             ],
         ),
@@ -703,7 +781,7 @@
         compiler_params=params(63),
         cost_estimate=cost(4 * depth * model * columns, 4 * model * columns + 8 * depth * columns),
         name="weight_grads",
-    )(at, left, *keeps, *received)
+    )(at, *lefts, *keeps, *received)
 
 
 def combine_kernel(plan, count, bits_ref, *rest):
@@ -805,25 +883,24 @@
     )(value)
 
 
-def place_kernel(y_ref, own_ref, first_ref, second_ref, out_ref):
-    mine = pl.program_id(0) == y_ref[0]
+def place_kernel(steps, y_ref, own_ref, first_ref, second_ref, out_ref):
+    mine = pl.program_id(0) // steps == y_ref[0]
     got = jnp.concatenate([first_ref[...], second_ref[...]], axis=1)
     out_ref[...] = jnp.where(mine, own_ref[...].astype(F32), got).astype(BF16)
 
 
 def place_rows(y, own, first, second):
     half, model = own.shape
+    rows = min(128, half)
+    steps = half // rows
+    tile = lambda w: pl.BlockSpec((rows, w), lambda i, s: (i % steps, 0))
     return pl.pallas_call(
-        place_kernel,
+        functools.partial(place_kernel, steps),
         grid_spec=pltpu.PrefetchScalarGridSpec(
             num_scalar_prefetch=1,
-            grid=(2,),
-            in_specs=[
-                whole_block(own.shape),
-                pl.BlockSpec((half, model // 2), lambda i, s: (0, 1)),
-                whole_block(second.shape),
-            ],
-            out_specs=pl.BlockSpec((half, model), lambda i, s: (i, 0)),
+            grid=(2 * steps,),
+            in_specs=[tile(model), tile(model // 2), tile(model // 2)],
+            out_specs=pl.BlockSpec((rows, model), lambda i, s: (i, 0)),
         ),
         out_shape=struct((2 * half, model), BF16),
         compiler_params=params(63),
@@ -873,7 +950,7 @@
     me = d % SLICES
     core = d % 2
     rows = model // devices
-    near_mask, far_mask = 96 // rows, 192 // rows
+    near_mask, far_mask = 192 // rows, 96 // rows
     at = jnp.stack([y, me, (d // near_mask) % 2, (d // far_mask) % 2]).astype(jnp.int32)
     tie = lax.optimization_barrier
 
@@ -931,55 +1008,60 @@
         [output_bias, attn_gain, attn_shift, outer_bias, final_gain, final_shift, outer_bias, outer_bias]
     )
     bias = jnp.concatenate([inner_bias, far_bias, inner_bias, far_bias]).reshape(8, hidden // 2)
+    ca, cb = first_cut(hidden // 2), hidden // 2
+    da, db = hidden // 2 - ca, 0
     (
-        out_rows, out_late, d_first, dco, first_cross, left, keep0, keep1, keep2, early_send, late_send,
-        sums, inner_sums,
-    ) = middle(
+        out_rows, out_first, out_late, low, d_low, keep2, early_send, slope, n1, inv1, d_second, late_sums,
+        far_early, far_late,
+    ) = forward(
         at, x, cotangent[0], live, context, got, output_weight, inner_weight, outer_weight,
         early, late, vec, bias,
     )
+    early_got = swap(early_send, 1)
+    got_first = cross(out_first)
+    d_first, dco, dcf, d_attn, keep0, keep1, late_send, first_sums, inner_sums = backward(
+        at, slope, n1, inv1, d_second, d_low, context, got, output_weight, vec, inner_weight, outer_weight,
+        far_early, far_late,
+    )
     inner_columns = inner_sums[:4].reshape(2, model, 2)
-    columns = jnp.concatenate([sums[:6].T, inner_columns[0], inner_columns[1]], axis=1)
-    d_got = cross(first_cross)
-    early_got = swap(early_send, 1)
+    columns = jnp.concatenate([first_sums[:3].T, late_sums[:3].T, inner_columns[0], inner_columns[1]], axis=1)
+    early_got, got_first, late_send, dcf, columns = tie((early_got, got_first, late_send, dcf, columns))
     late_got = swap(late_send, 1)
-    early_got, columns = tie((early_got, columns))
-
-    ca, cb = group_cuts(hidden // 2)
-    da, db = hidden // 2 - ca, hidden // 2 - cb
-    normed_at, d_second_at, d_attn_at = (1, 0), (0, 0), (1, model)
+    d_got = cross(dcf)
+
+    low_at, d_attn_at = (0, 2 * cb + model), (1, hidden)
+    g2_keep, g2_send = weight_grads(
+        at, (d_low,), (keep2,), (early_got,),
+        (
+            (
+                3, far_mask * rows,
+                ((0, (0, 0), (0, model), 0, cb), (0, (0, 0), (0, model + cb), cb, 2 * cb)),
+            ),
+        ),
+    )
     g0_keep, g0_send, g1_keep, g1_send = weight_grads(
-        at, left, (keep0, keep1), (early_got, late_got),
+        at, (low, d_attn), (keep0, keep1), (early_got, late_got),
         (
             (
                 2, near_mask * rows,
                 (
-                    (0, normed_at, 0, ca), (0, normed_at, ca, 2 * ca),
-                    (2, d_attn_at, 2 * ca, 2 * ca + width),
+                    (0, low_at, (1, 0), 0, ca), (0, low_at, (1, ca), ca, 2 * ca),
+                    (1, d_attn_at, (0, 2 * model + hidden), 2 * ca, 2 * ca + width),
                 ),
-                (1, 2 * model),
             ),
             (
                 None, None,
-                (
-                    (0, normed_at, 0, da), (1, d_second_at, da, da + db),
-                    (0, normed_at, da + db, 2 * da + db), (1, d_second_at, 2 * da + db, 2 * (da + db)),
-                ),
-                (1, 2 * model + 2 * ca + width),
+                ((0, low_at, (1, 2 * ca), 0, da), (0, low_at, (1, 2 * ca + da), da, 2 * da)),
             ),
         ),
     )
-    early_got, g0_send = tie((early_got, g0_send))
-    g2_keep, g2_send = weight_grads(
-        at, left, (keep2,), (early_got,),
-        ((3, far_mask * rows, ((1, (0, 0), 0, cb), (1, (0, 0), cb, 2 * cb)), (0, model)),),
-    )
+    g0_send, g1_send, d_got = tie((g0_send, g1_send, d_got))
     g0_got = swap(g0_send, near_mask)
     g2_got = swap(g2_send, far_mask)
     g1_got = cross(g1_send)
 
     g0_send, g1_send, g2_send, dco, d_got = tie((g0_send, g1_send, g2_send, dco, d_got))
-    chunks = tuple(length * k // 32 for k in (2, 4, 14, 12))
+    chunks = tuple(length * k // 32 for k in (3, 4, 14, 11))
     group = rows if rows % 8 == 0 else None
     results = attend_back(
         at, q2, extra, k2, v, context, dco, d_got, live, kind, columns, pick,
@@ -1035,14 +1117,13 @@
     g0 = [term(g0_keep, near_mask), term(g0_got, near_mask)]
     g1 = [term(g1_keep), term(g1_got)]
     g2 = [term(g2_keep, far_mask), term(g2_got, far_mask)]
-    sends = combine(
-        bit_values, [[columns_of(g0, ca, 2 * ca + width)], [other(g1, near_mask)], [other(g2, near_mask)]]
-    )
+    (g2_send,) = combine(bit_values, [[other(g2, near_mask)]])
+    sends = combine(bit_values, [[columns_of(g0, ca, 2 * ca + width)], [other(g1, near_mask)]])
     e_got, c_got, sends, parts = tie((e_got, c_got, sends, parts))
     e.append(whole_of(e_got))
     c.append(whole_of(c_got))
+    g2_got = swap(g2_send, near_mask)
     g0_got = cross(sends[0])
-    g2_got = swap(sends[2], near_mask)
     g1_got = swap(sends[1], near_mask)
     (e_send,) = combine(bit_values, [[other(e, far_mask)]])
     e_got = swap(e_send, far_mask)
@@ -1057,18 +1138,12 @@
     g2 = [*kept(g2, near_mask), whole_of(g2_got)]
     e = [*kept(e, far_mask), whole_of(e_got)]
 
-    sends = combine(
-        bit_values,
-        [
-            [other(terms, far_mask) for terms in (g0, t, g1)],
-            [columns_of(g2, cb, 2 * cb)],
-            [other(c, near_mask)],
-        ],
-    )
+    (three_send,) = combine(bit_values, [[other(terms, far_mask) for terms in (g0, t, g1)]])
+    sends = combine(bit_values, [[columns_of(g2, cb, 2 * cb)], [other(c, near_mask)]])
     sends, parts = tie((sends, parts))
-    g2_got = cross(sends[1])
-    three_got = swap(sends[0], far_mask)
-    c_got = swap(sends[2], near_mask)
+    three_got = swap(three_send, far_mask)
+    g2_got = cross(sends[0])
+    c_got = swap(sends[1], near_mask)
     part1 = cross(parts[1])
     three_got, g2_got, c_got, part1, parts = tie((three_got, g2_got, c_got, part1, parts))
     g0 = [*kept(g0, far_mask), part_of(three_got, 0, ca)]
@@ -1081,16 +1156,15 @@
     sizes = (ca, da + db, cb, width)
     ends = [sum(sizes[:k]) for k in range(len(sizes) + 1)]
     mask = rest_masks[0]
-    sends = combine(
-        bit_values,
-        [[other(terms, mask) for terms in main], [other(e, near_mask)], [other(c, far_mask)]],
-    )
+    (main_send,) = combine(bit_values, [[other(terms, mask) for terms in main]])
+    main_send, late_bits = tie((main_send, bit_values))
+    sends = combine(late_bits, [[other(e, near_mask)], [other(c, far_mask)]])
     sends, parts = tie((sends, parts))
-    got_z = swap(sends[0], mask)
+    got_z = swap(main_send, mask)
     part2 = cross(parts[2])
-    c_got = swap(sends[2], far_mask)
-    e_got = swap(sends[1], near_mask)
-    layer_out = place_rows(at, out_rows, d_got, got_out)
+    c_got = swap(sends[1], far_mask)
+    e_got = swap(sends[0], near_mask)
+    layer_out = place_rows(at, out_rows, got_first, got_out)
     got_z, e_got, c_got, part2, parts, layer_out = tie((got_z, e_got, c_got, part2, parts, layer_out))
     main = [[*kept(terms, mask), part_of(got_z, ends[n], ends[n + 1])] for n, terms in enumerate(main)]
     e = [*kept(e, near_mask), whole_of(e_got)]
@@ -1101,26 +1175,22 @@
         main = [[*kept(terms, mask), part_of(got_z, ends[n], ends[n + 1])] for n, terms in enumerate(main)]
 
     for k, mask in enumerate(rest_masks):
-        outputs = [[other(c, mask), other(e, mask)], [kept(c, mask), kept(e, mask)]]
+        (pair_send,) = combine(bit_values, [[other(c, mask), other(e, mask)]])
+        outputs = [[kept(c, mask), kept(e, mask)]]
         if k == 0:
             outputs += [[other(terms, 1) for terms in main], [kept(terms, 1) for terms in main]]
         sends = combine(bit_values, outputs)
         if k == 0:
             sends, parts = tie((sends, parts))
-        pair_got = swap(sends[0], mask)
+        pair_got = swap(pair_send, mask)
         if k == 0:
             part3 = cross(parts[3])
-            got_last = swap(sends[2], 1)
-            keep = sends[3]
-            pair_got, got_last, part3 = tie((pair_got, got_last, part3))
-        c = [part_of(sends[1], 0, 3 * width), part_of(pair_got, 0, 3 * width)]
-        e = [part_of(sends[1], 3 * width, sends[1].shape[-1]), part_of(pair_got, 3 * width, sends[1].shape[-1])]
-    pair = (sends[1] + pair_got).reshape(rows, -1)
-    c, e = pair[:, : 3 * width], pair[:, 3 * width :]
-    last = e[:, 3 * width + 6 : 3 * width + 16]
-    last_got = cross(last)
-    small = last[:, :6] + last_got[:, :6]
-    inner_two = last[:, 6:8] + last_got[:, 8:]
+            got_last = swap(sends[1], 1)
+            keep = sends[2]
+        pair_keep = sends[0]
+        wide = pair_keep.shape[-1]
+        c = [part_of(pair_keep, 0, 3 * width), part_of(pair_got, 0, 3 * width)]
+        e = [part_of(pair_keep, 3 * width, wide), part_of(pair_got, 3 * width, wide)]
 
     got_last = got_last.reshape(rows, -1)
     keep = keep.reshape(rows, -1)
@@ -1133,8 +1203,17 @@
     t = keep[:, at3:] + got_last[:, at3:]
     grad_inner = jnp.concatenate(inner_half(low_half) + inner_half(high_half), axis=1)
     grad_outer = jnp.concatenate(outer_half(low_half) + outer_half(high_half), axis=1).T
-    sent_parts = (part0, part1, part2, part3)
-    input_grad = jnp.concatenate([(a + b).astype(BF16) for a, b in zip(parts, sent_parts)], axis=0)
+    grad_output = t.T
+    sent_parts = (part0, part1, part2)
+    input_first = jnp.concatenate([(a + b).astype(BF16) for a, b in zip(parts, sent_parts)], axis=0)
+    pair_got, part3, input_first = tie((pair_got, part3, input_first))
+    pair = (pair_keep + pair_got).reshape(rows, -1)
+    c, e = pair[:, : 3 * width], pair[:, 3 * width :]
+    last = e[:, 3 * width + 6 : 3 * width + 16]
+    last_got = cross(last)
+    small = last[:, :6] + last_got[:, :6]
+    inner_two = last[:, 6:8] + last_got[:, 8:]
+    input_grad = jnp.concatenate([input_first, (parts[3] + part3).astype(BF16)], axis=0)
 
     piece = lambda array, k: array[:, width * k : width * (k + 1)]
     grad_query_weight = jnp.stack([piece(c, 0), piece(c, 1), piece(c, 2), piece(e, 0)])
@@ -1148,7 +1227,7 @@
         biases[4],
         piece(e, 2),
         biases[5],
-        t.T,
+        grad_output,
         small[:, 0],
         small[:, 1],
         small[:, 2],

time: 364 us -> 356 us (0.978); the launches traced: 358 us -> 354 us
  waiting for transfers between devices: 153 us -> 129 us
  Pallas kernels: 135 us -> 155 us
    ppermute x15 -> x16, waiting for transfers between devices: 75.5 us -> 60.3 us  [cross(): return lax.ppermute(value, 'tensor', [(0, 1), (1, 0)])]
    pallas_call x4 -> x5, Pallas kernels: 51.7 us -> 61.7 us  [the longest x1 21.2 us: forward(): pl.pallas_call(forward_kernel, grid_spec=pltpu.PrefetchScalarGridSpec(num...]
    pallas_call x5 -> x9, Pallas kernels: 22.9 us -> 31.9 us  [combine(): pl.pallas_call(functools.partial(combine_kernel, plan, len(arrays)), grid...]
    ppermute x29, waiting for transfers between devices: 77.3 us -> 69 us  [swap(): return lax.ppermute(value, 'dp', [(i, i ^ mask) for i in range(devices)])]
    ppermute x15 -> x16, starting transfers between devices: 14.9 us -> 16.5 us  [cross(): return lax.ppermute(value, 'tensor', [(0, 1), (1, 0)])]
  transfers between devices with their start and end apart: 44 -> 45, of which waited for: 18 -> 20; matrix products, arithmetic and copies ran while one was open for 6% -> 6% of each run, Pallas kernels for 25% -> 33%
where the time goes in v4:
time: 356 us; the launch traced here: 354 us
  Pallas kernels  155 us (44%)
  waiting for transfers between devices  129 us (36%)
  starting transfers between devices  38.2 us (11%)
  local copies, waits for them, and re-layouts  15 us (4%)
  other arithmetic  14.4 us (4%)
    ppermute x29, waiting for transfers between devices, swap(): return lax.ppermute(value, 'dp', [(i, i ^ mask) for i in range(devices)])  69 us
    ppermute x16, waiting for transfers between devices, cross(): return lax.ppermute(value, 'tensor', [(0, 1), (1, 0)])  60.3 us
    pallas_call x1, Pallas kernels, attend_back(): pl.pallas_call(functools.partial(attend_back_kernel, len(chunks), group),...  35.3 us
    pallas_call x9, Pallas kernels, combine(): pl.pallas_call(functools.partial(combine_kernel, plan, len(arrays)), grid...  31.9 us
    ppermute x29, starting transfers between devices, swap(): return lax.ppermute(value, 'dp', [(i, i ^ mask) for i in range(devices)])  21.7 us
    pallas_call x1, Pallas kernels, forward(): pl.pallas_call(forward_kernel, grid_spec=pltpu.PrefetchScalarGridSpec(num...  21.2 us
    pallas_call x2, Pallas kernels, weight_grads(): pl.pallas_call(functools.partial(weight_kernel, plan, len(received), len(...  17.1 us
    pallas_call x1, Pallas kernels, backward(): pl.pallas_call(backward_kernel, grid_spec=pltpu.PrefetchScalarGridSpec(nu...  16.6 us
  transfers between devices with their start and end apart: 45, of which 20 were waited for; matrix products, arithmetic and copies ran while one was open for 6% of the time, Pallas kernels for 33%

profile of v4, /device:TPU:0, one launch (start us, length us, event | category | flops | bytes accessed | tf_op | source)
XLA Modules:
  0.0 354.0 jit_solution(16234759235956745858)
XLA Ops:
  8.0 8.2 %project.1 = (bf16[1024,768]{1,0:T(8,128)(2,1)}, bf16[1024,768]{1,0:T(8,128)(2,1)}, bf16[1024,384]{1,0:T(8,128)(2,1)}) custom-call(bf16[1024,768]{1,0:T(8,128)(2,1)} %bitcast.74, f32[1024,1]{1,0:T(8,128)} %copy.46.kind_ref, bf16[4,768,384]{2,1,0:T(8,128)(2,1)} %wq_hbm.1, f32[4,384]{1,0:T(4,128)} %bq_ref.1, bf16[768,384]{1,0:T(8,128)(2,1)} %wk_hbm.1, ...), custom_call_target="tpu_custom_call" | custom-call | flops 3623878656 | bytes 9437184 | tf_op jit(solution)/shard_map/project/pallas_call | solution.py:87
  18.3 4.1 %collective-permute-done.1 = f32[1536]{0:T(1024)S(1)} collective-permute-done((f32[1536]{0:T(1024)S(1)}, f32[1536]{0:T(1024)S(1)}, u32[]{:S(2)}, u32[]{:S(2)}) %collective-permute-start.1) | collective-permute-done | bytes 6176 | tf_op jit(solution)/shard_map/ppermute | solution.py:948
  28.8 14.1 %attend.1 = (bf16[1024,384]{1,0:T(8,128)(2,1)}, bf16[1024,768]{1,0:T(8,128)(2,1)}) custom-call(bf16[1024,768]{1,0:T(8,128)(2,1)} %get-tuple-element.175.q2_ref, bf16[1024,768]{1,0:T(8,128)(2,1)} %get-tuple-element.176.k2_ref, bf16[1024,384]{1,0:T(8,128)(2,1)} %get-tuple-element.177.v_ref, f32[1024,1]{1,0:T(8,128)} %fusion.1.live_ref), custom_call_target="tpu_custom_call" | custom-call | flops 4026531840 | bytes 7864320 | tf_op jit(solution)/shard_map/attend/pallas_call | solution.py:154
  47.4 3.7 %turn.1.turned_hbm = bf16[768,1024]{1,0:T(8,128)(2,1)} custom-call(bf16[1024,768]{1,0:T(8,128)(2,1)} %bitcast.75), custom_call_target="tpu_custom_call" | custom-call | flops 786432 | bytes 3145728 | tf_op jit(solution)/shard_map/turn/pallas_call | solution.py:874
  52.8 7.9 %collective-permute-done.10.rest_12_ = f32[192,768]{1,0:T(8,128)} collective-permute-done((f32[192,768]{1,0:T(8,128)}, f32[192,768]{1,0:T(8,128)}, u32[]{:S(2)}, u32[]{:S(2)}) %collective-permute-start.10) | collective-permute-done | bytes 589856 | tf_op jit(solution)/shard_map/ppermute | solution.py:945
  63.0 15.5 %collective-permute-done.8.rest_14_ = f32[192,768]{1,0:T(8,128)} collective-permute-done((f32[192,768]{1,0:T(8,128)}, f32[192,768]{1,0:T(8,128)}, u32[]{:S(2)}, u32[]{:S(2)}) %collective-permute-start.8) | collective-permute-done | bytes 589856 | tf_op jit(solution)/shard_map/ppermute | solution.py:948
  85.6 21.2 %forward.1 = (bf16[512,768]{1,0:T(8,128)(2,1)}, f32[512,384]{1,0:T(8,128)}, f32[512,384]{1,0:T(8,128)}, bf16[512,768]{1,0:T(8,128)(2,1)}, bf16[512,768]{1,0:T(8,...) custom-call(s32[4]{0:T(128)} %pad_add_fusion.1.at_ref.bit_ref.y_ref,, ...), custom_call_target="tpu_custom_call" | custom-call | flops 4831838208 | bytes 28311552 | tf_op jit(solution)/shard_map/forward/pallas_call | solution.py:541
  107.6 16.6 %backward.1 = (f32[512,768]{1,0:T(8,128)}, f32[512,384]{1,0:T(8,128)}, f32[512,384]{1,0:T(8,128)}, bf16[512,768]{1,0:T(8,128)(2,1)}, bf16[512,1152]{1,0:T(8,128)...) custom-call(s32[4]{0:T(128)} %pad_add_fusion.1.at_ref.bit_ref.y_ref, ...), custom_call_target="tpu_custom_call" | custom-call | flops 4831838208 | bytes 28311552 | tf_op jit(solution)/shard_map/backward/pallas_call | solution.py:657
  127.8 8.2 %weight_grads.3 = (f32[384,1536]{1,0:T(8,128)}, f32[384,1536]{1,0:T(8,128)}) custom-call(s32[4]{0:T(128)} %pad_add_fusion.1.at_ref.bit_ref.y_ref, bf16[512,768]{1,0:T(8,128)(2,1)} %get-tuple-element.206.d_low_ref.rest_0_, bf16[512,1536]{1,0:T(8,128)(2,1)} %get-tuple-element.227.rest_1_, f32[512,3456]{1,0:T(8,128)} %collective-permute-done.18.rest_4_.rest_2_), custom_call_target="tpu_custom_call" | custom-call | flops 2415919104 | bytes 11010048 | tf_op jit(solution)/shard_map/weight_grads/pallas_call | solution.py:763
  137.2 8.9 %weight_grads.2 = (f32[384,1152]{1,0:T(8,128)}, f32[384,1152]{1,0:T(8,128)}, f32[768,384]{1,0:T(8,128)}, f32[768,384]{1,0:T(8,128)}) custom-call(s32[4]{0:T(128)} %pad_add_fusion.1.at_ref.bit_ref.y_ref, bf16[512,768]{1,0:T(8,128)(2,1)} %get-tuple-element.201.rest_0_, bf16[512,768]{1,0:T(8,128)(2,1)} %get-tuple-element.209.rest_1_, ...), custom_call_target="tpu_custom_call" | custom-call | flops 3019898880 | bytes 13762560 | tf_op jit(solution)/shard_map/weight_grads/pallas_call | solution.py:763
  151.6 35.3 %attend_back.1 = (f32[96,768]{1,0:T(8,128)}, f32[128,768]{1,0:T(8,128)}, f32[448,768]{1,0:T(8,128)}, f32[352,768]{1,0:T(8,128)}, f32[384,1152]{1,0:T(8,128)}, /*...) custom-call(s32[4]{0:T(128)} %pad_add_fusion.1.at_ref.bit_ref.y_ref, ...), custom_call_target="tpu_custom_call" | custom-call | flops 8053063680 | bytes 15728640 | tf_op jit(solution)/shard_map/attend_back/pallas_call | solution.py:327
  187.0 6.0 %collective-permute-done.25.second_ref = f32[512,384]{1,0:T(8,128)S(1)} collective-permute-done((f32[512,384]{1,0:T(8,128)}, f32[512,384]{1,0:T(8,128)S(1)}, u32[]{:S(2)}, u32[]{:S(2)}) %collective-permute-start.25) | collective-permute-done | bytes 786464 | tf_op jit(solution)/shard_map/ppermute | solution.py:948
  194.1 3.4 combine.10
  198.4 3.7 %combine.9 = (f32[2,1,2,2,48,768]{5,4,3,2,1,0:T(8,128)}, f32[2,1,2,2,48,384]{5,4,3,2,1,0:T(8,128)}) custom-call(s32[4]{0:T(128)} %pad_add_fusion.bits_ref, f32[2,1,2,2,48,1152]{5,4,3,2,1,0:T(8,128)} %bitcast.66, f32[2,1,2,2,48,1152]{5,4,3,2,1,0:T(8,128)} %bitcast.15.rest_1_.rest_9_, f32[2,2,2,2,48,384]{5,4,3,2,1,0:T(8,128)} %bitcast.70, ...), custom_call_target="tpu_custom_call" | custom-call | flops 3538944 | bytes 7077888 | tf_op jit(solution)/shard_map/combine/pallas_call | solution.py:848
  210.3 16.5 %collective-permute-done.30.rest_2_.rest_9_.rest_18_ = f32[2,1,1,2,48,1536]{5,4,3,2,1,0:T(8,128)} collective-permute-done((f32[2,1,1,2,48,1536]{5,4,3,2,1,0:T(8,128)}, f32[2,1,1,2,48,1536]{5,4,3,2,1,0:T(8,128)}, u32[]{:S(2)}, u32[]{:S(2)}) %collective-permute-start.30) | collective-permute-done | bytes 1179680 | tf_op jit(solution)/shard_map/ppermute | solution.py:945
  226.8 9.6 %collective-permute-done.32 = f32[96,768]{1,0:T(8,128)S(1)} collective-permute-done((f32[96,768]{1,0:T(8,128)}, f32[96,768]{1,0:T(8,128)S(1)}, u32[]{:S(2)}, u32[]{:S(2)}) %collective-permute-start.32) | collective-permute-done | bytes 294944 | tf_op jit(solution)/shard_map/ppermute | solution.py:948
  244.1 3.7 %combine.13 = (f32[2,1,1,2,48,768]{5,4,3,2,1,0:T(8,128)}, f32[2,1,2,1,48,1152]{5,4,3,2,1,0:T(8,128)}) custom-call(s32[4]{0:T(128)} %pad_add_fusion.bits_ref, f32[2,2,1,2,48,1536]{5,4,3,2,1,0:T(8,128)} %bitcast.55, f32[2,2,1,2,48,1536]{5,4,3,2,1,0:T(8,128)} %bitcast.21.rest_1_.rest_8_.rest_17_, ...), custom_call_target="tpu_custom_call" | custom-call | flops 3538944 | bytes 7077888 | tf_op jit(solution)/shard_map/combine/pallas_call | solution.py:848
  250.3 20.5 %collective-permute-done.36 = f32[128,768]{1,0:T(8,128)S(1)} collective-permute-done((f32[128,768]{1,0:T(8,128)}, f32[128,768]{1,0:T(8,128)S(1)}, u32[]{:S(2)}, u32[]{:S(2)}) %collective-permute-start.36) | collective-permute-done | bytes 393248 | tf_op jit(solution)/shard_map/ppermute | solution.py:948
  271.8 3.4 combine.14
  284.1 6.8 %place_rows.1 = bf16[1024,768]{1,0:T(8,128)(2,1)} custom-call(s32[4]{0:T(128)} %pad_add_fusion.1.at_ref.bit_ref.y_ref, bf16[512,768]{1,0:T(8,128)(2,1)} %get-tuple-element.303.own_ref, f32[512,384]{1,0:T(8,128)} %copy-done.8, f32[512,384]{1,0:T(8,128)} %copy-done.9), custom_call_target="tpu_custom_call" | custom-call | flops 393216 | bytes 4718592 | tf_op jit(solution)/shard_map/place_rows/pallas_call | solution.py:897
  292.5 13.5 %collective-permute-done.38.rest_7_ = f32[2,1,1,1,48,1280]{5,4,3,2,1,0:T(8,128)S(1)} collective-permute-done((f32[2,1,1,1,48,1280]{5,4,3,2,1,0:T(8,128)}, f32[2,1,1,1,48,1280]{5,4,3,2,1,0:T(8,128)S(1)}, u32[]{:S(2)}, u32[]{:S(2)}) %collective-permute-start.38) | collective-permute-done | bytes 491552 | tf_op jit(solution)/shard_map/ppermute | solution.py:945
  306.0 6.0 %collective-permute-done.37.rest_12_ = f32[1,1,1,2,48,1920]{5,4,3,2,1,0:T(8,128)} collective-permute-done((f32[1,1,1,2,48,1920]{5,4,3,2,1,0:T(8,128)}, f32[1,1,1,2,48,1920]{5,4,3,2,1,0:T(8,128)}, u32[]{:S(2)}, u32[]{:S(2)}) %collective-permute-start.37) | collective-permute-done | bytes 737312 | tf_op jit(solution)/shard_map/ppermute | solution.py:945
  315.1 4.9 %combine.17 = (f32[1,1,1,1,48,2432]{5,4,3,2,1,0:T(8,128)}, f32[1,1,1,1,48,1920]{5,4,3,2,1,0:T(8,128)}, f32[1,1,1,1,48,1920]{5,4,3,2,1,0:T(8,128)}) custom-call(s32[4]{0:T(128)} %pad_add_fusion.bits_ref, f32[2,2,2,1,48,1152]{5,4,3,2,1,0:T(8,128)} %bitcast.65, f32[2,2,2,1,48,1152]{5,4,3,2,1,0:T(8,128)} %collective-permute-done.27.rest_4_.rest_1_, ...), custom_call_target="tpu_custom_call" | custom-call | flops 5554176 | bytes 11108352 | tf_op jit(solution)/shard_map/combine/pallas_call | solution.py:848
  326.9 17.2 %collective-permute-done.41 = f32[1,1,1,1,48,2432]{5,4,3,2,1,0:T(8,128)S(1)} collective-permute-done((f32[1,1,1,1,48,2432]{5,4,3,2,1,0:T(8,128)S(1)}, f32[1,1,1,1,48,2432]{5,4,3,2,1,0:T(8,128)S(1)}, u32[]{:S(2)}, u32[]{:S(2)}) %collective-permute-start.41) | collective-permute-done | bytes 466976 | tf_op jit(solution)/shard_map/ppermute | solution.py:945
  (212 shorter events, 92.9 us)
Async XLA Ops:
  22.4 22.5 %collective-permute-start.4 = (f32[240,768]{1,0:T(8,128)}, f32[240,768]{1,0:T(8,128)S(1)}, u32[]{:S(2)}, u32[]{:S(2)}) collective-permute-start(f32[240,768]{1,0:T(8,128)} %collective-permute-done.rest_0_), channel_id=1, source_target_pairs={{0,8},{2,10},{4,12},{6,14},{8,0},{10,2},{12,4},{14,6},{16,24},{18,... | collective-permute-start | bytes 2211848 | tf_op jit(solution)/shard_map/ppermute | solution.py:945
  24.2 20.7 %collective-permute-start.3 = (f32[240,768]{1,0:T(8,128)}, f32[240,768]{1,0:T(8,128)}, u32[]{:S(2)}, u32[]{:S(2)}) collective-permute-start(f32[240,768]{1,0:T(8,128)} %collective-permute-done.rest_0_), channel_id=1, source_target_pairs={{0,4},{2,6},{4,0},{6,2},{8,12},{10,14},{12,8},{14,10},{16,20},{18,... | collective-permute-start | bytes 2211848 | tf_op jit(solution)/shard_map/ppermute | solution.py:945
  46.0 32.4 %collective-permute-start.6 = (f32[512,384]{1,0:T(8,128)}, f32[512,384]{1,0:T(8,128)S(1)}, u32[]{:S(2)}, u32[]{:S(2)}) collective-permute-start(f32[512,384]{1,0:T(8,128)} %dynamic-slice_convert_fusion), channel_id=1, source_target_pairs={{0,1},{1,0},{2,3},{3,2},{4,5},{5,4},{6,7},{7,6},{8,9},{9,8},{10,11... | collective-permute-start | bytes 2359304 | tf_op jit(solution)/shard_map/ppermute | solution.py:948
  51.1 27.3 %collective-permute-start.7 = (f32[240,768]{1,0:T(8,128)}, f32[240,768]{1,0:T(8,128)S(1)}, u32[]{:S(2)}, u32[]{:S(2)}) collective-permute-start(f32[240,768]{1,0:T(8,128)} %copy-done.10), channel_id=1, source_target_pairs={{0,4},{2,6},{4,0},{6,2},{8,12},{10,14},{12,8},{14,10},{16,20},{18,... | collective-permute-start | bytes 2211848 | tf_op jit(solution)/shard_map/ppermute | solution.py:945
  106.9 20.2 %collective-permute-start.18 = (f32[512,3456]{1,0:T(8,128)}, f32[512,3456]{1,0:T(8,128)}, u32[]{:S(2)}, u32[]{:S(2)}) collective-permute-start(f32[512,3456]{1,0:T(8,128)} %get-tuple-element.212), channel_id=1, source_target_pairs={{0,2},{2,0},{4,6},{6,4},{8,10},{10,8},{12,14},{14,12},{16,18},{18,... | collective-permute-start | bytes 21233672 | tf_op jit(solution)/shard_map/ppermute | solution.py:945
  127.1 20.3 %collective-permute-start.21 = (f32[512,384]{1,0:T(8,128)}, f32[512,384]{1,0:T(8,128)}, u32[]{:S(2)}, u32[]{:S(2)}) collective-permute-start(f32[512,384]{1,0:T(8,128)} %get-tuple-element.224), channel_id=1, source_target_pairs={{0,1},{1,0},{2,3},{3,2},{4,5},{5,4},{6,7},{7,6},{8,9},{9,8},{10,11... | collective-permute-start | bytes 2359304 | tf_op jit(solution)/shard_map/ppermute | solution.py:948
  136.0 57.0 %collective-permute-start.24 = (f32[384,1536]{1,0:T(8,128)}, f32[384,1536]{1,0:T(8,128)}, u32[]{:S(2)}, u32[]{:S(2)}) collective-permute-start(f32[384,1536]{1,0:T(8,128)} %get-tuple-element.228), channel_id=1, source_target_pairs={{0,4},{2,6},{4,0},{6,2},{8,12},{10,14},{12,8},{14,10},{16,20},{18,... | collective-permute-start | bytes 7077896 | tf_op jit(solution)/shard_map/ppermute | solution.py:945
  147.4 45.6 %collective-permute-start.22 = (f32[384,1152]{1,0:T(8,128)}, f32[384,1152]{1,0:T(8,128)}, u32[]{:S(2)}, u32[]{:S(2)}) collective-permute-start(f32[384,1152]{1,0:T(8,128)} %get-tuple-element.225), channel_id=1, source_target_pairs={{0,8},{2,10},{4,12},{6,14},{8,0},{10,2},{12,4},{14,6},{16,24},{18,... | collective-permute-start | bytes 5308424 | tf_op jit(solution)/shard_map/ppermute | solution.py:945
  148.6 44.3 %collective-permute-start.23 = (f32[768,384]{1,0:T(8,128)}, f32[768,384]{1,0:T(8,128)}, u32[]{:S(2)}, u32[]{:S(2)}) collective-permute-start(f32[768,384]{1,0:T(8,128)} %get-tuple-element.226), channel_id=1, source_target_pairs={{0,1},{1,0},{2,3},{3,2},{4,5},{5,4},{6,7},{7,6},{8,9},{9,8},{10,11... | collective-permute-start | bytes 3538952 | tf_op jit(solution)/shard_map/ppermute | solution.py:948
  149.3 43.7 %collective-permute-start.25 = (f32[512,384]{1,0:T(8,128)}, f32[512,384]{1,0:T(8,128)S(1)}, u32[]{:S(2)}, u32[]{:S(2)}) collective-permute-start(f32[512,384]{1,0:T(8,128)} %get-tuple-element.229), channel_id=1, source_target_pairs={{0,1},{1,0},{2,3},{3,2},{4,5},{5,4},{6,7},{7,6},{8,9},{9,8},{10,11... | collective-permute-start | bytes 2359304 | tf_op jit(solution)/shard_map/ppermute | solution.py:948
  197.6 29.2 %collective-permute-start.30 = (f32[2,1,1,2,48,1536]{5,4,3,2,1,0:T(8,128)}, f32[2,1,1,2,48,1536]{5,4,3,2,1,0:T(8,128)}, u32[]{:S(2)}, u32[]{:S(2)}) collective-permute-start(f32[2,1,1,2,48,1536]{5,4,3,2,1,0:T(8,128)} %combine.10), channel_id=1, source_target_pairs={{0,8},{2,10},{4,12},{6,14},{8,0},{10,2},{12,4},{14,6},{16,24},{18,... | collective-permute-start | bytes 3538952 | tf_op jit(solution)/shard_map/ppermute | solution.py:945
  202.1 37.2 %collective-permute-start.28 = (f32[2,1,2,2,48,768]{5,4,3,2,1,0:T(8,128)}, f32[2,1,2,2,48,768]{5,4,3,2,1,0:T(8,128)}, u32[]{:S(2)}, u32[]{:S(2)}) collective-permute-start(f32[2,1,2,2,48,768]{5,4,3,2,1,0:T(8,128)} %get-tuple-element.258), channel_id=1, source_target_pairs={{0,1},{1,0},{2,3},{3,2},{4,5},{5,4},{6,7},{7,6},{8,9},{9,8},{10,11... | collective-permute-start | bytes 3538952 | tf_op jit(solution)/shard_map/ppermute | solution.py:948
  206.0 32.4 %collective-permute-start.31 = (f32[2,2,1,1,48,1280]{5,4,3,2,1,0:T(8,128)}, f32[2,2,1,1,48,1280]{5,4,3,2,1,0:T(8,128)S(1)}, u32[]{:S(2)}, u32[]{:S(2)}) collective-permute-start(f32[2,2,1,1,48,1280]{5,4,3,2,1,0:T(8,128)} %combine.11), channel_id=1, source_target_pairs={{0,4},{2,6},{4,0},{6,2},{8,12},{10,14},{12,8},{14,10},{16,20},{18,... | collective-permute-start | bytes 2949128 | tf_op jit(solution)/shard_map/ppermute | solution.py:945
  207.3 31.2 %collective-permute-start.29 = (f32[2,1,2,2,48,384]{5,4,3,2,1,0:T(8,128)}, f32[2,1,2,2,48,384]{5,4,3,2,1,0:T(8,128)S(1)}, u32[]{:S(2)}, u32[]{:S(2)}) collective-permute-start(f32[2,1,2,2,48,384]{5,4,3,2,1,0:T(8,128)} %get-tuple-element.259), channel_id=1, source_target_pairs={{0,8},{2,10},{4,12},{6,14},{8,0},{10,2},{12,4},{14,6},{16,24},{18,... | collective-permute-start | bytes 1769480 | tf_op jit(solution)/shard_map/ppermute | solution.py:945
  208.9 27.5 %collective-permute-start.32 = (f32[96,768]{1,0:T(8,128)}, f32[96,768]{1,0:T(8,128)S(1)}, u32[]{:S(2)}, u32[]{:S(2)}) collective-permute-start(f32[96,768]{1,0:T(8,128)} %get-tuple-element.318), channel_id=1, source_target_pairs={{0,1},{1,0},{2,3},{3,2},{4,5},{5,4},{6,7},{7,6},{8,9},{9,8},{10,11... | collective-permute-start | bytes 884744 | tf_op jit(solution)/shard_map/ppermute | solution.py:948
  242.5 29.2 %collective-permute-start.33 = (f32[2,1,1,2,48,1152]{5,4,3,2,1,0:T(8,128)}, f32[2,1,1,2,48,1152]{5,4,3,2,1,0:T(8,128)}, u32[]{:S(2)}, u32[]{:S(2)}) collective-permute-start(f32[2,1,1,2,48,1152]{5,4,3,2,1,0:T(8,128)} %combine.12), channel_id=1, source_target_pairs={{0,4},{2,6},{4,0},{6,2},{8,12},{10,14},{12,8},{14,10},{16,20},{18,... | collective-permute-start | bytes 2654216 | tf_op jit(solution)/shard_map/ppermute | solution.py:945
  247.8 24.0 %collective-permute-start.35 = (f32[2,1,2,1,48,1152]{5,4,3,2,1,0:T(8,128)}, f32[2,1,2,1,48,1152]{5,4,3,2,1,0:T(8,128)S(1)}, u32[]{:S(2)}, u32[]{:S(2)}) collective-permute-start(f32[2,1,2,1,48,1152]{5,4,3,2,1,0:T(8,128)} %get-tuple-element.280), channel_id=1, source_target_pairs={{0,8},{2,10},{4,12},{6,14},{8,0},{10,2},{12,4},{14,6},{16,24},{18,... | collective-permute-start | bytes 2654216 | tf_op jit(solution)/shard_map/ppermute | solution.py:945
  248.3 22.6 %collective-permute-start.34 = (f32[2,1,1,2,48,768]{5,4,3,2,1,0:T(8,128)}, f32[2,1,1,2,48,768]{5,4,3,2,1,0:T(8,128)S(1)}, u32[]{:S(2)}, u32[]{:S(2)}) collective-permute-start(f32[2,1,1,2,48,768]{5,4,3,2,1,0:T(8,128)} %get-tuple-element.279), channel_id=1, source_target_pairs={{0,1},{1,0},{2,3},{3,2},{4,5},{5,4},{6,7},{7,6},{8,9},{9,8},{10,11... | collective-permute-start | bytes 1769480 | tf_op jit(solution)/shard_map/ppermute | solution.py:948
  248.9 21.9 %collective-permute-start.36 = (f32[128,768]{1,0:T(8,128)}, f32[128,768]{1,0:T(8,128)S(1)}, u32[]{:S(2)}, u32[]{:S(2)}) collective-permute-start(f32[128,768]{1,0:T(8,128)} %get-tuple-element.320), channel_id=1, source_target_pairs={{0,1},{1,0},{2,3},{3,2},{4,5},{5,4},{6,7},{7,6},{8,9},{9,8},{10,11... | collective-permute-start | bytes 1179656 | tf_op jit(solution)/shard_map/ppermute | solution.py:948
  278.5 33.6 %collective-permute-start.40 = (f32[448,768]{1,0:T(8,128)}, f32[448,768]{1,0:T(8,128)}, u32[]{:S(2)}, u32[]{:S(2)}) collective-permute-start(f32[448,768]{1,0:T(8,128)} %get-tuple-element.322), channel_id=1, source_target_pairs={{0,1},{1,0},{2,3},{3,2},{4,5},{5,4},{6,7},{7,6},{8,9},{9,8},{10,11... | collective-permute-start | bytes 4128776 | tf_op jit(solution)/shard_map/ppermute | solution.py:948
  279.1 32.9 %collective-permute-start.37 = (f32[1,1,1,2,48,1920]{5,4,3,2,1,0:T(8,128)}, f32[1,1,1,2,48,1920]{5,4,3,2,1,0:T(8,128)}, u32[]{:S(2)}, u32[]{:S(2)}) collective-permute-start(f32[1,1,1,2,48,1920]{5,4,3,2,1,0:T(8,128)} %combine.14), channel_id=1, source_target_pairs={{0,16},{2,18},{4,20},{6,22},{8,24},{10,26},{12,28},{14,30},{16,0},... | collective-permute-start | bytes 2211848 | tf_op jit(solution)/shard_map/ppermute | solution.py:945
  281.7 24.3 %collective-permute-start.38 = (f32[2,1,1,1,48,1280]{5,4,3,2,1,0:T(8,128)}, f32[2,1,1,1,48,1280]{5,4,3,2,1,0:T(8,128)S(1)}, u32[]{:S(2)}, u32[]{:S(2)}) collective-permute-start(f32[2,1,1,1,48,1280]{5,4,3,2,1,0:T(8,128)} %get-tuple-element.297), channel_id=1, source_target_pairs={{0,8},{2,10},{4,12},{6,14},{8,0},{10,2},{12,4},{14,6},{16,24},{18,... | collective-permute-start | bytes 1474568 | tf_op jit(solution)/shard_map/ppermute | solution.py:945
  320.1 24.0 %collective-permute-start.41 = (f32[1,1,1,1,48,2432]{5,4,3,2,1,0:T(8,128)S(1)}, f32[1,1,1,1,48,2432]{5,4,3,2,1,0:T(8,128)S(1)}, u32[]{:S(2)}, u32[]{:S(2)}) collective-permute-start(f32[1,1,1,1,48,2432]{5,4,3,2,1,0:T(8,128)S(1)} %copy-done.16), channel_id=1, source_target_pairs={{0,16},{2,18},{4,20},{6,22},{8,24},{10,26},{12,28},{14,30},{16,0},... | collective-permute-start | bytes 1400840 | tf_op jit(solution)/shard_map/ppermute | solution.py:945
  320.2 26.4 %collective-permute-start.42 = (f32[352,768]{1,0:T(8,128)}, f32[352,768]{1,0:T(8,128)S(1)}, u32[]{:S(2)}, u32[]{:S(2)}) collective-permute-start(f32[352,768]{1,0:T(8,128)} %get-tuple-element.317), channel_id=1, source_target_pairs={{0,1},{1,0},{2,3},{3,2},{4,5},{5,4},{6,7},{7,6},{8,9},{9,8},{10,11... | collective-permute-start | bytes 3244040 | tf_op jit(solution)/shard_map/ppermute | solution.py:948
  (56 other events, 606.9 us)

commit v5 on v4

--- a/solution.py
+++ b/solution.py
@@ -273,8 +273,14 @@
         pieces = jnp.concatenate([piece.astype(BF16) for piece in three_pieces(sums)], axis=0)
         picked = mm(pick_ref[...], pieces, NT)
         biases = picked[:, :6] + picked[:, 8:14] + picked[:, 16:22]
+        seen = columns_ref.shape[1] // 2
+        rest_zero = jnp.zeros((model, 128 - 6 - seen), F32)
         extra = jnp.concatenate(
-            [biases, columns_ref[...], jnp.zeros((model, 128 - 6 - columns_ref.shape[1]), F32)], axis=1
+            [
+                biases, columns_ref[:, :seen], rest_zero,
+                jnp.zeros((model, 6), F32), columns_ref[:, seen:], rest_zero,
+            ],
+            axis=1,
         )
         lower = y_ref[1] % 2 == 0
 
@@ -299,8 +305,8 @@
             lax.fori_loop(0, 3, one, 0)
             wide = 3 * width
             if array:
-                place(array, slice(wide, wide + 128), extra)
-                wide += 128
+                place(array, slice(wide, wide + 256), extra)
+                wide += 256
             if group is None:
                 leave(grads_ref.at[array, :, :wide], grads_hbm[array])
             else:
@@ -322,7 +328,7 @@
     part = pl.BlockSpec((half, 2 * HD), lambda p, h, *_: (0, p))
     anywhere = pl.BlockSpec(memory_space=pl.ANY)
     shapes = [struct((rows, model), F32) for rows in chunks]
-    for wide in (3 * width, 3 * width + 128):
+    for wide in (3 * width, 3 * width + 256):
         shapes += [struct((model, wide), F32)] if group is None else [struct((model // 2, wide), F32)] * 2
     return pl.pallas_call(
         functools.partial(attend_back_kernel, len(chunks), group),
@@ -345,7 +351,7 @@
                 pltpu.VMEM((model, length), BF16),
                 pltpu.VMEM((half, model), F32),
                 pltpu.VMEM((length, model), F32),
-                pltpu.VMEM((2, model, 3 * width + 128), F32),
+                pltpu.VMEM((2, model, 3 * width + 256), F32),
                 pltpu.SemaphoreType.DMA((8,)),
                 pltpu.SemaphoreType.DMA((len(shapes),)),
             ],
@@ -1024,7 +1030,8 @@
         far_early, far_late,
     )
     inner_columns = inner_sums[:4].reshape(2, model, 2)
-    columns = jnp.concatenate([first_sums[:3].T, late_sums[:3].T, inner_columns[0], inner_columns[1]], axis=1)
+    shared = [first_sums[:3].T, late_sums[:3].T]
+    columns = jnp.concatenate([*shared, inner_columns[0], *shared, inner_columns[1]], axis=1)
     early_got, got_first, late_send, dcf, columns = tie((early_got, got_first, late_send, dcf, columns))
     late_got = swap(late_send, 1)
     d_got = cross(dcf)
@@ -1061,7 +1068,7 @@
     g1_got = cross(g1_send)
 
     g0_send, g1_send, g2_send, dco, d_got = tie((g0_send, g1_send, g2_send, dco, d_got))
-    chunks = tuple(length * k // 32 for k in (3, 4, 14, 11))
+    chunks = tuple(length * k // 32 for k in (3, 4, 16, 9))
     group = rows if rows % 8 == 0 else None
     results = attend_back(
         at, q2, extra, k2, v, context, dco, d_got, live, kind, columns, pick,
@@ -1125,10 +1132,12 @@
     g2_got = swap(g2_send, near_mask)
     g0_got = cross(sends[0])
     g1_got = swap(sends[1], near_mask)
-    (e_send,) = combine(bit_values, [[other(e, far_mask)]])
+    e_send, c_send = combine(bit_values, [[other(e, far_mask)], [other(c, near_mask)]])
     e_got = swap(e_send, far_mask)
     part0 = cross(parts[0])
-    g0_got, g1_got, g2_got, e_got, part0, parts = tie((g0_got, g1_got, g2_got, e_got, part0, parts))
+    g0_got, g1_got, g2_got, e_got, part0, parts, c_send = tie(
+        (g0_got, g1_got, g2_got, e_got, part0, parts, c_send)
+    )
     t = [
         *on_core(columns_of(g0, 2 * ca, 2 * ca + width), 0),
         *on_core([part_of(g0_got, ca, ca + width)], 1),
@@ -1139,13 +1148,21 @@
     e = [*kept(e, far_mask), whole_of(e_got)]
 
     (three_send,) = combine(bit_values, [[other(terms, far_mask) for terms in (g0, t, g1)]])
-    sends = combine(bit_values, [[columns_of(g2, cb, 2 * cb)], [other(c, near_mask)]])
-    sends, parts = tie((sends, parts))
+    sends = combine(
+        bit_values, [[columns_of(g2, cb, 2 * cb)], [columns_of(e, 3 * width + 128, 3 * width + 256)]]
+    )
     three_got = swap(three_send, far_mask)
     g2_got = cross(sends[0])
-    c_got = swap(sends[1], near_mask)
-    part1 = cross(parts[1])
-    three_got, g2_got, c_got, part1, parts = tie((three_got, g2_got, c_got, part1, parts))
+    small_got = cross(sends[1])
+    c_got = swap(c_send, near_mask)
+    in1 = (parts[1] + cross(parts[1])).astype(BF16)
+    in1, own0, part0 = tie((in1, parts[0], part0))
+    in0 = (own0 + part0).astype(BF16)
+    three_got, g2_got, c_got, small_got, in0, in1, parts = tie(
+        (three_got, g2_got, c_got, small_got, in0, in1, parts)
+    )
+    small = [*columns_of(e, 3 * width, 3 * width + 128), whole_of(small_got)]
+    e = columns_of(e, 0, 3 * width)
     g0 = [*kept(g0, far_mask), part_of(three_got, 0, ca)]
     t = [*kept(t, far_mask), part_of(three_got, ca, ca + width)]
     g1 = [*kept(g1, far_mask), part_of(three_got, ca + width, three_got.shape[-1])]
@@ -1157,17 +1174,17 @@
     ends = [sum(sizes[:k]) for k in range(len(sizes) + 1)]
     mask = rest_masks[0]
     (main_send,) = combine(bit_values, [[other(terms, mask) for terms in main]])
-    main_send, late_bits = tie((main_send, bit_values))
-    sends = combine(late_bits, [[other(e, near_mask)], [other(c, far_mask)]])
-    sends, parts = tie((sends, parts))
+    _, late_bits = tie((main_send, bit_values))
+    sends = combine(late_bits, [[other(e, near_mask), other(small, near_mask)], [other(c, far_mask)]])
     got_z = swap(main_send, mask)
-    part2 = cross(parts[2])
+    in2 = (parts[2] + cross(parts[2])).astype(BF16)
     c_got = swap(sends[1], far_mask)
     e_got = swap(sends[0], near_mask)
     layer_out = place_rows(at, out_rows, got_first, got_out)
-    got_z, e_got, c_got, part2, parts, layer_out = tie((got_z, e_got, c_got, part2, parts, layer_out))
+    got_z, e_got, c_got, in2, parts, layer_out = tie((got_z, e_got, c_got, in2, parts, layer_out))
     main = [[*kept(terms, mask), part_of(got_z, ends[n], ends[n + 1])] for n, terms in enumerate(main)]
-    e = [*kept(e, near_mask), whole_of(e_got)]
+    e = [*kept(e, near_mask), part_of(e_got, 0, 3 * width)]
+    small = [*kept(small, near_mask), part_of(e_got, 3 * width, 3 * width + 128)]
     c = [*kept(c, far_mask), whole_of(c_got)]
     for mask in rest_masks[1:]:
         (send,) = combine(bit_values, [[other(terms, mask) for terms in main]])
@@ -1175,23 +1192,25 @@
         main = [[*kept(terms, mask), part_of(got_z, ends[n], ends[n + 1])] for n, terms in enumerate(main)]
 
     for k, mask in enumerate(rest_masks):
-        (pair_send,) = combine(bit_values, [[other(c, mask), other(e, mask)]])
-        outputs = [[kept(c, mask), kept(e, mask)]]
+        (pair_send,) = combine(bit_values, [[other(c, mask), other(e, mask), other(small, mask)]])
+        outputs = [[kept(c, mask), kept(e, mask), kept(small, mask)]]
         if k == 0:
             outputs += [[other(terms, 1) for terms in main], [kept(terms, 1) for terms in main]]
-        sends = combine(bit_values, outputs)
-        if k == 0:
-            sends, parts = tie((sends, parts))
+        _, late_bits = tie((pair_send, bit_values))
+        sends = combine(late_bits, outputs)
         pair_got = swap(pair_send, mask)
         if k == 0:
-            part3 = cross(parts[3])
+            in3 = (parts[3] + cross(parts[3])).astype(BF16)
             got_last = swap(sends[1], 1)
             keep = sends[2]
         pair_keep = sends[0]
         wide = pair_keep.shape[-1]
         c = [part_of(pair_keep, 0, 3 * width), part_of(pair_got, 0, 3 * width)]
-        e = [part_of(pair_keep, 3 * width, wide), part_of(pair_got, 3 * width, wide)]
-
+        e = [part_of(pair_keep, 3 * width, 6 * width), part_of(pair_got, 3 * width, 6 * width)]
+        small = [part_of(pair_keep, 6 * width, wide), part_of(pair_got, 6 * width, wide)]
+
+    input_grad = jnp.concatenate([in0, in1, in2, in3], axis=0)
+    got_last, keep, input_grad = tie((got_last, keep, input_grad))
     got_last = got_last.reshape(rows, -1)
     keep = keep.reshape(rows, -1)
     low_half = jnp.where(core == 0, keep, got_last)
@@ -1204,16 +1223,11 @@
     grad_inner = jnp.concatenate(inner_half(low_half) + inner_half(high_half), axis=1)
     grad_outer = jnp.concatenate(outer_half(low_half) + outer_half(high_half), axis=1).T
     grad_output = t.T
-    sent_parts = (part0, part1, part2)
-    input_first = jnp.concatenate([(a + b).astype(BF16) for a, b in zip(parts, sent_parts)], axis=0)
-    pair_got, part3, input_first = tie((pair_got, part3, input_first))
+    pair_got, grad_inner, grad_outer, grad_output = tie((pair_got, grad_inner, grad_outer, grad_output))
     pair = (pair_keep + pair_got).reshape(rows, -1)
     c, e = pair[:, : 3 * width], pair[:, 3 * width :]
-    last = e[:, 3 * width + 6 : 3 * width + 16]
-    last_got = cross(last)
-    small = last[:, :6] + last_got[:, :6]
-    inner_two = last[:, 6:8] + last_got[:, 8:]
-    input_grad = jnp.concatenate([input_first, (parts[3] + part3).astype(BF16)], axis=0)
+    small = e[:, 3 * width + 6 : 3 * width + 12]
+    inner_two = e[:, 3 * width + 12 : 3 * width + 14]
 
     piece = lambda array, k: array[:, width * k : width * (k + 1)]
     grad_query_weight = jnp.stack([piece(c, 0), piece(c, 1), piece(c, 2), piece(e, 0)])

time: 356 us -> 336 us (0.944)
  waiting for transfers between devices: 129 us -> 106 us
  other arithmetic: 14.4 us -> 20.2 us
    ppermute x29, waiting for transfers between devices: 69 us -> 32.6 us  [swap(): return lax.ppermute(value, 'dp', [(i, i ^ mask) for i in range(devices)])]
    ppermute x16, waiting for transfers between devices: 60.3 us -> 73.7 us  [cross(): return lax.ppermute(value, 'tensor', [(0, 1), (1, 0)])]
    convert_element_type x4, other arithmetic: 2.08 us -> 7.11 us  [the longest x1 2.03 us: per_device(): in2 = (parts[2] + cross(parts[2])).astype(BF16)]
  transfers between devices with their start and end apart: 45 -> 45, of which waited for: 20 -> 20; matrix products, arithmetic and copies ran while one was open for 6% -> 7% of each run, Pallas kernels for 33% -> 40%
where the time goes in v5:
time: 336 us; the launch traced here: 335 us
  Pallas kernels  155 us (46%)
  waiting for transfers between devices  106 us (32%)
  starting transfers between devices  39 us (12%)
  other arithmetic  20.2 us (6%)
  local copies, waits for them, and re-layouts  12.4 us (4%)
    ppermute x16, waiting for transfers between devices, cross(): return lax.ppermute(value, 'tensor', [(0, 1), (1, 0)])  73.7 us
    pallas_call x1, Pallas kernels, attend_back(): pl.pallas_call(functools.partial(attend_back_kernel, len(chunks), group),...  35.5 us
    ppermute x29, waiting for transfers between devices, swap(): return lax.ppermute(value, 'dp', [(i, i ^ mask) for i in range(devices)])  32.6 us
    pallas_call x9, Pallas kernels, combine(): pl.pallas_call(functools.partial(combine_kernel, plan, len(arrays)), grid...  31.9 us
    ppermute x29, starting transfers between devices, swap(): return lax.ppermute(value, 'dp', [(i, i ^ mask) for i in range(devices)])  22.8 us
    pallas_call x1, Pallas kernels, forward(): pl.pallas_call(forward_kernel, grid_spec=pltpu.PrefetchScalarGridSpec(num...  21.2 us
    pallas_call x2, Pallas kernels, weight_grads(): pl.pallas_call(functools.partial(weight_kernel, plan, len(received), len(...  17.1 us
    pallas_call x1, Pallas kernels, backward(): pl.pallas_call(backward_kernel, grid_spec=pltpu.PrefetchScalarGridSpec(nu...  16.6 us
  transfers between devices with their start and end apart: 45, of which 20 were waited for; matrix products, arithmetic and copies ran while one was open for 7% of the time, Pallas kernels for 40%

profile of v5, /device:TPU:0, one launch (start us, length us, event | category | flops | bytes accessed | tf_op | source)
XLA Modules:
  0.0 334.8 jit_solution(16328935108227454416)
XLA Ops:
  8.0 8.2 %project.1 = (bf16[1024,768]{1,0:T(8,128)(2,1)}, bf16[1024,768]{1,0:T(8,128)(2,1)}, bf16[1024,384]{1,0:T(8,128)(2,1)}) custom-call(bf16[1024,768]{1,0:T(8,128)(2,1)} %bitcast.74, f32[1024,1]{1,0:T(8,128)} %copy.46.kind_ref, bf16[4,768,384]{2,1,0:T(8,128)(2,1)} %wq_hbm.1, f32[4,384]{1,0:T(4,128)} %bq_ref.1, bf16[768,384]{1,0:T(8,128)(2,1)} %wk_hbm.1, ...), custom_call_target="tpu_custom_call" | custom-call | flops 3623878656 | bytes 9437184 | tf_op jit(solution)/shard_map/project/pallas_call | solution.py:87
  18.3 4.1 %collective-permute-done.1 = f32[1536]{0:T(1024)S(1)} collective-permute-done((f32[1536]{0:T(1024)S(1)}, f32[1536]{0:T(1024)S(1)}, u32[]{:S(2)}, u32[]{:S(2)}) %collective-permute-start.1) | collective-permute-done | bytes 6176 | tf_op jit(solution)/shard_map/ppermute | solution.py:954
  28.8 14.0 %attend.1 = (bf16[1024,384]{1,0:T(8,128)(2,1)}, bf16[1024,768]{1,0:T(8,128)(2,1)}) custom-call(bf16[1024,768]{1,0:T(8,128)(2,1)} %get-tuple-element.163.q2_ref, bf16[1024,768]{1,0:T(8,128)(2,1)} %get-tuple-element.164.k2_ref, bf16[1024,384]{1,0:T(8,128)(2,1)} %get-tuple-element.165.v_ref, f32[1024,1]{1,0:T(8,128)} %fusion.1.live_ref), custom_call_target="tpu_custom_call" | custom-call | flops 4026531840 | bytes 7864320 | tf_op jit(solution)/shard_map/attend/pallas_call | solution.py:154
  47.3 3.7 %turn.1.turned_hbm = bf16[768,1024]{1,0:T(8,128)(2,1)} custom-call(bf16[1024,768]{1,0:T(8,128)(2,1)} %bitcast.75), custom_call_target="tpu_custom_call" | custom-call | flops 786432 | bytes 3145728 | tf_op jit(solution)/shard_map/turn/pallas_call | solution.py:880
  52.7 7.9 %collective-permute-done.10.rest_12_ = f32[192,768]{1,0:T(8,128)} collective-permute-done((f32[192,768]{1,0:T(8,128)}, f32[192,768]{1,0:T(8,128)}, u32[]{:S(2)}, u32[]{:S(2)}) %collective-permute-start.10) | collective-permute-done | bytes 589856 | tf_op jit(solution)/shard_map/ppermute | solution.py:951
  62.8 15.5 %collective-permute-done.8.rest_14_ = f32[192,768]{1,0:T(8,128)} collective-permute-done((f32[192,768]{1,0:T(8,128)}, f32[192,768]{1,0:T(8,128)}, u32[]{:S(2)}, u32[]{:S(2)}) %collective-permute-start.8) | collective-permute-done | bytes 589856 | tf_op jit(solution)/shard_map/ppermute | solution.py:954
  85.5 21.2 %forward.1 = (bf16[512,768]{1,0:T(8,128)(2,1)}, f32[512,384]{1,0:T(8,128)}, f32[512,384]{1,0:T(8,128)}, bf16[512,768]{1,0:T(8,128)(2,1)}, bf16[512,768]{1,0:T(8,...) custom-call(s32[4]{0:T(128)} %pad_add_fusion.1.at_ref.bit_ref.y_ref,, ...), custom_call_target="tpu_custom_call" | custom-call | flops 4831838208 | bytes 28311552 | tf_op jit(solution)/shard_map/forward/pallas_call | solution.py:547
  107.4 16.6 %backward.1 = (f32[512,768]{1,0:T(8,128)}, f32[512,384]{1,0:T(8,128)}, f32[512,384]{1,0:T(8,128)}, bf16[512,768]{1,0:T(8,128)(2,1)}, bf16[512,1152]{1,0:T(8,128)...) custom-call(s32[4]{0:T(128)} %pad_add_fusion.1.at_ref.bit_ref.y_ref, ...), custom_call_target="tpu_custom_call" | custom-call | flops 4831838208 | bytes 28311552 | tf_op jit(solution)/shard_map/backward/pallas_call | solution.py:663
  127.6 8.2 %weight_grads.3 = (f32[384,1536]{1,0:T(8,128)}, f32[384,1536]{1,0:T(8,128)}) custom-call(s32[4]{0:T(128)} %pad_add_fusion.1.at_ref.bit_ref.y_ref, bf16[512,768]{1,0:T(8,128)(2,1)} %get-tuple-element.194.d_low_ref.rest_0_, bf16[512,1536]{1,0:T(8,128)(2,1)} %get-tuple-element.215.rest_1_, f32[512,3456]{1,0:T(8,128)} %collective-permute-done.18.rest_4_.rest_2_), custom_call_target="tpu_custom_call" | custom-call | flops 2415919104 | bytes 11010048 | tf_op jit(solution)/shard_map/weight_grads/pallas_call | solution.py:769
  137.1 8.9 %weight_grads.2 = (f32[384,1152]{1,0:T(8,128)}, f32[384,1152]{1,0:T(8,128)}, f32[768,384]{1,0:T(8,128)}, f32[768,384]{1,0:T(8,128)}) custom-call(s32[4]{0:T(128)} %pad_add_fusion.1.at_ref.bit_ref.y_ref, bf16[512,768]{1,0:T(8,128)(2,1)} %get-tuple-element.189.rest_0_, bf16[512,768]{1,0:T(8,128)(2,1)} %get-tuple-element.197.rest_1_, ...), custom_call_target="tpu_custom_call" | custom-call | flops 3019898880 | bytes 13762560 | tf_op jit(solution)/shard_map/weight_grads/pallas_call | solution.py:769
  151.5 35.5 %attend_back.1 = (f32[96,768]{1,0:T(8,128)}, f32[128,768]{1,0:T(8,128)}, f32[512,768]{1,0:T(8,128)}, f32[288,768]{1,0:T(8,128)}, f32[384,1152]{1,0:T(8,128)}, /*...) custom-call(s32[4]{0:T(128)} %pad_add_fusion.1.at_ref.bit_ref.y_ref, ...), custom_call_target="tpu_custom_call" | custom-call | flops 8053063680 | bytes 15728640 | tf_op jit(solution)/shard_map/attend_back/pallas_call | solution.py:333
  186.9 5.9 %collective-permute-done.25.second_ref = f32[512,384]{1,0:T(8,128)S(1)} collective-permute-done((f32[512,384]{1,0:T(8,128)}, f32[512,384]{1,0:T(8,128)S(1)}, u32[]{:S(2)}, u32[]{:S(2)}) %collective-permute-start.25) | collective-permute-done | bytes 786464 | tf_op jit(solution)/shard_map/ppermute | solution.py:954
  194.0 3.4 %combine.10 = f32[2,1,1,2,48,1536]{5,4,3,2,1,0:T(8,128)} custom-call(s32[4]{0:T(128)} %pad_add_fusion.bits_ref, f32[2,2,1,2,48,1536]{5,4,3,2,1,0:T(8,128)} %bitcast.58, f32[2,2,1,2,48,1536]{5,4,3,2,1,0:T(8,128)} %bitcast.21.rest_1_.rest_8_.rest_18_), custom_call_target="tpu_custom_call" | custom-call | flops 2359296 | bytes 4718592 | tf_op jit(solution)/shard_map/combine/pallas_call | solution.py:854
  198.3 3.7 %combine.9 = (f32[2,1,2,2,48,768]{5,4,3,2,1,0:T(8,128)}, f32[2,1,2,2,48,384]{5,4,3,2,1,0:T(8,128)}) custom-call(s32[4]{0:T(128)} %pad_add_fusion.bits_ref, f32[2,1,2,2,48,1152]{5,4,3,2,1,0:T(8,128)} %bitcast.66, f32[2,1,2,2,48,1152]{5,4,3,2,1,0:T(8,128)} %bitcast.15.rest_1_.rest_10_, f32[2,2,2,2,48,384]{5,4,3,2,1,0:T(8,128)} %bitcast.70, ...), custom_call_target="tpu_custom_call" | custom-call | flops 3538944 | bytes 7077888 | tf_op jit(solution)/shard_map/combine/pallas_call | solution.py:854
  202.7 3.9 %combine.11 = (f32[2,2,1,1,48,1408]{5,4,3,2,1,0:T(8,128)}, f32[2,1,2,1,48,1152]{5,4,3,2,1,0:T(8,128)}) custom-call(s32[4]{0:T(128)} %pad_add_fusion.bits_ref, f32[2,2,2,1,48,1408]{5,4,3,2,1,0:T(8,128)} %bitcast.53, f32[2,2,2,1,48,1408]{5,4,3,2,1,0:T(8,128)} %collective-permute-done.26.rest_1_.rest_4_.rest_5_, f32[2,2,2,1,48,1152]{5,4,3,2,1,0:T(8,128)} %bitcast.62, ...), custom_call_target="tpu_custom_call" | custom-call | flops 3932160 | bytes 7864320 | tf_op jit(solution)/shard_map/combine/pallas_call | solution.py:854
  210.9 15.8 %collective-permute-done.30.rest_2_.rest_9_.rest_19_ = f32[2,1,1,2,48,1536]{5,4,3,2,1,0:T(8,128)} collective-permute-done((f32[2,1,1,2,48,1536]{5,4,3,2,1,0:T(8,128)}, f32[2,1,1,2,48,1536]{5,4,3,2,1,0:T(8,128)}, u32[]{:S(2)}, u32[]{:S(2)}) %collective-permute-start.30) | collective-permute-done | bytes 1179680 | tf_op jit(solution)/shard_map/ppermute | solution.py:951
  226.7 9.6 %collective-permute-done.32 = f32[96,768]{1,0:T(8,128)S(1)} collective-permute-done((f32[96,768]{1,0:T(8,128)S(1)}, f32[96,768]{1,0:T(8,128)S(1)}, u32[]{:S(2)}, u32[]{:S(2)}) %collective-permute-start.32) | collective-permute-done | bytes 294944 | tf_op jit(solution)/shard_map/ppermute | solution.py:954
  253.1 10.6 %collective-permute-done.36.rest_3_.rest_8_ = f32[2,2,1,1,48,128]{5,4,3,2,1,0:T(8,128)S(1)} collective-permute-done((f32[2,2,1,1,48,128]{5,4,3,2,1,0:T(8,128)}, f32[2,2,1,1,48,128]{5,4,3,2,1,0:T(8,128)S(1)}, u32[]{:S(2)}, u32[]{:S(2)}) %collective-permute-start.36) | collective-permute-done | bytes 98336 | tf_op jit(solution)/shard_map/ppermute | solution.py:954
  265.7 3.4 %combine.14 = f32[1,1,1,2,48,1920]{5,4,3,2,1,0:T(8,128)} custom-call(s32[4]{0:T(128)} %pad_add_fusion.bits_ref, f32[2,1,2,2,48,1152]{5,4,3,2,1,0:T(8,128)} %bitcast.68, f32[2,1,2,2,48,1152]{5,4,3,2,1,0:T(8,128)} %bitcast.15.rest_1_.rest_10_, f32[2,1,2,2,48,768]{5,4,3,2,1,0:T(8,128)} %collective-permute-done.28.rest_2_.rest_11_, ...), custom_call_target="tpu_custom_call" | custom-call | flops 2949120 | bytes 5898240 | tf_op jit(solution)/shard_map/combine/pallas_call | solution.py:854
  271.7 3.3 combine.15
  277.2 6.8 %place_rows.1 = bf16[1024,768]{1,0:T(8,128)(2,1)} custom-call(s32[4]{0:T(128)} %pad_add_fusion.1.at_ref.bit_ref.y_ref, bf16[512,768]{1,0:T(8,128)(2,1)} %get-tuple-element.284.own_ref, f32[512,384]{1,0:T(8,128)} %copy-done.5, f32[512,384]{1,0:T(8,128)} %copy-done.6), custom_call_target="tpu_custom_call" | custom-call | flops 393216 | bytes 4718592 | tf_op jit(solution)/shard_map/place_rows/pallas_call | solution.py:903
  284.0 15.4 %collective-permute-done.41 = f32[512,768]{1,0:T(8,128)} collective-permute-done((f32[512,768]{1,0:T(8,128)}, f32[512,768]{1,0:T(8,128)}, u32[]{:S(2)}, u32[]{:S(2)}) %collective-permute-start.41) | collective-permute-done | bytes 1572896 | tf_op jit(solution)/shard_map/ppermute | solution.py:954
  308.0 4.8 %combine.17 = (f32[1,1,1,1,48,2432]{5,4,3,2,1,0:T(8,128)}, f32[1,1,1,1,48,1920]{5,4,3,2,1,0:T(8,128)}, f32[1,1,1,1,48,1920]{5,4,3,2,1,0:T(8,128)}) custom-call(s32[4]{0:T(128)} %pad_add_fusion.bits_ref, f32[2,2,2,1,48,1152]{5,4,3,2,1,0:T(8,128)} %bitcast.65, f32[2,2,2,1,48,1152]{5,4,3,2,1,0:T(8,128)} %collective-permute-done.27.rest_3_.rest_5_.rest_1_, ...), custom_call_target="tpu_custom_call" | custom-call | flops 5578752 | bytes 11157504 | tf_op jit(solution)/shard_map/combine/pallas_call | solution.py:854
  312.9 10.4 %collective-permute-done.43 = f32[288,768]{1,0:T(8,128)} collective-permute-done((f32[288,768]{1,0:T(8,128)}, f32[288,768]{1,0:T(8,128)}, u32[]{:S(2)}, u32[]{:S(2)}) %collective-permute-start.43) | collective-permute-done | bytes 884768 | tf_op jit(solution)/shard_map/ppermute | solution.py:954
  (197 shorter events, 91.9 us)
Async XLA Ops:
  22.4 22.4 %collective-permute-start.4 = (f32[240,768]{1,0:T(8,128)}, f32[240,768]{1,0:T(8,128)S(1)}, u32[]{:S(2)}, u32[]{:S(2)}) collective-permute-start(f32[240,768]{1,0:T(8,128)} %collective-permute-done.rest_0_), channel_id=1, source_target_pairs={{0,8},{2,10},{4,12},{6,14},{8,0},{10,2},{12,4},{14,6},{16,24},{18,... | collective-permute-start | bytes 2211848 | tf_op jit(solution)/shard_map/ppermute | solution.py:951
  24.2 20.6 %collective-permute-start.3 = (f32[240,768]{1,0:T(8,128)}, f32[240,768]{1,0:T(8,128)}, u32[]{:S(2)}, u32[]{:S(2)}) collective-permute-start(f32[240,768]{1,0:T(8,128)} %collective-permute-done.rest_0_), channel_id=1, source_target_pairs={{0,4},{2,6},{4,0},{6,2},{8,12},{10,14},{12,8},{14,10},{16,20},{18,... | collective-permute-start | bytes 2211848 | tf_op jit(solution)/shard_map/ppermute | solution.py:951
  45.9 32.4 %collective-permute-start.6 = (f32[512,384]{1,0:T(8,128)}, f32[512,384]{1,0:T(8,128)S(1)}, u32[]{:S(2)}, u32[]{:S(2)}) collective-permute-start(f32[512,384]{1,0:T(8,128)} %dynamic-slice_convert_fusion), channel_id=1, source_target_pairs={{0,1},{1,0},{2,3},{3,2},{4,5},{5,4},{6,7},{7,6},{8,9},{9,8},{10,11... | collective-permute-start | bytes 2359304 | tf_op jit(solution)/shard_map/ppermute | solution.py:954
  51.0 27.3 %collective-permute-start.7 = (f32[240,768]{1,0:T(8,128)}, f32[240,768]{1,0:T(8,128)S(1)}, u32[]{:S(2)}, u32[]{:S(2)}) collective-permute-start(f32[240,768]{1,0:T(8,128)} %copy-done.8), channel_id=1, source_target_pairs={{0,4},{2,6},{4,0},{6,2},{8,12},{10,14},{12,8},{14,10},{16,20},{18,... | collective-permute-start | bytes 2211848 | tf_op jit(solution)/shard_map/ppermute | solution.py:951
  106.7 20.2 %collective-permute-start.18 = (f32[512,3456]{1,0:T(8,128)}, f32[512,3456]{1,0:T(8,128)}, u32[]{:S(2)}, u32[]{:S(2)}) collective-permute-start(f32[512,3456]{1,0:T(8,128)} %get-tuple-element.200), channel_id=1, source_target_pairs={{0,2},{2,0},{4,6},{6,4},{8,10},{10,8},{12,14},{14,12},{16,18},{18,... | collective-permute-start | bytes 21233672 | tf_op jit(solution)/shard_map/ppermute | solution.py:951
  106.9 20.0 %collective-permute-start.19 = (f32[512,384]{1,0:T(8,128)}, f32[512,384]{1,0:T(8,128)S(1)}, u32[]{:S(2)}, u32[]{:S(2)}) collective-permute-start(f32[512,384]{1,0:T(8,128)} %get-tuple-element.201), channel_id=1, source_target_pairs={{0,1},{1,0},{2,3},{3,2},{4,5},{5,4},{6,7},{7,6},{8,9},{9,8},{10,11... | collective-permute-start | bytes 2359304 | tf_op jit(solution)/shard_map/ppermute | solution.py:954
  127.0 20.3 %collective-permute-start.21 = (f32[512,384]{1,0:T(8,128)}, f32[512,384]{1,0:T(8,128)}, u32[]{:S(2)}, u32[]{:S(2)}) collective-permute-start(f32[512,384]{1,0:T(8,128)} %get-tuple-element.212), channel_id=1, source_target_pairs={{0,1},{1,0},{2,3},{3,2},{4,5},{5,4},{6,7},{7,6},{8,9},{9,8},{10,11... | collective-permute-start | bytes 2359304 | tf_op jit(solution)/shard_map/ppermute | solution.py:954
  135.9 57.0 %collective-permute-start.24 = (f32[384,1536]{1,0:T(8,128)}, f32[384,1536]{1,0:T(8,128)}, u32[]{:S(2)}, u32[]{:S(2)}) collective-permute-start(f32[384,1536]{1,0:T(8,128)} %get-tuple-element.216), channel_id=1, source_target_pairs={{0,4},{2,6},{4,0},{6,2},{8,12},{10,14},{12,8},{14,10},{16,20},{18,... | collective-permute-start | bytes 7077896 | tf_op jit(solution)/shard_map/ppermute | solution.py:951
  147.2 45.6 %collective-permute-start.22 = (f32[384,1152]{1,0:T(8,128)}, f32[384,1152]{1,0:T(8,128)}, u32[]{:S(2)}, u32[]{:S(2)}) collective-permute-start(f32[384,1152]{1,0:T(8,128)} %get-tuple-element.213), channel_id=1, source_target_pairs={{0,8},{2,10},{4,12},{6,14},{8,0},{10,2},{12,4},{14,6},{16,24},{18,... | collective-permute-start | bytes 5308424 | tf_op jit(solution)/shard_map/ppermute | solution.py:951
  148.5 44.3 %collective-permute-start.23 = (f32[768,384]{1,0:T(8,128)}, f32[768,384]{1,0:T(8,128)}, u32[]{:S(2)}, u32[]{:S(2)}) collective-permute-start(f32[768,384]{1,0:T(8,128)} %get-tuple-element.214), channel_id=1, source_target_pairs={{0,1},{1,0},{2,3},{3,2},{4,5},{5,4},{6,7},{7,6},{8,9},{9,8},{10,11... | collective-permute-start | bytes 3538952 | tf_op jit(solution)/shard_map/ppermute | solution.py:954
  149.1 43.7 %collective-permute-start.25 = (f32[512,384]{1,0:T(8,128)}, f32[512,384]{1,0:T(8,128)S(1)}, u32[]{:S(2)}, u32[]{:S(2)}) collective-permute-start(f32[512,384]{1,0:T(8,128)} %get-tuple-element.217), channel_id=1, source_target_pairs={{0,1},{1,0},{2,3},{3,2},{4,5},{5,4},{6,7},{7,6},{8,9},{9,8},{10,11... | collective-permute-start | bytes 2359304 | tf_op jit(solution)/shard_map/ppermute | solution.py:954
  197.5 29.2 %collective-permute-start.30 = (f32[2,1,1,2,48,1536]{5,4,3,2,1,0:T(8,128)}, f32[2,1,1,2,48,1536]{5,4,3,2,1,0:T(8,128)}, u32[]{:S(2)}, u32[]{:S(2)}) collective-permute-start(f32[2,1,1,2,48,1536]{5,4,3,2,1,0:T(8,128)} %combine.10), channel_id=1, source_target_pairs={{0,8},{2,10},{4,12},{6,14},{8,0},{10,2},{12,4},{14,6},{16,24},{18,... | collective-permute-start | bytes 3538952 | tf_op jit(solution)/shard_map/ppermute | solution.py:951
  202.0 36.4 %collective-permute-start.28 = (f32[2,1,2,2,48,768]{5,4,3,2,1,0:T(8,128)}, f32[2,1,2,2,48,768]{5,4,3,2,1,0:T(8,128)}, u32[]{:S(2)}, u32[]{:S(2)}) collective-permute-start(f32[2,1,2,2,48,768]{5,4,3,2,1,0:T(8,128)} %get-tuple-element.246), channel_id=1, source_target_pairs={{0,1},{1,0},{2,3},{3,2},{4,5},{5,4},{6,7},{7,6},{8,9},{9,8},{10,11... | collective-permute-start | bytes 3538952 | tf_op jit(solution)/shard_map/ppermute | solution.py:954
  206.6 31.7 %collective-permute-start.31 = (f32[2,2,1,1,48,1408]{5,4,3,2,1,0:T(8,128)}, f32[2,2,1,1,48,1408]{5,4,3,2,1,0:T(8,128)}, u32[]{:S(2)}, u32[]{:S(2)}) collective-permute-start(f32[2,2,1,1,48,1408]{5,4,3,2,1,0:T(8,128)} %get-tuple-element.254), channel_id=1, source_target_pairs={{0,4},{2,6},{4,0},{6,2},{8,12},{10,14},{12,8},{14,10},{16,20},{18,... | collective-permute-start | bytes 3244040 | tf_op jit(solution)/shard_map/ppermute | solution.py:951
  207.9 30.5 %collective-permute-start.29 = (f32[2,1,2,2,48,384]{5,4,3,2,1,0:T(8,128)}, f32[2,1,2,2,48,384]{5,4,3,2,1,0:T(8,128)S(1)}, u32[]{:S(2)}, u32[]{:S(2)}) collective-permute-start(f32[2,1,2,2,48,384]{5,4,3,2,1,0:T(8,128)} %get-tuple-element.247), channel_id=1, source_target_pairs={{0,8},{2,10},{4,12},{6,14},{8,0},{10,2},{12,4},{14,6},{16,24},{18,... | collective-permute-start | bytes 1769480 | tf_op jit(solution)/shard_map/ppermute | solution.py:951
  209.5 26.8 %collective-permute-start.32 = (f32[96,768]{1,0:T(8,128)S(1)}, f32[96,768]{1,0:T(8,128)S(1)}, u32[]{:S(2)}, u32[]{:S(2)}) collective-permute-start(f32[96,768]{1,0:T(8,128)S(1)} %copy-done.15), channel_id=1, source_target_pairs={{0,1},{1,0},{2,3},{3,2},{4,5},{5,4},{6,7},{7,6},{8,9},{9,8},{10,11... | collective-permute-start | bytes 884744 | tf_op jit(solution)/shard_map/ppermute | solution.py:954
  242.5 21.3 %collective-permute-start.33 = (f32[2,1,1,2,48,1152]{5,4,3,2,1,0:T(8,128)}, f32[2,1,1,2,48,1152]{5,4,3,2,1,0:T(8,128)}, u32[]{:S(2)}, u32[]{:S(2)}) collective-permute-start(f32[2,1,1,2,48,1152]{5,4,3,2,1,0:T(8,128)} %combine.12), channel_id=1, source_target_pairs={{0,4},{2,6},{4,0},{6,2},{8,12},{10,14},{12,8},{14,10},{16,20},{18,... | collective-permute-start | bytes 2654216 | tf_op jit(solution)/shard_map/ppermute | solution.py:951
  243.9 20.7 %collective-permute-start.35 = (f32[2,1,2,1,48,1152]{5,4,3,2,1,0:T(8,128)}, f32[2,1,2,1,48,1152]{5,4,3,2,1,0:T(8,128)S(1)}, u32[]{:S(2)}, u32[]{:S(2)}) collective-permute-start(f32[2,1,2,1,48,1152]{5,4,3,2,1,0:T(8,128)} %get-tuple-element.265), channel_id=1, source_target_pairs={{0,8},{2,10},{4,12},{6,14},{8,0},{10,2},{12,4},{14,6},{16,24},{18,... | collective-permute-start | bytes 2654216 | tf_op jit(solution)/shard_map/ppermute | solution.py:951
  264.7 34.8 %collective-permute-start.41 = (f32[512,768]{1,0:T(8,128)}, f32[512,768]{1,0:T(8,128)}, u32[]{:S(2)}, u32[]{:S(2)}) collective-permute-start(f32[512,768]{1,0:T(8,128)} %get-tuple-element.282), channel_id=1, source_target_pairs={{0,1},{1,0},{2,3},{3,2},{4,5},{5,4},{6,7},{7,6},{8,9},{9,8},{10,11... | collective-permute-start | bytes 4718600 | tf_op jit(solution)/shard_map/ppermute | solution.py:954
  269.1 33.1 %collective-permute-start.38 = (f32[1,1,1,2,48,1920]{5,4,3,2,1,0:T(8,128)}, f32[1,1,1,2,48,1920]{5,4,3,2,1,0:T(8,128)}, u32[]{:S(2)}, u32[]{:S(2)}) collective-permute-start(f32[1,1,1,2,48,1920]{5,4,3,2,1,0:T(8,128)} %combine.14), channel_id=1, source_target_pairs={{0,16},{2,18},{4,20},{6,22},{8,24},{10,26},{12,28},{14,30},{16,0},... | collective-permute-start | bytes 2211848 | tf_op jit(solution)/shard_map/ppermute | solution.py:951
  275.1 26.4 %collective-permute-start.39 = (f32[2,1,1,1,48,1280]{5,4,3,2,1,0:T(8,128)}, f32[2,1,1,1,48,1280]{5,4,3,2,1,0:T(8,128)}, u32[]{:S(2)}, u32[]{:S(2)}) collective-permute-start(f32[2,1,1,1,48,1280]{5,4,3,2,1,0:T(8,128)} %get-tuple-element.280), channel_id=1, source_target_pairs={{0,8},{2,10},{4,12},{6,14},{8,0},{10,2},{12,4},{14,6},{16,24},{18,... | collective-permute-start | bytes 1474568 | tf_op jit(solution)/shard_map/ppermute | solution.py:951
  276.7 24.8 %collective-permute-start.40 = (f32[2,1,1,1,48,1152]{5,4,3,2,1,0:T(8,128)}, f32[2,1,1,1,48,1152]{5,4,3,2,1,0:T(8,128)}, u32[]{:S(2)}, u32[]{:S(2)}) collective-permute-start(f32[2,1,1,1,48,1152]{5,4,3,2,1,0:T(8,128)} %get-tuple-element.281), channel_id=1, source_target_pairs={{0,4},{2,6},{4,0},{6,2},{8,12},{10,14},{12,8},{14,10},{16,20},{18,... | collective-permute-start | bytes 1327112 | tf_op jit(solution)/shard_map/ppermute | solution.py:951
  302.1 21.1 %collective-permute-start.43 = (f32[288,768]{1,0:T(8,128)}, f32[288,768]{1,0:T(8,128)}, u32[]{:S(2)}, u32[]{:S(2)}) collective-permute-start(f32[288,768]{1,0:T(8,128)} %get-tuple-element.297), channel_id=1, source_target_pairs={{0,1},{1,0},{2,3},{3,2},{4,5},{5,4},{6,7},{7,6},{8,9},{9,8},{10,11... | collective-permute-start | bytes 2654216 | tf_op jit(solution)/shard_map/ppermute | solution.py:954
  306.5 22.9 %collective-permute-start.44 = (f32[1,1,1,1,48,2432]{5,4,3,2,1,0:T(8,128)}, f32[1,1,1,1,48,2432]{5,4,3,2,1,0:T(8,128)}, u32[]{:S(2)}, u32[]{:S(2)}) collective-permute-start(f32[1,1,1,1,48,2432]{5,4,3,2,1,0:T(8,128)} %combine.16), channel_id=1, source_target_pairs={{0,16},{2,18},{4,20},{6,22},{8,24},{10,26},{12,28},{14,30},{16,0},... | collective-permute-start | bytes 1400840 | tf_op jit(solution)/shard_map/ppermute | solution.py:951
  (50 other events, 572.9 us)

commit v6 on v5

--- a/solution.py
+++ b/solution.py
@@ -1068,7 +1068,7 @@
     g1_got = cross(g1_send)
 
     g0_send, g1_send, g2_send, dco, d_got = tie((g0_send, g1_send, g2_send, dco, d_got))
-    chunks = tuple(length * k // 32 for k in (3, 4, 16, 9))
+    chunks = tuple(length * k // 32 for k in (7, 16, 9))
     group = rows if rows % 8 == 0 else None
     results = attend_back(
         at, q2, extra, k2, v, context, dco, d_got, live, kind, columns, pick,
@@ -1124,43 +1124,43 @@
     g0 = [term(g0_keep, near_mask), term(g0_got, near_mask)]
     g1 = [term(g1_keep), term(g1_got)]
     g2 = [term(g2_keep, far_mask), term(g2_got, far_mask)]
-    (g2_send,) = combine(bit_values, [[other(g2, near_mask)]])
     sends = combine(bit_values, [[columns_of(g0, ca, 2 * ca + width)], [other(g1, near_mask)]])
-    e_got, c_got, sends, parts = tie((e_got, c_got, sends, parts))
+    _, late_bits = tie((sends, bit_values))
+    (g2_send,) = combine(late_bits, [[other(g2, near_mask)]])
+    e_got, c_got, parts, _ = tie((e_got, c_got, parts, g2_send))
     e.append(whole_of(e_got))
     c.append(whole_of(c_got))
+    g1_got = swap(sends[1], near_mask)
+    g0_got = cross(sends[0])
     g2_got = swap(g2_send, near_mask)
-    g0_got = cross(sends[0])
-    g1_got = swap(sends[1], near_mask)
     e_send, c_send = combine(bit_values, [[other(e, far_mask)], [other(c, near_mask)]])
     e_got = swap(e_send, far_mask)
     part0 = cross(parts[0])
-    g0_got, g1_got, g2_got, e_got, part0, parts, c_send = tie(
-        (g0_got, g1_got, g2_got, e_got, part0, parts, c_send)
-    )
+    near_bit, near_axis = (d // near_mask) % 2, bits - near_mask.bit_length()
+    for array, *_ in g1:
+        g1_got = tie(g1_got + lax.dynamic_slice_in_dim(array, near_bit, 1, near_axis))
+    g0_got, g1_sum = tie((g0_got, g1_got))
     t = [
         *on_core(columns_of(g0, 2 * ca, 2 * ca + width), 0),
         *on_core([part_of(g0_got, ca, ca + width)], 1),
     ]
     g0 = [*columns_of(g0, 0, ca), part_of(g0_got, 0, ca)]
-    g1 = [*kept(g1, near_mask), whole_of(g1_got)]
+    g1 = [whole_of(g1_sum)]
+
+    (three_send,) = combine(bit_values, [[other(terms, far_mask) for terms in (g0, t, g1)]])
+    three_got = swap(three_send, far_mask)
+    g2_got, e_got, part0, parts, _ = tie((g2_got, e_got, part0, parts, three_send))
     g2 = [*kept(g2, near_mask), whole_of(g2_got)]
     e = [*kept(e, far_mask), whole_of(e_got)]
-
-    (three_send,) = combine(bit_values, [[other(terms, far_mask) for terms in (g0, t, g1)]])
     sends = combine(
         bit_values, [[columns_of(g2, cb, 2 * cb)], [columns_of(e, 3 * width + 128, 3 * width + 256)]]
     )
-    three_got = swap(three_send, far_mask)
     g2_got = cross(sends[0])
     small_got = cross(sends[1])
     c_got = swap(c_send, near_mask)
-    in1 = (parts[1] + cross(parts[1])).astype(BF16)
-    in1, own0, part0 = tie((in1, parts[0], part0))
+    three_got, c_got, own0, part0 = tie((three_got, c_got, parts[0], part0))
     in0 = (own0 + part0).astype(BF16)
-    three_got, g2_got, c_got, small_got, in0, in1, parts = tie(
-        (three_got, g2_got, c_got, small_got, in0, in1, parts)
-    )
+    three_got, g2_got, c_got, small_got, in0, parts = tie((three_got, g2_got, c_got, small_got, in0, parts))
     small = [*columns_of(e, 3 * width, 3 * width + 128), whole_of(small_got)]
     e = columns_of(e, 0, 3 * width)
     g0 = [*kept(g0, far_mask), part_of(three_got, 0, ca)]
@@ -1177,11 +1177,11 @@
     _, late_bits = tie((main_send, bit_values))
     sends = combine(late_bits, [[other(e, near_mask), other(small, near_mask)], [other(c, far_mask)]])
     got_z = swap(main_send, mask)
-    in2 = (parts[2] + cross(parts[2])).astype(BF16)
+    in1 = (parts[1] + cross(parts[1])).astype(BF16)
     c_got = swap(sends[1], far_mask)
     e_got = swap(sends[0], near_mask)
     layer_out = place_rows(at, out_rows, got_first, got_out)
-    got_z, e_got, c_got, in2, parts, layer_out = tie((got_z, e_got, c_got, in2, parts, layer_out))
+    got_z, e_got, c_got, in1, parts, layer_out = tie((got_z, e_got, c_got, in1, parts, layer_out))
     main = [[*kept(terms, mask), part_of(got_z, ends[n], ends[n + 1])] for n, terms in enumerate(main)]
     e = [*kept(e, near_mask), part_of(e_got, 0, 3 * width)]
     small = [*kept(small, near_mask), part_of(e_got, 3 * width, 3 * width + 128)]
@@ -1200,7 +1200,7 @@
         sends = combine(late_bits, outputs)
         pair_got = swap(pair_send, mask)
         if k == 0:
-            in3 = (parts[3] + cross(parts[3])).astype(BF16)
+            in2 = (parts[2] + cross(parts[2])).astype(BF16)
             got_last = swap(sends[1], 1)
             keep = sends[2]
         pair_keep = sends[0]
@@ -1209,7 +1209,7 @@
         e = [part_of(pair_keep, 3 * width, 6 * width), part_of(pair_got, 3 * width, 6 * width)]
         small = [part_of(pair_keep, 6 * width, wide), part_of(pair_got, 6 * width, wide)]
 
-    input_grad = jnp.concatenate([in0, in1, in2, in3], axis=0)
+    input_grad = jnp.concatenate([in0, in1, in2], axis=0)
     got_last, keep, input_grad = tie((got_last, keep, input_grad))
     got_last = got_last.reshape(rows, -1)
     keep = keep.reshape(rows, -1)

time: 336 us -> 334 us (level)
    ppermute x16 -> x15, waiting for transfers between devices: 73.7 us -> 63.1 us  [cross(): return lax.ppermute(value, 'tensor', [(0, 1), (1, 0)])]
    ppermute x29, waiting for transfers between devices: 32.6 us -> 40.6 us  [swap(): return lax.ppermute(value, 'dp', [(i, i ^ mask) for i in range(devices)])]
    ppermute x16 -> x15, starting transfers between devices: 16.2 us -> 15 us  [cross(): return lax.ppermute(value, 'tensor', [(0, 1), (1, 0)])]
  transfers between devices with their start and end apart: 45 -> 44, of which waited for: 20 -> 21; matrix products, arithmetic and copies ran while one was open for 7% -> 8% of each run, Pallas kernels for 40% -> 40%
where the time goes in v6:
time: 334 us; the launch traced here: 333 us
  Pallas kernels  154 us (46%)
  waiting for transfers between devices  104 us (31%)
  starting transfers between devices  38.3 us (11%)
  other arithmetic  21.8 us (7%)
  local copies, waits for them, and re-layouts  12.4 us (4%)
    ppermute x15, waiting for transfers between devices, cross(): return lax.ppermute(value, 'tensor', [(0, 1), (1, 0)])  63.1 us
    ppermute x29, waiting for transfers between devices, swap(): return lax.ppermute(value, 'dp', [(i, i ^ mask) for i in range(devices)])  40.6 us
    pallas_call x1, Pallas kernels, attend_back(): pl.pallas_call(functools.partial(attend_back_kernel, len(chunks), group),...  35.5 us
    pallas_call x9, Pallas kernels, combine(): pl.pallas_call(functools.partial(combine_kernel, plan, len(arrays)), grid...  31.3 us
    ppermute x29, starting transfers between devices, swap(): return lax.ppermute(value, 'dp', [(i, i ^ mask) for i in range(devices)])  23.3 us
    pallas_call x1, Pallas kernels, forward(): pl.pallas_call(forward_kernel, grid_spec=pltpu.PrefetchScalarGridSpec(num...  21.2 us
    pallas_call x2, Pallas kernels, weight_grads(): pl.pallas_call(functools.partial(weight_kernel, plan, len(received), len(...  17.1 us
    pallas_call x1, Pallas kernels, backward(): pl.pallas_call(backward_kernel, grid_spec=pltpu.PrefetchScalarGridSpec(nu...  16.6 us
  transfers between devices with their start and end apart: 44, of which 21 were waited for; matrix products, arithmetic and copies ran while one was open for 8% of the time, Pallas kernels for 40%

profile of v6, /device:TPU:0, one launch (start us, length us, event | category | flops | bytes accessed | tf_op | source)
XLA Modules:
  0.0 332.6 jit_solution(9208167369211494229)
XLA Ops:
  8.0 8.2 %project.1 = (bf16[1024,768]{1,0:T(8,128)(2,1)}, bf16[1024,768]{1,0:T(8,128)(2,1)}, bf16[1024,384]{1,0:T(8,128)(2,1)}) custom-call(bf16[1024,768]{1,0:T(8,128)(2,1)} %bitcast.70, f32[1024,1]{1,0:T(8,128)} %copy.46.kind_ref, bf16[4,768,384]{2,1,0:T(8,128)(2,1)} %wq_hbm.1, f32[4,384]{1,0:T(4,128)} %bq_ref.1, bf16[768,384]{1,0:T(8,128)(2,1)} %wk_hbm.1, ...), custom_call_target="tpu_custom_call" | custom-call | flops 3623878656 | bytes 9437184 | tf_op jit(solution)/shard_map/project/pallas_call | solution.py:87
  18.3 4.1 %collective-permute-done.1 = f32[1536]{0:T(1024)S(1)} collective-permute-done((f32[1536]{0:T(1024)S(1)}, f32[1536]{0:T(1024)S(1)}, u32[]{:S(2)}, u32[]{:S(2)}) %collective-permute-start.1) | collective-permute-done | bytes 6176 | tf_op jit(solution)/shard_map/ppermute | solution.py:954
  28.8 14.0 %attend.1 = (bf16[1024,384]{1,0:T(8,128)(2,1)}, bf16[1024,768]{1,0:T(8,128)(2,1)}) custom-call(bf16[1024,768]{1,0:T(8,128)(2,1)} %get-tuple-element.157.q2_ref, bf16[1024,768]{1,0:T(8,128)(2,1)} %get-tuple-element.158.k2_ref, bf16[1024,384]{1,0:T(8,128)(2,1)} %get-tuple-element.159.v_ref, f32[1024,1]{1,0:T(8,128)} %fusion.1.live_ref), custom_call_target="tpu_custom_call" | custom-call | flops 4026531840 | bytes 7864320 | tf_op jit(solution)/shard_map/attend/pallas_call | solution.py:154
  47.2 3.7 %turn.1.turned_hbm = bf16[768,1024]{1,0:T(8,128)(2,1)} custom-call(bf16[1024,768]{1,0:T(8,128)(2,1)} %bitcast.71), custom_call_target="tpu_custom_call" | custom-call | flops 786432 | bytes 3145728 | tf_op jit(solution)/shard_map/turn/pallas_call | solution.py:880
  52.7 8.0 %collective-permute-done.10.rest_12_ = f32[192,768]{1,0:T(8,128)} collective-permute-done((f32[192,768]{1,0:T(8,128)}, f32[192,768]{1,0:T(8,128)}, u32[]{:S(2)}, u32[]{:S(2)}) %collective-permute-start.10) | collective-permute-done | bytes 589856 | tf_op jit(solution)/shard_map/ppermute | solution.py:951
  62.8 15.4 %collective-permute-done.8.rest_14_ = f32[192,768]{1,0:T(8,128)} collective-permute-done((f32[192,768]{1,0:T(8,128)}, f32[192,768]{1,0:T(8,128)}, u32[]{:S(2)}, u32[]{:S(2)}) %collective-permute-start.8) | collective-permute-done | bytes 589856 | tf_op jit(solution)/shard_map/ppermute | solution.py:954
  85.4 21.2 %forward.1 = (bf16[512,768]{1,0:T(8,128)(2,1)}, f32[512,384]{1,0:T(8,128)}, f32[512,384]{1,0:T(8,128)}, bf16[512,768]{1,0:T(8,128)(2,1)}, bf16[512,768]{1,0:T(8,...) custom-call(s32[4]{0:T(128)} %pad_add_fusion.1.at_ref.bit_ref.y_ref,, ...), custom_call_target="tpu_custom_call" | custom-call | flops 4831838208 | bytes 28311552 | tf_op jit(solution)/shard_map/forward/pallas_call | solution.py:547
  107.4 16.6 %backward.1 = (f32[512,768]{1,0:T(8,128)}, f32[512,384]{1,0:T(8,128)}, f32[512,384]{1,0:T(8,128)}, bf16[512,768]{1,0:T(8,128)(2,1)}, bf16[512,1152]{1,0:T(8,128)...) custom-call(s32[4]{0:T(128)} %pad_add_fusion.1.at_ref.bit_ref.y_ref, ...), custom_call_target="tpu_custom_call" | custom-call | flops 4831838208 | bytes 28311552 | tf_op jit(solution)/shard_map/backward/pallas_call | solution.py:663
  127.6 8.2 %weight_grads.3 = (f32[384,1536]{1,0:T(8,128)}, f32[384,1536]{1,0:T(8,128)}) custom-call(s32[4]{0:T(128)} %pad_add_fusion.1.at_ref.bit_ref.y_ref, bf16[512,768]{1,0:T(8,128)(2,1)} %get-tuple-element.188.d_low_ref.rest_0_, bf16[512,1536]{1,0:T(8,128)(2,1)} %get-tuple-element.209.rest_1_, f32[512,3456]{1,0:T(8,128)} %collective-permute-done.18.rest_4_.rest_2_), custom_call_target="tpu_custom_call" | custom-call | flops 2415919104 | bytes 11010048 | tf_op jit(solution)/shard_map/weight_grads/pallas_call | solution.py:769
  137.1 8.9 %weight_grads.2 = (f32[384,1152]{1,0:T(8,128)}, f32[384,1152]{1,0:T(8,128)}, f32[768,384]{1,0:T(8,128)}, f32[768,384]{1,0:T(8,128)}) custom-call(s32[4]{0:T(128)} %pad_add_fusion.1.at_ref.bit_ref.y_ref, bf16[512,768]{1,0:T(8,128)(2,1)} %get-tuple-element.183.rest_0_, bf16[512,768]{1,0:T(8,128)(2,1)} %get-tuple-element.191.rest_1_, ...), custom_call_target="tpu_custom_call" | custom-call | flops 3019898880 | bytes 13762560 | tf_op jit(solution)/shard_map/weight_grads/pallas_call | solution.py:769
  151.4 35.5 %attend_back.1 = (f32[224,768]{1,0:T(8,128)}, f32[512,768]{1,0:T(8,128)}, f32[288,768]{1,0:T(8,128)}, f32[384,1152]{1,0:T(8,128)}, f32[384,1152]{1,0:T(8,128)}, ...) custom-call(s32[4]{0:T(128)} %pad_add_fusion.1.at_ref.bit_ref.y_ref, bf16[1024,768]{1,0:T(8,128)(2,1)} %get-tuple-element.157.q2_ref, ...), custom_call_target="tpu_custom_call" | custom-call | flops 8053063680 | bytes 15728640 | tf_op jit(solution)/shard_map/attend_back/pallas_call | solution.py:333
  187.0 5.8 %collective-permute-done.25.second_ref = f32[512,384]{1,0:T(8,128)S(1)} collective-permute-done((f32[512,384]{1,0:T(8,128)}, f32[512,384]{1,0:T(8,128)S(1)}, u32[]{:S(2)}, u32[]{:S(2)}) %collective-permute-start.25) | collective-permute-done | bytes 786464 | tf_op jit(solution)/shard_map/ppermute | solution.py:954
  194.0 3.6 %combine.9 = (f32[2,1,2,2,48,768]{5,4,3,2,1,0:T(8,128)}, f32[2,1,2,2,48,384]{5,4,3,2,1,0:T(8,128)}) custom-call(s32[4]{0:T(128)} %pad_add_fusion.bits_ref, f32[2,1,2,2,48,1152]{5,4,3,2,1,0:T(8,128)} %bitcast.66, f32[2,1,2,2,48,1152]{5,4,3,2,1,0:T(8,128)} %bitcast.15.rest_1_.rest_10_, f32[2,2,2,2,48,384]{5,4,3,2,1,0:T(8,128)} %bitcast.73, ...), custom_call_target="tpu_custom_call" | custom-call | flops 3538944 | bytes 7077888 | tf_op jit(solution)/shard_map/combine/pallas_call | solution.py:854
  199.0 3.4 %combine.11 = f32[2,1,1,2,48,1536]{5,4,3,2,1,0:T(8,128)} custom-call(s32[4]{0:T(128)} %pad_add_fusion.bits_ref, f32[2,2,1,2,48,1536]{5,4,3,2,1,0:T(8,128)} %bitcast.58, f32[2,2,1,2,48,1536]{5,4,3,2,1,0:T(8,128)} %bitcast.22.rest_1_.rest_6_.rest_16_), custom_call_target="tpu_custom_call" | custom-call | flops 2359296 | bytes 4718592 | tf_op jit(solution)/shard_map/combine/pallas_call | solution.py:854
  204.1 3.8 %combine.12 = (f32[2,2,1,1,48,1408]{5,4,3,2,1,0:T(8,128)}, f32[2,1,2,1,48,1152]{5,4,3,2,1,0:T(8,128)}) custom-call(s32[4]{0:T(128)} %pad_add_fusion.bits_ref, f32[2,2,2,1,48,1408]{5,4,3,2,1,0:T(8,128)} %bitcast.53, f32[2,2,2,1,48,1408]{5,4,3,2,1,0:T(8,128)} %collective-permute-done.29.rest_1_.rest_4_.rest_5_, f32[2,2,2,1,48,1152]{5,4,3,2,1,0:T(8,128)} %bitcast.62, ...), custom_call_target="tpu_custom_call" | custom-call | flops 3932160 | bytes 7864320 | tf_op jit(solution)/shard_map/combine/pallas_call | solution.py:854
  209.3 5.7 %collective-permute-done.27 = f32[2,1,2,2,48,384]{5,4,3,2,1,0:T(8,128)S(1)} collective-permute-done((f32[2,1,2,2,48,384]{5,4,3,2,1,0:T(8,128)}, f32[2,1,2,2,48,384]{5,4,3,2,1,0:T(8,128)S(1)}, u32[]{:S(2)}, u32[]{:S(2)}) %collective-permute-start.27) | collective-permute-done | bytes 589856 | tf_op jit(solution)/shard_map/ppermute | solution.py:951
  219.3 7.5 %collective-permute-done.26.rest_2_.rest_11_ = f32[2,1,2,2,48,768]{5,4,3,2,1,0:T(8,128)} collective-permute-done((f32[2,1,2,2,48,768]{5,4,3,2,1,0:T(8,128)}, f32[2,1,2,2,48,768]{5,4,3,2,1,0:T(8,128)}, u32[]{:S(2)}, u32[]{:S(2)}) %collective-permute-start.26) | collective-permute-done | bytes 1179680 | tf_op jit(solution)/shard_map/ppermute | solution.py:954
  231.9 8.5 %collective-permute-done.32.rest_2_.rest_7_.rest_17_ = f32[2,1,1,2,48,1536]{5,4,3,2,1,0:T(8,128)} collective-permute-done((f32[2,1,1,2,48,1536]{5,4,3,2,1,0:T(8,128)}, f32[2,1,1,2,48,1536]{5,4,3,2,1,0:T(8,128)}, u32[]{:S(2)}, u32[]{:S(2)}) %collective-permute-start.32) | collective-permute-done | bytes 1179680 | tf_op jit(solution)/shard_map/ppermute | solution.py:951
  244.7 7.6 %collective-permute-done.28.rest_3_.rest_12_ = f32[2,1,1,2,48,1152]{5,4,3,2,1,0:T(8,128)} collective-permute-done((f32[2,1,1,2,48,1152]{5,4,3,2,1,0:T(8,128)}, f32[2,1,1,2,48,1152]{5,4,3,2,1,0:T(8,128)}, u32[]{:S(2)}, u32[]{:S(2)}) %collective-permute-start.28) | collective-permute-done | bytes 884768 | tf_op jit(solution)/shard_map/ppermute | solution.py:951
  252.2 5.8 %collective-permute-done.31.rest_6_.rest_2_ = f32[2,1,2,1,48,1152]{5,4,3,2,1,0:T(8,128)S(1)} collective-permute-done((f32[2,1,2,1,48,1152]{5,4,3,2,1,0:T(8,128)}, f32[2,1,2,1,48,1152]{5,4,3,2,1,0:T(8,128)S(1)}, u32[]{:S(2)}, u32[]{:S(2)}) %collective-permute-start.31) | collective-permute-done | bytes 884768 | tf_op jit(solution)/shard_map/ppermute | solution.py:951
  275.4 6.8 %place_rows.1 = bf16[1024,768]{1,0:T(8,128)(2,1)} custom-call(s32[4]{0:T(128)} %pad_add_fusion.1.at_ref.bit_ref.y_ref, bf16[512,768]{1,0:T(8,128)(2,1)} %get-tuple-element.273.own_ref, f32[512,384]{1,0:T(8,128)} %copy-done.4, f32[512,384]{1,0:T(8,128)} %copy-done.5), custom_call_target="tpu_custom_call" | custom-call | flops 393216 | bytes 4718592 | tf_op jit(solution)/shard_map/place_rows/pallas_call | solution.py:903
  282.2 15.2 %collective-permute-done.40 = f32[512,768]{1,0:T(8,128)} collective-permute-done((f32[512,768]{1,0:T(8,128)}, f32[512,768]{1,0:T(8,128)}, u32[]{:S(2)}, u32[]{:S(2)}) %collective-permute-start.40) | collective-permute-done | bytes 1572896 | tf_op jit(solution)/shard_map/ppermute | solution.py:954
  306.4 4.7 %combine.17 = (f32[1,1,1,1,48,2432]{5,4,3,2,1,0:T(8,128)}, f32[1,1,1,1,48,1920]{5,4,3,2,1,0:T(8,128)}, f32[1,1,1,1,48,1920]{5,4,3,2,1,0:T(8,128)}) custom-call(s32[4]{0:T(128)} %pad_add_fusion.bits_ref, f32[2,2,2,1,48,1152]{5,4,3,2,1,0:T(8,128)} %bitcast.65, f32[2,2,2,1,48,1152]{5,4,3,2,1,0:T(8,128)} %collective-permute-done.30.rest_3_.rest_5_.rest_1_, ...), custom_call_target="tpu_custom_call" | custom-call | flops 5283840 | bytes 10567680 | tf_op jit(solution)/shard_map/combine/pallas_call | solution.py:854
  311.2 11.0 %collective-permute-done.42 = f32[288,768]{1,0:T(8,128)} collective-permute-done((f32[288,768]{1,0:T(8,128)}, f32[288,768]{1,0:T(8,128)}, u32[]{:S(2)}, u32[]{:S(2)}) %collective-permute-start.42) | collective-permute-done | bytes 884768 | tf_op jit(solution)/shard_map/ppermute | solution.py:954
  (186 shorter events, 97.4 us)
Async XLA Ops:
  2.7 19.7 %collective-permute-start = (f32[240,768]{1,0:T(8,128)S(1)}, f32[240,768]{1,0:T(8,128)}, u32[]{:S(2)}, u32[]{:S(2)}) collective-permute-start(f32[240,768]{1,0:T(8,128)S(1)} %maximum_convert_fusion), channel_id=1, source_target_pairs={{0,1},{1,0},{2,3},{3,2},{4,5},{5,4},{6,7},{7,6},{8,9},{9,8},{10,11... | collective-permute-start | bytes 2211848 | tf_op jit(solution)/shard_map/ppermute | solution.py:954
  22.4 22.3 %collective-permute-start.4 = (f32[240,768]{1,0:T(8,128)}, f32[240,768]{1,0:T(8,128)S(1)}, u32[]{:S(2)}, u32[]{:S(2)}) collective-permute-start(f32[240,768]{1,0:T(8,128)} %collective-permute-done.rest_0_), channel_id=1, source_target_pairs={{0,8},{2,10},{4,12},{6,14},{8,0},{10,2},{12,4},{14,6},{16,24},{18,... | collective-permute-start | bytes 2211848 | tf_op jit(solution)/shard_map/ppermute | solution.py:951
  24.2 20.6 %collective-permute-start.3 = (f32[240,768]{1,0:T(8,128)}, f32[240,768]{1,0:T(8,128)}, u32[]{:S(2)}, u32[]{:S(2)}) collective-permute-start(f32[240,768]{1,0:T(8,128)} %collective-permute-done.rest_0_), channel_id=1, source_target_pairs={{0,4},{2,6},{4,0},{6,2},{8,12},{10,14},{12,8},{14,10},{16,20},{18,... | collective-permute-start | bytes 2211848 | tf_op jit(solution)/shard_map/ppermute | solution.py:951
  45.9 32.4 %collective-permute-start.6 = (f32[512,384]{1,0:T(8,128)}, f32[512,384]{1,0:T(8,128)S(1)}, u32[]{:S(2)}, u32[]{:S(2)}) collective-permute-start(f32[512,384]{1,0:T(8,128)} %dynamic-slice_convert_fusion), channel_id=1, source_target_pairs={{0,1},{1,0},{2,3},{3,2},{4,5},{5,4},{6,7},{7,6},{8,9},{9,8},{10,11... | collective-permute-start | bytes 2359304 | tf_op jit(solution)/shard_map/ppermute | solution.py:954
  50.9 27.3 %collective-permute-start.7 = (f32[240,768]{1,0:T(8,128)}, f32[240,768]{1,0:T(8,128)S(1)}, u32[]{:S(2)}, u32[]{:S(2)}) collective-permute-start(f32[240,768]{1,0:T(8,128)} %copy-done.6), channel_id=1, source_target_pairs={{0,4},{2,6},{4,0},{6,2},{8,12},{10,14},{12,8},{14,10},{16,20},{18,... | collective-permute-start | bytes 2211848 | tf_op jit(solution)/shard_map/ppermute | solution.py:951
  106.7 20.2 %collective-permute-start.18 = (f32[512,3456]{1,0:T(8,128)}, f32[512,3456]{1,0:T(8,128)}, u32[]{:S(2)}, u32[]{:S(2)}) collective-permute-start(f32[512,3456]{1,0:T(8,128)} %get-tuple-element.194), channel_id=1, source_target_pairs={{0,2},{2,0},{4,6},{6,4},{8,10},{10,8},{12,14},{14,12},{16,18},{18,... | collective-permute-start | bytes 21233672 | tf_op jit(solution)/shard_map/ppermute | solution.py:951
  106.9 20.0 %collective-permute-start.19 = (f32[512,384]{1,0:T(8,128)}, f32[512,384]{1,0:T(8,128)S(1)}, u32[]{:S(2)}, u32[]{:S(2)}) collective-permute-start(f32[512,384]{1,0:T(8,128)} %get-tuple-element.195), channel_id=1, source_target_pairs={{0,1},{1,0},{2,3},{3,2},{4,5},{5,4},{6,7},{7,6},{8,9},{9,8},{10,11... | collective-permute-start | bytes 2359304 | tf_op jit(solution)/shard_map/ppermute | solution.py:954
  126.9 20.3 %collective-permute-start.21 = (f32[512,384]{1,0:T(8,128)}, f32[512,384]{1,0:T(8,128)}, u32[]{:S(2)}, u32[]{:S(2)}) collective-permute-start(f32[512,384]{1,0:T(8,128)} %get-tuple-element.206), channel_id=1, source_target_pairs={{0,1},{1,0},{2,3},{3,2},{4,5},{5,4},{6,7},{7,6},{8,9},{9,8},{10,11... | collective-permute-start | bytes 2359304 | tf_op jit(solution)/shard_map/ppermute | solution.py:954
  135.8 57.0 %collective-permute-start.24 = (f32[384,1536]{1,0:T(8,128)}, f32[384,1536]{1,0:T(8,128)}, u32[]{:S(2)}, u32[]{:S(2)}) collective-permute-start(f32[384,1536]{1,0:T(8,128)} %get-tuple-element.210), channel_id=1, source_target_pairs={{0,4},{2,6},{4,0},{6,2},{8,12},{10,14},{12,8},{14,10},{16,20},{18,... | collective-permute-start | bytes 7077896 | tf_op jit(solution)/shard_map/ppermute | solution.py:951
  147.2 45.6 %collective-permute-start.22 = (f32[384,1152]{1,0:T(8,128)}, f32[384,1152]{1,0:T(8,128)}, u32[]{:S(2)}, u32[]{:S(2)}) collective-permute-start(f32[384,1152]{1,0:T(8,128)} %get-tuple-element.207), channel_id=1, source_target_pairs={{0,8},{2,10},{4,12},{6,14},{8,0},{10,2},{12,4},{14,6},{16,24},{18,... | collective-permute-start | bytes 5308424 | tf_op jit(solution)/shard_map/ppermute | solution.py:951
  148.5 44.3 %collective-permute-start.23 = (f32[768,384]{1,0:T(8,128)}, f32[768,384]{1,0:T(8,128)}, u32[]{:S(2)}, u32[]{:S(2)}) collective-permute-start(f32[768,384]{1,0:T(8,128)} %get-tuple-element.208), channel_id=1, source_target_pairs={{0,1},{1,0},{2,3},{3,2},{4,5},{5,4},{6,7},{7,6},{8,9},{9,8},{10,11... | collective-permute-start | bytes 3538952 | tf_op jit(solution)/shard_map/ppermute | solution.py:954
  149.1 43.7 %collective-permute-start.25 = (f32[512,384]{1,0:T(8,128)}, f32[512,384]{1,0:T(8,128)S(1)}, u32[]{:S(2)}, u32[]{:S(2)}) collective-permute-start(f32[512,384]{1,0:T(8,128)} %get-tuple-element.211), channel_id=1, source_target_pairs={{0,1},{1,0},{2,3},{3,2},{4,5},{5,4},{6,7},{7,6},{8,9},{9,8},{10,11... | collective-permute-start | bytes 2359304 | tf_op jit(solution)/shard_map/ppermute | solution.py:954
  197.7 29.2 %collective-permute-start.26 = (f32[2,1,2,2,48,768]{5,4,3,2,1,0:T(8,128)}, f32[2,1,2,2,48,768]{5,4,3,2,1,0:T(8,128)}, u32[]{:S(2)}, u32[]{:S(2)}) collective-permute-start(f32[2,1,2,2,48,768]{5,4,3,2,1,0:T(8,128)} %get-tuple-element.231), channel_id=1, source_target_pairs={{0,1},{1,0},{2,3},{3,2},{4,5},{5,4},{6,7},{7,6},{8,9},{9,8},{10,11... | collective-permute-start | bytes 3538952 | tf_op jit(solution)/shard_map/ppermute | solution.py:954
  202.5 37.9 %collective-permute-start.32 = (f32[2,1,1,2,48,1536]{5,4,3,2,1,0:T(8,128)}, f32[2,1,1,2,48,1536]{5,4,3,2,1,0:T(8,128)}, u32[]{:S(2)}, u32[]{:S(2)}) collective-permute-start(f32[2,1,1,2,48,1536]{5,4,3,2,1,0:T(8,128)} %combine.11), channel_id=1, source_target_pairs={{0,8},{2,10},{4,12},{6,14},{8,0},{10,2},{12,4},{14,6},{16,24},{18,... | collective-permute-start | bytes 3538952 | tf_op jit(solution)/shard_map/ppermute | solution.py:951
  207.9 32.8 %collective-permute-start.33 = (f32[2,2,1,1,48,1408]{5,4,3,2,1,0:T(8,128)}, f32[2,2,1,1,48,1408]{5,4,3,2,1,0:T(8,128)}, u32[]{:S(2)}, u32[]{:S(2)}) collective-permute-start(f32[2,2,1,1,48,1408]{5,4,3,2,1,0:T(8,128)} %get-tuple-element.248), channel_id=1, source_target_pairs={{0,4},{2,6},{4,0},{6,2},{8,12},{10,14},{12,8},{14,10},{16,20},{18,... | collective-permute-start | bytes 3244040 | tf_op jit(solution)/shard_map/ppermute | solution.py:951
  216.1 24.6 %collective-permute-start.34 = (f32[224,768]{1,0:T(8,128)}, f32[224,768]{1,0:T(8,128)}, u32[]{:S(2)}, u32[]{:S(2)}) collective-permute-start(f32[224,768]{1,0:T(8,128)} %get-tuple-element.260), channel_id=1, source_target_pairs={{0,1},{1,0},{2,3},{3,2},{4,5},{5,4},{6,7},{7,6},{8,9},{9,8},{10,11... | collective-permute-start | bytes 2064392 | tf_op jit(solution)/shard_map/ppermute | solution.py:954
  229.9 22.4 %collective-permute-start.28 = (f32[2,1,1,2,48,1152]{5,4,3,2,1,0:T(8,128)}, f32[2,1,1,2,48,1152]{5,4,3,2,1,0:T(8,128)}, u32[]{:S(2)}, u32[]{:S(2)}) collective-permute-start(f32[2,1,1,2,48,1152]{5,4,3,2,1,0:T(8,128)} %combine.10), channel_id=1, source_target_pairs={{0,4},{2,6},{4,0},{6,2},{8,12},{10,14},{12,8},{14,10},{16,20},{18,... | collective-permute-start | bytes 2654216 | tf_op jit(solution)/shard_map/ppermute | solution.py:951
  231.4 26.6 %collective-permute-start.31 = (f32[2,1,2,1,48,1152]{5,4,3,2,1,0:T(8,128)}, f32[2,1,2,1,48,1152]{5,4,3,2,1,0:T(8,128)S(1)}, u32[]{:S(2)}, u32[]{:S(2)}) collective-permute-start(f32[2,1,2,1,48,1152]{5,4,3,2,1,0:T(8,128)} %get-tuple-element.247), channel_id=1, source_target_pairs={{0,8},{2,10},{4,12},{6,14},{8,0},{10,2},{12,4},{14,6},{16,24},{18,... | collective-permute-start | bytes 2654216 | tf_op jit(solution)/shard_map/ppermute | solution.py:951
  262.9 34.5 %collective-permute-start.40 = (f32[512,768]{1,0:T(8,128)}, f32[512,768]{1,0:T(8,128)}, u32[]{:S(2)}, u32[]{:S(2)}) collective-permute-start(f32[512,768]{1,0:T(8,128)} %get-tuple-element.271), channel_id=1, source_target_pairs={{0,1},{1,0},{2,3},{3,2},{4,5},{5,4},{6,7},{7,6},{8,9},{9,8},{10,11... | collective-permute-start | bytes 4718600 | tf_op jit(solution)/shard_map/ppermute | solution.py:954
  267.4 33.1 %collective-permute-start.37 = (f32[1,1,1,2,48,1920]{5,4,3,2,1,0:T(8,128)}, f32[1,1,1,2,48,1920]{5,4,3,2,1,0:T(8,128)}, u32[]{:S(2)}, u32[]{:S(2)}) collective-permute-start(f32[1,1,1,2,48,1920]{5,4,3,2,1,0:T(8,128)} %combine.14), channel_id=1, source_target_pairs={{0,16},{2,18},{4,20},{6,22},{8,24},{10,26},{12,28},{14,30},{16,0},... | collective-permute-start | bytes 2211848 | tf_op jit(solution)/shard_map/ppermute | solution.py:951
  273.4 26.0 %collective-permute-start.38 = (f32[2,1,1,1,48,1280]{5,4,3,2,1,0:T(8,128)}, f32[2,1,1,1,48,1280]{5,4,3,2,1,0:T(8,128)}, u32[]{:S(2)}, u32[]{:S(2)}) collective-permute-start(f32[2,1,1,1,48,1280]{5,4,3,2,1,0:T(8,128)} %get-tuple-element.269), channel_id=1, source_target_pairs={{0,8},{2,10},{4,12},{6,14},{8,0},{10,2},{12,4},{14,6},{16,24},{18,... | collective-permute-start | bytes 1474568 | tf_op jit(solution)/shard_map/ppermute | solution.py:951
  274.2 25.2 %collective-permute-start.39 = (f32[2,1,1,1,48,1152]{5,4,3,2,1,0:T(8,128)}, f32[2,1,1,1,48,1152]{5,4,3,2,1,0:T(8,128)}, u32[]{:S(2)}, u32[]{:S(2)}) collective-permute-start(f32[2,1,1,1,48,1152]{5,4,3,2,1,0:T(8,128)} %get-tuple-element.270), channel_id=1, source_target_pairs={{0,4},{2,6},{4,0},{6,2},{8,12},{10,14},{12,8},{14,10},{16,20},{18,... | collective-permute-start | bytes 1327112 | tf_op jit(solution)/shard_map/ppermute | solution.py:951
  300.4 21.7 %collective-permute-start.42 = (f32[288,768]{1,0:T(8,128)}, f32[288,768]{1,0:T(8,128)}, u32[]{:S(2)}, u32[]{:S(2)}) collective-permute-start(f32[288,768]{1,0:T(8,128)} %get-tuple-element.285), channel_id=1, source_target_pairs={{0,1},{1,0},{2,3},{3,2},{4,5},{5,4},{6,7},{7,6},{8,9},{9,8},{10,11... | collective-permute-start | bytes 2654216 | tf_op jit(solution)/shard_map/ppermute | solution.py:954
  304.3 22.9 %collective-permute-start.43 = (f32[1,1,1,1,48,2432]{5,4,3,2,1,0:T(8,128)}, f32[1,1,1,1,48,2432]{5,4,3,2,1,0:T(8,128)}, u32[]{:S(2)}, u32[]{:S(2)}) collective-permute-start(f32[1,1,1,1,48,2432]{5,4,3,2,1,0:T(8,128)} %combine.16), channel_id=1, source_target_pairs={{0,16},{2,18},{4,20},{6,22},{8,24},{10,26},{12,28},{14,30},{16,0},... | collective-permute-start | bytes 1400840 | tf_op jit(solution)/shard_map/ppermute | solution.py:951
  (44 other events, 536.8 us)

commit v7 on v6

--- a/solution.py
+++ b/solution.py
@@ -1149,14 +1149,14 @@
 
     (three_send,) = combine(bit_values, [[other(terms, far_mask) for terms in (g0, t, g1)]])
     three_got = swap(three_send, far_mask)
-    g2_got, e_got, part0, parts, _ = tie((g2_got, e_got, part0, parts, three_send))
+    e_got, _ = tie((e_got, three_send))
+    e = [*kept(e, far_mask), whole_of(e_got)]
+    (small_send,) = combine(bit_values, [[columns_of(e, 3 * width + 128, 3 * width + 256)]])
+    small_got = cross(small_send)
+    g2_got, part0, parts, small_got = tie((g2_got, part0, parts, small_got))
     g2 = [*kept(g2, near_mask), whole_of(g2_got)]
-    e = [*kept(e, far_mask), whole_of(e_got)]
-    sends = combine(
-        bit_values, [[columns_of(g2, cb, 2 * cb)], [columns_of(e, 3 * width + 128, 3 * width + 256)]]
-    )
-    g2_got = cross(sends[0])
-    small_got = cross(sends[1])
+    (g2_send,) = combine(bit_values, [[columns_of(g2, cb, 2 * cb)]])
+    g2_got = cross(g2_send)
     c_got = swap(c_send, near_mask)
     three_got, c_got, own0, part0 = tie((three_got, c_got, parts[0], part0))
     in0 = (own0 + part0).astype(BF16)

time: 334 us -> 333 us (level)
  waiting for transfers between devices: 104 us -> 99.4 us
    ppermute x29, waiting for transfers between devices: 40.6 us -> 34.4 us  [swap(): return lax.ppermute(value, 'dp', [(i, i ^ mask) for i in range(devices)])]
    pallas_call x9 -> x10, Pallas kernels: 31.3 us -> 33.6 us  [combine(): pl.pallas_call(functools.partial(combine_kernel, plan, len(arrays)), grid...]
  transfers between devices with their start and end apart: 44 -> 44, of which waited for: 21 -> 23; matrix products, arithmetic and copies ran while one was open for 8% -> 8% of each run, Pallas kernels for 40% -> 41%
where the time goes in v7:
time: 333 us; the launch traced here: 331 us
  Pallas kernels  157 us (47%)
  waiting for transfers between devices  99.4 us (30%)
  starting transfers between devices  38.8 us (12%)
  other arithmetic  22.1 us (7%)
  local copies, waits for them, and re-layouts  12.4 us (4%)
    ppermute x15, waiting for transfers between devices, cross(): return lax.ppermute(value, 'tensor', [(0, 1), (1, 0)])  65 us
    pallas_call x1, Pallas kernels, attend_back(): pl.pallas_call(functools.partial(attend_back_kernel, len(chunks), group),...  35.5 us
    ppermute x29, waiting for transfers between devices, swap(): return lax.ppermute(value, 'dp', [(i, i ^ mask) for i in range(devices)])  34.4 us
    pallas_call x10, Pallas kernels, combine(): pl.pallas_call(functools.partial(combine_kernel, plan, len(arrays)), grid...  33.6 us
    ppermute x29, starting transfers between devices, swap(): return lax.ppermute(value, 'dp', [(i, i ^ mask) for i in range(devices)])  23.2 us
    pallas_call x1, Pallas kernels, forward(): pl.pallas_call(forward_kernel, grid_spec=pltpu.PrefetchScalarGridSpec(num...  21.2 us
    pallas_call x2, Pallas kernels, weight_grads(): pl.pallas_call(functools.partial(weight_kernel, plan, len(received), len(...  17.1 us
    pallas_call x1, Pallas kernels, backward(): pl.pallas_call(backward_kernel, grid_spec=pltpu.PrefetchScalarGridSpec(nu...  16.6 us
  transfers between devices with their start and end apart: 44, of which 23 were waited for; matrix products, arithmetic and copies ran while one was open for 8% of the time, Pallas kernels for 41%

profile of v7, /device:TPU:0, one launch (start us, length us, event | category | flops | bytes accessed | tf_op | source)
XLA Modules:
  0.0 331.4 jit_solution(15960538630199032566)
XLA Ops:
  8.0 8.2 %project.1 = (bf16[1024,768]{1,0:T(8,128)(2,1)}, bf16[1024,768]{1,0:T(8,128)(2,1)}, bf16[1024,384]{1,0:T(8,128)(2,1)}) custom-call(bf16[1024,768]{1,0:T(8,128)(2,1)} %bitcast.70, f32[1024,1]{1,0:T(8,128)} %copy.46.kind_ref, bf16[4,768,384]{2,1,0:T(8,128)(2,1)} %wq_hbm.1, f32[4,384]{1,0:T(4,128)} %bq_ref.1, bf16[768,384]{1,0:T(8,128)(2,1)} %wk_hbm.1, ...), custom_call_target="tpu_custom_call" | custom-call | flops 3623878656 | bytes 9437184 | tf_op jit(solution)/shard_map/project/pallas_call | solution.py:87
  18.3 4.1 %collective-permute-done.1 = f32[1536]{0:T(1024)S(1)} collective-permute-done((f32[1536]{0:T(1024)S(1)}, f32[1536]{0:T(1024)S(1)}, u32[]{:S(2)}, u32[]{:S(2)}) %collective-permute-start.1) | collective-permute-done | bytes 6176 | tf_op jit(solution)/shard_map/ppermute | solution.py:954
  28.8 14.0 %attend.1 = (bf16[1024,384]{1,0:T(8,128)(2,1)}, bf16[1024,768]{1,0:T(8,128)(2,1)}) custom-call(bf16[1024,768]{1,0:T(8,128)(2,1)} %get-tuple-element.156.q2_ref, bf16[1024,768]{1,0:T(8,128)(2,1)} %get-tuple-element.157.k2_ref, bf16[1024,384]{1,0:T(8,128)(2,1)} %get-tuple-element.158.v_ref, f32[1024,1]{1,0:T(8,128)} %fusion.1.live_ref), custom_call_target="tpu_custom_call" | custom-call | flops 4026531840 | bytes 7864320 | tf_op jit(solution)/shard_map/attend/pallas_call | solution.py:154
  47.3 3.7 %turn.1.turned_hbm = bf16[768,1024]{1,0:T(8,128)(2,1)} custom-call(bf16[1024,768]{1,0:T(8,128)(2,1)} %bitcast.71), custom_call_target="tpu_custom_call" | custom-call | flops 786432 | bytes 3145728 | tf_op jit(solution)/shard_map/turn/pallas_call | solution.py:880
  52.7 8.0 %collective-permute-done.10.rest_12_ = f32[192,768]{1,0:T(8,128)} collective-permute-done((f32[192,768]{1,0:T(8,128)}, f32[192,768]{1,0:T(8,128)}, u32[]{:S(2)}, u32[]{:S(2)}) %collective-permute-start.10) | collective-permute-done | bytes 589856 | tf_op jit(solution)/shard_map/ppermute | solution.py:951
  62.9 15.4 %collective-permute-done.8.rest_14_ = f32[192,768]{1,0:T(8,128)} collective-permute-done((f32[192,768]{1,0:T(8,128)}, f32[192,768]{1,0:T(8,128)}, u32[]{:S(2)}, u32[]{:S(2)}) %collective-permute-start.8) | collective-permute-done | bytes 589856 | tf_op jit(solution)/shard_map/ppermute | solution.py:954
  85.5 21.2 %forward.1 = (bf16[512,768]{1,0:T(8,128)(2,1)}, f32[512,384]{1,0:T(8,128)}, f32[512,384]{1,0:T(8,128)}, bf16[512,768]{1,0:T(8,128)(2,1)}, bf16[512,768]{1,0:T(8,...) custom-call(s32[4]{0:T(128)} %pad_add_fusion.1.at_ref.bit_ref.y_ref,, ...), custom_call_target="tpu_custom_call" | custom-call | flops 4831838208 | bytes 28311552 | tf_op jit(solution)/shard_map/forward/pallas_call | solution.py:547
  107.4 16.6 %backward.1 = (f32[512,768]{1,0:T(8,128)}, f32[512,384]{1,0:T(8,128)}, f32[512,384]{1,0:T(8,128)}, bf16[512,768]{1,0:T(8,128)(2,1)}, bf16[512,1152]{1,0:T(8,128)...) custom-call(s32[4]{0:T(128)} %pad_add_fusion.1.at_ref.bit_ref.y_ref, ...), custom_call_target="tpu_custom_call" | custom-call | flops 4831838208 | bytes 28311552 | tf_op jit(solution)/shard_map/backward/pallas_call | solution.py:663
  127.6 8.2 %weight_grads.3 = (f32[384,1536]{1,0:T(8,128)}, f32[384,1536]{1,0:T(8,128)}) custom-call(s32[4]{0:T(128)} %pad_add_fusion.1.at_ref.bit_ref.y_ref, bf16[512,768]{1,0:T(8,128)(2,1)} %get-tuple-element.187.d_low_ref.rest_0_, bf16[512,1536]{1,0:T(8,128)(2,1)} %get-tuple-element.208.rest_1_, f32[512,3456]{1,0:T(8,128)} %collective-permute-done.18.rest_4_.rest_2_), custom_call_target="tpu_custom_call" | custom-call | flops 2415919104 | bytes 11010048 | tf_op jit(solution)/shard_map/weight_grads/pallas_call | solution.py:769
  137.1 8.9 %weight_grads.2 = (f32[384,1152]{1,0:T(8,128)}, f32[384,1152]{1,0:T(8,128)}, f32[768,384]{1,0:T(8,128)}, f32[768,384]{1,0:T(8,128)}) custom-call(s32[4]{0:T(128)} %pad_add_fusion.1.at_ref.bit_ref.y_ref, bf16[512,768]{1,0:T(8,128)(2,1)} %get-tuple-element.182.rest_0_, bf16[512,768]{1,0:T(8,128)(2,1)} %get-tuple-element.190.rest_1_, ...), custom_call_target="tpu_custom_call" | custom-call | flops 3019898880 | bytes 13762560 | tf_op jit(solution)/shard_map/weight_grads/pallas_call | solution.py:769
  151.5 35.5 %attend_back.1 = (f32[224,768]{1,0:T(8,128)}, f32[512,768]{1,0:T(8,128)}, f32[288,768]{1,0:T(8,128)}, f32[384,1152]{1,0:T(8,128)}, f32[384,1152]{1,0:T(8,128)}, ...) custom-call(s32[4]{0:T(128)} %pad_add_fusion.1.at_ref.bit_ref.y_ref, bf16[1024,768]{1,0:T(8,128)(2,1)} %get-tuple-element.156.q2_ref, ...), custom_call_target="tpu_custom_call" | custom-call | flops 8053063680 | bytes 15728640 | tf_op jit(solution)/shard_map/attend_back/pallas_call | solution.py:333
  187.0 5.9 %collective-permute-done.25.second_ref = f32[512,384]{1,0:T(8,128)S(1)} collective-permute-done((f32[512,384]{1,0:T(8,128)}, f32[512,384]{1,0:T(8,128)S(1)}, u32[]{:S(2)}, u32[]{:S(2)}) %collective-permute-start.25) | collective-permute-done | bytes 786464 | tf_op jit(solution)/shard_map/ppermute | solution.py:954
  194.0 3.6 %combine.10 = (f32[2,1,2,2,48,768]{5,4,3,2,1,0:T(8,128)}, f32[2,1,2,2,48,384]{5,4,3,2,1,0:T(8,128)}) custom-call(s32[4]{0:T(128)} %pad_add_fusion.bits_ref, f32[2,1,2,2,48,1152]{5,4,3,2,1,0:T(8,128)} %bitcast.66, f32[2,1,2,2,48,1152]{5,4,3,2,1,0:T(8,128)} %bitcast.15.rest_1_.rest_10_, f32[2,2,2,2,48,384]{5,4,3,2,1,0:T(8,128)} %bitcast.73, ...), custom_call_target="tpu_custom_call" | custom-call | flops 3538944 | bytes 7077888 | tf_op jit(solution)/shard_map/combine/pallas_call | solution.py:854
  199.1 3.4 %combine.12 = f32[2,1,1,2,48,1536]{5,4,3,2,1,0:T(8,128)} custom-call(s32[4]{0:T(128)} %pad_add_fusion.bits_ref, f32[2,2,1,2,48,1536]{5,4,3,2,1,0:T(8,128)} %bitcast.58, f32[2,2,1,2,48,1536]{5,4,3,2,1,0:T(8,128)} %bitcast.22.rest_1_.rest_6_.rest_16_), custom_call_target="tpu_custom_call" | custom-call | flops 2359296 | bytes 4718592 | tf_op jit(solution)/shard_map/combine/pallas_call | solution.py:854
  202.6 3.8 %combine.13 = (f32[2,2,1,1,48,1408]{5,4,3,2,1,0:T(8,128)}, f32[2,1,2,1,48,1152]{5,4,3,2,1,0:T(8,128)}) custom-call(s32[4]{0:T(128)} %pad_add_fusion.bits_ref, f32[2,2,2,1,48,1408]{5,4,3,2,1,0:T(8,128)} %bitcast.53, f32[2,2,2,1,48,1408]{5,4,3,2,1,0:T(8,128)} %collective-permute-done.29.rest_1_.rest_5_, f32[2,2,2,1,48,1152]{5,4,3,2,1,0:T(8,128)} %bitcast.62, ...), custom_call_target="tpu_custom_call" | custom-call | flops 3932160 | bytes 7864320 | tf_op jit(solution)/shard_map/combine/pallas_call | solution.py:854
  209.2 5.8 %collective-permute-done.27 = f32[2,1,2,2,48,384]{5,4,3,2,1,0:T(8,128)S(1)} collective-permute-done((f32[2,1,2,2,48,384]{5,4,3,2,1,0:T(8,128)}, f32[2,1,2,2,48,384]{5,4,3,2,1,0:T(8,128)S(1)}, u32[]{:S(2)}, u32[]{:S(2)}) %collective-permute-start.27) | collective-permute-done | bytes 589856 | tf_op jit(solution)/shard_map/ppermute | solution.py:951
  219.4 7.5 %collective-permute-done.26.rest_2_.rest_11_ = f32[2,1,2,2,48,768]{5,4,3,2,1,0:T(8,128)} collective-permute-done((f32[2,1,2,2,48,768]{5,4,3,2,1,0:T(8,128)}, f32[2,1,2,2,48,768]{5,4,3,2,1,0:T(8,128)}, u32[]{:S(2)}, u32[]{:S(2)}) %collective-permute-start.26) | collective-permute-done | bytes 1179680 | tf_op jit(solution)/shard_map/ppermute | solution.py:954
  246.7 4.3 %collective-permute-done.28.rest_3_.rest_12_ = f32[2,1,1,2,48,1152]{5,4,3,2,1,0:T(8,128)} collective-permute-done((f32[2,1,1,2,48,1152]{5,4,3,2,1,0:T(8,128)}, f32[2,1,1,2,48,1152]{5,4,3,2,1,0:T(8,128)}, u32[]{:S(2)}, u32[]{:S(2)}) %collective-permute-start.28) | collective-permute-done | bytes 884768 | tf_op jit(solution)/shard_map/ppermute | solution.py:951
  251.0 7.1 %collective-permute-done.31.rest_6_.rest_2_ = f32[2,1,2,1,48,1152]{5,4,3,2,1,0:T(8,128)S(1)} collective-permute-done((f32[2,1,2,1,48,1152]{5,4,3,2,1,0:T(8,128)}, f32[2,1,2,1,48,1152]{5,4,3,2,1,0:T(8,128)S(1)}, u32[]{:S(2)}, u32[]{:S(2)}) %collective-permute-start.31) | collective-permute-done | bytes 884768 | tf_op jit(solution)/shard_map/ppermute | solution.py:951
  267.7 3.4 %combine.17 = (f32[2,1,1,1,48,1280]{5,4,3,2,1,0:T(8,128)}, f32[2,1,1,1,48,1152]{5,4,3,2,1,0:T(8,128)}) custom-call(s32[4]{0:T(128)} %pad_add_fusion.bits_ref, f32[2,2,2,1,48,1408]{5,4,3,2,1,0:T(8,128)} %bitcast.55, f32[2,2,2,1,48,1408]{5,4,3,2,1,0:T(8,128)} %collective-permute-done.29.rest_1_.rest_5_, ...), custom_call_target="tpu_custom_call" | custom-call | flops 2850816 | bytes 5701632 | tf_op jit(solution)/shard_map/combine/pallas_call | solution.py:854
  273.1 6.8 %place_rows.1 = bf16[1024,768]{1,0:T(8,128)(2,1)} custom-call(s32[4]{0:T(128)} %pad_add_fusion.1.at_ref.bit_ref.y_ref, bf16[512,768]{1,0:T(8,128)(2,1)} %get-tuple-element.271.own_ref, f32[512,384]{1,0:T(8,128)} %copy-done.4, f32[512,384]{1,0:T(8,128)} %copy-done.5), custom_call_target="tpu_custom_call" | custom-call | flops 393216 | bytes 4718592 | tf_op jit(solution)/shard_map/place_rows/pallas_call | solution.py:903
  279.9 16.3 %collective-permute-done.40 = f32[512,768]{1,0:T(8,128)} collective-permute-done((f32[512,768]{1,0:T(8,128)}, f32[512,768]{1,0:T(8,128)}, u32[]{:S(2)}, u32[]{:S(2)}) %collective-permute-start.40) | collective-permute-done | bytes 1572896 | tf_op jit(solution)/shard_map/ppermute | solution.py:954
  305.2 4.7 %combine.19 = (f32[1,1,1,1,48,2432]{5,4,3,2,1,0:T(8,128)}, f32[1,1,1,1,48,1920]{5,4,3,2,1,0:T(8,128)}, f32[1,1,1,1,48,1920]{5,4,3,2,1,0:T(8,128)}) custom-call(s32[4]{0:T(128)} %pad_add_fusion.bits_ref, f32[2,2,2,1,48,1152]{5,4,3,2,1,0:T(8,128)} %bitcast.65, f32[2,2,2,1,48,1152]{5,4,3,2,1,0:T(8,128)} %collective-permute-done.30.rest_3_.rest_5_.rest_1_, ...), custom_call_target="tpu_custom_call" | custom-call | flops 5283840 | bytes 10567680 | tf_op jit(solution)/shard_map/combine/pallas_call | solution.py:854
  310.0 11.0 %collective-permute-done.42 = f32[288,768]{1,0:T(8,128)} collective-permute-done((f32[288,768]{1,0:T(8,128)}, f32[288,768]{1,0:T(8,128)}, u32[]{:S(2)}, u32[]{:S(2)}) %collective-permute-start.42) | collective-permute-done | bytes 884768 | tf_op jit(solution)/shard_map/ppermute | solution.py:954
  (187 shorter events, 102.0 us)
Async XLA Ops:
  2.7 19.7 %collective-permute-start = (f32[240,768]{1,0:T(8,128)S(1)}, f32[240,768]{1,0:T(8,128)}, u32[]{:S(2)}, u32[]{:S(2)}) collective-permute-start(f32[240,768]{1,0:T(8,128)S(1)} %maximum_convert_fusion), channel_id=1, source_target_pairs={{0,1},{1,0},{2,3},{3,2},{4,5},{5,4},{6,7},{7,6},{8,9},{9,8},{10,11... | collective-permute-start | bytes 2211848 | tf_op jit(solution)/shard_map/ppermute | solution.py:954
  22.4 22.4 %collective-permute-start.4 = (f32[240,768]{1,0:T(8,128)}, f32[240,768]{1,0:T(8,128)S(1)}, u32[]{:S(2)}, u32[]{:S(2)}) collective-permute-start(f32[240,768]{1,0:T(8,128)} %collective-permute-done.rest_0_), channel_id=1, source_target_pairs={{0,8},{2,10},{4,12},{6,14},{8,0},{10,2},{12,4},{14,6},{16,24},{18,... | collective-permute-start | bytes 2211848 | tf_op jit(solution)/shard_map/ppermute | solution.py:951
  24.2 20.6 %collective-permute-start.3 = (f32[240,768]{1,0:T(8,128)}, f32[240,768]{1,0:T(8,128)}, u32[]{:S(2)}, u32[]{:S(2)}) collective-permute-start(f32[240,768]{1,0:T(8,128)} %collective-permute-done.rest_0_), channel_id=1, source_target_pairs={{0,4},{2,6},{4,0},{6,2},{8,12},{10,14},{12,8},{14,10},{16,20},{18,... | collective-permute-start | bytes 2211848 | tf_op jit(solution)/shard_map/ppermute | solution.py:951
  45.9 32.4 %collective-permute-start.6 = (f32[512,384]{1,0:T(8,128)}, f32[512,384]{1,0:T(8,128)S(1)}, u32[]{:S(2)}, u32[]{:S(2)}) collective-permute-start(f32[512,384]{1,0:T(8,128)} %dynamic-slice_convert_fusion), channel_id=1, source_target_pairs={{0,1},{1,0},{2,3},{3,2},{4,5},{5,4},{6,7},{7,6},{8,9},{9,8},{10,11... | collective-permute-start | bytes 2359304 | tf_op jit(solution)/shard_map/ppermute | solution.py:954
  51.0 27.3 %collective-permute-start.7 = (f32[240,768]{1,0:T(8,128)}, f32[240,768]{1,0:T(8,128)S(1)}, u32[]{:S(2)}, u32[]{:S(2)}) collective-permute-start(f32[240,768]{1,0:T(8,128)} %copy-done.6), channel_id=1, source_target_pairs={{0,4},{2,6},{4,0},{6,2},{8,12},{10,14},{12,8},{14,10},{16,20},{18,... | collective-permute-start | bytes 2211848 | tf_op jit(solution)/shard_map/ppermute | solution.py:951
  106.7 20.2 %collective-permute-start.18 = (f32[512,3456]{1,0:T(8,128)}, f32[512,3456]{1,0:T(8,128)}, u32[]{:S(2)}, u32[]{:S(2)}) collective-permute-start(f32[512,3456]{1,0:T(8,128)} %get-tuple-element.193), channel_id=1, source_target_pairs={{0,2},{2,0},{4,6},{6,4},{8,10},{10,8},{12,14},{14,12},{16,18},{18,... | collective-permute-start | bytes 21233672 | tf_op jit(solution)/shard_map/ppermute | solution.py:951
  106.9 20.0 %collective-permute-start.19 = (f32[512,384]{1,0:T(8,128)}, f32[512,384]{1,0:T(8,128)S(1)}, u32[]{:S(2)}, u32[]{:S(2)}) collective-permute-start(f32[512,384]{1,0:T(8,128)} %get-tuple-element.194), channel_id=1, source_target_pairs={{0,1},{1,0},{2,3},{3,2},{4,5},{5,4},{6,7},{7,6},{8,9},{9,8},{10,11... | collective-permute-start | bytes 2359304 | tf_op jit(solution)/shard_map/ppermute | solution.py:954
  127.0 20.3 %collective-permute-start.21 = (f32[512,384]{1,0:T(8,128)}, f32[512,384]{1,0:T(8,128)}, u32[]{:S(2)}, u32[]{:S(2)}) collective-permute-start(f32[512,384]{1,0:T(8,128)} %get-tuple-element.205), channel_id=1, source_target_pairs={{0,1},{1,0},{2,3},{3,2},{4,5},{5,4},{6,7},{7,6},{8,9},{9,8},{10,11... | collective-permute-start | bytes 2359304 | tf_op jit(solution)/shard_map/ppermute | solution.py:954
  135.8 57.0 %collective-permute-start.24 = (f32[384,1536]{1,0:T(8,128)}, f32[384,1536]{1,0:T(8,128)}, u32[]{:S(2)}, u32[]{:S(2)}) collective-permute-start(f32[384,1536]{1,0:T(8,128)} %get-tuple-element.209), channel_id=1, source_target_pairs={{0,4},{2,6},{4,0},{6,2},{8,12},{10,14},{12,8},{14,10},{16,20},{18,... | collective-permute-start | bytes 7077896 | tf_op jit(solution)/shard_map/ppermute | solution.py:951
  147.2 45.6 %collective-permute-start.22 = (f32[384,1152]{1,0:T(8,128)}, f32[384,1152]{1,0:T(8,128)}, u32[]{:S(2)}, u32[]{:S(2)}) collective-permute-start(f32[384,1152]{1,0:T(8,128)} %get-tuple-element.206), channel_id=1, source_target_pairs={{0,8},{2,10},{4,12},{6,14},{8,0},{10,2},{12,4},{14,6},{16,24},{18,... | collective-permute-start | bytes 5308424 | tf_op jit(solution)/shard_map/ppermute | solution.py:951
  148.5 44.3 %collective-permute-start.23 = (f32[768,384]{1,0:T(8,128)}, f32[768,384]{1,0:T(8,128)}, u32[]{:S(2)}, u32[]{:S(2)}) collective-permute-start(f32[768,384]{1,0:T(8,128)} %get-tuple-element.207), channel_id=1, source_target_pairs={{0,1},{1,0},{2,3},{3,2},{4,5},{5,4},{6,7},{7,6},{8,9},{9,8},{10,11... | collective-permute-start | bytes 3538952 | tf_op jit(solution)/shard_map/ppermute | solution.py:954
  149.2 43.7 %collective-permute-start.25 = (f32[512,384]{1,0:T(8,128)}, f32[512,384]{1,0:T(8,128)S(1)}, u32[]{:S(2)}, u32[]{:S(2)}) collective-permute-start(f32[512,384]{1,0:T(8,128)} %get-tuple-element.210), channel_id=1, source_target_pairs={{0,1},{1,0},{2,3},{3,2},{4,5},{5,4},{6,7},{7,6},{8,9},{9,8},{10,11... | collective-permute-start | bytes 2359304 | tf_op jit(solution)/shard_map/ppermute | solution.py:954
  197.7 29.2 %collective-permute-start.26 = (f32[2,1,2,2,48,768]{5,4,3,2,1,0:T(8,128)}, f32[2,1,2,2,48,768]{5,4,3,2,1,0:T(8,128)}, u32[]{:S(2)}, u32[]{:S(2)}) collective-permute-start(f32[2,1,2,2,48,768]{5,4,3,2,1,0:T(8,128)} %get-tuple-element.230), channel_id=1, source_target_pairs={{0,1},{1,0},{2,3},{3,2},{4,5},{5,4},{6,7},{7,6},{8,9},{9,8},{10,11... | collective-permute-start | bytes 3538952 | tf_op jit(solution)/shard_map/ppermute | solution.py:954
  206.4 26.4 %collective-permute-start.34 = (f32[2,2,1,1,48,1408]{5,4,3,2,1,0:T(8,128)}, f32[2,2,1,1,48,1408]{5,4,3,2,1,0:T(8,128)}, u32[]{:S(2)}, u32[]{:S(2)}) collective-permute-start(f32[2,2,1,1,48,1408]{5,4,3,2,1,0:T(8,128)} %get-tuple-element.250), channel_id=1, source_target_pairs={{0,4},{2,6},{4,0},{6,2},{8,12},{10,14},{12,8},{14,10},{16,20},{18,... | collective-permute-start | bytes 3244040 | tf_op jit(solution)/shard_map/ppermute | solution.py:951
  207.7 32.8 %collective-permute-start.32 = (f32[2,1,1,2,48,1536]{5,4,3,2,1,0:T(8,128)}, f32[2,1,1,2,48,1536]{5,4,3,2,1,0:T(8,128)}, u32[]{:S(2)}, u32[]{:S(2)}) collective-permute-start(f32[2,1,1,2,48,1536]{5,4,3,2,1,0:T(8,128)} %combine.12), channel_id=1, source_target_pairs={{0,8},{2,10},{4,12},{6,14},{8,0},{10,2},{12,4},{14,6},{16,24},{18,... | collective-permute-start | bytes 3538952 | tf_op jit(solution)/shard_map/ppermute | solution.py:951
  216.2 25.5 %collective-permute-start.33 = (f32[224,768]{1,0:T(8,128)}, f32[224,768]{1,0:T(8,128)}, u32[]{:S(2)}, u32[]{:S(2)}) collective-permute-start(f32[224,768]{1,0:T(8,128)} %get-tuple-element.258), channel_id=1, source_target_pairs={{0,1},{1,0},{2,3},{3,2},{4,5},{5,4},{6,7},{7,6},{8,9},{9,8},{10,11... | collective-permute-start | bytes 2064392 | tf_op jit(solution)/shard_map/ppermute | solution.py:954
  229.9 21.1 %collective-permute-start.28 = (f32[2,1,1,2,48,1152]{5,4,3,2,1,0:T(8,128)}, f32[2,1,1,2,48,1152]{5,4,3,2,1,0:T(8,128)}, u32[]{:S(2)}, u32[]{:S(2)}) collective-permute-start(f32[2,1,1,2,48,1152]{5,4,3,2,1,0:T(8,128)} %combine.11), channel_id=1, source_target_pairs={{0,4},{2,6},{4,0},{6,2},{8,12},{10,14},{12,8},{14,10},{16,20},{18,... | collective-permute-start | bytes 2654216 | tf_op jit(solution)/shard_map/ppermute | solution.py:951
  231.5 26.6 %collective-permute-start.31 = (f32[2,1,2,1,48,1152]{5,4,3,2,1,0:T(8,128)}, f32[2,1,2,1,48,1152]{5,4,3,2,1,0:T(8,128)S(1)}, u32[]{:S(2)}, u32[]{:S(2)}) collective-permute-start(f32[2,1,2,1,48,1152]{5,4,3,2,1,0:T(8,128)} %get-tuple-element.246), channel_id=1, source_target_pairs={{0,8},{2,10},{4,12},{6,14},{8,0},{10,2},{12,4},{14,6},{16,24},{18,... | collective-permute-start | bytes 2654216 | tf_op jit(solution)/shard_map/ppermute | solution.py:951
  260.7 35.4 %collective-permute-start.40 = (f32[512,768]{1,0:T(8,128)}, f32[512,768]{1,0:T(8,128)}, u32[]{:S(2)}, u32[]{:S(2)}) collective-permute-start(f32[512,768]{1,0:T(8,128)} %get-tuple-element.269), channel_id=1, source_target_pairs={{0,1},{1,0},{2,3},{3,2},{4,5},{5,4},{6,7},{7,6},{8,9},{9,8},{10,11... | collective-permute-start | bytes 4718600 | tf_op jit(solution)/shard_map/ppermute | solution.py:954
  265.0 34.2 %collective-permute-start.37 = (f32[1,1,1,2,48,1920]{5,4,3,2,1,0:T(8,128)}, f32[1,1,1,2,48,1920]{5,4,3,2,1,0:T(8,128)}, u32[]{:S(2)}, u32[]{:S(2)}) collective-permute-start(f32[1,1,1,2,48,1920]{5,4,3,2,1,0:T(8,128)} %combine.16), channel_id=1, source_target_pairs={{0,16},{2,18},{4,20},{6,22},{8,24},{10,26},{12,28},{14,30},{16,0},... | collective-permute-start | bytes 2211848 | tf_op jit(solution)/shard_map/ppermute | solution.py:951
  271.1 27.1 %collective-permute-start.38 = (f32[2,1,1,1,48,1280]{5,4,3,2,1,0:T(8,128)}, f32[2,1,1,1,48,1280]{5,4,3,2,1,0:T(8,128)}, u32[]{:S(2)}, u32[]{:S(2)}) collective-permute-start(f32[2,1,1,1,48,1280]{5,4,3,2,1,0:T(8,128)} %get-tuple-element.267), channel_id=1, source_target_pairs={{0,8},{2,10},{4,12},{6,14},{8,0},{10,2},{12,4},{14,6},{16,24},{18,... | collective-permute-start | bytes 1474568 | tf_op jit(solution)/shard_map/ppermute | solution.py:951
  271.9 26.4 %collective-permute-start.39 = (f32[2,1,1,1,48,1152]{5,4,3,2,1,0:T(8,128)}, f32[2,1,1,1,48,1152]{5,4,3,2,1,0:T(8,128)}, u32[]{:S(2)}, u32[]{:S(2)}) collective-permute-start(f32[2,1,1,1,48,1152]{5,4,3,2,1,0:T(8,128)} %get-tuple-element.268), channel_id=1, source_target_pairs={{0,4},{2,6},{4,0},{6,2},{8,12},{10,14},{12,8},{14,10},{16,20},{18,... | collective-permute-start | bytes 1327112 | tf_op jit(solution)/shard_map/ppermute | solution.py:951
  299.3 21.7 %collective-permute-start.42 = (f32[288,768]{1,0:T(8,128)}, f32[288,768]{1,0:T(8,128)}, u32[]{:S(2)}, u32[]{:S(2)}) collective-permute-start(f32[288,768]{1,0:T(8,128)} %get-tuple-element.283), channel_id=1, source_target_pairs={{0,1},{1,0},{2,3},{3,2},{4,5},{5,4},{6,7},{7,6},{8,9},{9,8},{10,11... | collective-permute-start | bytes 2654216 | tf_op jit(solution)/shard_map/ppermute | solution.py:954
  303.1 22.9 %collective-permute-start.43 = (f32[1,1,1,1,48,2432]{5,4,3,2,1,0:T(8,128)}, f32[1,1,1,1,48,2432]{5,4,3,2,1,0:T(8,128)}, u32[]{:S(2)}, u32[]{:S(2)}) collective-permute-start(f32[1,1,1,1,48,2432]{5,4,3,2,1,0:T(8,128)} %combine.18), channel_id=1, source_target_pairs={{0,16},{2,18},{4,20},{6,22},{8,24},{10,26},{12,28},{14,30},{16,0},... | collective-permute-start | bytes 1400840 | tf_op jit(solution)/shard_map/ppermute | solution.py:951
  (44 other events, 528.6 us)

commit v8 on v7

--- a/solution.py
+++ b/solution.py
@@ -1068,7 +1068,7 @@
     g1_got = cross(g1_send)
 
     g0_send, g1_send, g2_send, dco, d_got = tie((g0_send, g1_send, g2_send, dco, d_got))
-    chunks = tuple(length * k // 32 for k in (7, 16, 9))
+    chunks = tuple(length * k // 32 for k in (7, 17, 8))
     group = rows if rows % 8 == 0 else None
     results = attend_back(
         at, q2, extra, k2, v, context, dco, d_got, live, kind, columns, pick,

time: 333 us -> 333 us (level)
  no operation moved by 1% of the time
where the time goes in v8:
time: 333 us; the launch traced here: 332 us
  Pallas kernels  157 us (47%)
  waiting for transfers between devices  98.9 us (30%)
  starting transfers between devices  39.8 us (12%)
  other arithmetic  22.1 us (7%)
  local copies, waits for them, and re-layouts  12.3 us (4%)
    ppermute x15, waiting for transfers between devices, cross(): return lax.ppermute(value, 'tensor', [(0, 1), (1, 0)])  62.8 us
    ppermute x29, waiting for transfers between devices, swap(): return lax.ppermute(value, 'dp', [(i, i ^ mask) for i in range(devices)])  36.1 us
    pallas_call x1, Pallas kernels, attend_back(): pl.pallas_call(functools.partial(attend_back_kernel, len(chunks), group),...  35.5 us
    pallas_call x10, Pallas kernels, combine(): pl.pallas_call(functools.partial(combine_kernel, plan, len(arrays)), grid...  33.7 us
    ppermute x29, starting transfers between devices, swap(): return lax.ppermute(value, 'dp', [(i, i ^ mask) for i in range(devices)])  23.7 us
    pallas_call x1, Pallas kernels, forward(): pl.pallas_call(forward_kernel, grid_spec=pltpu.PrefetchScalarGridSpec(num...  21.2 us
    pallas_call x2, Pallas kernels, weight_grads(): pl.pallas_call(functools.partial(weight_kernel, plan, len(received), len(...  17.1 us
    pallas_call x1, Pallas kernels, backward(): pl.pallas_call(backward_kernel, grid_spec=pltpu.PrefetchScalarGridSpec(nu...  16.6 us
  transfers between devices with their start and end apart: 44, of which 23 were waited for; matrix products, arithmetic and copies ran while one was open for 8% of the time, Pallas kernels for 41%

profile of v8, /device:TPU:0, one launch (start us, length us, event | category | flops | bytes accessed | tf_op | source)
XLA Modules:
  0.0 331.8 jit_solution(6747892235499728529)
XLA Ops:
  8.0 8.2 %project.1 = (bf16[1024,768]{1,0:T(8,128)(2,1)}, bf16[1024,768]{1,0:T(8,128)(2,1)}, bf16[1024,384]{1,0:T(8,128)(2,1)}) custom-call(bf16[1024,768]{1,0:T(8,128)(2,1)} %bitcast.70, f32[1024,1]{1,0:T(8,128)} %copy.46.kind_ref, bf16[4,768,384]{2,1,0:T(8,128)(2,1)} %wq_hbm.1, f32[4,384]{1,0:T(4,128)} %bq_ref.1, bf16[768,384]{1,0:T(8,128)(2,1)} %wk_hbm.1, ...), custom_call_target="tpu_custom_call" | custom-call | flops 3623878656 | bytes 9437184 | tf_op jit(solution)/shard_map/project/pallas_call | solution.py:87
  18.3 4.1 %collective-permute-done.1 = f32[1536]{0:T(1024)S(1)} collective-permute-done((f32[1536]{0:T(1024)S(1)}, f32[1536]{0:T(1024)S(1)}, u32[]{:S(2)}, u32[]{:S(2)}) %collective-permute-start.1) | collective-permute-done | bytes 6176 | tf_op jit(solution)/shard_map/ppermute | solution.py:954
  28.8 14.0 %attend.1 = (bf16[1024,384]{1,0:T(8,128)(2,1)}, bf16[1024,768]{1,0:T(8,128)(2,1)}) custom-call(bf16[1024,768]{1,0:T(8,128)(2,1)} %get-tuple-element.156.q2_ref, bf16[1024,768]{1,0:T(8,128)(2,1)} %get-tuple-element.157.k2_ref, bf16[1024,384]{1,0:T(8,128)(2,1)} %get-tuple-element.158.v_ref, f32[1024,1]{1,0:T(8,128)} %fusion.1.live_ref), custom_call_target="tpu_custom_call" | custom-call | flops 4026531840 | bytes 7864320 | tf_op jit(solution)/shard_map/attend/pallas_call | solution.py:154
  47.2 3.7 %turn.1.turned_hbm = bf16[768,1024]{1,0:T(8,128)(2,1)} custom-call(bf16[1024,768]{1,0:T(8,128)(2,1)} %bitcast.71), custom_call_target="tpu_custom_call" | custom-call | flops 786432 | bytes 3145728 | tf_op jit(solution)/shard_map/turn/pallas_call | solution.py:880
  52.6 7.9 %collective-permute-done.10.rest_12_ = f32[192,768]{1,0:T(8,128)} collective-permute-done((f32[192,768]{1,0:T(8,128)}, f32[192,768]{1,0:T(8,128)}, u32[]{:S(2)}, u32[]{:S(2)}) %collective-permute-start.10) | collective-permute-done | bytes 589856 | tf_op jit(solution)/shard_map/ppermute | solution.py:951
  62.8 15.5 %collective-permute-done.8.rest_14_ = f32[192,768]{1,0:T(8,128)} collective-permute-done((f32[192,768]{1,0:T(8,128)}, f32[192,768]{1,0:T(8,128)}, u32[]{:S(2)}, u32[]{:S(2)}) %collective-permute-start.8) | collective-permute-done | bytes 589856 | tf_op jit(solution)/shard_map/ppermute | solution.py:954
  85.3 21.2 %forward.1 = (bf16[512,768]{1,0:T(8,128)(2,1)}, f32[512,384]{1,0:T(8,128)}, f32[512,384]{1,0:T(8,128)}, bf16[512,768]{1,0:T(8,128)(2,1)}, bf16[512,768]{1,0:T(8,...) custom-call(s32[4]{0:T(128)} %pad_add_fusion.1.at_ref.bit_ref.y_ref,, ...), custom_call_target="tpu_custom_call" | custom-call | flops 4831838208 | bytes 28311552 | tf_op jit(solution)/shard_map/forward/pallas_call | solution.py:547
  107.3 16.6 %backward.1 = (f32[512,768]{1,0:T(8,128)}, f32[512,384]{1,0:T(8,128)}, f32[512,384]{1,0:T(8,128)}, bf16[512,768]{1,0:T(8,128)(2,1)}, bf16[512,1152]{1,0:T(8,128)...) custom-call(s32[4]{0:T(128)} %pad_add_fusion.1.at_ref.bit_ref.y_ref, ...), custom_call_target="tpu_custom_call" | custom-call | flops 4831838208 | bytes 28311552 | tf_op jit(solution)/shard_map/backward/pallas_call | solution.py:663
  127.5 8.2 %weight_grads.3 = (f32[384,1536]{1,0:T(8,128)}, f32[384,1536]{1,0:T(8,128)}) custom-call(s32[4]{0:T(128)} %pad_add_fusion.1.at_ref.bit_ref.y_ref, bf16[512,768]{1,0:T(8,128)(2,1)} %get-tuple-element.187.d_low_ref.rest_0_, bf16[512,1536]{1,0:T(8,128)(2,1)} %get-tuple-element.208.rest_1_, f32[512,3456]{1,0:T(8,128)} %collective-permute-done.18.rest_4_.rest_2_), custom_call_target="tpu_custom_call" | custom-call | flops 2415919104 | bytes 11010048 | tf_op jit(solution)/shard_map/weight_grads/pallas_call | solution.py:769
  136.9 8.9 %weight_grads.2 = (f32[384,1152]{1,0:T(8,128)}, f32[384,1152]{1,0:T(8,128)}, f32[768,384]{1,0:T(8,128)}, f32[768,384]{1,0:T(8,128)}) custom-call(s32[4]{0:T(128)} %pad_add_fusion.1.at_ref.bit_ref.y_ref, bf16[512,768]{1,0:T(8,128)(2,1)} %get-tuple-element.182.rest_0_, bf16[512,768]{1,0:T(8,128)(2,1)} %get-tuple-element.190.rest_1_, ...), custom_call_target="tpu_custom_call" | custom-call | flops 3019898880 | bytes 13762560 | tf_op jit(solution)/shard_map/weight_grads/pallas_call | solution.py:769
  151.3 35.5 %attend_back.1 = (f32[224,768]{1,0:T(8,128)}, f32[544,768]{1,0:T(8,128)}, f32[256,768]{1,0:T(8,128)}, f32[384,1152]{1,0:T(8,128)}, f32[384,1152]{1,0:T(8,128)}, ...) custom-call(s32[4]{0:T(128)} %pad_add_fusion.1.at_ref.bit_ref.y_ref, bf16[1024,768]{1,0:T(8,128)(2,1)} %get-tuple-element.156.q2_ref, ...), custom_call_target="tpu_custom_call" | custom-call | flops 8053063680 | bytes 15728640 | tf_op jit(solution)/shard_map/attend_back/pallas_call | solution.py:333
  186.8 5.8 %collective-permute-done.25.second_ref = f32[512,384]{1,0:T(8,128)S(1)} collective-permute-done((f32[512,384]{1,0:T(8,128)}, f32[512,384]{1,0:T(8,128)S(1)}, u32[]{:S(2)}, u32[]{:S(2)}) %collective-permute-start.25) | collective-permute-done | bytes 786464 | tf_op jit(solution)/shard_map/ppermute | solution.py:954
  193.8 3.7 %combine.10 = (f32[2,1,2,2,48,768]{5,4,3,2,1,0:T(8,128)}, f32[2,1,2,2,48,384]{5,4,3,2,1,0:T(8,128)}) custom-call(s32[4]{0:T(128)} %pad_add_fusion.bits_ref, f32[2,1,2,2,48,1152]{5,4,3,2,1,0:T(8,128)} %bitcast.66, f32[2,1,2,2,48,1152]{5,4,3,2,1,0:T(8,128)} %bitcast.15.rest_1_.rest_10_, f32[2,2,2,2,48,384]{5,4,3,2,1,0:T(8,128)} %bitcast.73, ...), custom_call_target="tpu_custom_call" | custom-call | flops 3538944 | bytes 7077888 | tf_op jit(solution)/shard_map/combine/pallas_call | solution.py:854
  199.0 3.4 %combine.12 = f32[2,1,1,2,48,1536]{5,4,3,2,1,0:T(8,128)} custom-call(s32[4]{0:T(128)} %pad_add_fusion.bits_ref, f32[2,2,1,2,48,1536]{5,4,3,2,1,0:T(8,128)} %bitcast.58, f32[2,2,1,2,48,1536]{5,4,3,2,1,0:T(8,128)} %bitcast.22.rest_1_.rest_6_.rest_16_), custom_call_target="tpu_custom_call" | custom-call | flops 2359296 | bytes 4718592 | tf_op jit(solution)/shard_map/combine/pallas_call | solution.py:854
  202.4 3.8 %combine.13 = (f32[2,2,1,1,48,1408]{5,4,3,2,1,0:T(8,128)}, f32[2,1,2,1,48,1152]{5,4,3,2,1,0:T(8,128)}) custom-call(s32[4]{0:T(128)} %pad_add_fusion.bits_ref, f32[2,2,2,1,48,1408]{5,4,3,2,1,0:T(8,128)} %bitcast.53, f32[2,2,2,1,48,1408]{5,4,3,2,1,0:T(8,128)} %collective-permute-done.29.rest_1_.rest_5_, f32[2,2,2,1,48,1152]{5,4,3,2,1,0:T(8,128)} %bitcast.62, ...), custom_call_target="tpu_custom_call" | custom-call | flops 3932160 | bytes 7864320 | tf_op jit(solution)/shard_map/combine/pallas_call | solution.py:854
  209.1 5.8 %collective-permute-done.27 = f32[2,1,2,2,48,384]{5,4,3,2,1,0:T(8,128)S(1)} collective-permute-done((f32[2,1,2,2,48,384]{5,4,3,2,1,0:T(8,128)}, f32[2,1,2,2,48,384]{5,4,3,2,1,0:T(8,128)S(1)}, u32[]{:S(2)}, u32[]{:S(2)}) %collective-permute-start.27) | collective-permute-done | bytes 589856 | tf_op jit(solution)/shard_map/ppermute | solution.py:951
  219.2 7.6 %collective-permute-done.26.rest_2_.rest_11_ = f32[2,1,2,2,48,768]{5,4,3,2,1,0:T(8,128)} collective-permute-done((f32[2,1,2,2,48,768]{5,4,3,2,1,0:T(8,128)}, f32[2,1,2,2,48,768]{5,4,3,2,1,0:T(8,128)}, u32[]{:S(2)}, u32[]{:S(2)}) %collective-permute-start.26) | collective-permute-done | bytes 1179680 | tf_op jit(solution)/shard_map/ppermute | solution.py:954
  246.5 4.3 %collective-permute-done.28.rest_3_.rest_12_ = f32[2,1,1,2,48,1152]{5,4,3,2,1,0:T(8,128)} collective-permute-done((f32[2,1,1,2,48,1152]{5,4,3,2,1,0:T(8,128)}, f32[2,1,1,2,48,1152]{5,4,3,2,1,0:T(8,128)}, u32[]{:S(2)}, u32[]{:S(2)}) %collective-permute-start.28) | collective-permute-done | bytes 884768 | tf_op jit(solution)/shard_map/ppermute | solution.py:951
  250.9 7.1 %collective-permute-done.31.rest_6_.rest_2_ = f32[2,1,2,1,48,1152]{5,4,3,2,1,0:T(8,128)S(1)} collective-permute-done((f32[2,1,2,1,48,1152]{5,4,3,2,1,0:T(8,128)}, f32[2,1,2,1,48,1152]{5,4,3,2,1,0:T(8,128)S(1)}, u32[]{:S(2)}, u32[]{:S(2)}) %collective-permute-start.31) | collective-permute-done | bytes 884768 | tf_op jit(solution)/shard_map/ppermute | solution.py:951
  267.5 3.4 %combine.17 = (f32[2,1,1,1,48,1280]{5,4,3,2,1,0:T(8,128)}, f32[2,1,1,1,48,1152]{5,4,3,2,1,0:T(8,128)}) custom-call(s32[4]{0:T(128)} %pad_add_fusion.bits_ref, f32[2,2,2,1,48,1408]{5,4,3,2,1,0:T(8,128)} %bitcast.55, f32[2,2,2,1,48,1408]{5,4,3,2,1,0:T(8,128)} %collective-permute-done.29.rest_1_.rest_5_, ...), custom_call_target="tpu_custom_call" | custom-call | flops 2850816 | bytes 5701632 | tf_op jit(solution)/shard_map/combine/pallas_call | solution.py:854
  272.9 6.8 %place_rows.1 = bf16[1024,768]{1,0:T(8,128)(2,1)} custom-call(s32[4]{0:T(128)} %pad_add_fusion.1.at_ref.bit_ref.y_ref, bf16[512,768]{1,0:T(8,128)(2,1)} %get-tuple-element.271.own_ref, f32[512,384]{1,0:T(8,128)} %copy-done.4, f32[512,384]{1,0:T(8,128)} %copy-done.5), custom_call_target="tpu_custom_call" | custom-call | flops 393216 | bytes 4718592 | tf_op jit(solution)/shard_map/place_rows/pallas_call | solution.py:903
  279.7 18.4 %collective-permute-done.40 = f32[544,768]{1,0:T(8,128)} collective-permute-done((f32[544,768]{1,0:T(8,128)}, f32[544,768]{1,0:T(8,128)}, u32[]{:S(2)}, u32[]{:S(2)}) %collective-permute-start.40) | collective-permute-done | bytes 1671200 | tf_op jit(solution)/shard_map/ppermute | solution.py:954
  307.2 4.7 %combine.19 = (f32[1,1,1,1,48,2432]{5,4,3,2,1,0:T(8,128)}, f32[1,1,1,1,48,1920]{5,4,3,2,1,0:T(8,128)}, f32[1,1,1,1,48,1920]{5,4,3,2,1,0:T(8,128)}) custom-call(s32[4]{0:T(128)} %pad_add_fusion.bits_ref, f32[2,2,2,1,48,1152]{5,4,3,2,1,0:T(8,128)} %bitcast.65, f32[2,2,2,1,48,1152]{5,4,3,2,1,0:T(8,128)} %collective-permute-done.30.rest_3_.rest_5_.rest_1_, ...), custom_call_target="tpu_custom_call" | custom-call | flops 5283840 | bytes 10567680 | tf_op jit(solution)/shard_map/combine/pallas_call | solution.py:854
  312.0 6.7 %collective-permute-done.42 = f32[256,768]{1,0:T(8,128)} collective-permute-done((f32[256,768]{1,0:T(8,128)}, f32[256,768]{1,0:T(8,128)}, u32[]{:S(2)}, u32[]{:S(2)}) %collective-permute-start.42) | collective-permute-done | bytes 786464 | tf_op jit(solution)/shard_map/ppermute | solution.py:954
  (187 shorter events, 104.7 us)
Async XLA Ops:
  2.7 19.7 %collective-permute-start = (f32[240,768]{1,0:T(8,128)S(1)}, f32[240,768]{1,0:T(8,128)}, u32[]{:S(2)}, u32[]{:S(2)}) collective-permute-start(f32[240,768]{1,0:T(8,128)S(1)} %maximum_convert_fusion), channel_id=1, source_target_pairs={{0,1},{1,0},{2,3},{3,2},{4,5},{5,4},{6,7},{7,6},{8,9},{9,8},{10,11... | collective-permute-start | bytes 2211848 | tf_op jit(solution)/shard_map/ppermute | solution.py:954
  22.4 22.3 %collective-permute-start.4 = (f32[240,768]{1,0:T(8,128)}, f32[240,768]{1,0:T(8,128)S(1)}, u32[]{:S(2)}, u32[]{:S(2)}) collective-permute-start(f32[240,768]{1,0:T(8,128)} %collective-permute-done.rest_0_), channel_id=1, source_target_pairs={{0,8},{2,10},{4,12},{6,14},{8,0},{10,2},{12,4},{14,6},{16,24},{18,... | collective-permute-start | bytes 2211848 | tf_op jit(solution)/shard_map/ppermute | solution.py:951
  24.2 20.5 %collective-permute-start.3 = (f32[240,768]{1,0:T(8,128)}, f32[240,768]{1,0:T(8,128)}, u32[]{:S(2)}, u32[]{:S(2)}) collective-permute-start(f32[240,768]{1,0:T(8,128)} %collective-permute-done.rest_0_), channel_id=1, source_target_pairs={{0,4},{2,6},{4,0},{6,2},{8,12},{10,14},{12,8},{14,10},{16,20},{18,... | collective-permute-start | bytes 2211848 | tf_op jit(solution)/shard_map/ppermute | solution.py:951
  25.7 19.0 %collective-permute-start.2 = (f32[240,768]{1,0:T(8,128)}, f32[240,768]{1,0:T(8,128)}, u32[]{:S(2)}, u32[]{:S(2)}) collective-permute-start(f32[240,768]{1,0:T(8,128)} %collective-permute-done.rest_0_), channel_id=1, source_target_pairs={{0,2},{2,0},{4,6},{6,4},{8,10},{10,8},{12,14},{14,12},{16,18},{18,... | collective-permute-start | bytes 2211848 | tf_op jit(solution)/shard_map/ppermute | solution.py:951
  45.8 32.4 %collective-permute-start.6 = (f32[512,384]{1,0:T(8,128)}, f32[512,384]{1,0:T(8,128)S(1)}, u32[]{:S(2)}, u32[]{:S(2)}) collective-permute-start(f32[512,384]{1,0:T(8,128)} %dynamic-slice_convert_fusion), channel_id=1, source_target_pairs={{0,1},{1,0},{2,3},{3,2},{4,5},{5,4},{6,7},{7,6},{8,9},{9,8},{10,11... | collective-permute-start | bytes 2359304 | tf_op jit(solution)/shard_map/ppermute | solution.py:954
  50.9 27.3 %collective-permute-start.7 = (f32[240,768]{1,0:T(8,128)}, f32[240,768]{1,0:T(8,128)S(1)}, u32[]{:S(2)}, u32[]{:S(2)}) collective-permute-start(f32[240,768]{1,0:T(8,128)} %copy-done.6), channel_id=1, source_target_pairs={{0,4},{2,6},{4,0},{6,2},{8,12},{10,14},{12,8},{14,10},{16,20},{18,... | collective-permute-start | bytes 2211848 | tf_op jit(solution)/shard_map/ppermute | solution.py:951
  106.5 20.2 %collective-permute-start.18 = (f32[512,3456]{1,0:T(8,128)}, f32[512,3456]{1,0:T(8,128)}, u32[]{:S(2)}, u32[]{:S(2)}) collective-permute-start(f32[512,3456]{1,0:T(8,128)} %get-tuple-element.193), channel_id=1, source_target_pairs={{0,2},{2,0},{4,6},{6,4},{8,10},{10,8},{12,14},{14,12},{16,18},{18,... | collective-permute-start | bytes 21233672 | tf_op jit(solution)/shard_map/ppermute | solution.py:951
  106.7 20.0 %collective-permute-start.19 = (f32[512,384]{1,0:T(8,128)}, f32[512,384]{1,0:T(8,128)S(1)}, u32[]{:S(2)}, u32[]{:S(2)}) collective-permute-start(f32[512,384]{1,0:T(8,128)} %get-tuple-element.194), channel_id=1, source_target_pairs={{0,1},{1,0},{2,3},{3,2},{4,5},{5,4},{6,7},{7,6},{8,9},{9,8},{10,11... | collective-permute-start | bytes 2359304 | tf_op jit(solution)/shard_map/ppermute | solution.py:954
  126.8 20.3 %collective-permute-start.21 = (f32[512,384]{1,0:T(8,128)}, f32[512,384]{1,0:T(8,128)}, u32[]{:S(2)}, u32[]{:S(2)}) collective-permute-start(f32[512,384]{1,0:T(8,128)} %get-tuple-element.205), channel_id=1, source_target_pairs={{0,1},{1,0},{2,3},{3,2},{4,5},{5,4},{6,7},{7,6},{8,9},{9,8},{10,11... | collective-permute-start | bytes 2359304 | tf_op jit(solution)/shard_map/ppermute | solution.py:954
  135.7 57.0 %collective-permute-start.24 = (f32[384,1536]{1,0:T(8,128)}, f32[384,1536]{1,0:T(8,128)}, u32[]{:S(2)}, u32[]{:S(2)}) collective-permute-start(f32[384,1536]{1,0:T(8,128)} %get-tuple-element.209), channel_id=1, source_target_pairs={{0,4},{2,6},{4,0},{6,2},{8,12},{10,14},{12,8},{14,10},{16,20},{18,... | collective-permute-start | bytes 7077896 | tf_op jit(solution)/shard_map/ppermute | solution.py:951
  147.1 45.6 %collective-permute-start.22 = (f32[384,1152]{1,0:T(8,128)}, f32[384,1152]{1,0:T(8,128)}, u32[]{:S(2)}, u32[]{:S(2)}) collective-permute-start(f32[384,1152]{1,0:T(8,128)} %get-tuple-element.206), channel_id=1, source_target_pairs={{0,8},{2,10},{4,12},{6,14},{8,0},{10,2},{12,4},{14,6},{16,24},{18,... | collective-permute-start | bytes 5308424 | tf_op jit(solution)/shard_map/ppermute | solution.py:951
  148.4 44.3 %collective-permute-start.23 = (f32[768,384]{1,0:T(8,128)}, f32[768,384]{1,0:T(8,128)}, u32[]{:S(2)}, u32[]{:S(2)}) collective-permute-start(f32[768,384]{1,0:T(8,128)} %get-tuple-element.207), channel_id=1, source_target_pairs={{0,1},{1,0},{2,3},{3,2},{4,5},{5,4},{6,7},{7,6},{8,9},{9,8},{10,11... | collective-permute-start | bytes 3538952 | tf_op jit(solution)/shard_map/ppermute | solution.py:954
  149.0 43.7 %collective-permute-start.25 = (f32[512,384]{1,0:T(8,128)}, f32[512,384]{1,0:T(8,128)S(1)}, u32[]{:S(2)}, u32[]{:S(2)}) collective-permute-start(f32[512,384]{1,0:T(8,128)} %get-tuple-element.210), channel_id=1, source_target_pairs={{0,1},{1,0},{2,3},{3,2},{4,5},{5,4},{6,7},{7,6},{8,9},{9,8},{10,11... | collective-permute-start | bytes 2359304 | tf_op jit(solution)/shard_map/ppermute | solution.py:954
  197.6 29.2 %collective-permute-start.26 = (f32[2,1,2,2,48,768]{5,4,3,2,1,0:T(8,128)}, f32[2,1,2,2,48,768]{5,4,3,2,1,0:T(8,128)}, u32[]{:S(2)}, u32[]{:S(2)}) collective-permute-start(f32[2,1,2,2,48,768]{5,4,3,2,1,0:T(8,128)} %get-tuple-element.230), channel_id=1, source_target_pairs={{0,1},{1,0},{2,3},{3,2},{4,5},{5,4},{6,7},{7,6},{8,9},{9,8},{10,11... | collective-permute-start | bytes 3538952 | tf_op jit(solution)/shard_map/ppermute | solution.py:954
  206.2 26.4 %collective-permute-start.34 = (f32[2,2,1,1,48,1408]{5,4,3,2,1,0:T(8,128)}, f32[2,2,1,1,48,1408]{5,4,3,2,1,0:T(8,128)}, u32[]{:S(2)}, u32[]{:S(2)}) collective-permute-start(f32[2,2,1,1,48,1408]{5,4,3,2,1,0:T(8,128)} %get-tuple-element.250), channel_id=1, source_target_pairs={{0,4},{2,6},{4,0},{6,2},{8,12},{10,14},{12,8},{14,10},{16,20},{18,... | collective-permute-start | bytes 3244040 | tf_op jit(solution)/shard_map/ppermute | solution.py:951
  207.5 32.8 %collective-permute-start.32 = (f32[2,1,1,2,48,1536]{5,4,3,2,1,0:T(8,128)}, f32[2,1,1,2,48,1536]{5,4,3,2,1,0:T(8,128)}, u32[]{:S(2)}, u32[]{:S(2)}) collective-permute-start(f32[2,1,1,2,48,1536]{5,4,3,2,1,0:T(8,128)} %combine.12), channel_id=1, source_target_pairs={{0,8},{2,10},{4,12},{6,14},{8,0},{10,2},{12,4},{14,6},{16,24},{18,... | collective-permute-start | bytes 3538952 | tf_op jit(solution)/shard_map/ppermute | solution.py:951
  216.0 25.5 %collective-permute-start.33 = (f32[224,768]{1,0:T(8,128)}, f32[224,768]{1,0:T(8,128)}, u32[]{:S(2)}, u32[]{:S(2)}) collective-permute-start(f32[224,768]{1,0:T(8,128)} %get-tuple-element.258), channel_id=1, source_target_pairs={{0,1},{1,0},{2,3},{3,2},{4,5},{5,4},{6,7},{7,6},{8,9},{9,8},{10,11... | collective-permute-start | bytes 2064392 | tf_op jit(solution)/shard_map/ppermute | solution.py:954
  229.8 21.1 %collective-permute-start.28 = (f32[2,1,1,2,48,1152]{5,4,3,2,1,0:T(8,128)}, f32[2,1,1,2,48,1152]{5,4,3,2,1,0:T(8,128)}, u32[]{:S(2)}, u32[]{:S(2)}) collective-permute-start(f32[2,1,1,2,48,1152]{5,4,3,2,1,0:T(8,128)} %combine.11), channel_id=1, source_target_pairs={{0,4},{2,6},{4,0},{6,2},{8,12},{10,14},{12,8},{14,10},{16,20},{18,... | collective-permute-start | bytes 2654216 | tf_op jit(solution)/shard_map/ppermute | solution.py:951
  231.3 26.6 %collective-permute-start.31 = (f32[2,1,2,1,48,1152]{5,4,3,2,1,0:T(8,128)}, f32[2,1,2,1,48,1152]{5,4,3,2,1,0:T(8,128)S(1)}, u32[]{:S(2)}, u32[]{:S(2)}) collective-permute-start(f32[2,1,2,1,48,1152]{5,4,3,2,1,0:T(8,128)} %get-tuple-element.246), channel_id=1, source_target_pairs={{0,8},{2,10},{4,12},{6,14},{8,0},{10,2},{12,4},{14,6},{16,24},{18,... | collective-permute-start | bytes 2654216 | tf_op jit(solution)/shard_map/ppermute | solution.py:951
  260.6 37.5 %collective-permute-start.40 = (f32[544,768]{1,0:T(8,128)}, f32[544,768]{1,0:T(8,128)}, u32[]{:S(2)}, u32[]{:S(2)}) collective-permute-start(f32[544,768]{1,0:T(8,128)} %get-tuple-element.269), channel_id=1, source_target_pairs={{0,1},{1,0},{2,3},{3,2},{4,5},{5,4},{6,7},{7,6},{8,9},{9,8},{10,11... | collective-permute-start | bytes 5013512 | tf_op jit(solution)/shard_map/ppermute | solution.py:954
  264.9 35.4 %collective-permute-start.37 = (f32[1,1,1,2,48,1920]{5,4,3,2,1,0:T(8,128)}, f32[1,1,1,2,48,1920]{5,4,3,2,1,0:T(8,128)}, u32[]{:S(2)}, u32[]{:S(2)}) collective-permute-start(f32[1,1,1,2,48,1920]{5,4,3,2,1,0:T(8,128)} %combine.16), channel_id=1, source_target_pairs={{0,16},{2,18},{4,20},{6,22},{8,24},{10,26},{12,28},{14,30},{16,0},... | collective-permute-start | bytes 2211848 | tf_op jit(solution)/shard_map/ppermute | solution.py:951
  270.9 29.3 %collective-permute-start.38 = (f32[2,1,1,1,48,1280]{5,4,3,2,1,0:T(8,128)}, f32[2,1,1,1,48,1280]{5,4,3,2,1,0:T(8,128)}, u32[]{:S(2)}, u32[]{:S(2)}) collective-permute-start(f32[2,1,1,1,48,1280]{5,4,3,2,1,0:T(8,128)} %get-tuple-element.267), channel_id=1, source_target_pairs={{0,8},{2,10},{4,12},{6,14},{8,0},{10,2},{12,4},{14,6},{16,24},{18,... | collective-permute-start | bytes 1474568 | tf_op jit(solution)/shard_map/ppermute | solution.py:951
  271.7 28.5 %collective-permute-start.39 = (f32[2,1,1,1,48,1152]{5,4,3,2,1,0:T(8,128)}, f32[2,1,1,1,48,1152]{5,4,3,2,1,0:T(8,128)}, u32[]{:S(2)}, u32[]{:S(2)}) collective-permute-start(f32[2,1,1,1,48,1152]{5,4,3,2,1,0:T(8,128)} %get-tuple-element.268), channel_id=1, source_target_pairs={{0,4},{2,6},{4,0},{6,2},{8,12},{10,14},{12,8},{14,10},{16,20},{18,... | collective-permute-start | bytes 1327112 | tf_op jit(solution)/shard_map/ppermute | solution.py:951
  304.6 21.9 %collective-permute-start.43 = (f32[1,1,1,1,48,2432]{5,4,3,2,1,0:T(8,128)}, f32[1,1,1,1,48,2432]{5,4,3,2,1,0:T(8,128)}, u32[]{:S(2)}, u32[]{:S(2)}) collective-permute-start(f32[1,1,1,1,48,2432]{5,4,3,2,1,0:T(8,128)} %combine.18), channel_id=1, source_target_pairs={{0,16},{2,18},{4,20},{6,22},{8,24},{10,26},{12,28},{14,30},{16,0},... | collective-permute-start | bytes 1400840 | tf_op jit(solution)/shard_map/ppermute | solution.py:951
  (44 other events, 521.3 us)
